TPU v7x, 256 devices: a whole 4x4x8 slice. The times are simulated.
256 devices in a mesh: row: 16 (over x_lo, y, core), col: 16 (over x_hi, z).
Axes of the slice: x: 4 (x_hi: 2, x_lo: 2; x = x_hi * 2 + x_lo), y: 4, z: 8, core: 2. Of those that a mesh axis runs over, the one named last changes fastest.
Arguments:
- tokens: bfloat16 [512, 8192], P('col', 'row'), may hold values from -6 to 6
- cotangent: bfloat16 [512, 8192], P('col', 'row'), may hold values from -6 to 6
- gate_weight: bfloat16 [8192, 28672], P('row', 'col'), may hold values from -0.09375 to 0.09375
- up_weight: bfloat16 [8192, 28672], P('row', 'col'), may hold values from -0.09375 to 0.09375
- down_weight: bfloat16 [28672, 8192], P('col', 'row'), may hold values from -0.0625 to 0.0625
- gate_mask: int32 [64, 224], P('row', 'col'), may hold values 0 or 1
- up_mask: int32 [64, 224], P('row', 'col'), may hold values 0 or 1
- down_mask: int32 [224, 64], P('col', 'row'), may hold values 0 or 1
Outputs:
- output: bfloat16 [512, 8192], P('col', 'row')
- d_tokens: bfloat16 [512, 8192], P('col', 'row')
- grad_gate: bfloat16 [8192, 28672], P('row', 'col')
- grad_up: bfloat16 [8192, 28672], P('row', 'col')
- grad_down: bfloat16 [28672, 8192], P('col', 'row')
Inputs may be any that keep to these rules, and one draw needn't show every extreme that they name: `gate_mask`: 1 keeps a block, 0 prunes it. `up_mask`: 1 keeps a block, 0 prunes it. `down_mask`: 1 keeps a block, 0 prunes it.
All inputs are finite; a program needn't handle non-finite values.
Results may differ from a plain program's by a relative error of at most 0.0049.
Values may be sent and summed in bfloat16 or wider, within the bound.
No kernel may reach another device: no remote copies, remote signals or barrier semaphores. Data moves between devices by JAX's collectives and lax.ppermute only.
A program may use at most 128 MiB of HBM per device.

v0:
```python
import jax
import jax.numpy as jnp
from jax import lax
from jax.sharding import PartitionSpec as P


def masked(weight, block_mask):
    block_rows, block_cols = block_mask.shape
    total_rows, total_cols = weight.shape
    shaped = weight.reshape(
        block_rows, total_rows // block_rows, block_cols, total_cols // block_cols
    )
    return (shaped * block_mask.astype(weight.dtype)[:, None, :, None]).reshape(
        total_rows, total_cols
    )


def right_product(left, right):
    return lax.dot_general(
        left, right, (((1,), (1,)), ((), ())), preferred_element_type=jnp.float32
    )


def left_product(left, right):
    return lax.dot_general(
        left, right, (((0,), (0,)), ((), ())), preferred_element_type=jnp.float32
    )


def per_device(
    tokens, cotangent, gate_weight, up_weight, down_weight, gate_mask, up_mask, down_mask
):
    gate_eff = masked(gate_weight, gate_mask)
    up_eff = masked(up_weight, up_mask)
    down_eff = masked(down_weight, down_mask)
    rows_all, cot_all = (
        lax.all_gather(tokens, "col", axis=0, tiled=True),
        lax.all_gather(cotangent, "col", axis=0, tiled=True),
    )
    gate_part = jnp.dot(rows_all, gate_eff, preferred_element_type=jnp.float32)
    up_part = jnp.dot(rows_all, up_eff, preferred_element_type=jnp.float32)
    row_share = rows_all.shape[0] // lax.axis_size("row")
    gate_full, up_full = lax.psum((gate_part, up_part), "row")
    activated_full = gate_full * jax.nn.sigmoid(gate_full)
    hidden_all = (activated_full * up_full).astype(jnp.bfloat16)
    row_start = lax.axis_index("row") * row_share
    gate_share = lax.dynamic_slice_in_dim(gate_full, row_start, row_share, 0)
    up_share = lax.dynamic_slice_in_dim(up_full, row_start, row_share, 0)
    output = lax.psum_scatter(
        jnp.dot(hidden_all, down_eff, preferred_element_type=jnp.float32),
        "col",
        scatter_dimension=0,
        tiled=True,
    ).astype(jnp.bfloat16)
    hidden_part = right_product(cot_all, down_eff)
    hidden_grad = lax.psum_scatter(hidden_part, "row", scatter_dimension=0, tiled=True)
    sigmoid_gate = jax.nn.sigmoid(gate_share)
    activated = gate_share * sigmoid_gate
    gate_grad = (
        hidden_grad * up_share * sigmoid_gate * (1.0 + gate_share * (1.0 - sigmoid_gate))
    ).astype(jnp.bfloat16)
    up_grad = (hidden_grad * activated).astype(jnp.bfloat16)
    gate_grad_all, up_grad_all = (
        lax.all_gather(gate_grad, "row", axis=0, tiled=True),
        lax.all_gather(up_grad, "row", axis=0, tiled=True),
    )
    grad_down = masked(left_product(hidden_all, cot_all), down_mask).astype(jnp.bfloat16)
    grad_gate = masked(left_product(rows_all, gate_grad_all), gate_mask).astype(jnp.bfloat16)
    grad_up = masked(left_product(rows_all, up_grad_all), up_mask).astype(jnp.bfloat16)
    d_tokens = lax.psum_scatter(
        right_product(gate_grad_all, gate_eff) + right_product(up_grad_all, up_eff),
        "col",
        scatter_dimension=0,
        tiled=True,
    ).astype(jnp.bfloat16)
    return (output, d_tokens, grad_gate, grad_up, grad_down)


def solution(mesh):
    in_specs = (
        P("col", "row"),
        P("col", "row"),
        P("row", "col"),
        P("row", "col"),
        P("col", "row"),
        P("row", "col"),
        P("row", "col"),
        P("col", "row"),
    )
    out_specs = (
        P("col", "row"),
        P("col", "row"),
        P("row", "col"),
        P("row", "col"),
        P("col", "row"),
    )
    return jax.shard_map(
        per_device, mesh=mesh, in_specs=in_specs, out_specs=out_specs, check_vma=False
    )
```

profile of v0, /device:TPU:8, one launch (start us, length us, event | category | flops | bytes accessed | tf_op | source)
XLA Modules:
  0.0 772.1 jit_solution(7239612085857985313)
XLA Ops:
  7.2 47.2 %all_gather.12 = bf16[512,512]{1,0:T(8,128)(2,1)S(1)} all-gather(bf16[32,512]{1,0:T(8,128)(2,1)} %param.8), channel_id=1, replica_groups=mesh['row'=16,'col'=16] {'col'}, dimensions={0}, use_global_device_ids=true | all-gather | bytes 557056 | tf_op jit(solution)/shard_map/all_gather | solution.py:37
  54.4 0.8 fusion.6
  55.2 0.1 copy.44
  55.3 2.8 copy.45
  58.2 0.1 copy.41
  58.3 4.4 copy.42
  62.6 0.5 mul.97
  63.2 3.1 convolution_bitcast_fusion.1
  66.3 0.5 mul.93
  66.9 1.2 copy-done.4
  68.1 3.1 convolution_bitcast_fusion.2
  71.2 0.6 copy-done.12
  71.9 0.1 copy.47
  72.0 38.3 %all_gather.13 = bf16[512,512]{1,0:T(8,128)(2,1)S(1)} all-gather(bf16[32,512]{1,0:T(8,128)(2,1)S(1)} %copy-done.10), channel_id=1, replica_groups=mesh['row'=16,'col'=16] {'col'}, dimensions={0}, use_global_device_ids=true | all-gather | bytes 557056 | tf_op jit(solution)/shard_map/all_gather | solution.py:38
  110.3 0.5 mul.101
  110.8 4.6 convolution_bitcast_fusion
  115.4 5.2 copy.57
  120.6 0.0 all-gather.3.cloned.1.call-start
  120.7 86.0 %all-reduce.3.cloned.1.call-done = (f32[512,1792]{1,0:T(8,128)}, f32[512,1792]{1,0:T(8,128)}) async-done(((f32[512,1792]{1,0:T(8,128)}, f32[512,1792]{1,0:T(8,128)}), (f32[512,1792]{1,0:T(8,128)}, f32[512,1792]{1,0:T(8,128)})) %all-reduce.3.cloned.1.call-update) | async-done | bytes 7340048 | tf_op jit(solution)/shard_map/psum | solution.py:43
  206.7 71.8 %reduce-scatter.10.cloned.1.call-done = f32[32,1792]{1,0:T(8,128)} async-done(((f32[512,1792]{1,0:T(8,128)}), f32[32,1792]{1,0:T(8,128)}) %reduce-scatter.10.cloned.1.call-update) | async-done | bytes 229392 | tf_op jit(solution)/shard_map/reduce_scatter | solution.py:56
  278.5 2.0 multiply_convert_fusion.1
  280.5 0.5 all-gather.5.cloned.1.call-update
  281.1 4.3 multiply_convert_fusion
  285.4 1.3 copy-done.5
  286.7 2.1 fusion.4
  288.9 0.2 reduce-scatter.8.cloned.1.call-start
  289.1 29.6 %all-gather.3.cloned.1.call-done = bf16[512,1792]{1,0:T(8,128)(2,1)} async-done(((bf16[32,1792]{1,0:T(8,128)(2,1)}), bf16[512,1792]{1,0:T(8,128)(2,1)}) %all-gather.3.cloned.1.call-update) | async-done | bytes 1835024 | tf_op jit(solution)/shard_map/all_gather | solution.py:64
  318.7 4.7 fusion.3
  323.5 33.0 %all-gather.5.cloned.1.call-done = bf16[512,1792]{1,0:T(8,128)(2,1)} async-done(((bf16[32,1792]{1,0:T(8,128)(2,1)}), bf16[512,1792]{1,0:T(8,128)(2,1)}) %all-gather.5.cloned.1.call-update) | async-done | bytes 1835024 | tf_op jit(solution)/shard_map/all_gather | solution.py:65
  356.5 4.5 convolution_add_fusion
  360.9 0.1 copy.50
  361.0 0.1 copy.51
  361.1 0.1 copy.52
  361.2 0.5 mul.117
  361.8 1.0 copy-done.6
  362.7 2.4 fusion
  365.1 196.2 %reduce-scatter.6.cloned.1.call-done = f32[32,512]{1,0:T(8,128)} async-done(((f32[512,512]{1,0:T(8,128)}), f32[32,512]{1,0:T(8,128)}) %reduce-scatter.6.cloned.1.call-update) | async-done | bytes 65552 | tf_op jit(solution)/shard_map/reduce_scatter | solution.py:49
  561.3 1.5 convert_element_type.46
  562.8 0.5 mul.111
  563.3 1.0 copy-done.8
  564.3 1.2 fusion.2
  565.5 2.4 copy.53
  567.9 0.5 mul.114
  568.4 1.0 copy-done.9
  569.4 1.2 fusion.1
  570.5 2.4 copy.54
  572.9 190.9 %reduce-scatter.8.cloned.1.call-done = f32[32,512]{1,0:T(8,128)} async-done(((f32[512,512]{1,0:T(8,128)}), f32[32,512]{1,0:T(8,128)}) %reduce-scatter.8.cloned.1.call-update) | async-done | bytes 65552 | tf_op jit(solution)/shard_map/reduce_scatter | solution.py:70
  763.8 1.5 convert_element_type.49
  (31 shorter events, 0.3 us)
Async XLA Ops:
  7.2 199.5 %all-reduce.3.cloned.1.call-start = ((), (), s32[]{:S(2)}) async-start(), calls=%async_computation.8 | async-start | bytes 14680064 | tf_op jit(solution)/shard_map/psum | solution.py:43
  55.3 2.8 copy-start.11
  58.1 5.0 copy-start
  63.2 3.1 copy-start.2
  66.3 1.8 copy-start.3
  66.9 1.2 copy-start.4
  71.2 0.7 copy-start.12
  71.2 0.8 copy-start.10
  71.2 207.3 %reduce-scatter.10.cloned.1.call-start = ((), (), s32[]{:S(2)}) async-start(), calls=%async_computation.7 | async-start | bytes 3899392 | tf_op jit(solution)/shard_map/reduce_scatter | solution.py:56
  120.6 198.1 %all-gather.3.cloned.1.call-start = ((), (), s32[]{:S(2)}) async-start(), calls=%async_computation.4 | async-start | bytes 1949696 | tf_op jit(solution)/shard_map/all_gather | solution.py:64
  280.5 76.0 %all-gather.5.cloned.1.call-start = ((), (), s32[]{:S(2)}) async-start(), calls=%async_computation.5 | async-start | bytes 1949696 | tf_op jit(solution)/shard_map/all_gather | solution.py:65
  281.0 280.3 %reduce-scatter.6.cloned.1.call-start = ((), (), s32[]{:S(2)}) async-start(), calls=%async_computation.3 | async-start | bytes 1114112 | tf_op jit(solution)/shard_map/reduce_scatter | solution.py:49
  281.1 5.6 copy-start.7
  285.4 1.3 copy-start.5
  288.9 67.6 %copy-start.1 = (bf16[512,1792]{0,1:T(8,128)(2,1)S(1)}, bf16[512,1792]{0,1:T(8,128)(2,1)}, u32[]{:S(2)}) copy-start(bf16[512,1792]{0,1:T(8,128)(2,1)} %copy-done) | copy-start | bytes 5505028
  288.9 474.9 %reduce-scatter.8.cloned.1.call-start = ((), (), s32[]{:S(2)}) async-start(), calls=%async_computation.6 | async-start | bytes 1114112 | tf_op jit(solution)/shard_map/reduce_scatter | solution.py:70
  361.2 1.5 copy-start.6
  562.8 1.5 copy-start.8
  567.9 1.5 copy-start.9
Sparse Core Ops, SparseCore 0:
  71.3 135.3 all-reduce.2
  209.3 69.1 reduce-scatter.9
  280.6 38.1 all-gather.2
  320.4 35.9 all-gather.4
  360.1 201.1 reduce-scatter.5
  565.0 198.7 reduce-scatter.7
where the time goes:
time: 773 us; the launch traced here: 772 us
  waiting for transfers between devices  608 us (79%)
  blocking collectives  85.5 us (11%)
  local copies, waits for them, and re-layouts  27 us (3%)
  matrix products  26.8 us (3%)
  between operations  14.3 us (2%)
  other arithmetic  9.96 us (1%)
    reduce_scatter x1, waiting for transfers between devices, per_device(): lax.psum_scatter(jnp.dot(hidden_all, down_eff, preferred_element_type=jnp...  196 us
    reduce_scatter x1, waiting for transfers between devices, per_device(): lax.psum_scatter(right_product(gate_grad_all, gate_eff) + right_product(u...  191 us
    psum x1, waiting for transfers between devices, per_device(): gate_full, up_full = lax.psum((gate_part, up_part), 'row')  86 us
    reduce_scatter x1, waiting for transfers between devices, per_device(): lax.psum_scatter(hidden_part, 'row', scatter_dimension=0, tiled=True)  71.8 us
    all_gather x1, blocking collectives, per_device(): lax.all_gather(tokens, 'col', axis=0, tiled=True)  47.2 us
    all_gather x1, blocking collectives, per_device(): lax.all_gather(cotangent, 'col', axis=0, tiled=True)  38.3 us
    all_gather x1, waiting for transfers between devices, per_device(): lax.all_gather(up_grad, 'row', axis=0, tiled=True)  33 us
    all_gather x1, waiting for transfers between devices, per_device(): lax.all_gather(gate_grad, 'row', axis=0, tiled=True)  29.6 us
  transfers between devices with their start and end apart: 6, of which 6 were waited for; matrix products, arithmetic and copies ran while one was open for 5% of the time, Pallas kernels for 0%

commit v1 on v0

v1 whole, which is shorter than its diff:
```python
import jax
import jax.numpy as jnp
from jax import lax
from jax.sharding import Mesh
from jax.sharding import PartitionSpec as P

ROW = ("x_lo", "y", "core")
COL = ("x_hi", "z")
BF = jnp.bfloat16
F32 = jnp.float32


def masked(weight, block_mask):
    block_rows, block_cols = block_mask.shape
    total_rows, total_cols = weight.shape
    shaped = weight.reshape(
        block_rows, total_rows // block_rows, block_cols, total_cols // block_cols
    )
    return (shaped * block_mask.astype(weight.dtype)[:, None, :, None]).reshape(
        total_rows, total_cols
    )


def right_product(left, right):
    return lax.dot_general(left, right, (((1,), (1,)), ((), ())), preferred_element_type=F32)


def left_product(left, right):
    return lax.dot_general(left, right, (((0,), (0,)), ((), ())), preferred_element_type=F32)


def swap(array, axis):
    return lax.ppermute(array, axis, [(0, 1), (1, 0)])


def per_device(
    tokens, cotangent, gate_weight, up_weight, down_weight, gate_mask, up_mask, down_mask
):
    width = tokens.shape[1]
    hid = gate_weight.shape[1]
    share = tokens.shape[0]
    col_n = lax.axis_size(COL)
    pair_n = lax.axis_size(("x_lo", "y"))
    core = lax.axis_index("core")
    gate_eff = masked(gate_weight, gate_mask)
    up_eff = masked(up_weight, up_mask)
    down_eff = masked(down_weight, down_mask)

    both = jnp.concatenate([tokens, cotangent], axis=1)
    both_all = lax.all_to_all(
        jnp.broadcast_to(both, (col_n,) + both.shape), COL, 0, 0, tiled=True
    ).reshape(col_n * share, 2 * width)
    rows_all = both_all[:, :width]
    cot_all = both_all[:, width:]

    parts = jnp.concatenate(
        [
            jnp.dot(rows_all, gate_eff, preferred_element_type=F32),
            jnp.dot(rows_all, up_eff, preferred_element_type=F32),
            right_product(cot_all, down_eff),
        ],
        axis=1,
    ).reshape(pair_n, 2, share, 3 * hid)
    kept = lax.dynamic_index_in_dim(parts, core, 1, keepdims=False)
    given = lax.dynamic_index_in_dim(parts, 1 - core, 1, keepdims=False).astype(BF)
    pair_sum = (kept + swap(given, "core").astype(F32)).astype(BF)
    sums = jnp.sum(
        lax.all_to_all(pair_sum, ("x_lo", "y"), 0, 0, tiled=True).astype(F32), axis=0
    )
    gate, up, hidden_grad = sums[:, :hid], sums[:, hid : 2 * hid], sums[:, 2 * hid :]

    sigmoid_gate = jax.nn.sigmoid(gate)
    activated = gate * sigmoid_gate
    hidden = (activated * up).astype(BF)
    gate_grad = (
        hidden_grad * up * sigmoid_gate * (1.0 + gate * (1.0 - sigmoid_gate))
    ).astype(BF)
    up_grad = (hidden_grad * activated).astype(BF)

    mine = jnp.concatenate([hidden, gate_grad, up_grad], axis=1)
    own_half = lax.all_to_all(
        jnp.broadcast_to(mine, (pair_n,) + mine.shape), ("x_lo", "y"), 0, 0, tiled=True
    )
    other_half = swap(own_half, "core")
    first = jnp.where(core == 0, own_half, other_half)
    second = jnp.where(core == 0, other_half, own_half)
    acts = jnp.stack([first, second], axis=1).reshape(col_n * share, 3 * hid)
    hidden_all, gate_grad_all, up_grad_all = (
        acts[:, :hid],
        acts[:, hid : 2 * hid],
        acts[:, 2 * hid :],
    )

    output_part = jnp.dot(hidden_all, down_eff, preferred_element_type=F32)
    tokens_part = right_product(gate_grad_all, gate_eff) + right_product(up_grad_all, up_eff)
    out_parts = jnp.concatenate([output_part, tokens_part], axis=1).astype(BF)
    out_sums = jnp.sum(
        lax.all_to_all(
            out_parts.reshape(col_n, share, 2 * width), COL, 0, 0, tiled=True
        ).astype(F32),
        axis=0,
    ).astype(BF)
    output, d_tokens = out_sums[:, :width], out_sums[:, width:]

    grad_down = masked(left_product(hidden_all, cot_all), down_mask).astype(BF)
    grad_gate = masked(left_product(rows_all, gate_grad_all), gate_mask).astype(BF)
    grad_up = masked(left_product(rows_all, up_grad_all), up_mask).astype(BF)
    return (output, d_tokens, grad_gate, grad_up, grad_down)


def solution(mesh):
    fine = Mesh(mesh.devices.reshape(2, 4, 2, 2, 8), ROW + COL)
    in_specs = (
        P(COL, ROW),
        P(COL, ROW),
        P(ROW, COL),
        P(ROW, COL),
        P(COL, ROW),
        P(ROW, COL),
        P(ROW, COL),
        P(COL, ROW),
    )
    out_specs = (P(COL, ROW), P(COL, ROW), P(ROW, COL), P(ROW, COL), P(COL, ROW))
    return jax.shard_map(
        per_device, mesh=fine, in_specs=in_specs, out_specs=out_specs, check_vma=False
    )
```

time: 773 us -> 195 us (0.25)
  waiting for transfers between devices: 608 us -> 34.6 us
  starting transfers between devices: 0.42 us -> 16.1 us
  local copies, waits for them, and re-layouts: 27 us -> 40.9 us
  between operations: 14.3 us -> 0.97 us
  blocking collectives: 85.5 us -> 73.7 us
  matrix products: 26.8 us -> 17 us
    reduce_scatter x3 -> x0, waiting for transfers between devices: 459 us -> none  [the longest x1 196 us: per_device(): lax.psum_scatter(jnp.dot(hidden_all, down_eff, preferred_element_type=jnp...]
    psum x1 -> x0, waiting for transfers between devices: 86 us -> none  [per_device(): gate_full, up_full = lax.psum((gate_part, up_part), 'row')]
    all_gather x2 -> x0, blocking collectives: 85.5 us -> none  [the longest x1 47.2 us: per_device(): lax.all_gather(tokens, 'col', axis=0, tiled=True)]
    all_to_all x0 -> x2, blocking collectives: none -> 73.7 us  [the longest x1 37.5 us: per_device(): lax.all_to_all(pair_sum, ('x_lo', 'y'), 0, 0, tiled=True).astype(F32)]
    all_gather x2 -> x0, waiting for transfers between devices: 62.6 us -> none  [the longest x1 33 us: per_device(): lax.all_gather(up_grad, 'row', axis=0, tiled=True)]
    all_to_all x0 -> x2, waiting for transfers between devices: none -> 23.7 us  [the longest x1 21.6 us: per_device(): lax.all_to_all(jnp.broadcast_to(both, (col_n,) + both.shape), COL, 0, 0,...]
    all_to_all x0 -> x2, starting transfers between devices: none -> 16.1 us  [the longest x1 11.2 us: per_device(): lax.all_to_all(jnp.broadcast_to(both, (col_n,) + both.shape), COL, 0, 0,...]
    ppermute x0 -> x2, waiting for transfers between devices: none -> 10.9 us  [swap(): return lax.ppermute(array, axis, [(0, 1), (1, 0)])]
  transfers between devices with their start and end apart: 6 -> 4, of which waited for: 6 -> 4; matrix products, arithmetic and copies ran while one was open for 5% -> 17% of each run, Pallas kernels for 0% -> 0%
where the time goes in v1:
time: 195 us; the launch traced here: 194 us
  blocking collectives  73.7 us (38%)
  local copies, waits for them, and re-layouts  40.9 us (21%)
  waiting for transfers between devices  34.6 us (18%)
  matrix products  17 us (9%)
  starting transfers between devices  16.1 us (8%)
  other arithmetic  11 us (6%)
    all_to_all x1, blocking collectives, per_device(): lax.all_to_all(pair_sum, ('x_lo', 'y'), 0, 0, tiled=True).astype(F32)  37.5 us
    all_to_all x1, blocking collectives, per_device(): lax.all_to_all(jnp.broadcast_to(mine, (pair_n,) + mine.shape), ('x_lo', '...  36.2 us
    unnamed x40, local copies, waits for them, and re-layouts  22.9 us
    all_to_all x1, waiting for transfers between devices, per_device(): lax.all_to_all(jnp.broadcast_to(both, (col_n,) + both.shape), COL, 0, 0,...  21.6 us
    mul x8, local copies, waits for them, and re-layouts, masked(): shaped * block_mask.astype(weight.dtype)[:, None, :, None]  13.7 us
    all_to_all x1, starting transfers between devices, per_device(): lax.all_to_all(jnp.broadcast_to(both, (col_n,) + both.shape), COL, 0, 0,...  11.2 us
    ppermute x2, waiting for transfers between devices, swap(): return lax.ppermute(array, axis, [(0, 1), (1, 0)])  10.9 us
    dot_general x3, matrix products, left_product(): lax.dot_general(left, right, (((0,), (0,)), ((), ())), preferred_element_...  9.97 us
  transfers between devices with their start and end apart: 4, of which 4 were waited for; matrix products, arithmetic and copies ran while one was open for 17% of the time, Pallas kernels for 0%

profile of v1, /device:TPU:8, one launch (start us, length us, event | category | flops | bytes accessed | tf_op | source)
XLA Modules:
  0.0 194.3 jit_solution(7190502191693122905)
XLA Ops:
  0.6 0.8 pad_maximum_fusion.4
  1.4 1.1 broadcast_in_dim.4
  2.5 11.2 %all-to-all-start = ((bf16[16,32,1024]{2,1,0:T(8,128)(2,1)}), bf16[16,32,1024]{2,1,0:T(8,128)(2,1)S(1)}, u32[]{:S(2)}, u32[]{:S(2)}) async-start(bf16[16,32,1024]{2,1,0:T(8,128)(2,1)} %broadcast_in_dim.4), calls=%async_computation | async-start | bytes 2097152 | tf_op jit(solution)/shard_map/all_to_all | solution.py:50
  13.8 2.8 %copy.16 = bf16[512,1792]{0,1:T(8,128)(2,1)S(1)} copy(bf16[512,1792]{1,0:T(8,128)(2,1)} %param.10) | data formatting | bytes 3670016 | tf_op args[2]
  16.8 3.8 %copy.18 = bf16[512,1792]{0,1:T(8,128)(2,1)} copy(bf16[512,1792]{1,0:T(8,128)(2,1)} %param.11) | data formatting | bytes 3670016 | tf_op args[3]
  20.7 21.6 %all-to-all-done = bf16[16,32,1024]{2,1,0:T(8,128)(2,1)S(1)} async-done(((bf16[16,32,1024]{2,1,0:T(8,128)(2,1)}), bf16[16,32,1024]{2,1,0:T(8,128)(2,1)S(1)}, u32[]{:S(2)}, u32[]{:S(2)}) %all-to-all-start) | async-done | bytes 1048608 | tf_op jit(solution)/shard_map/all_to_all | solution.py:50
  42.3 0.5 mul.87
  42.9 1.2 copy-done.5
  44.1 1.2 fusion.21
  45.3 0.5 mul.90
  45.9 0.9 copy-done.3
  46.8 1.2 fusion.22
  48.0 0.5 mul.93
  48.6 1.3 copy-done.9
  49.8 1.2 fusion.23
  51.0 1.0 pad_maximum_fusion
  52.1 4.2 %copy-done = f32[512,5376]{1,0:T(8,128)} copy-done((f32[512,5376]{1,0:T(8,128)}, f32[512,5376]{1,0:T(8,128)S(1)}, u32[]{:S(2)}) %copy-start) | copy-done | bytes 11010072
  56.2 1.8 fusion.2
  58.0 5.4 %collective-permute-done = bf16[8,32,5376]{2,1,0:T(8,128)(2,1)} collective-permute-done((bf16[8,32,5376]{2,1,0:T(8,128)(2,1)}, bf16[8,32,5376]{2,1,0:T(8,128)(2,1)}, u32[]{:S(2)}, u32[]{:S(2)}) %collective-permute-start) | collective-permute-done | bytes 2752544 | tf_op jit(solution)/shard_map/ppermute | solution.py:33
  63.5 3.9 %fusion = bf16[8,32,5376]{2,1,0:T(8,128)(2,1)S(1)} fusion(bf16[8,32,5376]{2,1,0:T(8,128)(2,1)} %collective-permute-done, f32[8,2,32,5376]{3,2,1,0:T(8,128)} %bitcast.60, s32[]{:T(128)S(6)} %select_n.20), kind=kLoop, calls=%fused_computation.3 | loop fusion | flops 4128768 | bytes 11010052 | tf_op jit(solution)/shard_map/convert_element_type | solution.py:66
  67.4 37.5 %all_to_all.20 = bf16[8,32,5376]{2,1,0:T(8,128)(2,1)S(1)} all-to-all(bf16[8,32,5376]{2,1,0:T(8,128)(2,1)S(1)} %fusion), channel_id=1, replica_groups=mesh['x_lo'=2,'y'=4,'core'=2,'x_hi'=2,'z'=8] {'x_lo','y'}, dimensions={0} | all-to-all | bytes 5505024 | tf_op jit(solution)/shard_map/all_to_all | solution.py:68
  104.9 0.4 convert_reduce_fusion
  105.6 36.2 %all_to_all.21 = bf16[8,32,5376]{2,1,0:T(8,128)(2,1)} all-to-all(bf16[8,32,5376]{2,1,0:T(8,128)(2,1)S(1)} %broadcast_in_dim.5), channel_id=1, replica_groups=mesh['x_lo'=2,'y'=4,'core'=2,'x_hi'=2,'z'=8] {'x_lo','y'}, dimensions={0} | all-to-all | bytes 5505024 | tf_op jit(solution)/shard_map/all_to_all | solution.py:81
  141.9 5.4 %collective-permute-done.1 = bf16[8,32,5376]{2,1,0:T(8,128)(2,1)} collective-permute-done((bf16[8,32,5376]{2,1,0:T(8,128)(2,1)}, bf16[8,32,5376]{2,1,0:T(8,128)(2,1)}, u32[]{:S(2)}, u32[]{:S(2)}) %collective-permute-start.1) | collective-permute-done | bytes 2752544 | tf_op jit(solution)/shard_map/ppermute | solution.py:33
  147.3 3.0 %select_bitcast_fusion.1 = (bf16[8,1,32,5376]{3,2,1,0:T(8,128)(2,1)S(1)}, bf16[8,1,32,5376]{3,2,1,0:T(8,128)(2,1)S(1)}) fusion(bf16[8,32,5376]{2,1,0:T(8,128)(2,1)} %all_to_all.21, bf16[8,32,5376]{2,1,0:T(8,128)(2,1)} %collective-permute-done.1, pred[]{:T(512)S(6)} %eq.4), kind=kLoop, calls=%fused_computation.14 | loop fusion | flops 2752512 | bytes 11010049 | tf_op jit(solution)/shard_map/stack | solution.py:87
  150.3 0.5 pad_maximum_fusion.1
  150.8 1.0 copy-done.10
  151.8 1.9 copy-done.12
  153.7 1.1 fusion.15
  154.8 0.4 copy-done.4
  155.2 0.6 copy-done.8
  155.7 1.1 fusion.4
  156.9 0.4 copy-done.6
  157.2 1.2 fusion.18
  158.4 1.1 pad_maximum_fusion.2
  159.5 5.0 %all-to-all-start.3 = ((bf16[16,32,1024]{2,1,0:T(8,128)(2,1)}), bf16[16,32,1024]{2,1,0:T(8,128)(2,1)S(1)}, u32[]{:S(2)}, u32[]{:S(2)}) async-start(bf16[16,32,1024]{2,1,0:T(8,128)(2,1)} %pad_maximum_fusion.2), calls=%async_computation.3 | async-start | bytes 2097152 | tf_op jit(solution)/shard_map/all_to_all | solution.py:98
  164.6 0.5 mul.106
  165.1 2.2 %copy.44 = f32[224,8,4,128]{3,1,2,0:T(8,128)} copy(f32[224,8,4,128]{3,2,1,0:T(4,128)S(1)} %bitcast.75) | data formatting | bytes 7340032
  167.4 5.2 %copy.24 = f32[512,1792]{1,0:T(8,128)} copy(f32[512,1792]{0,1:T(8,128)} %bitcast.76) | data formatting | bytes 7340032 | tf_op jit(solution)/shard_map/mul | solution.py:19
  172.6 0.5 mul.103
  173.2 2.1 %copy.45 = f32[224,8,4,128]{3,1,2,0:T(8,128)} copy(f32[224,8,4,128]{3,2,1,0:T(4,128)S(1)} %bitcast.77) | data formatting | bytes 7340032
  175.3 5.3 %copy.22 = f32[512,1792]{1,0:T(8,128)} copy(f32[512,1792]{0,1:T(8,128)} %bitcast.78) | data formatting | bytes 7340032 | tf_op jit(solution)/shard_map/mul | solution.py:19
  180.8 5.1 %multiply_convert_fusion = bf16[512,1792]{1,0:T(8,128)(2,1)} fusion(f32[512,1792]{1,0:T(8,128)} %copy.24, bf16[512,5376]{1,0:T(8,128)(2,1)} %bitcast.70, bf16[512,1024]{1,0:T(8,128)(2,1)S(1)} %bitcast.64), kind=kOutput, calls=%fused_computation.10 | convolution fusion | flops 941359104 | bytes 7864320 | tf_op jit(solution)/shard_map/dot_general | solution.py:29
  185.9 2.5 %multiply_convert_fusion.1 = bf16[512,1792]{1,0:T(8,128)(2,1)} fusion(f32[512,1792]{1,0:T(8,128)S(1)} %copy-done.2, bf16[512,5376]{1,0:T(8,128)(2,1)S(1)} %bitcast.73, bf16[512,1024]{1,0:T(8,128)(2,1)S(1)} %bitcast.65), kind=kOutput, calls=%fused_computation.11 | convolution fusion | flops 941359104 | bytes 7864320 | tf_op jit(solution)/shard_map/dot_general | solution.py:29
  188.4 0.5 mul.109
  188.9 2.4 %fusion.1 = bf16[1792,512]{1,0:T(8,128)(2,1)} fusion(f32[224,8,4,128]{3,2,1,0:T(4,128)S(1)} %bitcast.85, bf16[512,5376]{1,0:T(8,128)(2,1)S(1)} %bitcast.74, bf16[512,1024]{1,0:T(8,128)(2,1)S(1)} %bitcast.66), kind=kOutput, calls=%fused_computation.7 | convolution fusion | flops 941359104 | bytes 7864320 | tf_op jit(solution)/shard_map/dot_general | solution.py:29
  191.3 2.1 %all-to-all-done.3 = bf16[16,32,1024]{2,1,0:T(8,128)(2,1)S(1)} async-done(((bf16[16,32,1024]{2,1,0:T(8,128)(2,1)}), bf16[16,32,1024]{2,1,0:T(8,128)(2,1)S(1)}, u32[]{:S(2)}, u32[]{:S(2)}) %all-to-all-start.3) | async-done | bytes 1048608 | tf_op jit(solution)/shard_map/all_to_all | solution.py:98
  193.6 0.6 fusion.31
  (43 shorter events, 1.2 us)
Async XLA Ops:
  0.6 13.1 %copy-start.13 = (s32[4,14]{1,0:T(4,128)S(1)}, s32[4,14]{1,0:T(4,128)}, u32[]{:S(2)}) copy-start(s32[4,14]{1,0:T(4,128)} %param.13) | copy-start | bytes 676
  2.5 14.1 %copy-start.14 = (s32[4,14]{1,0:T(4,128)S(1)}, s32[4,14]{1,0:T(4,128)}, u32[]{:S(2)}) copy-start(s32[4,14]{1,0:T(4,128)} %param.14) | copy-start | bytes 676
  2.5 39.8 %all-to-all-start = ((bf16[16,32,1024]{2,1,0:T(8,128)(2,1)}), bf16[16,32,1024]{2,1,0:T(8,128)(2,1)S(1)}, u32[]{:S(2)}, u32[]{:S(2)}) async-start(bf16[16,32,1024]{2,1,0:T(8,128)(2,1)} %broadcast_in_dim.4), calls=%async_computation | async-start | bytes 2097152 | tf_op jit(solution)/shard_map/all_to_all | solution.py:50
  16.7 4.0 %copy-start.15 = (s32[14,4]{0,1:T(4,128)S(1)}, s32[14,4]{0,1:T(4,128)}, u32[]{:S(2)}) copy-start(s32[14,4]{0,1:T(4,128)} %param.15) | copy-start | bytes 676
  42.9 1.2 copy-start.5
  45.3 1.5 copy-start.3
  45.9 2.1 %copy-start.7 = (bf16[4,128,14,128]{1,0,3,2:T(4,128)(2,1)}, bf16[4,128,14,128]{1,0,3,2:T(4,128)(2,1)S(1)}, u32[]{:S(2)}) copy-start(bf16[4,128,14,128]{1,0,3,2:T(4,128)(2,1)S(1)} %mul.90) | copy-start | bytes 5505028
  48.0 1.8 copy-start.11
  48.6 1.3 copy-start.9
  52.0 4.2 %copy-start = (f32[512,5376]{1,0:T(8,128)}, f32[512,5376]{1,0:T(8,128)S(1)}, u32[]{:S(2)}) copy-start(f32[512,5376]{1,0:T(8,128)S(1)} %pad_maximum_fusion) | copy-start | bytes 33030148
  58.0 5.4 %collective-permute-start = (bf16[8,32,5376]{2,1,0:T(8,128)(2,1)}, bf16[8,32,5376]{2,1,0:T(8,128)(2,1)}, u32[]{:S(2)}, u32[]{:S(2)}) collective-permute-start(bf16[8,32,5376]{2,1,0:T(8,128)(2,1)} %fusion.2), channel_id=1, source_target_pairs={{0,16},{16,0},{1,17},{17,1},{2,18},{18,2},{3,19},{19,3},{4,20},{20... | collective-permute-start | bytes 8257544 | tf_op jit(solution)/shard_map/ppermute | solution.py:33
  141.8 5.4 %collective-permute-start.1 = (bf16[8,32,5376]{2,1,0:T(8,128)(2,1)}, bf16[8,32,5376]{2,1,0:T(8,128)(2,1)}, u32[]{:S(2)}, u32[]{:S(2)}) collective-permute-start(bf16[8,32,5376]{2,1,0:T(8,128)(2,1)} %all_to_all.21), channel_id=1, source_target_pairs={{0,16},{16,0},{1,17},{17,1},{2,18},{18,2},{3,19},{19,3},{4,20},{20... | collective-permute-start | bytes 8257544 | tf_op jit(solution)/shard_map/ppermute | solution.py:33
  150.3 1.5 copy-start.10
  150.3 3.4 %copy-start.12 = (bf16[1792,512]{1,0:T(8,128)(2,1)S(1)}, bf16[1792,512]{1,0:T(8,128)(2,1)}, u32[]{:S(2)}) copy-start(bf16[1792,512]{1,0:T(8,128)(2,1)} %param.12) | copy-start | bytes 5505028
  150.8 6.1 %copy-start.1 = (bf16[8,2,32,5376]{3,2,1,0:T(8,128)(2,1)}, bf16[8,2,32,5376]{3,2,1,0:T(8,128)(2,1)S(1)}, u32[]{:S(2)}) copy-start(bf16[8,2,32,5376]{3,2,1,0:T(8,128)(2,1)S(1)} %pad_maximum_fusion.1) | copy-start | bytes 16515076
  153.7 1.5 copy-start.4
  153.7 2.0 %copy-start.8 = (bf16[4,128,14,128]{1,0,3,2:T(4,128)(2,1)S(1)}, bf16[4,128,14,128]{1,0,3,2:T(4,128)(2,1)}, u32[]{:S(2)}) copy-start(bf16[4,128,14,128]{1,0,3,2:T(4,128)(2,1)} %copy-done.7) | copy-start | bytes 5505028
  155.7 1.5 copy-start.6
  159.5 33.9 %all-to-all-start.3 = ((bf16[16,32,1024]{2,1,0:T(8,128)(2,1)}), bf16[16,32,1024]{2,1,0:T(8,128)(2,1)S(1)}, u32[]{:S(2)}, u32[]{:S(2)}) async-start(bf16[16,32,1024]{2,1,0:T(8,128)(2,1)} %pad_maximum_fusion.2), calls=%async_computation.3 | async-start | bytes 2097152 | tf_op jit(solution)/shard_map/all_to_all | solution.py:98
  175.3 10.6 %slice-start = ((s8[5505024]{0:T(1024)(128)(4,1)}), s8[1310720]{0:T(1024)(128)(4,1)S(1)}, s32[]{:S(2)}) async-start(s8[5505024]{0:T(1024)(128)(4,1)} %bitcast.71), calls=%async_computation.4 | async-start | bytes 2621440
  180.8 5.1 %slice-start.1 = ((s8[5505024]{0:T(1024)(128)(4,1)}), s8[4194304]{0:T(1024)(128)(4,1)S(1)}, s32[]{:S(2)}) async-start(s8[5505024]{0:T(1024)(128)(4,1)} %bitcast.71), calls=%async_computation.5 | async-start | bytes 8388608
  180.8 5.1 %copy-start.2 = (f32[512,1792]{1,0:T(8,128)S(1)}, f32[512,1792]{1,0:T(8,128)}, u32[]{:S(2)}) copy-start(f32[512,1792]{1,0:T(8,128)} %copy.22) | copy-start | bytes 11010052

commit v2 on v1

v2 whole, which is shorter than its diff:
```python
import jax
import jax.numpy as jnp
from jax import lax
from jax.experimental import pallas as pl
from jax.experimental.pallas import tpu as pltpu
from jax.sharding import Mesh
from jax.sharding import PartitionSpec as P


ROW = ("x_lo", "y", "core")
COL = ("x_hi", "z")
PAIR = ("x_lo", "y")
BF = jnp.bfloat16
F32 = jnp.float32
BLK = 128


def prepare_kernel(*refs):
    for weight, mask, eff, full in zip(refs[0:3], refs[3:6], refs[6:9], refs[9:12]):
        for i in range(mask.shape[0]):
            rows = pl.ds(i * BLK, BLK)
            keep = jnp.broadcast_to(mask[pl.ds(i, 1), :], (BLK, mask.shape[1])).astype(BF)
            full[rows, :] = keep
            eff[rows, :] = weight[rows, :] * keep


def prepare(weights, masks):
    wide = [jnp.repeat(mask.astype(F32), BLK, axis=1) for mask in masks]
    shapes = [jax.ShapeDtypeStruct(weight.shape, BF) for weight in weights]
    outs = pl.pallas_call(
        prepare_kernel,
        out_shape=shapes + shapes,
        in_specs=[pl.BlockSpec(memory_space=pltpu.VMEM)] * 6,
        out_specs=[pl.BlockSpec(memory_space=pltpu.VMEM)] * 6,
        name="prepare",
    )(*weights, *wide)
    return outs[:3], outs[3:]


def dot(left, right):
    return jnp.dot(left, right, preferred_element_type=F32)


def right_product(left, right):
    return lax.dot_general(left, right, (((1,), (1,)), ((), ())), preferred_element_type=F32)


def left_product(left, right):
    return lax.dot_general(left, right, (((0,), (0,)), ((), ())), preferred_element_type=F32)


def swap(array):
    return lax.ppermute(array, "core", [(0, 1), (1, 0)])


def gather(array, axes):
    copies = jnp.broadcast_to(array, (lax.axis_size(axes),) + array.shape)
    return lax.all_to_all(copies, axes, 0, 0, tiled=True)


def exchange(array, axes):
    parts = lax.axis_size(axes)
    split = array.reshape((parts, array.shape[0] // parts) + array.shape[1:])
    return lax.all_to_all(split, axes, 0, 0, tiled=True)


def send_down(array, axis, hops):
    size = lax.axis_size(axis)
    return lax.ppermute(array, axis, [(i, (i - hops) % size) for i in range(size)])


def arrange_kernel(place, *refs):
    parts, out = refs[:-1], refs[-1]
    size = len(parts)
    rows = parts[0].shape[1]
    for k, part in enumerate(parts):
        start = pl.multiple_of(lax.rem(place[0] + k, size) * rows, rows)
        out[:, pl.ds(start, rows), :] = part[...]


def arrange(place, parts):
    halves, rows, width = parts[0].shape
    return pl.pallas_call(
        arrange_kernel,
        out_shape=jax.ShapeDtypeStruct((halves, len(parts) * rows, width), BF),
        in_specs=[pl.BlockSpec(memory_space=pltpu.SMEM)]
        + [pl.BlockSpec(memory_space=pltpu.VMEM)] * len(parts),
        out_specs=pl.BlockSpec(memory_space=pltpu.VMEM),
        name="arrange",
    )(place, *parts)


def gather_by_permutes(array):
    high, z = lax.axis_index("x_hi"), lax.axis_index("z")
    size = lax.axis_size("z")
    facing = send_down(array, "x_hi", 1)
    pair = jnp.stack([jnp.where(high == 0, array, facing), jnp.where(high == 0, facing, array)])
    got = [pair] + [send_down(pair, "z", k) for k in range(1, size)]
    return arrange(z.reshape(1).astype(jnp.int32), got)


def exchange_by_permutes(kept, given, share):
    z = lax.axis_index("z")
    size = lax.axis_size("z")
    arrived = send_down(given, "x_hi", 1)
    parts = (kept + arrived.astype(F32)).reshape(size, share, -1)
    result = lax.dynamic_index_in_dim(parts, z, 0, keepdims=False)
    parts = parts.astype(BF)
    away = [
        lax.dynamic_index_in_dim(parts, (z + size - k) % size, 0, keepdims=False)
        for k in range(1, size)
    ]
    for k in range(1, size):
        result = result + send_down(away[k - 1], "z", k).astype(F32)
    return result


def layer(
    tokens, cotangent, gate_weight, up_weight, down_weight, gate_mask, up_mask, down_mask
):
    share, width = tokens.shape
    hid = gate_weight.shape[1]
    core = lax.axis_index("core")
    high = lax.axis_index("x_hi")

    def halves(gathered):
        split = gathered.reshape(2, -1, width)
        own = lax.dynamic_index_in_dim(split, core, 0, keepdims=False)
        other = lax.dynamic_index_in_dim(split, 1 - core, 0, keepdims=False)
        return own, other

    rows_all = gather(tokens, COL)
    (gate_eff, up_eff, down_eff), (gate_full, up_full, down_full) = prepare(
        (gate_weight, up_weight, down_weight), (gate_mask, up_mask, down_mask)
    )

    rows_own, rows_other = halves(rows_all)
    gate_recv = swap(dot(rows_other, gate_eff))
    up_recv = swap(dot(rows_other, up_eff))
    gate_pair = (dot(rows_own, gate_eff) + gate_recv).astype(BF)
    up_pair = (dot(rows_own, up_eff) + up_recv).astype(BF)
    gate_up = jnp.concatenate([gate_pair, up_pair], axis=1)
    gate_up, cot_in = lax.optimization_barrier((gate_up, cotangent))
    sums = jnp.sum(exchange(gate_up, PAIR).astype(F32), axis=0)
    gate, up = sums[:, :hid], sums[:, hid:]

    cot_own, cot_other = halves(gather_by_permutes(cot_in))
    back_recv = swap(right_product(cot_other, down_eff))
    back_pair = (right_product(cot_own, down_eff) + back_recv).astype(BF)

    sigmoid_gate = jax.nn.sigmoid(gate)
    activated = gate * sigmoid_gate
    hidden = (activated * up).astype(BF)
    hidden_own = gather(hidden, PAIR).reshape(-1, hid)
    hidden_own, back_pair = lax.optimization_barrier((hidden_own, back_pair))
    hidden_other = swap(hidden_own)

    back_got = exchange(back_pair, PAIR)
    hidden_grad = jnp.sum(back_got.astype(F32), axis=0)
    gate_grad = (
        hidden_grad * up * sigmoid_gate * (1.0 + gate * (1.0 - sigmoid_gate))
    ).astype(BF)
    up_grad = (hidden_grad * activated).astype(BF)
    both_grads = jnp.concatenate([gate_grad, up_grad], axis=1)
    grads_own = gather(both_grads, PAIR).reshape(-1, 2 * hid)
    grads_other = swap(grads_own)

    output_own, output_other = dot(hidden_own, down_eff), dot(hidden_other, down_eff)
    output_kept = jnp.where(core == high, output_own, output_other)
    output_given = jnp.where(core == high, output_other, output_own).astype(BF)
    output = exchange_by_permutes(output_kept, output_given, share).astype(BF)

    def back(grads):
        return right_product(grads[:, :hid], gate_eff) + right_product(grads[:, hid:], up_eff)

    back_own, back_other = back(grads_own), back(grads_other)
    tokens_part = jnp.concatenate(
        [jnp.where(core == 0, back_own, back_other), jnp.where(core == 0, back_other, back_own)],
        axis=0,
    ).astype(BF)
    tokens_got = exchange(tokens_part, COL)
    d_tokens = jnp.sum(tokens_got.astype(F32), axis=0).astype(BF)

    rows_local = jnp.concatenate([rows_own, rows_other], axis=0)
    cot_local = jnp.concatenate([cot_own, cot_other], axis=0)
    hidden_local = jnp.concatenate([hidden_own, hidden_other], axis=0)
    grads_local = jnp.concatenate([grads_own, grads_other], axis=0)
    grad_down = (left_product(hidden_local, cot_local) * down_full.astype(F32)).astype(BF)
    grad_gate = (left_product(rows_local, grads_local[:, :hid]) * gate_full.astype(F32)).astype(BF)
    grad_up = (
        left_product(rows_local, grads_local[:, hid:]) * up_full.astype(F32)
    ).astype(BF)
    return (output, d_tokens, grad_gate, grad_up, grad_down)


def solution(mesh):
    fine = Mesh(mesh.devices.reshape(2, 4, 2, 2, 8), ROW + COL)
    in_specs = (
        P(COL, ROW),
        P(COL, ROW),
        P(ROW, COL),
        P(ROW, COL),
        P(COL, ROW),
        P(ROW, COL),
        P(ROW, COL),
        P(COL, ROW),
    )
    out_specs = (P(COL, ROW), P(COL, ROW), P(ROW, COL), P(ROW, COL), P(COL, ROW))
    return jax.shard_map(layer, mesh=fine, in_specs=in_specs, out_specs=out_specs, check_vma=False)
```

time: 195 us -> 199 us (1.021)
  blocking collectives: 73.7 us -> 17.6 us
  starting transfers between devices: 16.1 us -> 65.3 us
  local copies, waits for them, and re-layouts: 40.9 us -> 8.08 us
  waiting for transfers between devices: 34.6 us -> 61.6 us
  matrix products: 17 us -> 27.7 us
  Pallas kernels: 0 us -> 8.77 us
  other arithmetic: 11 us -> 8.01 us
    all_to_all x2 -> x1, blocking collectives: 73.7 us -> 17.6 us  [exchange(): return lax.all_to_all(split, axes, 0, 0, tiled=True)]
    ppermute x2 -> x21, starting transfers between devices: 0.01 us -> 32.2 us  [the longest x16 31.5 us: send_down(): lax.ppermute(array, axis, [(i, (i - hops) % size) for i in range(size)])]
    unnamed x40 -> x50, local copies, waits for them, and re-layouts: 22.9 us -> 1.44 us
    all_to_all x2 -> x5, waiting for transfers between devices: 23.7 us -> 44.5 us  [the longest x3 38.5 us: gather(): return lax.all_to_all(copies, axes, 0, 0, tiled=True)]
    all_to_all x2 -> x5, starting transfers between devices: 16.1 us -> 33.2 us  [the longest x3 22.5 us: gather(): return lax.all_to_all(copies, axes, 0, 0, tiled=True)]
    mul x8 -> x0, local copies, waits for them, and re-layouts: 13.7 us -> none  [masked(): shaped * block_mask.astype(weight.dtype)[:, None, :, None]]
    pallas_call x0 -> x2, Pallas kernels: none -> 8.77 us  [the longest x1 6.89 us: prepare(): pl.pallas_call(prepare_kernel, out_shape=shapes + shapes, in_specs=[pl.Bl...]
    ppermute x2 -> x21, waiting for transfers between devices: 10.9 us -> 17.1 us  [the longest x16 12.6 us: send_down(): lax.ppermute(array, axis, [(i, (i - hops) % size) for i in range(size)])]
  transfers between devices with their start and end apart: 4 -> 26, of which waited for: 4 -> 11; matrix products, arithmetic and copies ran while one was open for 17% -> 18% of each run, Pallas kernels for 0% -> 4%
where the time goes in v2:
time: 199 us; the launch traced here: 198 us
  starting transfers between devices  65.3 us (33%)
  waiting for transfers between devices  61.6 us (31%)
  matrix products  27.7 us (14%)
  blocking collectives  17.6 us (9%)
  Pallas kernels  8.77 us (4%)
  local copies, waits for them, and re-layouts  8.08 us (4%)
  other arithmetic  8.01 us (4%)
    all_to_all x3, waiting for transfers between devices, gather(): return lax.all_to_all(copies, axes, 0, 0, tiled=True)  38.5 us
    ppermute x16, starting transfers between devices, send_down(): lax.ppermute(array, axis, [(i, (i - hops) % size) for i in range(size)])  31.5 us
    all_to_all x3, starting transfers between devices, gather(): return lax.all_to_all(copies, axes, 0, 0, tiled=True)  22.5 us
    all_to_all x1, blocking collectives, exchange(): return lax.all_to_all(split, axes, 0, 0, tiled=True)  17.6 us
    ppermute x16, waiting for transfers between devices, send_down(): lax.ppermute(array, axis, [(i, (i - hops) % size) for i in range(size)])  12.6 us
    dot_general x3, matrix products, left_product(): lax.dot_general(left, right, (((0,), (0,)), ((), ())), preferred_element_...  11.7 us
    all_to_all x2, starting transfers between devices, exchange(): return lax.all_to_all(split, axes, 0, 0, tiled=True)  10.7 us
    dot_general x6, matrix products, right_product(): lax.dot_general(left, right, (((1,), (1,)), ((), ())), preferred_element_...  9.23 us
  transfers between devices with their start and end apart: 26, of which 11 were waited for; matrix products, arithmetic and copies ran while one was open for 18% of the time, Pallas kernels for 4%

profile of v2, /device:TPU:8, one launch (start us, length us, event | category | flops | bytes accessed | tf_op | source)
XLA Modules:
  0.0 198.2 jit_solution(9011890031279134688)
XLA Ops:
  0.6 1.6 broadcast_in_dim.18
  2.3 11.0 %all-to-all-start = ((bf16[16,32,512]{2,1,0:T(8,128)(2,1)}), bf16[16,32,512]{2,1,0:T(8,128)(2,1)S(1)}, u32[]{:S(2)}, u32[]{:S(2)}) async-start(bf16[16,32,512]{2,1,0:T(8,128)(2,1)} %broadcast_in_dim.18), calls=%async_computation | async-start | bytes 1048576 | tf_op jit(solution)/shard_map/all_to_all | solution.py:58
  17.0 6.9 %prepare.1 = (bf16[512,1792]{1,0:T(8,128)(2,1)}, bf16[512,1792]{1,0:T(8,128)(2,1)}, bf16[1792,512]{1,0:T(8,128)(2,1)}, bf16[512,1792]{1,0:T(8,128)(2,1)}, bf16[5...) custom-call(bf16[512,1792]{1,0:T(8,128)(2,1)} %refs_0_.1, bf16[512,1792]{1,0:T(8,128)(2,1)} %refs_1_.1, ...), custom_call_target="tpu_custom_call" | custom-call | tf_op jit(solution)/shard_map/prepare/pallas_call | solution.py:30
  23.8 6.6 %all-to-all-done = bf16[16,32,512]{2,1,0:T(8,128)(2,1)S(1)} async-done(((bf16[16,32,512]{2,1,0:T(8,128)(2,1)}), bf16[16,32,512]{2,1,0:T(8,128)(2,1)S(1)}, u32[]{:S(2)}, u32[]{:S(2)}) %all-to-all-start) | async-done | bytes 524320 | tf_op jit(solution)/shard_map/all_to_all | solution.py:58
  30.5 2.3 %fusion.30 = f32[256,1792]{1,0:T(8,128)S(1)} fusion(bf16[256,512]{1,0:T(8,128)(2,1)S(1)} %get-tuple-element.32, bf16[512,1792]{1,0:T(8,128)(2,1)} %get-tuple-element.16), kind=kOutput, calls=%fused_computation.73 | convolution fusion | flops 469762048 | bytes 3932160 | tf_op jit(solution)/shard_map/dot_general | solution.py:41
  34.1 2.5 %collective-permute-done.1 = f32[256,1792]{1,0:T(8,128)S(1)} collective-permute-done((f32[256,1792]{1,0:T(8,128)S(1)}, f32[256,1792]{1,0:T(8,128)S(1)}, u32[]{:S(2)}, u32[]{:S(2)}) %collective-permute-start.1) | collective-permute-done | bytes 1835040 | tf_op jit(solution)/shard_map/ppermute | solution.py:53
  37.3 2.0 collective-permute-done
  40.0 1.4 pad_maximum_fusion.2
  41.4 0.7 collective-permute-start.2
  42.2 4.9 %all-to-all-start.1 = ((bf16[8,32,3584]{2,1,0:T(8,128)(2,1)}), bf16[8,32,3584]{2,1,0:T(8,128)(2,1)}, u32[]{:S(2)}, u32[]{:S(2)}) async-start(bf16[8,32,3584]{2,1,0:T(8,128)(2,1)} %bitcast.3), calls=%async_computation.1 | async-start | bytes 3670016 | tf_op jit(solution)/shard_map/all_to_all | solution.py:64
  47.2 2.7 %collective-permute-start.3 = (bf16[2,32,512]{2,1,0:T(8,128)(2,1)S(1)}, bf16[2,32,512]{2,1,0:T(8,128)(2,1)S(1)}, u32[]{:S(2)}, u32[]{:S(2)}) collective-permute-start(bf16[2,32,512]{2,1,0:T(8,128)(2,1)S(1)} %pad_maximum_fusion.8.refs_0_), channel_id=1, source_target_pairs={{0,7},{1,0},{2,1},{3,2},{4,3},{5,4},{6,5},{7,6},{8,15},{9,8},{10,9... | collective-permute-start | bytes 196616 | tf_op jit(solution)/shard_map/ppermute | solution.py:69
  50.5 3.2 %collective-permute-start.5 = (bf16[2,32,512]{2,1,0:T(8,128)(2,1)S(1)}, bf16[2,32,512]{2,1,0:T(8,128)(2,1)S(1)}, u32[]{:S(2)}, u32[]{:S(2)}) collective-permute-start(bf16[2,32,512]{2,1,0:T(8,128)(2,1)S(1)} %pad_maximum_fusion.8.refs_0_), channel_id=1, source_target_pairs={{0,5},{1,6},{2,7},{3,0},{4,1},{5,2},{6,3},{7,4},{8,13},{9,14},{10,... | collective-permute-start | bytes 196616 | tf_op jit(solution)/shard_map/ppermute | solution.py:69
  53.7 3.1 %collective-permute-start.6 = (bf16[2,32,512]{2,1,0:T(8,128)(2,1)S(1)}, bf16[2,32,512]{2,1,0:T(8,128)(2,1)S(1)}, u32[]{:S(2)}, u32[]{:S(2)}) collective-permute-start(bf16[2,32,512]{2,1,0:T(8,128)(2,1)S(1)} %pad_maximum_fusion.8.refs_0_), channel_id=1, source_target_pairs={{0,4},{1,5},{2,6},{3,7},{4,0},{5,1},{6,2},{7,3},{8,12},{9,13},{10,... | collective-permute-start | bytes 196616 | tf_op jit(solution)/shard_map/ppermute | solution.py:69
  56.8 1.5 collective-permute-start.7
  58.3 2.6 %collective-permute-start.8 = (bf16[2,32,512]{2,1,0:T(8,128)(2,1)S(1)}, bf16[2,32,512]{2,1,0:T(8,128)(2,1)S(1)}, u32[]{:S(2)}, u32[]{:S(2)}) collective-permute-start(bf16[2,32,512]{2,1,0:T(8,128)(2,1)S(1)} %pad_maximum_fusion.8.refs_0_), channel_id=1, source_target_pairs={{0,2},{1,3},{2,4},{3,5},{4,6},{5,7},{6,0},{7,1},{8,10},{9,11},{10,... | collective-permute-start | bytes 196616 | tf_op jit(solution)/shard_map/ppermute | solution.py:69
  60.9 2.5 %collective-permute-done.6.refs_4_ = bf16[2,32,512]{2,1,0:T(8,128)(2,1)S(1)} collective-permute-done((bf16[2,32,512]{2,1,0:T(8,128)(2,1)S(1)}, bf16[2,32,512]{2,1,0:T(8,128)(2,1)S(1)}, u32[]{:S(2)}, u32[]{:S(2)}) %collective-permute-start.6) | collective-permute-done | bytes 65568 | tf_op jit(solution)/shard_map/ppermute | solution.py:69
  63.4 2.5 %collective-permute-done.7.refs_5_ = bf16[2,32,512]{2,1,0:T(8,128)(2,1)S(1)} collective-permute-done((bf16[2,32,512]{2,1,0:T(8,128)(2,1)S(1)}, bf16[2,32,512]{2,1,0:T(8,128)(2,1)S(1)}, u32[]{:S(2)}, u32[]{:S(2)}) %collective-permute-start.7) | collective-permute-done | bytes 65568 | tf_op jit(solution)/shard_map/ppermute | solution.py:69
  65.9 2.6 %collective-permute-done.8.refs_6_ = bf16[2,32,512]{2,1,0:T(8,128)(2,1)S(1)} collective-permute-done((bf16[2,32,512]{2,1,0:T(8,128)(2,1)S(1)}, bf16[2,32,512]{2,1,0:T(8,128)(2,1)S(1)}, u32[]{:S(2)}, u32[]{:S(2)}) %collective-permute-start.8) | collective-permute-done | bytes 65568 | tf_op jit(solution)/shard_map/ppermute | solution.py:69
  69.8 1.9 arrange.1
  71.6 1.8 dynamic-slice_bitcast_fusion.1
  73.4 1.9 fusion.31
  75.3 1.8 convert_reduce_fusion
  77.2 1.0 broadcast_in_dim.22
  78.2 5.7 %all-to-all-start.2 = ((bf16[8,32,1792]{2,1,0:T(8,128)(2,1)}), bf16[8,32,1792]{2,1,0:T(8,128)(2,1)}, u32[]{:S(2)}, u32[]{:S(2)}) async-start(bf16[8,32,1792]{2,1,0:T(8,128)(2,1)} %broadcast_in_dim.22), calls=%async_computation.2 | async-start | bytes 1835008 | tf_op jit(solution)/shard_map/all_to_all | solution.py:58
  83.9 2.3 %fusion.2 = bf16[256,1792]{1,0:T(8,128)(2,1)S(1)} fusion(f32[256,1792]{1,0:T(8,128)} %collective-permute-done.10, bf16[256,512]{1,0:T(8,128)(2,1)} %get-tuple-element.29, bf16[1792,512]{1,0:T(8,128)(2,1)S(1)} %copy-done), kind=kOutput, calls=%fused_computation.11 | convolution fusion | flops 470679552 | bytes 4849664 | tf_op jit(solution)/shard_map/dot_general | solution.py:45
  86.2 10.7 %all-to-all-done.2 = bf16[8,32,1792]{2,1,0:T(8,128)(2,1)} async-done(((bf16[8,32,1792]{2,1,0:T(8,128)(2,1)}), bf16[8,32,1792]{2,1,0:T(8,128)(2,1)}, u32[]{:S(2)}, u32[]{:S(2)}) %all-to-all-start.2) | async-done | bytes 917536 | tf_op jit(solution)/shard_map/all_to_all | solution.py:58
  96.9 17.6 %all_to_all.30 = bf16[8,32,1792]{2,1,0:T(8,128)(2,1)S(1)} all-to-all(bf16[8,32,1792]{2,1,0:T(8,128)(2,1)S(1)} %bitcast.81), channel_id=1, replica_groups=mesh['x_lo'=2,'y'=4,'core'=2,'x_hi'=2,'z'=8] {'x_lo','y'}, dimensions={0} | all-to-all | bytes 1835008 | tf_op jit(solution)/shard_map/all_to_all | solution.py:64
  114.8 1.4 broadcast_in_dim.23
  116.2 5.7 %all-to-all-start.4 = ((bf16[8,32,3584]{2,1,0:T(8,128)(2,1)}), bf16[8,32,3584]{2,1,0:T(8,128)(2,1)}, u32[]{:S(2)}, u32[]{:S(2)}) async-start(bf16[8,32,3584]{2,1,0:T(8,128)(2,1)} %broadcast_in_dim.23), calls=%async_computation.4 | async-start | bytes 3670016 | tf_op jit(solution)/shard_map/all_to_all | solution.py:58
  121.9 21.2 %all-to-all-done.4 = bf16[8,32,3584]{2,1,0:T(8,128)(2,1)} async-done(((bf16[8,32,3584]{2,1,0:T(8,128)(2,1)}), bf16[8,32,3584]{2,1,0:T(8,128)(2,1)}, u32[]{:S(2)}, u32[]{:S(2)}) %all-to-all-start.4) | async-done | bytes 1835040 | tf_op jit(solution)/shard_map/all_to_all | solution.py:58
  143.1 1.8 fusion.32
  145.6 2.4 %collective-permute-start.12 = (bf16[256,512]{1,0:T(8,128)(2,1)S(1)}, bf16[256,512]{1,0:T(8,128)(2,1)S(1)}, u32[]{:S(2)}, u32[]{:S(2)}) collective-permute-start(bf16[256,512]{1,0:T(8,128)(2,1)S(1)} %get-tuple-element.42), channel_id=1, source_target_pairs={{0,8},{8,0},{1,9},{9,1},{2,10},{10,2},{3,11},{11,3},{4,12},{12,4},... | collective-permute-start | bytes 786440 | tf_op jit(solution)/shard_map/ppermute | solution.py:69
  148.0 3.6 %multiply_convert_fusion = bf16[1792,512]{1,0:T(8,128)(2,1)} fusion(bf16[1792,512]{1,0:T(8,128)(2,1)S(1)} %copy-done.20, bf16[256,1792]{1,0:T(8,128)(2,1)S(1)} %collective-permute-done.11, bf16[256,1792]{1,0:T(8,128)(2,1)} %bitcast.4, bf16[256,512]{1,0:T(8,128)(2,1)S(1)} %copy-done.9, bf16[256,512]{1,0:T(8,128)(2,1)S(1)} %copy-done.7), kind=kOutput, calls=%fused_computation.2 | convolution fusion | flops 946995200 | bytes 6029312 | tf_op jit(solution)/shard_map/dot_general | solution.py:49
  151.6 4.4 %collective-permute-done.12 = bf16[256,512]{1,0:T(8,128)(2,1)S(1)} collective-permute-done((bf16[256,512]{1,0:T(8,128)(2,1)S(1)}, bf16[256,512]{1,0:T(8,128)(2,1)S(1)}, u32[]{:S(2)}, u32[]{:S(2)}) %collective-permute-start.12) | collective-permute-done | bytes 262176 | tf_op jit(solution)/shard_map/ppermute | solution.py:69
  156.8 1.2 collective-permute-start.18
  158.0 2.5 %collective-permute-start.17 = (bf16[32,512]{1,0:T(8,128)(2,1)S(1)}, bf16[32,512]{1,0:T(8,128)(2,1)S(1)}, u32[]{:S(2)}, u32[]{:S(2)}) collective-permute-start(bf16[32,512]{1,0:T(8,128)(2,1)S(1)} %get-tuple-element.36), channel_id=1, source_target_pairs={{0,3},{1,4},{2,5},{3,6},{4,7},{5,0},{6,1},{7,2},{8,11},{9,12},{10,... | collective-permute-start | bytes 98312 | tf_op jit(solution)/shard_map/ppermute | solution.py:69
  160.5 3.1 %collective-permute-start.16 = (bf16[32,512]{1,0:T(8,128)(2,1)S(1)}, bf16[32,512]{1,0:T(8,128)(2,1)S(1)}, u32[]{:S(2)}, u32[]{:S(2)}) collective-permute-start(bf16[32,512]{1,0:T(8,128)(2,1)S(1)} %get-tuple-element.37), channel_id=1, source_target_pairs={{0,4},{1,5},{2,6},{3,7},{4,0},{5,1},{6,2},{7,3},{8,12},{9,13},{10,... | collective-permute-start | bytes 98312 | tf_op jit(solution)/shard_map/ppermute | solution.py:69
  163.6 1.8 fusion.13
  165.5 1.8 convolution_add_fusion.4
  167.4 2.2 %collective-permute-start.15 = (bf16[32,512]{1,0:T(8,128)(2,1)S(1)}, bf16[32,512]{1,0:T(8,128)(2,1)S(1)}, u32[]{:S(2)}, u32[]{:S(2)}) collective-permute-start(bf16[32,512]{1,0:T(8,128)(2,1)S(1)} %get-tuple-element.38), channel_id=1, source_target_pairs={{0,5},{1,6},{2,7},{3,0},{4,1},{5,2},{6,3},{7,4},{8,13},{9,14},{10,... | collective-permute-start | bytes 98312 | tf_op jit(solution)/shard_map/ppermute | solution.py:69
  171.0 3.7 %collective-permute-start.14 = (bf16[32,512]{1,0:T(8,128)(2,1)S(1)}, bf16[32,512]{1,0:T(8,128)(2,1)S(1)}, u32[]{:S(2)}, u32[]{:S(2)}) collective-permute-start(bf16[32,512]{1,0:T(8,128)(2,1)S(1)} %get-tuple-element.39), channel_id=1, source_target_pairs={{0,6},{1,7},{2,0},{3,1},{4,2},{5,3},{6,4},{7,5},{8,14},{9,15},{10,... | collective-permute-start | bytes 98312 | tf_op jit(solution)/shard_map/ppermute | solution.py:69
  174.7 1.3 collective-permute-start.13
  176.0 0.8 pad_maximum_fusion.3
  176.8 5.8 %all-to-all-start.5 = ((bf16[16,32,512]{2,1,0:T(8,128)(2,1)}), bf16[16,32,512]{2,1,0:T(8,128)(2,1)S(1)}, u32[]{:S(2)}, u32[]{:S(2)}) async-start(bf16[16,32,512]{2,1,0:T(8,128)(2,1)} %bitcast.21), calls=%async_computation.5 | async-start | bytes 1048576 | tf_op jit(solution)/shard_map/all_to_all | solution.py:64
  183.3 4.6 %multiply_convert_fusion.1 = bf16[512,1792]{1,0:T(8,128)(2,1)} fusion(bf16[512,1792]{1,0:T(8,128)(2,1)} %get-tuple-element.23, bf16[256,3584]{1,0:T(8,128)(2,1)} %copy-done.21, bf16[256,3584]{1,0:T(8,128)(2,1)} %bitcast.20, bf16[256,512]{1,0:T(8,128)(2,1)S(1)} %copy-done.6, bf16[256,512]{1,0:T(8,128)(2,1)S(1)} %get-tuple-element.31), kind=kOutput, calls=%fused_computation.3 | convolution fusion | flops 946995200 | bytes 7864320 | tf_op jit(solution)/shard_map/dot_general | solution.py:49
  187.9 3.6 %multiply_convert_fusion.2 = bf16[512,1792]{1,0:T(8,128)(2,1)} fusion(bf16[512,1792]{1,0:T(8,128)(2,1)S(1)} %copy-done.19, bf16[256,3584]{1,0:T(8,128)(2,1)} %bitcast.20, bf16[256,3584]{1,0:T(8,128)(2,1)S(1)} %copy-done.22, bf16[256,512]{1,0:T(8,128)(2,1)S(1)} %copy-done.6, bf16[256,512]{1,0:T(8,128)(2,1)S(1)} %get-tuple-element.31), kind=kOutput, calls=%fused_computation.4 | convolution fusion | flops 946995200 | bytes 7864320 | tf_op jit(solution)/shard_map/dot_general | solution.py:49
  191.5 6.0 %all-to-all-done.5 = bf16[16,32,512]{2,1,0:T(8,128)(2,1)S(1)} async-done(((bf16[16,32,512]{2,1,0:T(8,128)(2,1)}), bf16[16,32,512]{2,1,0:T(8,128)(2,1)S(1)}, u32[]{:S(2)}, u32[]{:S(2)}) %all-to-all-start.5) | async-done | bytes 524320 | tf_op jit(solution)/shard_map/all_to_all | solution.py:64
  197.5 0.7 reduce_sum.32
  (97 shorter events, 12.0 us)
Async XLA Ops:
  2.3 28.2 %all-to-all-start = ((bf16[16,32,512]{2,1,0:T(8,128)(2,1)}), bf16[16,32,512]{2,1,0:T(8,128)(2,1)S(1)}, u32[]{:S(2)}, u32[]{:S(2)}) async-start(bf16[16,32,512]{2,1,0:T(8,128)(2,1)} %broadcast_in_dim.18), calls=%async_computation | async-start | bytes 1048576 | tf_op jit(solution)/shard_map/all_to_all | solution.py:58
  30.5 2.4 %copy-start.5 = (bf16[256,512]{1,0:T(8,128)(2,1)}, bf16[256,512]{1,0:T(8,128)(2,1)S(1)}, u32[]{:S(2)}) copy-start(bf16[256,512]{1,0:T(8,128)(2,1)S(1)} %get-tuple-element.32) | copy-start | bytes 786436
  30.5 2.4 %copy-start.1 = (bf16[512,1792]{1,0:T(8,128)(2,1)S(1)}, bf16[512,1792]{1,0:T(8,128)(2,1)}, u32[]{:S(2)}) copy-start(bf16[512,1792]{1,0:T(8,128)(2,1)} %get-tuple-element.15) | copy-start | bytes 5505028
  32.8 3.9 %collective-permute-start.1 = (f32[256,1792]{1,0:T(8,128)S(1)}, f32[256,1792]{1,0:T(8,128)S(1)}, u32[]{:S(2)}, u32[]{:S(2)}) collective-permute-start(f32[256,1792]{1,0:T(8,128)S(1)} %fusion.30), channel_id=1, source_target_pairs={{0,16},{16,0},{1,17},{17,1},{2,18},{18,2},{3,19},{19,3},{4,20},{20... | collective-permute-start | bytes 5505032 | tf_op jit(solution)/shard_map/ppermute | solution.py:53
  32.9 3.8 %copy-start.3 = (bf16[512,1792]{1,0:T(8,128)(2,1)S(1)}, bf16[512,1792]{1,0:T(8,128)(2,1)}, u32[]{:S(2)}) copy-start(bf16[512,1792]{1,0:T(8,128)(2,1)} %get-tuple-element.16) | copy-start | bytes 5505028
  33.6 5.7 %collective-permute-start = (f32[256,1792]{1,0:T(8,128)S(1)}, f32[256,1792]{1,0:T(8,128)S(1)}, u32[]{:S(2)}, u32[]{:S(2)}) collective-permute-start(f32[256,1792]{1,0:T(8,128)S(1)} %fusion.29), channel_id=1, source_target_pairs={{0,16},{16,0},{1,17},{17,1},{2,18},{18,2},{3,19},{19,3},{4,20},{20... | collective-permute-start | bytes 5505032 | tf_op jit(solution)/shard_map/ppermute | solution.py:53
  40.0 1.5 copy-start.18
  41.4 5.7 %collective-permute-start.2 = (bf16[32,512]{1,0:T(8,128)(2,1)S(1)}, bf16[32,512]{1,0:T(8,128)(2,1)S(1)}, u32[]{:S(2)}, u32[]{:S(2)}) collective-permute-start(bf16[32,512]{1,0:T(8,128)(2,1)S(1)} %copy-done.18), channel_id=1, source_target_pairs={{0,8},{8,0},{1,9},{9,1},{2,10},{10,2},{3,11},{11,3},{4,12},{12,4},... | collective-permute-start | bytes 98312 | tf_op jit(solution)/shard_map/ppermute | solution.py:69
  42.2 33.1 %all-to-all-start.1 = ((bf16[8,32,3584]{2,1,0:T(8,128)(2,1)}), bf16[8,32,3584]{2,1,0:T(8,128)(2,1)}, u32[]{:S(2)}, u32[]{:S(2)}) async-start(bf16[8,32,3584]{2,1,0:T(8,128)(2,1)} %bitcast.3), calls=%async_computation.1 | async-start | bytes 3670016 | tf_op jit(solution)/shard_map/all_to_all | solution.py:64
  47.1 26.3 %copy-start = (bf16[1792,512]{1,0:T(8,128)(2,1)S(1)}, bf16[1792,512]{1,0:T(8,128)(2,1)}, u32[]{:S(2)}) copy-start(bf16[1792,512]{1,0:T(8,128)(2,1)} %get-tuple-element.19) | copy-start | bytes 5505028
  47.2 22.0 %copy-start.10 = (bf16[2,32,512]{2,1,0:T(8,128)(2,1)}, bf16[2,32,512]{2,1,0:T(8,128)(2,1)S(1)}, u32[]{:S(2)}) copy-start(bf16[2,32,512]{2,1,0:T(8,128)(2,1)S(1)} %pad_maximum_fusion.8.refs_0_) | copy-start | bytes 196612
  47.2 11.1 %collective-permute-start.3 = (bf16[2,32,512]{2,1,0:T(8,128)(2,1)S(1)}, bf16[2,32,512]{2,1,0:T(8,128)(2,1)S(1)}, u32[]{:S(2)}, u32[]{:S(2)}) collective-permute-start(bf16[2,32,512]{2,1,0:T(8,128)(2,1)S(1)} %pad_maximum_fusion.8.refs_0_), channel_id=1, source_target_pairs={{0,7},{1,0},{2,1},{3,2},{4,3},{5,4},{6,5},{7,6},{8,15},{9,8},{10,9... | collective-permute-start | bytes 196616 | tf_op jit(solution)/shard_map/ppermute | solution.py:69
  49.9 11.0 %collective-permute-start.4 = (bf16[2,32,512]{2,1,0:T(8,128)(2,1)S(1)}, bf16[2,32,512]{2,1,0:T(8,128)(2,1)S(1)}, u32[]{:S(2)}, u32[]{:S(2)}) collective-permute-start(bf16[2,32,512]{2,1,0:T(8,128)(2,1)S(1)} %pad_maximum_fusion.8.refs_0_), channel_id=1, source_target_pairs={{0,6},{1,7},{2,0},{3,1},{4,2},{5,3},{6,4},{7,5},{8,14},{9,15},{10,... | collective-permute-start | bytes 196616 | tf_op jit(solution)/shard_map/ppermute | solution.py:69
  50.5 10.5 %collective-permute-start.5 = (bf16[2,32,512]{2,1,0:T(8,128)(2,1)S(1)}, bf16[2,32,512]{2,1,0:T(8,128)(2,1)S(1)}, u32[]{:S(2)}, u32[]{:S(2)}) collective-permute-start(bf16[2,32,512]{2,1,0:T(8,128)(2,1)S(1)} %pad_maximum_fusion.8.refs_0_), channel_id=1, source_target_pairs={{0,5},{1,6},{2,7},{3,0},{4,1},{5,2},{6,3},{7,4},{8,13},{9,14},{10,... | collective-permute-start | bytes 196616 | tf_op jit(solution)/shard_map/ppermute | solution.py:69
  53.7 9.7 %collective-permute-start.6 = (bf16[2,32,512]{2,1,0:T(8,128)(2,1)S(1)}, bf16[2,32,512]{2,1,0:T(8,128)(2,1)S(1)}, u32[]{:S(2)}, u32[]{:S(2)}) collective-permute-start(bf16[2,32,512]{2,1,0:T(8,128)(2,1)S(1)} %pad_maximum_fusion.8.refs_0_), channel_id=1, source_target_pairs={{0,4},{1,5},{2,6},{3,7},{4,0},{5,1},{6,2},{7,3},{8,12},{9,13},{10,... | collective-permute-start | bytes 196616 | tf_op jit(solution)/shard_map/ppermute | solution.py:69
  56.8 9.2 %collective-permute-start.7 = (bf16[2,32,512]{2,1,0:T(8,128)(2,1)S(1)}, bf16[2,32,512]{2,1,0:T(8,128)(2,1)S(1)}, u32[]{:S(2)}, u32[]{:S(2)}) collective-permute-start(bf16[2,32,512]{2,1,0:T(8,128)(2,1)S(1)} %pad_maximum_fusion.8.refs_0_), channel_id=1, source_target_pairs={{0,3},{1,4},{2,5},{3,6},{4,7},{5,0},{6,1},{7,2},{8,11},{9,12},{10,... | collective-permute-start | bytes 196616 | tf_op jit(solution)/shard_map/ppermute | solution.py:69
  58.3 10.9 %copy-start.11 = (bf16[2,32,512]{2,1,0:T(8,128)(2,1)}, bf16[2,32,512]{2,1,0:T(8,128)(2,1)S(1)}, u32[]{:S(2)}) copy-start(bf16[2,32,512]{2,1,0:T(8,128)(2,1)S(1)} %collective-permute-done.3.refs_1_) | copy-start | bytes 196612
  58.3 10.3 %collective-permute-start.8 = (bf16[2,32,512]{2,1,0:T(8,128)(2,1)S(1)}, bf16[2,32,512]{2,1,0:T(8,128)(2,1)S(1)}, u32[]{:S(2)}, u32[]{:S(2)}) collective-permute-start(bf16[2,32,512]{2,1,0:T(8,128)(2,1)S(1)} %pad_maximum_fusion.8.refs_0_), channel_id=1, source_target_pairs={{0,2},{1,3},{2,4},{3,5},{4,6},{5,7},{6,0},{7,1},{8,10},{9,11},{10,... | collective-permute-start | bytes 196616 | tf_op jit(solution)/shard_map/ppermute | solution.py:69
  60.9 8.2 %copy-start.12 = (bf16[2,32,512]{2,1,0:T(8,128)(2,1)}, bf16[2,32,512]{2,1,0:T(8,128)(2,1)S(1)}, u32[]{:S(2)}) copy-start(bf16[2,32,512]{2,1,0:T(8,128)(2,1)S(1)} %collective-permute-done.4.refs_2_) | copy-start | bytes 196612
  60.9 8.2 %collective-permute-start.9 = (bf16[2,32,512]{2,1,0:T(8,128)(2,1)S(1)}, bf16[2,32,512]{2,1,0:T(8,128)(2,1)S(1)}, u32[]{:S(2)}, u32[]{:S(2)}) collective-permute-start(bf16[2,32,512]{2,1,0:T(8,128)(2,1)S(1)} %pad_maximum_fusion.8.refs_0_), channel_id=1, source_target_pairs={{0,1},{1,2},{2,3},{3,4},{4,5},{5,6},{6,7},{7,0},{8,9},{9,10},{10,1... | collective-permute-start | bytes 196616 | tf_op jit(solution)/shard_map/ppermute | solution.py:69
  60.9 8.2 %copy-start.13 = (bf16[2,32,512]{2,1,0:T(8,128)(2,1)}, bf16[2,32,512]{2,1,0:T(8,128)(2,1)S(1)}, u32[]{:S(2)}) copy-start(bf16[2,32,512]{2,1,0:T(8,128)(2,1)S(1)} %collective-permute-done.5.refs_3_) | copy-start | bytes 196612
  63.4 5.7 %copy-start.14 = (bf16[2,32,512]{2,1,0:T(8,128)(2,1)}, bf16[2,32,512]{2,1,0:T(8,128)(2,1)S(1)}, u32[]{:S(2)}) copy-start(bf16[2,32,512]{2,1,0:T(8,128)(2,1)S(1)} %collective-permute-done.6.refs_4_) | copy-start | bytes 196612
  65.9 3.2 %copy-start.15 = (bf16[2,32,512]{2,1,0:T(8,128)(2,1)}, bf16[2,32,512]{2,1,0:T(8,128)(2,1)S(1)}, u32[]{:S(2)}) copy-start(bf16[2,32,512]{2,1,0:T(8,128)(2,1)S(1)} %collective-permute-done.7.refs_5_) | copy-start | bytes 196612
  68.5 0.6 copy-start.16
  73.4 1.9 copy-start.8
  75.3 8.6 %collective-permute-start.10 = (f32[256,1792]{1,0:T(8,128)}, f32[256,1792]{1,0:T(8,128)}, u32[]{:S(2)}, u32[]{:S(2)}) collective-permute-start(f32[256,1792]{1,0:T(8,128)} %fusion.31), channel_id=1, source_target_pairs={{0,16},{16,0},{1,17},{17,1},{2,18},{18,2},{3,19},{19,3},{4,20},{20... | collective-permute-start | bytes 5505032 | tf_op jit(solution)/shard_map/ppermute | solution.py:53
  78.2 18.7 %all-to-all-start.2 = ((bf16[8,32,1792]{2,1,0:T(8,128)(2,1)}), bf16[8,32,1792]{2,1,0:T(8,128)(2,1)}, u32[]{:S(2)}, u32[]{:S(2)}) async-start(bf16[8,32,1792]{2,1,0:T(8,128)(2,1)} %broadcast_in_dim.22), calls=%async_computation.2 | async-start | bytes 1835008 | tf_op jit(solution)/shard_map/all_to_all | solution.py:58
  116.2 26.9 %all-to-all-start.4 = ((bf16[8,32,3584]{2,1,0:T(8,128)(2,1)}), bf16[8,32,3584]{2,1,0:T(8,128)(2,1)}, u32[]{:S(2)}, u32[]{:S(2)}) async-start(bf16[8,32,3584]{2,1,0:T(8,128)(2,1)} %broadcast_in_dim.23), calls=%async_computation.4 | async-start | bytes 3670016 | tf_op jit(solution)/shard_map/all_to_all | solution.py:58
  121.9 23.0 %collective-permute-start.11 = (bf16[256,1792]{1,0:T(8,128)(2,1)}, bf16[256,1792]{1,0:T(8,128)(2,1)S(1)}, u32[]{:S(2)}, u32[]{:S(2)}) collective-permute-start(bf16[256,1792]{1,0:T(8,128)(2,1)} %bitcast.4), channel_id=1, source_target_pairs={{0,16},{16,0},{1,17},{17,1},{2,18},{18,2},{3,19},{19,3},{4,20},{20... | collective-permute-start | bytes 2752520 | tf_op jit(solution)/shard_map/ppermute | solution.py:53
  143.1 24.2 %collective-permute-start.20 = (bf16[256,3584]{1,0:T(8,128)(2,1)}, bf16[256,3584]{1,0:T(8,128)(2,1)S(1)}, u32[]{:S(2)}, u32[]{:S(2)}) collective-permute-start(bf16[256,3584]{1,0:T(8,128)(2,1)} %bitcast.20), channel_id=1, source_target_pairs={{0,16},{16,0},{1,17},{17,1},{2,18},{18,2},{3,19},{19,3},{4,20},{20... | collective-permute-start | bytes 5505032 | tf_op jit(solution)/shard_map/ppermute | solution.py:53
  144.9 3.1 %copy-start.7 = (bf16[256,512]{1,0:T(8,128)(2,1)S(1)}, bf16[256,512]{1,0:T(8,128)(2,1)}, u32[]{:S(2)}) copy-start(bf16[256,512]{1,0:T(8,128)(2,1)} %get-tuple-element.29) | copy-start | bytes 786436
  145.0 3.0 %copy-start.9 = (bf16[256,512]{1,0:T(8,128)(2,1)S(1)}, bf16[256,512]{1,0:T(8,128)(2,1)}, u32[]{:S(2)}) copy-start(bf16[256,512]{1,0:T(8,128)(2,1)} %copy-done.8) | copy-start | bytes 786436
  145.0 3.0 %copy-start.20 = (bf16[1792,512]{1,0:T(8,128)(2,1)S(1)}, bf16[1792,512]{1,0:T(8,128)(2,1)}, u32[]{:S(2)}) copy-start(bf16[1792,512]{1,0:T(8,128)(2,1)} %get-tuple-element.24) | copy-start | bytes 5505028
  145.6 10.3 %collective-permute-start.12 = (bf16[256,512]{1,0:T(8,128)(2,1)S(1)}, bf16[256,512]{1,0:T(8,128)(2,1)S(1)}, u32[]{:S(2)}, u32[]{:S(2)}) collective-permute-start(bf16[256,512]{1,0:T(8,128)(2,1)S(1)} %get-tuple-element.42), channel_id=1, source_target_pairs={{0,8},{8,0},{1,9},{9,1},{2,10},{10,2},{3,11},{11,3},{4,12},{12,4},... | collective-permute-start | bytes 786440 | tf_op jit(solution)/shard_map/ppermute | solution.py:69
  151.6 12.1 %copy-start.2 = (bf16[512,1792]{1,0:T(8,128)(2,1)S(1)}, bf16[512,1792]{1,0:T(8,128)(2,1)}, u32[]{:S(2)}) copy-start(bf16[512,1792]{1,0:T(8,128)(2,1)} %get-tuple-element.15) | copy-start | bytes 5505028
  156.2 9.3 %copy-start.4 = (bf16[512,1792]{1,0:T(8,128)(2,1)S(1)}, bf16[512,1792]{1,0:T(8,128)(2,1)}, u32[]{:S(2)}) copy-start(bf16[512,1792]{1,0:T(8,128)(2,1)} %get-tuple-element.16) | copy-start | bytes 5505028
  156.2 14.8 %collective-permute-start.19 = (bf16[32,512]{1,0:T(8,128)(2,1)S(1)}, bf16[32,512]{1,0:T(8,128)(2,1)S(1)}, u32[]{:S(2)}, u32[]{:S(2)}) collective-permute-start(bf16[32,512]{1,0:T(8,128)(2,1)S(1)} %get-tuple-element.34), channel_id=1, source_target_pairs={{0,1},{1,2},{2,3},{3,4},{4,5},{5,6},{6,7},{7,0},{8,9},{9,10},{10,1... | collective-permute-start | bytes 98312 | tf_op jit(solution)/shard_map/ppermute | solution.py:69
  156.8 17.8 %collective-permute-start.18 = (bf16[32,512]{1,0:T(8,128)(2,1)S(1)}, bf16[32,512]{1,0:T(8,128)(2,1)S(1)}, u32[]{:S(2)}, u32[]{:S(2)}) collective-permute-start(bf16[32,512]{1,0:T(8,128)(2,1)S(1)} %get-tuple-element.35), channel_id=1, source_target_pairs={{0,2},{1,3},{2,4},{3,5},{4,6},{5,7},{6,0},{7,1},{8,10},{9,11},{10,... | collective-permute-start | bytes 98312 | tf_op jit(solution)/shard_map/ppermute | solution.py:69
  158.0 24.6 %collective-permute-start.17 = (bf16[32,512]{1,0:T(8,128)(2,1)S(1)}, bf16[32,512]{1,0:T(8,128)(2,1)S(1)}, u32[]{:S(2)}, u32[]{:S(2)}) collective-permute-start(bf16[32,512]{1,0:T(8,128)(2,1)S(1)} %get-tuple-element.36), channel_id=1, source_target_pairs={{0,3},{1,4},{2,5},{3,6},{4,7},{5,0},{6,1},{7,2},{8,11},{9,12},{10,... | collective-permute-start | bytes 98312 | tf_op jit(solution)/shard_map/ppermute | solution.py:69
  160.5 22.1 %collective-permute-start.16 = (bf16[32,512]{1,0:T(8,128)(2,1)S(1)}, bf16[32,512]{1,0:T(8,128)(2,1)S(1)}, u32[]{:S(2)}, u32[]{:S(2)}) collective-permute-start(bf16[32,512]{1,0:T(8,128)(2,1)S(1)} %get-tuple-element.37), channel_id=1, source_target_pairs={{0,4},{1,5},{2,6},{3,7},{4,0},{5,1},{6,2},{7,3},{8,12},{9,13},{10,... | collective-permute-start | bytes 98312 | tf_op jit(solution)/shard_map/ppermute | solution.py:69
  167.3 3.6 %copy-start.21 = (bf16[256,3584]{1,0:T(8,128)(2,1)}, bf16[256,3584]{1,0:T(8,128)(2,1)S(1)}, u32[]{:S(2)}) copy-start(bf16[256,3584]{1,0:T(8,128)(2,1)S(1)} %collective-permute-done.20) | copy-start | bytes 5505028
  167.4 15.3 %collective-permute-start.15 = (bf16[32,512]{1,0:T(8,128)(2,1)S(1)}, bf16[32,512]{1,0:T(8,128)(2,1)S(1)}, u32[]{:S(2)}, u32[]{:S(2)}) collective-permute-start(bf16[32,512]{1,0:T(8,128)(2,1)S(1)} %get-tuple-element.38), channel_id=1, source_target_pairs={{0,5},{1,6},{2,7},{3,0},{4,1},{5,2},{6,3},{7,4},{8,13},{9,14},{10,... | collective-permute-start | bytes 98312 | tf_op jit(solution)/shard_map/ppermute | solution.py:69
  171.0 12.3 %copy-start.6 = (bf16[256,512]{1,0:T(8,128)(2,1)S(1)}, bf16[256,512]{1,0:T(8,128)(2,1)}, u32[]{:S(2)}) copy-start(bf16[256,512]{1,0:T(8,128)(2,1)} %copy-done.5) | copy-start | bytes 786436
  171.0 11.6 %collective-permute-start.14 = (bf16[32,512]{1,0:T(8,128)(2,1)S(1)}, bf16[32,512]{1,0:T(8,128)(2,1)S(1)}, u32[]{:S(2)}, u32[]{:S(2)}) collective-permute-start(bf16[32,512]{1,0:T(8,128)(2,1)S(1)} %get-tuple-element.39), channel_id=1, source_target_pairs={{0,6},{1,7},{2,0},{3,1},{4,2},{5,3},{6,4},{7,5},{8,14},{9,15},{10,... | collective-permute-start | bytes 98312 | tf_op jit(solution)/shard_map/ppermute | solution.py:69
  174.7 8.0 %collective-permute-start.13 = (bf16[32,512]{1,0:T(8,128)(2,1)S(1)}, bf16[32,512]{1,0:T(8,128)(2,1)S(1)}, u32[]{:S(2)}, u32[]{:S(2)}) collective-permute-start(bf16[32,512]{1,0:T(8,128)(2,1)S(1)} %get-tuple-element.33), channel_id=1, source_target_pairs={{0,7},{1,0},{2,1},{3,2},{4,3},{5,4},{6,5},{7,6},{8,15},{9,8},{10,9... | collective-permute-start | bytes 98312 | tf_op jit(solution)/shard_map/ppermute | solution.py:69
  176.8 20.7 %all-to-all-start.5 = ((bf16[16,32,512]{2,1,0:T(8,128)(2,1)}), bf16[16,32,512]{2,1,0:T(8,128)(2,1)S(1)}, u32[]{:S(2)}, u32[]{:S(2)}) async-start(bf16[16,32,512]{2,1,0:T(8,128)(2,1)} %bitcast.21), calls=%async_computation.5 | async-start | bytes 1048576 | tf_op jit(solution)/shard_map/all_to_all | solution.py:64
  183.3 4.6 %copy-start.19 = (bf16[512,1792]{1,0:T(8,128)(2,1)S(1)}, bf16[512,1792]{1,0:T(8,128)(2,1)}, u32[]{:S(2)}) copy-start(bf16[512,1792]{1,0:T(8,128)(2,1)} %get-tuple-element.22) | copy-start | bytes 5505028
  183.3 4.6 %copy-start.22 = (bf16[256,3584]{1,0:T(8,128)(2,1)S(1)}, bf16[256,3584]{1,0:T(8,128)(2,1)}, u32[]{:S(2)}) copy-start(bf16[256,3584]{1,0:T(8,128)(2,1)} %copy-done.21) | copy-start | bytes 5505028
  (1 other events, 0.6 us)

commit v3 on v1

v3 whole, which is shorter than its diff:
```python
import jax
import jax.numpy as jnp
from jax import lax
from jax.experimental import pallas as pl
from jax.experimental.pallas import tpu as pltpu
from jax.sharding import Mesh
from jax.sharding import PartitionSpec as P


ROW = ("x_lo", "y", "core")
COL = ("x_hi", "z")
PAIR = ("x_lo", "y")
BF = jnp.bfloat16
F32 = jnp.float32
BLK = 128
STEP = 256


def local_call(kernel, outs, *args):
    whole = pl.BlockSpec(memory_space=pltpu.VMEM)
    single = not isinstance(outs, list)
    return pl.pallas_call(
        kernel,
        out_shape=outs,
        in_specs=[whole] * len(args),
        out_specs=whole if single else [whole] * len(outs),
    )(*args)


def nn(left, right):
    return jnp.dot(left, right, preferred_element_type=F32)


def nt(left, right):
    return lax.dot_general(left, right, (((1,), (1,)), ((), ())), preferred_element_type=F32)


def prepare_kernel(*refs):
    for weight, mask, eff in zip(refs[0:3], refs[3:6], refs[6:9]):
        for i in range(mask.shape[0]):
            rows = pl.ds(i * BLK, BLK)
            keep = jnp.broadcast_to(mask[pl.ds(i, 1), :], (BLK, mask.shape[1])).astype(BF)
            eff[rows, :] = weight[rows, :] * keep


def partial_kernel(own, cross, gate, up, down, gate_x, up_x, down_x, out):
    width = gate.shape[0]
    hid = gate.shape[1]
    rows, rows_x = own[:, :width], cross[:, :width]
    cot, cot_x = own[:, width:], cross[:, width:]
    for j in range(hid // STEP):
        cols = pl.ds(j * STEP, STEP)
        out[:, cols] = (nn(rows, gate[:, cols]) + nn(rows_x, gate_x[:, cols])).astype(BF)
        out[:, pl.ds(hid + j * STEP, STEP)] = (
            nn(rows, up[:, cols]) + nn(rows_x, up_x[:, cols])
        ).astype(BF)
        out[:, pl.ds(2 * hid + j * STEP, STEP)] = (
            nt(cot, down[cols, :]) + nt(cot_x, down_x[cols, :])
        ).astype(BF)


def activation_kernel(got, out):
    copies = got.shape[0]
    hid = got.shape[2] // 3

    def total(start):
        cols = pl.ds(start, STEP)
        acc = got[0, :, cols].astype(F32)
        for i in range(1, copies):
            acc = acc + got[i, :, cols].astype(F32)
        return acc

    for j in range(hid // STEP):
        starts = [part * hid + j * STEP for part in range(3)]
        gate, up, d_hidden = [total(start) for start in starts]
        sigmoid = jax.nn.sigmoid(gate)
        activated = gate * sigmoid
        values = (
            activated * up,
            d_hidden * up * sigmoid * (1.0 + gate * (1.0 - sigmoid)),
            d_hidden * activated,
        )
        for start, value in zip(starts, values):
            rounded = value.astype(BF)
            for i in range(copies):
                out[i, :, pl.ds(start, STEP)] = rounded


def result_kernel(acts, gate, up, down, out):
    hid = gate.shape[1]
    width = gate.shape[0]
    out[:, :width] = nn(acts[:, :hid], down[...]).astype(BF)
    out[:, width:] = (
        nt(acts[:, hid : 2 * hid], gate[...]) + nt(acts[:, 2 * hid :], up[...])
    ).astype(BF)


def gradient_kernel(acts, acts_x, own, other, *refs):
    masks, (grad_gate, grad_up, grad_down) = refs[:3], refs[3:]
    width, hid = grad_gate.shape
    rows, rows_x = own[:, :width].T, other[:, :width].T
    cot, cot_x = own[:, width:], other[:, width:]
    for j in range(hid // STEP):
        for part, mask, grad in ((1, masks[0], grad_gate), (2, masks[1], grad_up)):
            cols = pl.ds(part * hid + j * STEP, STEP)
            here = pl.ds(j * STEP, STEP)
            value = nn(rows, acts[:, cols]) + nn(rows_x, acts_x[:, cols])
            for i in range(width // BLK):
                keep = mask[pl.ds(i, 1), here]
                grad[pl.ds(i * BLK, BLK), here] = (value[i * BLK : (i + 1) * BLK] * keep).astype(BF)
        cols = pl.ds(j * STEP, STEP)
        value = nn(acts[:, cols].T, cot) + nn(acts_x[:, cols].T, cot_x)
        for i in range(STEP // BLK):
            keep = masks[2][pl.ds(j * (STEP // BLK) + i, 1), :]
            grad_down[pl.ds(j * STEP + i * BLK, BLK), :] = (
                value[i * BLK : (i + 1) * BLK] * keep
            ).astype(BF)


def swap(array):
    return lax.ppermute(array, "core", [(0, 1), (1, 0)])


def layer(
    tokens, cotangent, gate_weight, up_weight, down_weight, gate_mask, up_mask, down_mask
):
    share, width = tokens.shape
    hid = gate_weight.shape[1]
    core = lax.axis_index("core")
    pairs = lax.axis_size(PAIR)
    cols = lax.axis_size(COL)
    half = share // 2

    both = jnp.concatenate([tokens, cotangent], axis=1)
    gathered = lax.all_to_all(
        jnp.broadcast_to(both, (cols,) + both.shape), COL, 0, 0, tiled=True
    )
    weights = (gate_weight, up_weight, down_weight)
    shapes = [jax.ShapeDtypeStruct(weight.shape, BF) for weight in weights]
    wide = [
        jnp.repeat(mask.astype(F32), BLK, axis=1) for mask in (gate_mask, up_mask, down_mask)
    ]
    effs = local_call(prepare_kernel, shapes, *weights, *wide)
    effs_x = [swap(eff) for eff in effs]

    own = lax.dynamic_slice_in_dim(gathered, core * half, half, 1).reshape(-1, 2 * width)
    other = lax.dynamic_slice_in_dim(gathered, (1 - core) * half, half, 1).reshape(-1, 2 * width)
    cross = swap(other)
    parts = local_call(
        partial_kernel,
        jax.ShapeDtypeStruct((own.shape[0], 3 * hid), BF),
        own,
        cross,
        *effs,
        *effs_x,
    ).reshape(pairs, -1, 3 * hid)
    got = lax.all_to_all(parts, PAIR, 0, 0, tiled=True)
    copies = local_call(activation_kernel, jax.ShapeDtypeStruct(got.shape, BF), got)
    acts = lax.all_to_all(copies, PAIR, 0, 0, tiled=True).reshape(-1, 3 * hid)

    result_shape = jax.ShapeDtypeStruct((acts.shape[0], 2 * width), BF)
    away = swap(local_call(result_kernel, result_shape, acts, *effs_x))
    here = local_call(result_kernel, result_shape, acts, *effs)
    send = jnp.concatenate(
        [here.reshape(cols, half, 2 * width), away.reshape(cols, half, 2 * width)], axis=1
    )
    arrived = lax.all_to_all(send, COL, 0, 0, tiled=True)
    sums = jnp.sum(arrived.astype(F32), axis=0)
    first, second = sums[:half], sums[half:]
    sums = jnp.concatenate(
        [jnp.where(core == 0, first, second), jnp.where(core == 0, second, first)], axis=0
    ).astype(BF)
    output, d_tokens = sums[:, :width], sums[:, width:]

    send, acts_late = lax.optimization_barrier((send, acts))
    acts_x = swap(acts_late)
    grad_gate, grad_up, grad_down = local_call(
        gradient_kernel, shapes, acts_late, acts_x, own, other, *wide
    )
    return (output, d_tokens, grad_gate, grad_up, grad_down)


def solution(mesh):
    fine = Mesh(mesh.devices.reshape(2, 4, 2, 2, 8), ROW + COL)
    in_specs = (
        P(COL, ROW),
        P(COL, ROW),
        P(ROW, COL),
        P(ROW, COL),
        P(COL, ROW),
        P(ROW, COL),
        P(ROW, COL),
        P(COL, ROW),
    )
    out_specs = (P(COL, ROW), P(COL, ROW), P(ROW, COL), P(ROW, COL), P(COL, ROW))
    return jax.shard_map(layer, mesh=fine, in_specs=in_specs, out_specs=out_specs, check_vma=False)
```

time: 195 us -> 193 us (0.990)
  Pallas kernels: 0 us -> 38 us
  local copies, waits for them, and re-layouts: 40.9 us -> 4.43 us
  waiting for transfers between devices: 34.6 us -> 52 us
  matrix products: 17 us -> 0 us
  other arithmetic: 11 us -> 4.95 us
    pallas_call x0 -> x6, Pallas kernels: none -> 38 us  [local_call(): pl.pallas_call(kernel, out_shape=outs, in_specs=[whole] * len(args), out_...]
    all_to_all x2, waiting for transfers between devices: 23.7 us -> 50.1 us  [the longest x1 28.8 us: layer(): arrived = lax.all_to_all(send, COL, 0, 0, tiled=True)]
    unnamed x40 -> x18, local copies, waits for them, and re-layouts: 22.9 us -> 1.6 us
    dot_general x9 -> x0, matrix products: 17 us -> none  [the longest x3 9.97 us: left_product(): lax.dot_general(left, right, (((0,), (0,)), ((), ())), preferred_element_...]
    mul x8 -> x0, local copies, waits for them, and re-layouts: 13.7 us -> none  [masked(): shaped * block_mask.astype(weight.dtype)[:, None, :, None]]
    ppermute x2 -> x6, waiting for transfers between devices: 10.9 us -> 1.88 us  [swap(): return lax.ppermute(array, 'core', [(0, 1), (1, 0)])]
    convert_element_type x5 -> x3, other arithmetic: 4.03 us -> 0.01 us  [layer(): mask.astype(F32)]
    another operation x2 -> x1, other arithmetic: 3.47 us -> 0.01 us  [per_device(): acts = jnp.stack([first, second], axis=1).reshape(col_n * share, 3 * hid)]
  transfers between devices with their start and end apart: 4 -> 8, of which waited for: 4 -> 3; matrix products, arithmetic and copies ran while one was open for 17% -> 2% of each run, Pallas kernels for 0% -> 6%
where the time goes in v3:
time: 193 us; the launch traced here: 192 us
  blocking collectives  75.4 us (39%)
  waiting for transfers between devices  52 us (27%)
  Pallas kernels  38 us (20%)
  starting transfers between devices  16.9 us (9%)
  other arithmetic  4.95 us (3%)
  local copies, waits for them, and re-layouts  4.43 us (2%)
    pallas_call x6, Pallas kernels, local_call(): pl.pallas_call(kernel, out_shape=outs, in_specs=[whole] * len(args), out_...  38 us
    all_to_all x1, blocking collectives, layer(): got = lax.all_to_all(parts, PAIR, 0, 0, tiled=True)  37.9 us
    all_to_all x1, blocking collectives, layer(): acts = lax.all_to_all(copies, PAIR, 0, 0, tiled=True).reshape(-1, 3 * hid)  37.6 us
    all_to_all x1, waiting for transfers between devices, layer(): arrived = lax.all_to_all(send, COL, 0, 0, tiled=True)  28.8 us
    all_to_all x1, waiting for transfers between devices, layer(): lax.all_to_all(jnp.broadcast_to(both, (cols,) + both.shape), COL, 0, 0, t...  21.3 us
    all_to_all x1, starting transfers between devices, layer(): lax.all_to_all(jnp.broadcast_to(both, (cols,) + both.shape), COL, 0, 0, t...  11 us
    all_to_all x1, starting transfers between devices, layer(): arrived = lax.all_to_all(send, COL, 0, 0, tiled=True)  4.82 us
  transfers between devices with their start and end apart: 8, of which 3 were waited for; matrix products, arithmetic and copies ran while one was open for 2% of the time, Pallas kernels for 6%

profile of v3, /device:TPU:8, one launch (start us, length us, event | category | flops | bytes accessed | tf_op | source)
XLA Modules:
  0.0 192.5 jit_solution(13455623123360412447)
XLA Ops:
  0.6 0.0 copy-start.4
  0.6 0.0 copy-start.5
  0.7 0.0 copy-start.6
  0.7 0.8 pad_maximum_fusion.1
  1.5 1.1 broadcast_in_dim.12
  2.6 11.0 %all-to-all-start = ((bf16[16,32,1024]{2,1,0:T(8,128)(2,1)}), bf16[16,32,1024]{2,1,0:T(8,128)(2,1)S(1)}, u32[]{:S(2)}, u32[]{:S(2)}) async-start(bf16[16,32,1024]{2,1,0:T(8,128)(2,1)} %broadcast_in_dim.12), calls=%async_computation | async-start | bytes 2097152 | tf_op jit(solution)/shard_map/all_to_all | solution.py:135
  13.6 0.0 copy-done.4
  13.6 0.0 copy-done.5
  13.7 0.0 copy-done.6
  13.7 0.1 copy.14
  13.8 0.1 broadcast_in_dim.15
  13.9 0.6 copy.17
  14.5 0.1 broadcast_bitcast_fusion
  14.6 0.1 broadcast_bitcast_fusion.1
  14.6 0.6 copy_bitcast_fusion
  15.3 5.2 %shard_map.119 = (bf16[512,1792]{1,0:T(8,128)(2,1)}, bf16[512,1792]{1,0:T(8,128)(2,1)}, bf16[1792,512]{1,0:T(8,128)(2,1)}) custom-call(bf16[512,1792]{1,0:T(8,128)(2,1)} %refs_0_.1, bf16[512,1792]{1,0:T(8,128)(2,1)} %refs_1_.1, bf16[1792,512]{1,0:T(8,128)(2,1)} %refs_2_.1, f32[4,1792]{1,0:T(4,128)} %get-tuple-element.26.refs_3_.refs_0_, ...), custom_call_target="tpu_custom_call" | custom-call | tf_op jit(solution)/shard_map/pallas_call | solution.py:22
  20.5 0.0 collective-permute-start.1
  20.5 0.5 collective-permute-start.2
  21.0 0.0 collective-permute-start.3
  21.0 21.3 %all-to-all-done = bf16[16,32,1024]{2,1,0:T(8,128)(2,1)S(1)} async-done(((bf16[16,32,1024]{2,1,0:T(8,128)(2,1)}), bf16[16,32,1024]{2,1,0:T(8,128)(2,1)S(1)}, u32[]{:S(2)}, u32[]{:S(2)}) %all-to-all-start) | async-done | bytes 1048608 | tf_op jit(solution)/shard_map/all_to_all | solution.py:135
  42.2 0.9 constant_dynamic-slice_fusion
  43.1 0.0 copy-start.2
  43.1 0.0 collective-permute-start
  43.1 0.0 collective-permute-done.1.gate_x.gate
  43.2 0.0 copy-start.1
  43.2 0.0 collective-permute-done.2.up_x.up
  43.2 0.0 collective-permute-done.3.down_x.down
  43.2 1.9 collective-permute-done.cross
  45.1 0.0 copy-done.1
  45.1 0.8 copy-done.3
  45.9 9.1 %shard_map.120 = bf16[256,5376]{1,0:T(8,128)(2,1)} custom-call(bf16[256,1024]{1,0:T(8,128)(2,1)} %bitcast.22, bf16[256,1024]{1,0:T(8,128)(2,1)} %copy-done.3, bf16[512,1792]{1,0:T(8,128)(2,1)} %get-tuple-element.12.gate, bf16[512,1792]{1,0:T(8,128)(2,1)} %get-tuple-element.13.up, bf16[1792,512]{1,0:T(8,128)(2,1)} %get-tuple-element.14.down, ...), custom_call_target="tpu_custom_call" | custom-call | tf_op jit(solution)/shard_map/pallas_call | solution.py:22
  54.9 0.0 copy-done.2
  54.9 37.9 %all_to_all.20.got = bf16[8,32,5376]{2,1,0:T(8,128)(2,1)} all-to-all(bf16[8,32,5376]{2,1,0:T(8,128)(2,1)} %bitcast.21), channel_id=1, replica_groups=mesh['x_lo'=2,'y'=4,'core'=2,'x_hi'=2,'z'=8] {'x_lo','y'}, dimensions={0} | all-to-all | bytes 5505024 | tf_op jit(solution)/shard_map/all_to_all | solution.py:157
  92.8 3.8 %shard_map.121 = bf16[8,32,5376]{2,1,0:T(8,128)(2,1)} custom-call(bf16[8,32,5376]{2,1,0:T(8,128)(2,1)} %all_to_all.20.got), custom_call_target="tpu_custom_call" | custom-call | tf_op jit(solution)/shard_map/pallas_call | solution.py:22
  96.6 37.6 %all_to_all.21 = bf16[8,32,5376]{2,1,0:T(8,128)(2,1)} all-to-all(bf16[8,32,5376]{2,1,0:T(8,128)(2,1)} %shard_map.121), channel_id=1, replica_groups=mesh['x_lo'=2,'y'=4,'core'=2,'x_hi'=2,'z'=8] {'x_lo','y'}, dimensions={0} | all-to-all | bytes 5505024 | tf_op jit(solution)/shard_map/all_to_all | solution.py:159
  134.1 5.8 %shard_map.123 = bf16[256,1024]{1,0:T(8,128)(2,1)} custom-call(bf16[256,5376]{1,0:T(8,128)(2,1)} %bitcast.17, bf16[512,1792]{1,0:T(8,128)(2,1)} %copy-done.1, bf16[512,1792]{1,0:T(8,128)(2,1)} %collective-permute-done.2.up_x.up, bf16[1792,512]{1,0:T(8,128)(2,1)} %collective-permute-done.3.down_x.down), custom_call_target="tpu_custom_call" | custom-call | tf_op jit(solution)/shard_map/pallas_call | solution.py:22
  140.0 0.0 collective-permute-start.4
  140.0 5.9 %shard_map.122 = bf16[256,1024]{1,0:T(8,128)(2,1)} custom-call(bf16[256,5376]{1,0:T(8,128)(2,1)} %bitcast.18, bf16[512,1792]{1,0:T(8,128)(2,1)} %get-tuple-element.12.gate, bf16[512,1792]{1,0:T(8,128)(2,1)} %get-tuple-element.13.up, bf16[1792,512]{1,0:T(8,128)(2,1)} %get-tuple-element.14.down), custom_call_target="tpu_custom_call" | custom-call | tf_op jit(solution)/shard_map/pallas_call | solution.py:22
  145.9 0.0 collective-permute-done.4
  145.9 2.1 %pad_maximum_fusion = bf16[16,32,1024]{2,1,0:T(8,128)(2,1)} fusion(bf16[16,16,1024]{2,1,0:T(8,128)(2,1)S(1)} %bitcast.27, bf16[16,16,1024]{2,1,0:T(8,128)(2,1)} %bitcast.26), kind=kLoop, calls=%fused_computation.1 | loop fusion | flops 2097152 | bytes 2097152 | tf_op jit(solution)/shard_map/concatenate | solution.py:164
  148.0 0.0 copy-done
  148.0 0.5 collective-permute-start.5
  148.5 4.8 %all-to-all-start.3 = ((bf16[16,32,1024]{2,1,0:T(8,128)(2,1)}), bf16[16,32,1024]{2,1,0:T(8,128)(2,1)}, u32[]{:S(2)}, u32[]{:S(2)}) async-start(bf16[16,32,1024]{2,1,0:T(8,128)(2,1)} %pad_maximum_fusion), calls=%async_computation.3 | async-start | bytes 2097152 | tf_op jit(solution)/shard_map/all_to_all | solution.py:167
  153.4 28.8 %all-to-all-done.3 = bf16[16,32,1024]{2,1,0:T(8,128)(2,1)} async-done(((bf16[16,32,1024]{2,1,0:T(8,128)(2,1)}), bf16[16,32,1024]{2,1,0:T(8,128)(2,1)}, u32[]{:S(2)}, u32[]{:S(2)}) %all-to-all-start.3) | async-done | bytes 1048608 | tf_op jit(solution)/shard_map/all_to_all | solution.py:167
  182.2 1.4 convert_reduce_fusion
  183.6 0.6 pad_maximum_fusion.2
  184.2 0.0 collective-permute-done.5.acts_x
  184.2 8.2 %shard_map.124 = (bf16[512,1792]{1,0:T(8,128)(2,1)}, bf16[512,1792]{1,0:T(8,128)(2,1)}, bf16[1792,512]{1,0:T(8,128)(2,1)}) custom-call(bf16[256,5376]{1,0:T(8,128)(2,1)} %bitcast.19, bf16[256,5376]{1,0:T(8,128)(2,1)} %collective-permute-done.5.acts_x, bf16[256,1024]{1,0:T(8,128)(2,1)} %bitcast.23, bf16[256,1024]{1,0:T(8,128)(2,1)} %bitcast.25, ...), custom_call_target="tpu_custom_call" | custom-call | tf_op jit(solution)/shard_map/pallas_call | solution.py:22
  (7 shorter events, 0.0 us)
Async XLA Ops:
  0.6 13.0 %copy-start.4 = (s32[4,14]{1,0:T(4,128)S(1)}, s32[4,14]{1,0:T(4,128)}, u32[]{:S(2)}) copy-start(s32[4,14]{1,0:T(4,128)} %param.13) | copy-start | bytes 676
  0.6 13.0 %copy-start.5 = (s32[4,14]{1,0:T(4,128)S(1)}, s32[4,14]{1,0:T(4,128)}, u32[]{:S(2)}) copy-start(s32[4,14]{1,0:T(4,128)} %param.14) | copy-start | bytes 676
  0.7 13.0 %copy-start.6 = (s32[14,4]{0,1:T(4,128)S(1)}, s32[14,4]{0,1:T(4,128)}, u32[]{:S(2)}) copy-start(s32[14,4]{0,1:T(4,128)} %param.15) | copy-start | bytes 676
  2.6 39.7 %all-to-all-start = ((bf16[16,32,1024]{2,1,0:T(8,128)(2,1)}), bf16[16,32,1024]{2,1,0:T(8,128)(2,1)S(1)}, u32[]{:S(2)}, u32[]{:S(2)}) async-start(bf16[16,32,1024]{2,1,0:T(8,128)(2,1)} %broadcast_in_dim.12), calls=%async_computation | async-start | bytes 2097152 | tf_op jit(solution)/shard_map/all_to_all | solution.py:135
  20.5 22.7 %collective-permute-start.1 = (bf16[512,1792]{1,0:T(8,128)(2,1)}, bf16[512,1792]{1,0:T(8,128)(2,1)S(1)}, u32[]{:S(2)}, u32[]{:S(2)}) collective-permute-start(bf16[512,1792]{1,0:T(8,128)(2,1)} %get-tuple-element.12.gate), channel_id=1, source_target_pairs={{0,16},{16,0},{1,17},{17,1},{2,18},{18,2},{3,19},{19,3},{4,20},{20... | collective-permute-start | bytes 5505032 | tf_op jit(solution)/shard_map/ppermute | solution.py:121
  20.5 22.7 %collective-permute-start.2 = (bf16[512,1792]{1,0:T(8,128)(2,1)}, bf16[512,1792]{1,0:T(8,128)(2,1)}, u32[]{:S(2)}, u32[]{:S(2)}) collective-permute-start(bf16[512,1792]{1,0:T(8,128)(2,1)} %get-tuple-element.13.up), channel_id=1, source_target_pairs={{0,16},{16,0},{1,17},{17,1},{2,18},{18,2},{3,19},{19,3},{4,20},{20... | collective-permute-start | bytes 5505032 | tf_op jit(solution)/shard_map/ppermute | solution.py:121
  21.0 22.2 %collective-permute-start.3 = (bf16[1792,512]{1,0:T(8,128)(2,1)}, bf16[1792,512]{1,0:T(8,128)(2,1)}, u32[]{:S(2)}, u32[]{:S(2)}) collective-permute-start(bf16[1792,512]{1,0:T(8,128)(2,1)} %get-tuple-element.14.down), channel_id=1, source_target_pairs={{0,16},{16,0},{1,17},{17,1},{2,18},{18,2},{3,19},{19,3},{4,20},{20... | collective-permute-start | bytes 5505032 | tf_op jit(solution)/shard_map/ppermute | solution.py:121
  43.1 11.8 %copy-start.2 = (bf16[16,16,1024]{2,1,0:T(8,128)(2,1)}, bf16[16,16,1024]{2,1,0:T(8,128)(2,1)S(1)}, u32[]{:S(2)}) copy-start(bf16[16,16,1024]{2,1,0:T(8,128)(2,1)S(1)} %get-tuple-element.19) | copy-start | bytes 1572868
  43.1 1.9 collective-permute-start
  43.2 1.9 copy-start.1
  45.1 0.8 copy-start.3
  140.0 6.0 %collective-permute-start.4 = (bf16[256,1024]{1,0:T(8,128)(2,1)}, bf16[256,1024]{1,0:T(8,128)(2,1)S(1)}, u32[]{:S(2)}, u32[]{:S(2)}) collective-permute-start(bf16[256,1024]{1,0:T(8,128)(2,1)} %shard_map.123), channel_id=1, source_target_pairs={{0,16},{16,0},{1,17},{17,1},{2,18},{18,2},{3,19},{19,3},{4,20},{20... | collective-permute-start | bytes 1572872 | tf_op jit(solution)/shard_map/ppermute | solution.py:121
  140.0 8.1 %copy-start = (bf16[8,32,5376]{2,1,0:T(8,128)(2,1)S(1)}, bf16[8,32,5376]{2,1,0:T(8,128)(2,1)}, u32[]{:S(2)}) copy-start(bf16[8,32,5376]{2,1,0:T(8,128)(2,1)} %all_to_all.21) | copy-start | bytes 8257540
  148.0 36.2 %collective-permute-start.5 = (bf16[256,5376]{1,0:T(8,128)(2,1)S(1)}, bf16[256,5376]{1,0:T(8,128)(2,1)}, u32[]{:S(2)}, u32[]{:S(2)}) collective-permute-start(bf16[256,5376]{1,0:T(8,128)(2,1)S(1)} %bitcast.20), channel_id=1, source_target_pairs={{0,16},{16,0},{1,17},{17,1},{2,18},{18,2},{3,19},{19,3},{4,20},{20... | collective-permute-start | bytes 8257544 | tf_op jit(solution)/shard_map/ppermute | solution.py:121
  148.5 33.7 %all-to-all-start.3 = ((bf16[16,32,1024]{2,1,0:T(8,128)(2,1)}), bf16[16,32,1024]{2,1,0:T(8,128)(2,1)}, u32[]{:S(2)}, u32[]{:S(2)}) async-start(bf16[16,32,1024]{2,1,0:T(8,128)(2,1)} %pad_maximum_fusion), calls=%async_computation.3 | async-start | bytes 2097152 | tf_op jit(solution)/shard_map/all_to_all | solution.py:167

commit v4 on v3

--- a/solution.py
+++ b/solution.py
@@ -43,56 +43,93 @@
             eff[rows, :] = weight[rows, :] * keep
 
 
-def partial_kernel(own, cross, gate, up, down, gate_x, up_x, down_x, out):
-    width = gate.shape[0]
-    hid = gate.shape[1]
-    rows, rows_x = own[:, :width], cross[:, :width]
-    cot, cot_x = own[:, width:], cross[:, width:]
+def partial_sums(place, own, cross, effs, effs_x):
+    gate = effs[0]
+    tokens, both = own.shape
+    width, hid = gate.shape
+    share = tokens // place.shape[0]
+
+    def kernel(place, own, cross, gate, up, down, gate_x, up_x, down_x, *refs):
+        outs, (left, left_x) = refs[:-2], refs[-2:]
+
+        @pl.when(pl.program_id(0) == 0)
+        def _():
+            for r in range(len(outs)):
+                source = pl.ds(pl.multiple_of(place[r] * share, share), share)
+                left[pl.ds(r * share, share), :] = own[source, :]
+                left_x[pl.ds(r * share, share), :] = cross[source, :]
+
+        values = (
+            nn(left[:, :width], gate[...]) + nn(left_x[:, :width], gate_x[...]),
+            nn(left[:, :width], up[...]) + nn(left_x[:, :width], up_x[...]),
+            nt(left[:, width:], down[...]) + nt(left_x[:, width:], down_x[...]),
+        )
+        for part, value in enumerate(values):
+            for r, out in enumerate(outs):
+                out[part] = value[r * share : (r + 1) * share].astype(out.dtype)
+
+    wide = pl.BlockSpec((width, STEP), lambda j: (0, j))
+    tall = pl.BlockSpec((STEP, width), lambda j: (j, 0))
+    fixed = pl.BlockSpec((tokens, both), lambda j: (0, 0))
+    shape = (3, share, hid)
+    return pl.pallas_call(
+        kernel,
+        out_shape=[
+            jax.ShapeDtypeStruct(shape, F32 if r == 0 else BF) for r in range(place.shape[0])
+        ],
+        grid=(hid // STEP,),
+        in_specs=[pl.BlockSpec(memory_space=pltpu.SMEM), fixed, fixed]
+        + [wide, wide, tall, wide, wide, tall],
+        out_specs=[pl.BlockSpec((3, share, STEP), lambda j: (0, 0, j))] * place.shape[0],
+        scratch_shapes=[pltpu.VMEM((tokens, both), BF)] * 2,
+        name="partial_sums",
+    )(place, own, cross, *effs, *effs_x)
+
+
+def activation_kernel(*refs):
+    got, out = refs[:-1], refs[-1]
+    hid = out.shape[2]
     for j in range(hid // STEP):
         cols = pl.ds(j * STEP, STEP)
-        out[:, cols] = (nn(rows, gate[:, cols]) + nn(rows_x, gate_x[:, cols])).astype(BF)
-        out[:, pl.ds(hid + j * STEP, STEP)] = (
-            nn(rows, up[:, cols]) + nn(rows_x, up_x[:, cols])
-        ).astype(BF)
-        out[:, pl.ds(2 * hid + j * STEP, STEP)] = (
-            nt(cot, down[cols, :]) + nt(cot_x, down_x[cols, :])
-        ).astype(BF)
-
-
-def activation_kernel(got, out):
-    copies = got.shape[0]
-    hid = got.shape[2] // 3
-
-    def total(start):
-        cols = pl.ds(start, STEP)
-        acc = got[0, :, cols].astype(F32)
-        for i in range(1, copies):
-            acc = acc + got[i, :, cols].astype(F32)
-        return acc
-
-    for j in range(hid // STEP):
-        starts = [part * hid + j * STEP for part in range(3)]
-        gate, up, d_hidden = [total(start) for start in starts]
+        sums = []
+        for part in range(3):
+            acc = got[0][part, :, cols]
+            for ref in got[1:]:
+                acc = acc + ref[part, :, cols].astype(F32)
+            sums.append(acc)
+        gate, up, d_hidden = sums
         sigmoid = jax.nn.sigmoid(gate)
         activated = gate * sigmoid
-        values = (
-            activated * up,
-            d_hidden * up * sigmoid * (1.0 + gate * (1.0 - sigmoid)),
-            d_hidden * activated,
-        )
-        for start, value in zip(starts, values):
-            rounded = value.astype(BF)
-            for i in range(copies):
-                out[i, :, pl.ds(start, STEP)] = rounded
+        out[0, :, cols] = (activated * up).astype(BF)
+        out[1, :, cols] = (
+            d_hidden * up * sigmoid * (1.0 + gate * (1.0 - sigmoid))
+        ).astype(BF)
+        out[2, :, cols] = (d_hidden * activated).astype(BF)
+
+
+def results(acts, gate, up, down, out):
+    width = gate.shape[0]
+    out[:, :width] = nn(acts[0], down[...]).astype(BF)
+    out[:, width:] = (nt(acts[1], gate[...]) + nt(acts[2], up[...])).astype(BF)
 
 
 def result_kernel(acts, gate, up, down, out):
-    hid = gate.shape[1]
-    width = gate.shape[0]
-    out[:, :width] = nn(acts[:, :hid], down[...]).astype(BF)
-    out[:, width:] = (
-        nt(acts[:, hid : 2 * hid], gate[...]) + nt(acts[:, 2 * hid :], up[...])
-    ).astype(BF)
+    results(acts, gate, up, down, out)
+
+
+def arrange_kernel(place, *refs):
+    shares, (gate, up, down), (acts, out) = refs[:10], refs[10:13], refs[13:]
+    share = shares[0].shape[1]
+    hid = acts.shape[2]
+    full = (0, 1, 3, 4, 5, 7)
+    for r, ref in zip(full, shares[:6]):
+        rows = pl.ds(pl.multiple_of(place[r] * share, share), share)
+        acts[:, rows, :] = ref[...]
+    for r, first, second in ((2, shares[6], shares[7]), (6, shares[8], shares[9])):
+        rows = pl.ds(pl.multiple_of(place[r] * share, share), share)
+        acts[:, rows, : hid // 2] = first[...]
+        acts[:, rows, hid // 2 :] = second[...]
+    results(acts, gate, up, down, out)
 
 
 def gradient_kernel(acts, acts_x, own, other, *refs):
@@ -101,15 +138,13 @@
     rows, rows_x = own[:, :width].T, other[:, :width].T
     cot, cot_x = own[:, width:], other[:, width:]
     for j in range(hid // STEP):
+        here = pl.ds(j * STEP, STEP)
         for part, mask, grad in ((1, masks[0], grad_gate), (2, masks[1], grad_up)):
-            cols = pl.ds(part * hid + j * STEP, STEP)
-            here = pl.ds(j * STEP, STEP)
-            value = nn(rows, acts[:, cols]) + nn(rows_x, acts_x[:, cols])
+            value = nn(rows, acts[part, :, here]) + nn(rows_x, acts_x[part, :, here])
             for i in range(width // BLK):
                 keep = mask[pl.ds(i, 1), here]
                 grad[pl.ds(i * BLK, BLK), here] = (value[i * BLK : (i + 1) * BLK] * keep).astype(BF)
-        cols = pl.ds(j * STEP, STEP)
-        value = nn(acts[:, cols].T, cot) + nn(acts_x[:, cols].T, cot_x)
+        value = nn(acts[0, :, here].T, cot) + nn(acts_x[0, :, here].T, cot_x)
         for i in range(STEP // BLK):
             keep = masks[2][pl.ds(j * (STEP // BLK) + i, 1), :]
             grad_down[pl.ds(j * STEP + i * BLK, BLK), :] = (
@@ -146,20 +181,50 @@
     own = lax.dynamic_slice_in_dim(gathered, core * half, half, 1).reshape(-1, 2 * width)
     other = lax.dynamic_slice_in_dim(gathered, (1 - core) * half, half, 1).reshape(-1, 2 * width)
     cross = swap(other)
-    parts = local_call(
-        partial_kernel,
-        jax.ShapeDtypeStruct((own.shape[0], 3 * hid), BF),
-        own,
-        cross,
-        *effs,
-        *effs_x,
-    ).reshape(pairs, -1, 3 * hid)
-    got = lax.all_to_all(parts, PAIR, 0, 0, tiled=True)
-    copies = local_call(activation_kernel, jax.ShapeDtypeStruct(got.shape, BF), got)
-    acts = lax.all_to_all(copies, PAIR, 0, 0, tiled=True).reshape(-1, 3 * hid)
-
-    result_shape = jax.ShapeDtypeStruct((acts.shape[0], 2 * width), BF)
-    away = swap(local_call(result_kernel, result_shape, acts, *effs_x))
+    x_lo, y = lax.axis_index("x_lo"), lax.axis_index("y")
+    y_n = lax.axis_size("y")
+    place = jnp.stack(
+        [(x_lo ^ (r // y_n)) * y_n + (y + r % y_n) % y_n for r in range(pairs)]
+    ).astype(jnp.int32)
+    parts = partial_sums(place, own, cross, effs, effs_x)
+
+    got = {0: parts[0]}
+    for r in (6, 5, 7, 2, 4, 1, 3):
+        moves = [
+            (i, ((i // y_n) ^ (r // y_n)) * y_n + (i % y_n + r % y_n) % y_n)
+            for i in range(pairs)
+        ]
+        got[r] = lax.ppermute(parts[r], PAIR, moves)
+    mine = local_call(
+        activation_kernel,
+        jax.ShapeDtypeStruct((3, parts[0].shape[1], hid), BF),
+        *[got[r] for r in range(pairs)],
+    )
+
+    def from_up(array):
+        return lax.ppermute(array, "y", [(i, (i - 1) % y_n) for i in range(y_n)])
+
+    def from_down(array):
+        return lax.ppermute(array, "y", [(i, (i + 1) % y_n) for i in range(y_n)])
+
+    mid = hid // 2
+    up_one, down_one = from_up(mine), from_down(mine)
+    facing = lax.ppermute(mine, "x_lo", [(0, 1), (1, 0)])
+    far = [from_up(up_one[:, :, :mid]), from_down(down_one[:, :, mid:])]
+    facing_up, facing_down = from_up(facing), from_down(facing)
+    far = far + [from_up(facing_up[:, :, :mid]), from_down(facing_down[:, :, mid:])]
+
+    tokens_n = own.shape[0]
+    result_shape = jax.ShapeDtypeStruct((tokens_n, 2 * width), BF)
+    acts, away = pl.pallas_call(
+        arrange_kernel,
+        out_shape=[jax.ShapeDtypeStruct((3, tokens_n, hid), BF), result_shape],
+        in_specs=[pl.BlockSpec(memory_space=pltpu.SMEM)]
+        + [pl.BlockSpec(memory_space=pltpu.VMEM)] * 13,
+        out_specs=[pl.BlockSpec(memory_space=pltpu.VMEM)] * 2,
+        name="arrange",
+    )(place, mine, up_one, down_one, facing, facing_up, facing_down, *far, *effs_x)
+    away = swap(away)
     here = local_call(result_kernel, result_shape, acts, *effs)
     send = jnp.concatenate(
         [here.reshape(cols, half, 2 * width), away.reshape(cols, half, 2 * width)], axis=1

time: 193 us -> 189 us (0.979)
  blocking collectives: 75.4 us -> 0 us
  starting transfers between devices: 16.9 us -> 52.4 us
  waiting for transfers between devices: 52 us -> 83.8 us
  local copies, waits for them, and re-layouts: 4.43 us -> 6.62 us
    all_to_all x2 -> x0, blocking collectives: 75.4 us -> none  [the longest x1 37.9 us: layer(): got = lax.all_to_all(parts, PAIR, 0, 0, tiled=True)]
    ppermute x0 -> x16, starting transfers between devices: none -> 36 us  [the longest x7 27.5 us: layer(): got[r] = lax.ppermute(parts[r], PAIR, moves)]
    ppermute x0 -> x16, waiting for transfers between devices: none -> 32.2 us  [the longest x7 14.2 us: layer(): got[r] = lax.ppermute(parts[r], PAIR, moves)]
    pallas_call x6 -> x4, Pallas kernels: 38 us -> 22.3 us  [local_call(): pl.pallas_call(kernel, out_shape=outs, in_specs=[whole] * len(args), out_...]
    pallas_call x0 -> x2, Pallas kernels: none -> 15.6 us  [the longest x1 9.56 us: partial_sums(): pl.pallas_call(kernel, out_shape=[jax.ShapeDtypeStruct(shape, F32 if r ==...]
  transfers between devices with their start and end apart: 8 -> 24, of which waited for: 3 -> 14; matrix products, arithmetic and copies ran while one was open for 2% -> 3% of each run, Pallas kernels for 6% -> 6%
where the time goes in v4:
time: 189 us; the launch traced here: 187 us
  waiting for transfers between devices  83.8 us (44%)
  starting transfers between devices  52.4 us (28%)
  Pallas kernels  37.9 us (20%)
  local copies, waits for them, and re-layouts  6.62 us (4%)
  other arithmetic  4.95 us (3%)
    all_to_all x1, waiting for transfers between devices, layer(): arrived = lax.all_to_all(send, COL, 0, 0, tiled=True)  29.1 us
    ppermute x7, starting transfers between devices, layer(): got[r] = lax.ppermute(parts[r], PAIR, moves)  27.5 us
    pallas_call x4, Pallas kernels, local_call(): pl.pallas_call(kernel, out_shape=outs, in_specs=[whole] * len(args), out_...  22.3 us
    all_to_all x1, waiting for transfers between devices, layer(): lax.all_to_all(jnp.broadcast_to(both, (cols,) + both.shape), COL, 0, 0, t...  21.3 us
    ppermute x7, waiting for transfers between devices, layer(): got[r] = lax.ppermute(parts[r], PAIR, moves)  14.2 us
    all_to_all x1, starting transfers between devices, layer(): lax.all_to_all(jnp.broadcast_to(both, (cols,) + both.shape), COL, 0, 0, t...  11 us
    ppermute x4, waiting for transfers between devices, from_down(): return lax.ppermute(array, 'y', [(i, (i + 1) % y_n) for i in range(y_n)])  9.94 us
    pallas_call x1, Pallas kernels, partial_sums(): pl.pallas_call(kernel, out_shape=[jax.ShapeDtypeStruct(shape, F32 if r ==...  9.56 us
  transfers between devices with their start and end apart: 24, of which 14 were waited for; matrix products, arithmetic and copies ran while one was open for 3% of the time, Pallas kernels for 6%

profile of v4, /device:TPU:8, one launch (start us, length us, event | category | flops | bytes accessed | tf_op | source)
XLA Modules:
  0.0 186.6 jit_solution(13436531184183179890)
XLA Ops:
  0.7 0.8 pad_maximum_fusion.1
  1.5 1.1 broadcast_in_dim.12
  2.6 11.0 %all-to-all-start = ((bf16[16,32,1024]{2,1,0:T(8,128)(2,1)}), bf16[16,32,1024]{2,1,0:T(8,128)(2,1)S(1)}, u32[]{:S(2)}, u32[]{:S(2)}) async-start(bf16[16,32,1024]{2,1,0:T(8,128)(2,1)} %broadcast_in_dim.12), calls=%async_computation | async-start | bytes 2097152 | tf_op jit(solution)/shard_map/all_to_all | solution.py:170
  13.9 0.6 copy.17
  14.6 0.7 copy_bitcast_fusion
  15.3 5.2 %shard_map.119 = (bf16[512,1792]{1,0:T(8,128)(2,1)}, bf16[512,1792]{1,0:T(8,128)(2,1)}, bf16[1792,512]{1,0:T(8,128)(2,1)}) custom-call(bf16[512,1792]{1,0:T(8,128)(2,1)} %refs_0_.1, bf16[512,1792]{1,0:T(8,128)(2,1)} %refs_1_.1, bf16[1792,512]{1,0:T(8,128)(2,1)} %refs_2_.1, f32[4,1792]{1,0:T(4,128)} %get-tuple-element.46.refs_3_.refs_0_, ...), custom_call_target="tpu_custom_call" | custom-call | tf_op jit(solution)/shard_map/pallas_call | solution.py:22
  20.5 0.5 collective-permute-start.2
  21.0 21.3 %all-to-all-done = bf16[16,32,1024]{2,1,0:T(8,128)(2,1)S(1)} async-done(((bf16[16,32,1024]{2,1,0:T(8,128)(2,1)}), bf16[16,32,1024]{2,1,0:T(8,128)(2,1)S(1)}, u32[]{:S(2)}, u32[]{:S(2)}) %all-to-all-start) | async-done | bytes 1048608 | tf_op jit(solution)/shard_map/all_to_all | solution.py:170
  42.2 0.9 constant_dynamic-slice_fusion
  43.2 0.7 stack.35.place
  43.9 1.2 collective-permute-done.cross
  45.2 0.7 copy-done.7
  45.9 9.6 %partial_sums.1 = (f32[3,32,1792]{2,1,0:T(8,128)}, bf16[3,32,1792]{2,1,0:T(8,128)(2,1)}, bf16[3,32,1792]{2,1,0:T(8,128)(2,1)}, bf16[3,32,1792]{2,1,0:T(8,128)(2,...) custom-call(s32[8]{0:T(128)} %stack.35.place, ...), custom_call_target="tpu_custom_call" | custom-call | tf_op jit(solution)/shard_map/partial_sums/pallas_call | solution.py:75
  55.5 1.7 collective-permute-start.4
  57.1 0.9 collective-permute-start.5
  58.1 2.4 %collective-permute-start.6 = (bf16[3,32,1792]{2,1,0:T(8,128)(2,1)}, bf16[3,32,1792]{2,1,0:T(8,128)(2,1)S(1)}, u32[]{:S(2)}, u32[]{:S(2)}) collective-permute-start(bf16[3,32,1792]{2,1,0:T(8,128)(2,1)} %get-tuple-element.28), channel_id=1, source_target_pairs={{0,96},{32,0},{64,32},{96,64},{128,224},{160,128},{192,160},{224,1... | collective-permute-start | bytes 1032200 | tf_op jit(solution)/shard_map/ppermute | solution.py:197
  60.5 0.6 collective-permute-start.7
  61.6 5.1 %collective-permute-done.4.refs_1_ = bf16[3,32,1792]{2,1,0:T(8,128)(2,1)S(1)} collective-permute-done((bf16[3,32,1792]{2,1,0:T(8,128)(2,1)}, bf16[3,32,1792]{2,1,0:T(8,128)(2,1)S(1)}, u32[]{:S(2)}, u32[]{:S(2)}) %collective-permute-start.4) | collective-permute-done | bytes 344096 | tf_op jit(solution)/shard_map/ppermute | solution.py:197
  66.7 2.3 %collective-permute-start.9 = (bf16[3,32,1792]{2,1,0:T(8,128)(2,1)}, bf16[3,32,1792]{2,1,0:T(8,128)(2,1)S(1)}, u32[]{:S(2)}, u32[]{:S(2)}) collective-permute-start(bf16[3,32,1792]{2,1,0:T(8,128)(2,1)} %get-tuple-element.31), channel_id=1, source_target_pairs={{0,192},{32,224},{64,128},{96,160},{128,64},{160,96},{192,0},{224,... | collective-permute-start | bytes 1032200 | tf_op jit(solution)/shard_map/ppermute | solution.py:197
  69.0 0.8 collective-permute-done.5.refs_2_
  69.8 19.1 %collective-permute-start.10 = (bf16[3,32,1792]{2,1,0:T(8,128)(2,1)}, bf16[3,32,1792]{2,1,0:T(8,128)(2,1)S(1)}, u32[]{:S(2)}, u32[]{:S(2)}) collective-permute-start(bf16[3,32,1792]{2,1,0:T(8,128)(2,1)} %get-tuple-element.32), channel_id=1, source_target_pairs={{0,224},{32,128},{64,160},{96,192},{128,96},{160,0},{192,32},{224,... | collective-permute-start | bytes 1032200 | tf_op jit(solution)/shard_map/ppermute | solution.py:197
  88.9 8.3 %collective-permute-done.10.refs_7_ = bf16[3,32,1792]{2,1,0:T(8,128)(2,1)S(1)} collective-permute-done((bf16[3,32,1792]{2,1,0:T(8,128)(2,1)}, bf16[3,32,1792]{2,1,0:T(8,128)(2,1)S(1)}, u32[]{:S(2)}, u32[]{:S(2)}) %collective-permute-start.10) | collective-permute-done | bytes 344096 | tf_op jit(solution)/shard_map/ppermute | solution.py:197
  97.3 0.7 copy-done.15
  98.0 3.0 %shard_map.120.refs_0_ = bf16[3,32,1792]{2,1,0:T(8,128)(2,1)} custom-call(f32[3,32,1792]{2,1,0:T(8,128)} %get-tuple-element.25.refs_0_, bf16[3,32,1792]{2,1,0:T(8,128)(2,1)} %copy-done.9, bf16[3,32,1792]{2,1,0:T(8,128)(2,1)} %copy-done.10, bf16[3,32,1792]{2,1,0:T(8,128)(2,1)} %copy-done.11, bf16[3,32,1792]{2,1,0:T(8,128)(2,1)} %copy-done.12, ...), custom_call_target="tpu_custom_call" | custom-call | tf_op jit(solution)/shard_map/pallas_call | solution.py:22
  100.9 1.4 collective-permute-start.13
  102.4 2.0 %collective-permute-start.11 = (bf16[3,32,1792]{2,1,0:T(8,128)(2,1)}, bf16[3,32,1792]{2,1,0:T(8,128)(2,1)S(1)}, u32[]{:S(2)}, u32[]{:S(2)}) collective-permute-start(bf16[3,32,1792]{2,1,0:T(8,128)(2,1)} %shard_map.120.refs_0_), channel_id=1, source_target_pairs={{0,96},{32,0},{64,32},{96,64},{1,97},{33,1},{65,33},{97,65},{2,98}... | collective-permute-start | bytes 1032200 | tf_op jit(solution)/shard_map/ppermute | solution.py:205
  104.4 4.0 %collective-permute-done.13.refs_3_ = bf16[3,32,1792]{2,1,0:T(8,128)(2,1)S(1)} collective-permute-done((bf16[3,32,1792]{2,1,0:T(8,128)(2,1)}, bf16[3,32,1792]{2,1,0:T(8,128)(2,1)S(1)}, u32[]{:S(2)}, u32[]{:S(2)}) %collective-permute-start.13) | collective-permute-done | bytes 344096 | tf_op jit(solution)/shard_map/ppermute | solution.py:212
  108.4 2.0 %collective-permute-start.14 = (bf16[3,32,1792]{2,1,0:T(8,128)(2,1)S(1)}, bf16[3,32,1792]{2,1,0:T(8,128)(2,1)S(1)}, u32[]{:S(2)}, u32[]{:S(2)}) collective-permute-start(bf16[3,32,1792]{2,1,0:T(8,128)(2,1)S(1)} %collective-permute-done.13.refs_3_), channel_id=1, source_target_pairs={{0,96},{32,0},{64,32},{96,64},{1,97},{33,1},{65,33},{97,65},{2,98}... | collective-permute-start | bytes 1032200 | tf_op jit(solution)/shard_map/ppermute | solution.py:205
  110.4 3.1 %collective-permute-done.12.refs_2_ = bf16[3,32,1792]{2,1,0:T(8,128)(2,1)S(1)} collective-permute-done((bf16[3,32,1792]{2,1,0:T(8,128)(2,1)}, bf16[3,32,1792]{2,1,0:T(8,128)(2,1)S(1)}, u32[]{:S(2)}, u32[]{:S(2)}) %collective-permute-start.12) | collective-permute-done | bytes 344096 | tf_op jit(solution)/shard_map/ppermute | solution.py:208
  113.5 1.3 collective-permute-start.17
  114.8 0.7 collective-permute-done.11.refs_1_
  115.6 0.6 collective-permute-start.16
  116.2 4.3 %collective-permute-done.15.refs_5_ = bf16[3,32,1792]{2,1,0:T(8,128)(2,1)S(1)} collective-permute-done((bf16[3,32,1792]{2,1,0:T(8,128)(2,1)S(1)}, bf16[3,32,1792]{2,1,0:T(8,128)(2,1)S(1)}, u32[]{:S(2)}, u32[]{:S(2)}) %collective-permute-start.15) | collective-permute-done | bytes 344096 | tf_op jit(solution)/shard_map/ppermute | solution.py:208
  120.6 1.5 collective-permute-done.14.refs_4_
  122.1 1.1 collective-permute-start.18
  123.2 0.7 collective-permute-done.16.refs_6_
  123.9 2.5 %collective-permute-done.19.refs_9_ = bf16[3,32,896]{2,1,0:T(8,128)(2,1)S(1)} collective-permute-done((bf16[3,32,896]{2,1,0:T(8,128)(2,1)S(1)}, bf16[3,32,896]{2,1,0:T(8,128)(2,1)S(1)}, u32[]{:S(2)}, u32[]{:S(2)}) %collective-permute-start.19) | collective-permute-done | bytes 172064 | tf_op jit(solution)/shard_map/ppermute | solution.py:208
  126.5 1.1 collective-permute-done.18.refs_8_
  127.6 0.7 copy-done.19
  128.3 6.0 %arrange.1 = (bf16[3,256,1792]{2,1,0:T(8,128)(2,1)}, bf16[256,1024]{1,0:T(8,128)(2,1)}) custom-call(s32[8]{0:T(128)} %stack.35.place, bf16[3,32,1792]{2,1,0:T(8,128)(2,1)} %shard_map.120.refs_0_, bf16[3,32,1792]{2,1,0:T(8,128)(2,1)} %copy-done.4, bf16[3,32,1792]{2,1,0:T(8,128)(2,1)} %copy-done.3, bf16[3,32,1792]{2,1,0:T(8,128)(2,1)} %copy-done.8, ...), custom_call_target="tpu_custom_call" | custom-call | tf_op jit(solution)/shard_map/arrange/pallas_call | solution.py:219
  134.3 6.0 %shard_map.121 = bf16[256,1024]{1,0:T(8,128)(2,1)} custom-call(bf16[3,256,1792]{2,1,0:T(8,128)(2,1)} %get-tuple-element.35.acts, bf16[512,1792]{1,0:T(8,128)(2,1)} %get-tuple-element.22.gate, bf16[512,1792]{1,0:T(8,128)(2,1)} %get-tuple-element.23.up, bf16[1792,512]{1,0:T(8,128)(2,1)} %get-tuple-element.24.down), custom_call_target="tpu_custom_call" | custom-call | tf_op jit(solution)/shard_map/pallas_call | solution.py:22
  140.3 2.1 %pad_maximum_fusion = bf16[16,32,1024]{2,1,0:T(8,128)(2,1)} fusion(bf16[16,16,1024]{2,1,0:T(8,128)(2,1)S(1)} %bitcast.28, bf16[16,16,1024]{2,1,0:T(8,128)(2,1)} %bitcast.27), kind=kLoop, calls=%fused_computation.1 | loop fusion | flops 2097152 | bytes 2097152 | tf_op jit(solution)/shard_map/concatenate | solution.py:229
  142.4 0.5 collective-permute-start.21
  142.9 4.3 %all-to-all-start.1 = ((bf16[16,32,1024]{2,1,0:T(8,128)(2,1)}), bf16[16,32,1024]{2,1,0:T(8,128)(2,1)}, u32[]{:S(2)}, u32[]{:S(2)}) async-start(bf16[16,32,1024]{2,1,0:T(8,128)(2,1)} %pad_maximum_fusion), calls=%async_computation.1 | async-start | bytes 2097152 | tf_op jit(solution)/shard_map/all_to_all | solution.py:232
  147.2 29.1 %all-to-all-done.1 = bf16[16,32,1024]{2,1,0:T(8,128)(2,1)} async-done(((bf16[16,32,1024]{2,1,0:T(8,128)(2,1)}), bf16[16,32,1024]{2,1,0:T(8,128)(2,1)}, u32[]{:S(2)}, u32[]{:S(2)}) %all-to-all-start.1) | async-done | bytes 1048608 | tf_op jit(solution)/shard_map/all_to_all | solution.py:232
  176.4 1.4 convert_reduce_fusion
  177.8 0.6 pad_maximum_fusion.2
  178.4 8.2 %shard_map.122 = (bf16[512,1792]{1,0:T(8,128)(2,1)}, bf16[512,1792]{1,0:T(8,128)(2,1)}, bf16[1792,512]{1,0:T(8,128)(2,1)}) custom-call(bf16[3,256,1792]{2,1,0:T(8,128)(2,1)} %get-tuple-element.35.acts, bf16[3,256,1792]{2,1,0:T(8,128)(2,1)} %collective-permute-done.21.acts_x, bf16[256,1024]{1,0:T(8,128)(2,1)} %bitcast.24, bf16[256,1024]{1,0:T(8,128)(2,1)} %bitcast.26, ...), custom_call_target="tpu_custom_call" | custom-call | tf_op jit(solution)/shard_map/pallas_call | solution.py:22
  (74 shorter events, 1.2 us)
Async XLA Ops:
  0.6 13.0 %copy-start.20 = (s32[4,14]{1,0:T(4,128)S(1)}, s32[4,14]{1,0:T(4,128)}, u32[]{:S(2)}) copy-start(s32[4,14]{1,0:T(4,128)} %param.13) | copy-start | bytes 676
  0.6 13.0 %copy-start.21 = (s32[4,14]{1,0:T(4,128)S(1)}, s32[4,14]{1,0:T(4,128)}, u32[]{:S(2)}) copy-start(s32[4,14]{1,0:T(4,128)} %param.14) | copy-start | bytes 676
  0.7 13.0 %copy-start.22 = (s32[14,4]{0,1:T(4,128)S(1)}, s32[14,4]{0,1:T(4,128)}, u32[]{:S(2)}) copy-start(s32[14,4]{0,1:T(4,128)} %param.15) | copy-start | bytes 676
  2.6 39.7 %all-to-all-start = ((bf16[16,32,1024]{2,1,0:T(8,128)(2,1)}), bf16[16,32,1024]{2,1,0:T(8,128)(2,1)S(1)}, u32[]{:S(2)}, u32[]{:S(2)}) async-start(bf16[16,32,1024]{2,1,0:T(8,128)(2,1)} %broadcast_in_dim.12), calls=%async_computation | async-start | bytes 2097152 | tf_op jit(solution)/shard_map/all_to_all | solution.py:170
  20.5 23.4 %collective-permute-start.1 = (bf16[512,1792]{1,0:T(8,128)(2,1)}, bf16[512,1792]{1,0:T(8,128)(2,1)S(1)}, u32[]{:S(2)}, u32[]{:S(2)}) collective-permute-start(bf16[512,1792]{1,0:T(8,128)(2,1)} %get-tuple-element.22.gate), channel_id=1, source_target_pairs={{0,16},{16,0},{1,17},{17,1},{2,18},{18,2},{3,19},{19,3},{4,20},{20... | collective-permute-start | bytes 5505032 | tf_op jit(solution)/shard_map/ppermute | solution.py:156
  20.5 23.4 %collective-permute-start.2 = (bf16[512,1792]{1,0:T(8,128)(2,1)}, bf16[512,1792]{1,0:T(8,128)(2,1)}, u32[]{:S(2)}, u32[]{:S(2)}) collective-permute-start(bf16[512,1792]{1,0:T(8,128)(2,1)} %get-tuple-element.23.up), channel_id=1, source_target_pairs={{0,16},{16,0},{1,17},{17,1},{2,18},{18,2},{3,19},{19,3},{4,20},{20... | collective-permute-start | bytes 5505032 | tf_op jit(solution)/shard_map/ppermute | solution.py:156
  21.0 22.9 %collective-permute-start.3 = (bf16[1792,512]{1,0:T(8,128)(2,1)}, bf16[1792,512]{1,0:T(8,128)(2,1)}, u32[]{:S(2)}, u32[]{:S(2)}) collective-permute-start(bf16[1792,512]{1,0:T(8,128)(2,1)} %get-tuple-element.24.down), channel_id=1, source_target_pairs={{0,16},{16,0},{1,17},{17,1},{2,18},{18,2},{3,19},{19,3},{4,20},{20... | collective-permute-start | bytes 5505032 | tf_op jit(solution)/shard_map/ppermute | solution.py:156
  43.2 12.3 %copy-start.2 = (bf16[16,16,1024]{2,1,0:T(8,128)(2,1)}, bf16[16,16,1024]{2,1,0:T(8,128)(2,1)S(1)}, u32[]{:S(2)}) copy-start(bf16[16,16,1024]{2,1,0:T(8,128)(2,1)S(1)} %get-tuple-element.39) | copy-start | bytes 1572868
  43.2 1.9 %collective-permute-start = (bf16[256,1024]{1,0:T(8,128)(2,1)S(1)}, bf16[256,1024]{1,0:T(8,128)(2,1)S(1)}, u32[]{:S(2)}, u32[]{:S(2)}) collective-permute-start(bf16[256,1024]{1,0:T(8,128)(2,1)S(1)} %bitcast.25), channel_id=1, source_target_pairs={{0,16},{16,0},{1,17},{17,1},{2,18},{18,2},{3,19},{19,3},{4,20},{20... | collective-permute-start | bytes 1572872 | tf_op jit(solution)/shard_map/ppermute | solution.py:156
  43.9 1.3 copy-start.1
  45.1 0.8 copy-start.7
  55.5 11.2 %collective-permute-start.4 = (bf16[3,32,1792]{2,1,0:T(8,128)(2,1)}, bf16[3,32,1792]{2,1,0:T(8,128)(2,1)S(1)}, u32[]{:S(2)}, u32[]{:S(2)}) collective-permute-start(bf16[3,32,1792]{2,1,0:T(8,128)(2,1)} %get-tuple-element.26), channel_id=1, source_target_pairs={{0,32},{32,64},{64,96},{96,0},{128,160},{160,192},{192,224},{224,1... | collective-permute-start | bytes 1032200 | tf_op jit(solution)/shard_map/ppermute | solution.py:197
  57.1 12.7 %collective-permute-start.5 = (bf16[3,32,1792]{2,1,0:T(8,128)(2,1)}, bf16[3,32,1792]{2,1,0:T(8,128)(2,1)S(1)}, u32[]{:S(2)}, u32[]{:S(2)}) collective-permute-start(bf16[3,32,1792]{2,1,0:T(8,128)(2,1)} %get-tuple-element.27), channel_id=1, source_target_pairs={{0,64},{32,96},{64,0},{96,32},{128,192},{160,224},{192,128},{224,1... | collective-permute-start | bytes 1032200 | tf_op jit(solution)/shard_map/ppermute | solution.py:197
  58.1 30.8 %collective-permute-start.6 = (bf16[3,32,1792]{2,1,0:T(8,128)(2,1)}, bf16[3,32,1792]{2,1,0:T(8,128)(2,1)S(1)}, u32[]{:S(2)}, u32[]{:S(2)}) collective-permute-start(bf16[3,32,1792]{2,1,0:T(8,128)(2,1)} %get-tuple-element.28), channel_id=1, source_target_pairs={{0,96},{32,0},{64,32},{96,64},{128,224},{160,128},{192,160},{224,1... | collective-permute-start | bytes 1032200 | tf_op jit(solution)/shard_map/ppermute | solution.py:197
  60.5 28.4 %collective-permute-start.7 = (bf16[3,32,1792]{2,1,0:T(8,128)(2,1)}, bf16[3,32,1792]{2,1,0:T(8,128)(2,1)S(1)}, u32[]{:S(2)}, u32[]{:S(2)}) collective-permute-start(bf16[3,32,1792]{2,1,0:T(8,128)(2,1)} %get-tuple-element.29), channel_id=1, source_target_pairs={{0,128},{32,160},{64,192},{96,224},{128,0},{160,32},{192,64},{224,... | collective-permute-start | bytes 1032200 | tf_op jit(solution)/shard_map/ppermute | solution.py:197
  61.1 27.8 %collective-permute-start.8 = (bf16[3,32,1792]{2,1,0:T(8,128)(2,1)}, bf16[3,32,1792]{2,1,0:T(8,128)(2,1)S(1)}, u32[]{:S(2)}, u32[]{:S(2)}) collective-permute-start(bf16[3,32,1792]{2,1,0:T(8,128)(2,1)} %get-tuple-element.30), channel_id=1, source_target_pairs={{0,160},{32,192},{64,224},{96,128},{128,32},{160,64},{192,96},{224... | collective-permute-start | bytes 1032200 | tf_op jit(solution)/shard_map/ppermute | solution.py:197
  66.7 30.5 %copy-start.9 = (bf16[3,32,1792]{2,1,0:T(8,128)(2,1)}, bf16[3,32,1792]{2,1,0:T(8,128)(2,1)S(1)}, u32[]{:S(2)}) copy-start(bf16[3,32,1792]{2,1,0:T(8,128)(2,1)S(1)} %collective-permute-done.4.refs_1_) | copy-start | bytes 1032196
  66.7 22.2 %collective-permute-start.9 = (bf16[3,32,1792]{2,1,0:T(8,128)(2,1)}, bf16[3,32,1792]{2,1,0:T(8,128)(2,1)S(1)}, u32[]{:S(2)}, u32[]{:S(2)}) collective-permute-start(bf16[3,32,1792]{2,1,0:T(8,128)(2,1)} %get-tuple-element.31), channel_id=1, source_target_pairs={{0,192},{32,224},{64,128},{96,160},{128,64},{160,96},{192,0},{224,... | collective-permute-start | bytes 1032200 | tf_op jit(solution)/shard_map/ppermute | solution.py:197
  69.8 27.5 %copy-start.10 = (bf16[3,32,1792]{2,1,0:T(8,128)(2,1)}, bf16[3,32,1792]{2,1,0:T(8,128)(2,1)S(1)}, u32[]{:S(2)}) copy-start(bf16[3,32,1792]{2,1,0:T(8,128)(2,1)S(1)} %collective-permute-done.5.refs_2_) | copy-start | bytes 1032196
  69.8 27.5 %collective-permute-start.10 = (bf16[3,32,1792]{2,1,0:T(8,128)(2,1)}, bf16[3,32,1792]{2,1,0:T(8,128)(2,1)S(1)}, u32[]{:S(2)}, u32[]{:S(2)}) collective-permute-start(bf16[3,32,1792]{2,1,0:T(8,128)(2,1)} %get-tuple-element.32), channel_id=1, source_target_pairs={{0,224},{32,128},{64,160},{96,192},{128,96},{160,0},{192,32},{224,... | collective-permute-start | bytes 1032200 | tf_op jit(solution)/shard_map/ppermute | solution.py:197
  88.9 8.4 %copy-start.11 = (bf16[3,32,1792]{2,1,0:T(8,128)(2,1)}, bf16[3,32,1792]{2,1,0:T(8,128)(2,1)S(1)}, u32[]{:S(2)}) copy-start(bf16[3,32,1792]{2,1,0:T(8,128)(2,1)S(1)} %collective-permute-done.6.refs_3_) | copy-start | bytes 1032196
  88.9 8.4 %copy-start.12 = (bf16[3,32,1792]{2,1,0:T(8,128)(2,1)}, bf16[3,32,1792]{2,1,0:T(8,128)(2,1)S(1)}, u32[]{:S(2)}) copy-start(bf16[3,32,1792]{2,1,0:T(8,128)(2,1)S(1)} %collective-permute-done.7.refs_4_) | copy-start | bytes 1032196
  88.9 8.4 %copy-start.13 = (bf16[3,32,1792]{2,1,0:T(8,128)(2,1)}, bf16[3,32,1792]{2,1,0:T(8,128)(2,1)S(1)}, u32[]{:S(2)}) copy-start(bf16[3,32,1792]{2,1,0:T(8,128)(2,1)S(1)} %collective-permute-done.8.refs_5_) | copy-start | bytes 1032196
  88.9 8.4 %copy-start.14 = (bf16[3,32,1792]{2,1,0:T(8,128)(2,1)}, bf16[3,32,1792]{2,1,0:T(8,128)(2,1)S(1)}, u32[]{:S(2)}) copy-start(bf16[3,32,1792]{2,1,0:T(8,128)(2,1)S(1)} %collective-permute-done.9.refs_6_) | copy-start | bytes 1032196
  97.2 0.7 copy-start.15
  100.9 7.5 %collective-permute-start.13 = (bf16[3,32,1792]{2,1,0:T(8,128)(2,1)}, bf16[3,32,1792]{2,1,0:T(8,128)(2,1)S(1)}, u32[]{:S(2)}, u32[]{:S(2)}) collective-permute-start(bf16[3,32,1792]{2,1,0:T(8,128)(2,1)} %shard_map.120.refs_0_), channel_id=1, source_target_pairs={{0,128},{128,0},{1,129},{129,1},{2,130},{130,2},{3,131},{131,3},{4... | collective-permute-start | bytes 1032200 | tf_op jit(solution)/shard_map/ppermute | solution.py:212
  102.4 11.1 %collective-permute-start.12 = (bf16[3,32,1792]{2,1,0:T(8,128)(2,1)}, bf16[3,32,1792]{2,1,0:T(8,128)(2,1)S(1)}, u32[]{:S(2)}, u32[]{:S(2)}) collective-permute-start(bf16[3,32,1792]{2,1,0:T(8,128)(2,1)} %shard_map.120.refs_0_), channel_id=1, source_target_pairs={{0,32},{32,64},{64,96},{96,0},{1,33},{33,65},{65,97},{97,1},{2,34}... | collective-permute-start | bytes 1032200 | tf_op jit(solution)/shard_map/ppermute | solution.py:208
  102.4 13.2 %collective-permute-start.11 = (bf16[3,32,1792]{2,1,0:T(8,128)(2,1)}, bf16[3,32,1792]{2,1,0:T(8,128)(2,1)S(1)}, u32[]{:S(2)}, u32[]{:S(2)}) collective-permute-start(bf16[3,32,1792]{2,1,0:T(8,128)(2,1)} %shard_map.120.refs_0_), channel_id=1, source_target_pairs={{0,96},{32,0},{64,32},{96,64},{1,97},{33,1},{65,33},{97,65},{2,98}... | collective-permute-start | bytes 1032200 | tf_op jit(solution)/shard_map/ppermute | solution.py:205
  108.4 19.2 %copy-start.8 = (bf16[3,32,1792]{2,1,0:T(8,128)(2,1)}, bf16[3,32,1792]{2,1,0:T(8,128)(2,1)S(1)}, u32[]{:S(2)}) copy-start(bf16[3,32,1792]{2,1,0:T(8,128)(2,1)S(1)} %collective-permute-done.13.refs_3_) | copy-start | bytes 1032196
  108.4 12.1 %collective-permute-start.15 = (bf16[3,32,1792]{2,1,0:T(8,128)(2,1)S(1)}, bf16[3,32,1792]{2,1,0:T(8,128)(2,1)S(1)}, u32[]{:S(2)}, u32[]{:S(2)}) collective-permute-start(bf16[3,32,1792]{2,1,0:T(8,128)(2,1)S(1)} %collective-permute-done.13.refs_3_), channel_id=1, source_target_pairs={{0,32},{32,64},{64,96},{96,0},{1,33},{33,65},{65,97},{97,1},{2,34}... | collective-permute-start | bytes 1032200 | tf_op jit(solution)/shard_map/ppermute | solution.py:208
  108.4 13.7 %collective-permute-start.14 = (bf16[3,32,1792]{2,1,0:T(8,128)(2,1)S(1)}, bf16[3,32,1792]{2,1,0:T(8,128)(2,1)S(1)}, u32[]{:S(2)}, u32[]{:S(2)}) collective-permute-start(bf16[3,32,1792]{2,1,0:T(8,128)(2,1)S(1)} %collective-permute-done.13.refs_3_), channel_id=1, source_target_pairs={{0,96},{32,0},{64,32},{96,64},{1,97},{33,1},{65,33},{97,65},{2,98}... | collective-permute-start | bytes 1032200 | tf_op jit(solution)/shard_map/ppermute | solution.py:205
  113.5 14.1 %copy-start.3 = (bf16[3,32,1792]{2,1,0:T(8,128)(2,1)}, bf16[3,32,1792]{2,1,0:T(8,128)(2,1)S(1)}, u32[]{:S(2)}) copy-start(bf16[3,32,1792]{2,1,0:T(8,128)(2,1)S(1)} %collective-permute-done.12.refs_2_) | copy-start | bytes 1032196
  113.5 9.7 %collective-permute-start.17 = (bf16[3,32,896]{2,1,0:T(8,128)(2,1)S(1)}, bf16[3,32,896]{2,1,0:T(8,128)(2,1)S(1)}, u32[]{:S(2)}, u32[]{:S(2)}) collective-permute-start(bf16[3,32,896]{2,1,0:T(8,128)(2,1)S(1)} %slice.33), channel_id=1, source_target_pairs={{0,32},{32,64},{64,96},{96,0},{1,33},{33,65},{65,97},{97,1},{2,34}... | collective-permute-start | bytes 516104 | tf_op jit(solution)/shard_map/ppermute | solution.py:208
  115.6 12.0 %copy-start.4 = (bf16[3,32,1792]{2,1,0:T(8,128)(2,1)}, bf16[3,32,1792]{2,1,0:T(8,128)(2,1)S(1)}, u32[]{:S(2)}) copy-start(bf16[3,32,1792]{2,1,0:T(8,128)(2,1)S(1)} %collective-permute-done.11.refs_1_) | copy-start | bytes 1032196
  115.6 8.3 %collective-permute-start.16 = (bf16[3,32,896]{2,1,0:T(8,128)(2,1)S(1)}, bf16[3,32,896]{2,1,0:T(8,128)(2,1)S(1)}, u32[]{:S(2)}, u32[]{:S(2)}) collective-permute-start(bf16[3,32,896]{2,1,0:T(8,128)(2,1)S(1)} %slice.32), channel_id=1, source_target_pairs={{0,96},{32,0},{64,32},{96,64},{1,97},{33,1},{65,33},{97,65},{2,98}... | collective-permute-start | bytes 516104 | tf_op jit(solution)/shard_map/ppermute | solution.py:205
  120.5 7.1 %copy-start.5 = (bf16[3,32,1792]{2,1,0:T(8,128)(2,1)}, bf16[3,32,1792]{2,1,0:T(8,128)(2,1)S(1)}, u32[]{:S(2)}) copy-start(bf16[3,32,1792]{2,1,0:T(8,128)(2,1)S(1)} %collective-permute-done.15.refs_5_) | copy-start | bytes 1032196
  120.5 6.0 %collective-permute-start.19 = (bf16[3,32,896]{2,1,0:T(8,128)(2,1)S(1)}, bf16[3,32,896]{2,1,0:T(8,128)(2,1)S(1)}, u32[]{:S(2)}, u32[]{:S(2)}) collective-permute-start(bf16[3,32,896]{2,1,0:T(8,128)(2,1)S(1)} %slice.35), channel_id=1, source_target_pairs={{0,32},{32,64},{64,96},{96,0},{1,33},{33,65},{65,97},{97,1},{2,34}... | collective-permute-start | bytes 516104 | tf_op jit(solution)/shard_map/ppermute | solution.py:208
  122.1 5.5 %copy-start.6 = (bf16[3,32,1792]{2,1,0:T(8,128)(2,1)}, bf16[3,32,1792]{2,1,0:T(8,128)(2,1)S(1)}, u32[]{:S(2)}) copy-start(bf16[3,32,1792]{2,1,0:T(8,128)(2,1)S(1)} %collective-permute-done.14.refs_4_) | copy-start | bytes 1032196
  122.1 5.5 %collective-permute-start.18 = (bf16[3,32,896]{2,1,0:T(8,128)(2,1)S(1)}, bf16[3,32,896]{2,1,0:T(8,128)(2,1)S(1)}, u32[]{:S(2)}, u32[]{:S(2)}) collective-permute-start(bf16[3,32,896]{2,1,0:T(8,128)(2,1)S(1)} %slice.34), channel_id=1, source_target_pairs={{0,96},{32,0},{64,32},{96,64},{1,97},{33,1},{65,33},{97,65},{2,98}... | collective-permute-start | bytes 516104 | tf_op jit(solution)/shard_map/ppermute | solution.py:205
  123.2 4.4 %copy-start.16 = (bf16[3,32,896]{2,1,0:T(8,128)(2,1)}, bf16[3,32,896]{2,1,0:T(8,128)(2,1)S(1)}, u32[]{:S(2)}) copy-start(bf16[3,32,896]{2,1,0:T(8,128)(2,1)S(1)} %collective-permute-done.17.refs_7_) | copy-start | bytes 516100
  123.9 3.7 %copy-start.17 = (bf16[3,32,896]{2,1,0:T(8,128)(2,1)}, bf16[3,32,896]{2,1,0:T(8,128)(2,1)S(1)}, u32[]{:S(2)}) copy-start(bf16[3,32,896]{2,1,0:T(8,128)(2,1)S(1)} %collective-permute-done.16.refs_6_) | copy-start | bytes 516100
  126.5 1.2 copy-start.18
  127.6 0.7 copy-start.19
  134.3 6.0 %collective-permute-start.20 = (bf16[256,1024]{1,0:T(8,128)(2,1)}, bf16[256,1024]{1,0:T(8,128)(2,1)S(1)}, u32[]{:S(2)}, u32[]{:S(2)}) collective-permute-start(bf16[256,1024]{1,0:T(8,128)(2,1)} %get-tuple-element.34), channel_id=1, source_target_pairs={{0,16},{16,0},{1,17},{17,1},{2,18},{18,2},{3,19},{19,3},{4,20},{20... | collective-permute-start | bytes 1572872 | tf_op jit(solution)/shard_map/ppermute | solution.py:156
  134.3 8.1 %copy-start = (bf16[3,256,1792]{2,1,0:T(8,128)(2,1)S(1)}, bf16[3,256,1792]{2,1,0:T(8,128)(2,1)}, u32[]{:S(2)}) copy-start(bf16[3,256,1792]{2,1,0:T(8,128)(2,1)} %get-tuple-element.35.acts) | copy-start | bytes 8257540
  142.4 36.0 %collective-permute-start.21 = (bf16[3,256,1792]{2,1,0:T(8,128)(2,1)S(1)}, bf16[3,256,1792]{2,1,0:T(8,128)(2,1)}, u32[]{:S(2)}, u32[]{:S(2)}) collective-permute-start(bf16[3,256,1792]{2,1,0:T(8,128)(2,1)S(1)} %copy-done), channel_id=1, source_target_pairs={{0,16},{16,0},{1,17},{17,1},{2,18},{18,2},{3,19},{19,3},{4,20},{20... | collective-permute-start | bytes 8257544 | tf_op jit(solution)/shard_map/ppermute | solution.py:156
  142.9 33.5 %all-to-all-start.1 = ((bf16[16,32,1024]{2,1,0:T(8,128)(2,1)}), bf16[16,32,1024]{2,1,0:T(8,128)(2,1)}, u32[]{:S(2)}, u32[]{:S(2)}) async-start(bf16[16,32,1024]{2,1,0:T(8,128)(2,1)} %pad_maximum_fusion), calls=%async_computation.1 | async-start | bytes 2097152 | tf_op jit(solution)/shard_map/all_to_all | solution.py:232

commit v5 on v4

--- a/solution.py
+++ b/solution.py
@@ -35,29 +35,45 @@
     return lax.dot_general(left, right, (((1,), (1,)), ((), ())), preferred_element_type=F32)
 
 
-def prepare_kernel(*refs):
-    for weight, mask, eff in zip(refs[0:3], refs[3:6], refs[6:9]):
-        for i in range(mask.shape[0]):
-            rows = pl.ds(i * BLK, BLK)
-            keep = jnp.broadcast_to(mask[pl.ds(i, 1), :], (BLK, mask.shape[1])).astype(BF)
-            eff[rows, :] = weight[rows, :] * keep
+def prepare_kernel(weight, mask, eff):
+    for i in range(mask.shape[0]):
+        rows = pl.ds(i * BLK, BLK)
+        keep = jnp.broadcast_to(mask[pl.ds(i, 1), :], (BLK, mask.shape[1])).astype(BF)
+        eff[rows, :] = weight[rows, :] * keep
+
+
+def split_kernel(place, *refs):
+    chunks, (own, other) = refs[:-2], refs[-2:]
+    half = chunks[0].shape[0] // 2
+    core = place[len(chunks)]
+    for i, chunk in enumerate(chunks):
+        rows = pl.ds(pl.multiple_of(place[i] * half, half), half)
+        own[rows, :] = chunk[pl.ds(pl.multiple_of(core * half, half), half), :]
+        other[rows, :] = chunk[pl.ds(pl.multiple_of((1 - core) * half, half), half), :]
 
 
 def partial_sums(place, own, cross, effs, effs_x):
     gate = effs[0]
     tokens, both = own.shape
     width, hid = gate.shape
-    share = tokens // place.shape[0]
+    chips = place.shape[0]
+    y_n = chips // 2
+    share = tokens // chips
+    half = share // 2
+    order = [(r, 0) for r in range(chips)]
+    order += [(x * y_n + y, 1) for y in range(y_n) for x in range(2)]
+    groups = [y_n * half, y_n * half] + [2 * half] * y_n
+    dtypes = [F32, BF, F32] + [BF] * (y_n - 1)
 
     def kernel(place, own, cross, gate, up, down, gate_x, up_x, down_x, *refs):
         outs, (left, left_x) = refs[:-2], refs[-2:]
 
         @pl.when(pl.program_id(0) == 0)
         def _():
-            for r in range(len(outs)):
-                source = pl.ds(pl.multiple_of(place[r] * share, share), share)
-                left[pl.ds(r * share, share), :] = own[source, :]
-                left_x[pl.ds(r * share, share), :] = cross[source, :]
+            for i, (r, part) in enumerate(order):
+                source = pl.ds(pl.multiple_of(place[r] * share + part * half, half), half)
+                left[pl.ds(i * half, half), :] = own[source, :]
+                left_x[pl.ds(i * half, half), :] = cross[source, :]
 
         values = (
             nn(left[:, :width], gate[...]) + nn(left_x[:, :width], gate_x[...]),
@@ -65,46 +81,61 @@
             nt(left[:, width:], down[...]) + nt(left_x[:, width:], down_x[...]),
         )
         for part, value in enumerate(values):
-            for r, out in enumerate(outs):
-                out[part] = value[r * share : (r + 1) * share].astype(out.dtype)
+            start = 0
+            for rows, out in zip(groups, outs):
+                out[part] = value[start : start + rows].astype(out.dtype)
+                start += rows
 
     wide = pl.BlockSpec((width, STEP), lambda j: (0, j))
     tall = pl.BlockSpec((STEP, width), lambda j: (j, 0))
     fixed = pl.BlockSpec((tokens, both), lambda j: (0, 0))
-    shape = (3, share, hid)
     return pl.pallas_call(
         kernel,
-        out_shape=[
-            jax.ShapeDtypeStruct(shape, F32 if r == 0 else BF) for r in range(place.shape[0])
-        ],
+        out_shape=[jax.ShapeDtypeStruct((3, n, hid), t) for n, t in zip(groups, dtypes)],
         grid=(hid // STEP,),
         in_specs=[pl.BlockSpec(memory_space=pltpu.SMEM), fixed, fixed]
         + [wide, wide, tall, wide, wide, tall],
-        out_specs=[pl.BlockSpec((3, share, STEP), lambda j: (0, 0, j))] * place.shape[0],
+        out_specs=[pl.BlockSpec((3, n, STEP), lambda j: (0, 0, j)) for n in groups],
         scratch_shapes=[pltpu.VMEM((tokens, both), BF)] * 2,
         name="partial_sums",
     )(place, own, cross, *effs, *effs_x)
 
 
-def activation_kernel(*refs):
-    got, out = refs[:-1], refs[-1]
+def middle_kernel(x_kept, x_got, y_kept, *refs):
+    y_got, outs = refs[:3], refs[3:]
+    half = outs[0].shape[1]
+    for i, out in enumerate(outs[:4]):
+        rows = pl.ds(i * half, half)
+        out[...] = (x_kept[:, rows, :] + x_got[:, rows, :].astype(F32)).astype(out.dtype)
+    for i, out in enumerate(outs[4:]):
+        rows = pl.ds(i * half, half)
+        total = y_kept[:, rows, :]
+        for ref in y_got:
+            total = total + ref[:, rows, :].astype(F32)
+        out[...] = total.astype(out.dtype)
+
+
+def activation_kernel(x_kept, x_one, x_two, x_three, y_kept, y_one, out):
     hid = out.shape[2]
-    for j in range(hid // STEP):
-        cols = pl.ds(j * STEP, STEP)
-        sums = []
-        for part in range(3):
-            acc = got[0][part, :, cols]
-            for ref in got[1:]:
-                acc = acc + ref[part, :, cols].astype(F32)
-            sums.append(acc)
-        gate, up, d_hidden = sums
-        sigmoid = jax.nn.sigmoid(gate)
-        activated = gate * sigmoid
-        out[0, :, cols] = (activated * up).astype(BF)
-        out[1, :, cols] = (
-            d_hidden * up * sigmoid * (1.0 + gate * (1.0 - sigmoid))
-        ).astype(BF)
-        out[2, :, cols] = (d_hidden * activated).astype(BF)
+    half = x_kept.shape[1]
+    for row, kept, got in ((0, x_kept, (x_one, x_two, x_three)), (half, y_kept, (y_one,))):
+        rows = pl.ds(row, half)
+        for j in range(hid // STEP):
+            cols = pl.ds(j * STEP, STEP)
+            sums = []
+            for part in range(3):
+                acc = kept[part, :, cols]
+                for ref in got:
+                    acc = acc + ref[part, :, cols].astype(F32)
+                sums.append(acc)
+            gate, up, d_hidden = sums
+            sigmoid = jax.nn.sigmoid(gate)
+            activated = gate * sigmoid
+            out[0, rows, cols] = (activated * up).astype(BF)
+            out[1, rows, cols] = (
+                d_hidden * up * sigmoid * (1.0 + gate * (1.0 - sigmoid))
+            ).astype(BF)
+            out[2, rows, cols] = (d_hidden * activated).astype(BF)
 
 
 def results(acts, gate, up, down, out):
@@ -166,20 +197,45 @@
     cols = lax.axis_size(COL)
     half = share // 2
 
+    high, z = lax.axis_index("x_hi"), lax.axis_index("z")
+    z_n = lax.axis_size("z")
+
+    def along(axis, array, hops):
+        n = lax.axis_size(axis)
+        return lax.ppermute(array, axis, [(i, (i - hops) % n) for i in range(n)])
+
     both = jnp.concatenate([tokens, cotangent], axis=1)
-    gathered = lax.all_to_all(
-        jnp.broadcast_to(both, (cols,) + both.shape), COL, 0, 0, tiled=True
-    )
+    pair = jnp.stack([both, along("x_hi", both, 1)])
+    ups, downs = [pair], [pair]
+    for _ in range(1, z_n // 2):
+        ups.append(along("z", ups[-1], 1))
+        downs.append(along("z", downs[-1], -1))
+    chunks = [(0, 0, both), (1, 0, pair[1])]
+    for k in range(1, z_n // 2):
+        for rel in range(2):
+            chunks += [(rel, k, ups[k][rel]), (rel, z_n - k, downs[k][rel])]
+    chunks += [(0, z_n // 2, along("z", ups[-1][0], 1)), (1, z_n // 2, along("z", downs[-1][1], -1))]
+    order = jnp.stack(
+        [(high ^ rel) * z_n + (z + k) % z_n for rel, k, _ in chunks] + [core]
+    ).astype(jnp.int32)
+
     weights = (gate_weight, up_weight, down_weight)
     shapes = [jax.ShapeDtypeStruct(weight.shape, BF) for weight in weights]
     wide = [
         jnp.repeat(mask.astype(F32), BLK, axis=1) for mask in (gate_mask, up_mask, down_mask)
     ]
-    effs = local_call(prepare_kernel, shapes, *weights, *wide)
+    effs = [local_call(prepare_kernel, *args) for args in zip(shapes, weights, wide)]
     effs_x = [swap(eff) for eff in effs]
 
-    own = lax.dynamic_slice_in_dim(gathered, core * half, half, 1).reshape(-1, 2 * width)
-    other = lax.dynamic_slice_in_dim(gathered, (1 - core) * half, half, 1).reshape(-1, 2 * width)
+    own_shape = jax.ShapeDtypeStruct((cols * half, 2 * width), BF)
+    own, other = pl.pallas_call(
+        split_kernel,
+        out_shape=[own_shape, own_shape],
+        in_specs=[pl.BlockSpec(memory_space=pltpu.SMEM)]
+        + [pl.BlockSpec(memory_space=pltpu.VMEM)] * len(chunks),
+        out_specs=[pl.BlockSpec(memory_space=pltpu.VMEM)] * 2,
+        name="split",
+    )(order, *[chunk for _, _, chunk in chunks])
     cross = swap(other)
     x_lo, y = lax.axis_index("x_lo"), lax.axis_index("y")
     y_n = lax.axis_size("y")
@@ -188,17 +244,25 @@
     ).astype(jnp.int32)
     parts = partial_sums(place, own, cross, effs, effs_x)
 
-    got = {0: parts[0]}
-    for r in (6, 5, 7, 2, 4, 1, 3):
-        moves = [
-            (i, ((i // y_n) ^ (r // y_n)) * y_n + (i % y_n + r % y_n) % y_n)
-            for i in range(pairs)
-        ]
-        got[r] = lax.ppermute(parts[r], PAIR, moves)
+    x_kept, x_given, y_kept = parts[:3]
+    quarter = [
+        jax.ShapeDtypeStruct((3, x_kept.shape[1] // y_n, hid), t) for t in (F32, BF, BF, BF, F32, BF)
+    ]
+    mids = local_call(
+        middle_kernel,
+        quarter,
+        x_kept,
+        along("x_lo", x_given, 1),
+        y_kept,
+        *[along("y", parts[2 + k], -k) for k in (1, 2, 3)],
+    )
     mine = local_call(
         activation_kernel,
-        jax.ShapeDtypeStruct((3, parts[0].shape[1], hid), BF),
-        *[got[r] for r in range(pairs)],
+        jax.ShapeDtypeStruct((3, 2 * quarter[0].shape[1], hid), BF),
+        mids[0],
+        *[along("y", mids[k], -k) for k in (1, 2, 3)],
+        mids[4],
+        along("x_lo", mids[5], 1),
     )
 
     def from_up(array):

time: 189 us -> 191 us (1.011)
  waiting for transfers between devices: 83.8 us -> 73.1 us
  Pallas kernels: 37.9 us -> 46.3 us
  local copies, waits for them, and re-layouts: 6.62 us -> 13.8 us
  starting transfers between devices: 52.4 us -> 49.2 us
    all_to_all x1 -> x0, waiting for transfers between devices: 21.3 us -> none  [layer(): lax.all_to_all(jnp.broadcast_to(both, (cols,) + both.shape), COL, 0, 0, t...]
    ppermute x7 -> x17, waiting for transfers between devices: 14.2 us -> 26.4 us  [along(): return lax.ppermute(array, axis, [(i, (i - hops) % n) for i in range(n)])]
    all_to_all x1 -> x0, starting transfers between devices: 11 us -> none  [layer(): lax.all_to_all(jnp.broadcast_to(both, (cols,) + both.shape), COL, 0, 0, t...]
    pallas_call x4 -> x7, Pallas kernels: 22.3 us -> 28.2 us  [local_call(): pl.pallas_call(kernel, out_shape=outs, in_specs=[whole] * len(args), out_...]
    unnamed x50 -> x63, local copies, waits for them, and re-layouts: 3.02 us -> 7.58 us
    squeeze x0 -> x6, local copies, waits for them, and re-layouts: none -> 3.95 us  [layer(): chunks += [(rel, k, ups[k][rel]), (rel, z_n - k, downs[k][rel])]]
    all_to_all x1, starting transfers between devices: 4.34 us -> 8.23 us  [layer(): arrived = lax.all_to_all(send, COL, 0, 0, tiled=True)]
    ppermute x4, waiting for transfers between devices: 4.03 us -> 0.53 us  [from_up(): return lax.ppermute(array, 'y', [(i, (i - 1) % y_n) for i in range(y_n)])]
  transfers between devices with their start and end apart: 24 -> 33, of which waited for: 14 -> 19; matrix products, arithmetic and copies ran while one was open for 3% -> 5% of each run, Pallas kernels for 6% -> 9%
where the time goes in v5:
time: 191 us; the launch traced here: 188 us
  waiting for transfers between devices  73.1 us (38%)
  starting transfers between devices  49.2 us (26%)
  Pallas kernels  46.3 us (24%)
  local copies, waits for them, and re-layouts  13.8 us (7%)
  other arithmetic  4.84 us (3%)
    ppermute x17, starting transfers between devices, along(): return lax.ppermute(array, axis, [(i, (i - hops) % n) for i in range(n)])  30.1 us
    all_to_all x1, waiting for transfers between devices, layer(): arrived = lax.all_to_all(send, COL, 0, 0, tiled=True)  28.9 us
    pallas_call x7, Pallas kernels, local_call(): pl.pallas_call(kernel, out_shape=outs, in_specs=[whole] * len(args), out_...  28.2 us
    ppermute x17, waiting for transfers between devices, along(): return lax.ppermute(array, axis, [(i, (i - hops) % n) for i in range(n)])  26.4 us
    pallas_call x1, Pallas kernels, partial_sums(): pl.pallas_call(kernel, out_shape=[jax.ShapeDtypeStruct((3, n, hid), t) fo...  9.79 us
    ppermute x4, waiting for transfers between devices, from_down(): return lax.ppermute(array, 'y', [(i, (i + 1) % y_n) for i in range(y_n)])  9.72 us
    all_to_all x1, starting transfers between devices, layer(): arrived = lax.all_to_all(send, COL, 0, 0, tiled=True)  8.23 us
    unnamed x63, local copies, waits for them, and re-layouts  7.58 us
  transfers between devices with their start and end apart: 33, of which 19 were waited for; matrix products, arithmetic and copies ran while one was open for 5% of the time, Pallas kernels for 9%

profile of v5, /device:TPU:8, one launch (start us, length us, event | category | flops | bytes accessed | tf_op | source)
XLA Modules:
  0.0 188.2 jit_solution(6343750988141439096)
XLA Ops:
  0.6 0.8 constant_dynamic-update-slice_fusion.1
  2.2 3.0 %collective-permute-start = (bf16[32,1024]{1,0:T(8,128)(2,1)S(1)}, bf16[32,1024]{1,0:T(8,128)(2,1)S(1)}, u32[]{:S(2)}, u32[]{:S(2)}) collective-permute-start(bf16[32,1024]{1,0:T(8,128)(2,1)S(1)} %constant_dynamic-update-slice_fusion.refs_0_), channel_id=1, source_target_pairs={{0,8},{8,0},{1,9},{9,1},{2,10},{10,2},{3,11},{11,3},{4,12},{12,4},... | collective-permute-start | bytes 196616 | tf_op jit(solution)/shard_map/ppermute | solution.py:205
  6.7 2.9 %shard_map.121.down = bf16[1792,512]{1,0:T(8,128)(2,1)} custom-call(bf16[1792,512]{1,0:T(8,128)(2,1)} %weight.5, f32[14,512]{1,0:T(8,128)} %bitcast.69), custom_call_target="tpu_custom_call" | custom-call | tf_op jit(solution)/shard_map/pallas_call | solution.py:22
  10.3 2.9 %shard_map.120.up = bf16[512,1792]{1,0:T(8,128)(2,1)} custom-call(bf16[512,1792]{1,0:T(8,128)(2,1)} %weight.4, f32[4,1792]{1,0:T(4,128)} %bitcast.72), custom_call_target="tpu_custom_call" | custom-call | tf_op jit(solution)/shard_map/pallas_call | solution.py:22
  13.7 2.0 %collective-permute-start.2 = (bf16[2,32,1024]{2,1,0:T(8,128)(2,1)S(1)}, bf16[2,32,1024]{2,1,0:T(8,128)(2,1)S(1)}, u32[]{:S(2)}, u32[]{:S(2)}) collective-permute-start(bf16[2,32,1024]{2,1,0:T(8,128)(2,1)S(1)} %pad_maximum_fusion.1), channel_id=1, source_target_pairs={{0,1},{1,2},{2,3},{3,4},{4,5},{5,6},{6,7},{7,0},{8,9},{9,10},{10,1... | collective-permute-start | bytes 393224 | tf_op jit(solution)/shard_map/ppermute | solution.py:205
  15.7 4.0 %collective-permute-start.1 = (bf16[2,32,1024]{2,1,0:T(8,128)(2,1)S(1)}, bf16[2,32,1024]{2,1,0:T(8,128)(2,1)S(1)}, u32[]{:S(2)}, u32[]{:S(2)}) collective-permute-start(bf16[2,32,1024]{2,1,0:T(8,128)(2,1)S(1)} %pad_maximum_fusion.1), channel_id=1, source_target_pairs={{0,7},{1,0},{2,1},{3,2},{4,3},{5,4},{6,5},{7,6},{8,15},{9,8},{10,9... | collective-permute-start | bytes 393224 | tf_op jit(solution)/shard_map/ppermute | solution.py:205
  20.4 2.9 %shard_map.119.gate = bf16[512,1792]{1,0:T(8,128)(2,1)} custom-call(bf16[512,1792]{1,0:T(8,128)(2,1)} %weight.3, f32[4,1792]{1,0:T(4,128)} %bitcast.74), custom_call_target="tpu_custom_call" | custom-call | tf_op jit(solution)/shard_map/pallas_call | solution.py:22
  23.9 3.2 %collective-permute-start.3 = (bf16[2,32,1024]{2,1,0:T(8,128)(2,1)S(1)}, bf16[2,32,1024]{2,1,0:T(8,128)(2,1)S(1)}, u32[]{:S(2)}, u32[]{:S(2)}) collective-permute-start(bf16[2,32,1024]{2,1,0:T(8,128)(2,1)S(1)} %collective-permute-done.1), channel_id=1, source_target_pairs={{0,7},{1,0},{2,1},{3,2},{4,3},{5,4},{6,5},{7,6},{8,15},{9,8},{10,9... | collective-permute-start | bytes 393224 | tf_op jit(solution)/shard_map/ppermute | solution.py:205
  28.4 2.6 %collective-permute-done.4 = bf16[2,32,1024]{2,1,0:T(8,128)(2,1)S(1)} collective-permute-done((bf16[2,32,1024]{2,1,0:T(8,128)(2,1)S(1)}, bf16[2,32,1024]{2,1,0:T(8,128)(2,1)S(1)}, u32[]{:S(2)}, u32[]{:S(2)}) %collective-permute-start.4) | collective-permute-done | bytes 131104 | tf_op jit(solution)/shard_map/ppermute | solution.py:205
  31.0 3.2 %collective-permute-start.5 = (bf16[2,32,1024]{2,1,0:T(8,128)(2,1)S(1)}, bf16[2,32,1024]{2,1,0:T(8,128)(2,1)S(1)}, u32[]{:S(2)}, u32[]{:S(2)}) collective-permute-start(bf16[2,32,1024]{2,1,0:T(8,128)(2,1)S(1)} %collective-permute-done.3), channel_id=1, source_target_pairs={{0,7},{1,0},{2,1},{3,2},{4,3},{5,4},{6,5},{7,6},{8,15},{9,8},{10,9... | collective-permute-start | bytes 393224 | tf_op jit(solution)/shard_map/ppermute | solution.py:205
  34.9 2.4 %collective-permute-done.6 = bf16[2,32,1024]{2,1,0:T(8,128)(2,1)S(1)} collective-permute-done((bf16[2,32,1024]{2,1,0:T(8,128)(2,1)S(1)}, bf16[2,32,1024]{2,1,0:T(8,128)(2,1)S(1)}, u32[]{:S(2)}, u32[]{:S(2)}) %collective-permute-start.6) | collective-permute-done | bytes 131104 | tf_op jit(solution)/shard_map/ppermute | solution.py:205
  38.6 3.2 %collective-permute-start.7 = (bf16[32,1024]{1,0:T(8,128)(2,1)S(1)}, bf16[32,1024]{1,0:T(8,128)(2,1)S(1)}, u32[]{:S(2)}, u32[]{:S(2)}) collective-permute-start(bf16[32,1024]{1,0:T(8,128)(2,1)S(1)} %get-tuple-element.48.refs_10_), channel_id=1, source_target_pairs={{0,7},{1,0},{2,1},{3,2},{4,3},{5,4},{6,5},{7,6},{8,15},{9,8},{10,9... | collective-permute-start | bytes 196616 | tf_op jit(solution)/shard_map/ppermute | solution.py:205
  42.5 0.9 collective-permute-done.8.refs_15_
  44.3 2.3 %split.1 = (bf16[256,1024]{1,0:T(8,128)(2,1)}, bf16[256,1024]{1,0:T(8,128)(2,1)}) custom-call(s32[17]{0:T(128)} %stack.116.place, bf16[32,1024]{1,0:T(8,128)(2,1)} %copy-done.8, bf16[32,1024]{1,0:T(8,128)(2,1)} %copy-done.13, bf16[32,1024]{1,0:T(8,128)(2,1)} %get-tuple-element.56.refs_2_, bf16[32,1024]{1,0:T(8,128)(2,1)} %get-tuple-element.54.refs_3_, ...), custom_call_target="tpu_custom_call" | custom-call | tf_op jit(solution)/shard_map/split/pallas_call | solution.py:231
  47.4 1.4 collective-permute-done.9.cross
  48.8 0.8 copy-done.7
  50.2 9.8 %partial_sums.1 = (f32[3,64,1792]{2,1,0:T(8,128)}, bf16[3,64,1792]{2,1,0:T(8,128)(2,1)}, f32[3,32,1792]{2,1,0:T(8,128)}, bf16[3,32,1792]{2,1,0:T(8,128)(2,1)}, b...) custom-call(s32[8]{0:T(128)} %stack.98.place, bf16[256,1024]{1,0:T(8,128)(2,1)} %get-tuple-element.25.own, ...), custom_call_target="tpu_custom_call" | custom-call | tf_op jit(solution)/shard_map/partial_sums/pallas_call | solution.py:92
  60.7 1.6 collective-permute-start.14
  62.3 0.9 collective-permute-start.15
  63.2 2.4 %collective-permute-start.16 = (bf16[3,32,1792]{2,1,0:T(8,128)(2,1)}, bf16[3,32,1792]{2,1,0:T(8,128)(2,1)S(1)}, u32[]{:S(2)}, u32[]{:S(2)}) collective-permute-start(bf16[3,32,1792]{2,1,0:T(8,128)(2,1)} %get-tuple-element.32), channel_id=1, source_target_pairs={{0,96},{32,0},{64,32},{96,64},{1,97},{33,1},{65,33},{97,65},{2,98}... | collective-permute-start | bytes 1032200 | tf_op jit(solution)/shard_map/ppermute | solution.py:205
  65.6 6.2 %collective-permute-done.14.refs_0_ = bf16[3,32,1792]{2,1,0:T(8,128)(2,1)S(1)} collective-permute-done((bf16[3,32,1792]{2,1,0:T(8,128)(2,1)}, bf16[3,32,1792]{2,1,0:T(8,128)(2,1)S(1)}, u32[]{:S(2)}, u32[]{:S(2)}) %collective-permute-start.14) | collective-permute-done | bytes 344096 | tf_op jit(solution)/shard_map/ppermute | solution.py:205
  71.8 3.1 %collective-permute-done.15.refs_1_ = bf16[3,32,1792]{2,1,0:T(8,128)(2,1)S(1)} collective-permute-done((bf16[3,32,1792]{2,1,0:T(8,128)(2,1)}, bf16[3,32,1792]{2,1,0:T(8,128)(2,1)S(1)}, u32[]{:S(2)}, u32[]{:S(2)}) %collective-permute-start.15) | collective-permute-done | bytes 344096 | tf_op jit(solution)/shard_map/ppermute | solution.py:205
  74.9 5.3 %collective-permute-done.16.refs_2_ = bf16[3,32,1792]{2,1,0:T(8,128)(2,1)S(1)} collective-permute-done((bf16[3,32,1792]{2,1,0:T(8,128)(2,1)}, bf16[3,32,1792]{2,1,0:T(8,128)(2,1)S(1)}, u32[]{:S(2)}, u32[]{:S(2)}) %collective-permute-start.16) | collective-permute-done | bytes 344096 | tf_op jit(solution)/shard_map/ppermute | solution.py:205
  81.2 3.2 %shard_map.122 = (f32[3,16,1792]{2,1,0:T(8,128)}, bf16[3,16,1792]{2,1,0:T(8,128)(2,1)}, bf16[3,16,1792]{2,1,0:T(8,128)(2,1)}, bf16[3,16,1792]{2,1,0:T(8,128)(2,1...) custom-call(f32[3,64,1792]{2,1,0:T(8,128)} %get-tuple-element.27.x_kept, bf16[3,64,1792]{2,1,0:T(8,128)(2,1)} %copy-done.6, ...), custom_call_target="tpu_custom_call" | custom-call | tf_op jit(solution)/shard_map/pallas_call | solution.py:22
  84.3 1.3 collective-permute-start.17
  85.7 1.7 collective-permute-start.18
  87.3 1.4 collective-permute-start.19
  88.7 1.4 collective-permute-start.20
  90.1 0.8 collective-permute-done.17.x_one
  90.9 3.2 %collective-permute-done.18.x_two = bf16[3,16,1792]{2,1,0:T(8,128)(2,1)S(1)} collective-permute-done((bf16[3,16,1792]{2,1,0:T(8,128)(2,1)}, bf16[3,16,1792]{2,1,0:T(8,128)(2,1)S(1)}, u32[]{:S(2)}, u32[]{:S(2)}) %collective-permute-start.18) | collective-permute-done | bytes 172064 | tf_op jit(solution)/shard_map/ppermute | solution.py:205
  94.1 1.7 collective-permute-done.19.x_three
  96.6 2.3 %shard_map.123.refs_0_ = bf16[3,32,1792]{2,1,0:T(8,128)(2,1)} custom-call(f32[3,16,1792]{2,1,0:T(8,128)} %get-tuple-element.33.x_kept, bf16[3,16,1792]{2,1,0:T(8,128)(2,1)} %copy-done.16, bf16[3,16,1792]{2,1,0:T(8,128)(2,1)} %copy-done.17, bf16[3,16,1792]{2,1,0:T(8,128)(2,1)} %copy-done.18, f32[3,16,1792]{2,1,0:T(8,128)} %get-tuple-element.37.y_kept, ...), custom_call_target="tpu_custom_call" | custom-call | tf_op jit(solution)/shard_map/pallas_call | solution.py:22
  98.9 1.4 collective-permute-start.23
  100.9 1.4 collective-permute-start.21
  102.3 6.1 %collective-permute-done.23.refs_3_ = bf16[3,32,1792]{2,1,0:T(8,128)(2,1)S(1)} collective-permute-done((bf16[3,32,1792]{2,1,0:T(8,128)(2,1)}, bf16[3,32,1792]{2,1,0:T(8,128)(2,1)S(1)}, u32[]{:S(2)}, u32[]{:S(2)}) %collective-permute-start.23) | collective-permute-done | bytes 344096 | tf_op jit(solution)/shard_map/ppermute | solution.py:276
  108.5 2.0 %collective-permute-start.24 = (bf16[3,32,1792]{2,1,0:T(8,128)(2,1)S(1)}, bf16[3,32,1792]{2,1,0:T(8,128)(2,1)S(1)}, u32[]{:S(2)}, u32[]{:S(2)}) collective-permute-start(bf16[3,32,1792]{2,1,0:T(8,128)(2,1)S(1)} %collective-permute-done.23.refs_3_), channel_id=1, source_target_pairs={{0,96},{32,0},{64,32},{96,64},{1,97},{33,1},{65,33},{97,65},{2,98}... | collective-permute-start | bytes 1032200 | tf_op jit(solution)/shard_map/ppermute | solution.py:269
  110.8 2.0 %collective-permute-start.26 = (bf16[3,32,896]{2,1,0:T(8,128)(2,1)S(1)}, bf16[3,32,896]{2,1,0:T(8,128)(2,1)S(1)}, u32[]{:S(2)}, u32[]{:S(2)}) collective-permute-start(bf16[3,32,896]{2,1,0:T(8,128)(2,1)S(1)} %slice.94), channel_id=1, source_target_pairs={{0,96},{32,0},{64,32},{96,64},{1,97},{33,1},{65,33},{97,65},{2,98}... | collective-permute-start | bytes 516104 | tf_op jit(solution)/shard_map/ppermute | solution.py:269
  112.8 6.6 %collective-permute-done.25.refs_5_ = bf16[3,32,1792]{2,1,0:T(8,128)(2,1)S(1)} collective-permute-done((bf16[3,32,1792]{2,1,0:T(8,128)(2,1)S(1)}, bf16[3,32,1792]{2,1,0:T(8,128)(2,1)S(1)}, u32[]{:S(2)}, u32[]{:S(2)}) %collective-permute-start.25) | collective-permute-done | bytes 344096 | tf_op jit(solution)/shard_map/ppermute | solution.py:272
  119.6 2.0 %collective-permute-start.28 = (bf16[3,32,896]{2,1,0:T(8,128)(2,1)S(1)}, bf16[3,32,896]{2,1,0:T(8,128)(2,1)S(1)}, u32[]{:S(2)}, u32[]{:S(2)}) collective-permute-start(bf16[3,32,896]{2,1,0:T(8,128)(2,1)S(1)} %slice.96), channel_id=1, source_target_pairs={{0,96},{32,0},{64,32},{96,64},{1,97},{33,1},{65,33},{97,65},{2,98}... | collective-permute-start | bytes 516104 | tf_op jit(solution)/shard_map/ppermute | solution.py:269
  121.6 0.9 collective-permute-done.27.refs_7_
  122.6 2.3 %collective-permute-done.29.refs_9_ = bf16[3,32,896]{2,1,0:T(8,128)(2,1)S(1)} collective-permute-done((bf16[3,32,896]{2,1,0:T(8,128)(2,1)S(1)}, bf16[3,32,896]{2,1,0:T(8,128)(2,1)S(1)}, u32[]{:S(2)}, u32[]{:S(2)}) %collective-permute-start.29) | collective-permute-done | bytes 172064 | tf_op jit(solution)/shard_map/ppermute | solution.py:272
  126.2 6.0 %arrange.1 = (bf16[3,256,1792]{2,1,0:T(8,128)(2,1)}, bf16[256,1024]{1,0:T(8,128)(2,1)}) custom-call(s32[8]{0:T(128)} %stack.98.place, bf16[3,32,1792]{2,1,0:T(8,128)(2,1)} %shard_map.123.refs_0_, bf16[3,32,1792]{2,1,0:T(8,128)(2,1)} %copy-done.3, bf16[3,32,1792]{2,1,0:T(8,128)(2,1)} %copy-done.2, bf16[3,32,1792]{2,1,0:T(8,128)(2,1)} %copy-done.9, ...), custom_call_target="tpu_custom_call" | custom-call | tf_op jit(solution)/shard_map/arrange/pallas_call | solution.py:283
  132.3 6.0 %shard_map.124 = bf16[256,1024]{1,0:T(8,128)(2,1)} custom-call(bf16[3,256,1792]{2,1,0:T(8,128)(2,1)} %get-tuple-element.41.acts, bf16[512,1792]{1,0:T(8,128)(2,1)} %shard_map.119.gate, bf16[512,1792]{1,0:T(8,128)(2,1)} %shard_map.120.up, bf16[1792,512]{1,0:T(8,128)(2,1)} %shard_map.121.down), custom_call_target="tpu_custom_call" | custom-call | tf_op jit(solution)/shard_map/pallas_call | solution.py:22
  138.2 2.1 %pad_maximum_fusion = bf16[16,32,1024]{2,1,0:T(8,128)(2,1)} fusion(bf16[16,16,1024]{2,1,0:T(8,128)(2,1)S(1)} %bitcast.67, bf16[16,16,1024]{2,1,0:T(8,128)(2,1)} %bitcast.66), kind=kLoop, calls=%fused_computation.1 | loop fusion | flops 2097152 | bytes 2097152 | tf_op jit(solution)/shard_map/concatenate | solution.py:293
  140.8 8.2 %all-to-all-start = ((bf16[16,32,1024]{2,1,0:T(8,128)(2,1)}), bf16[16,32,1024]{2,1,0:T(8,128)(2,1)}, u32[]{:S(2)}, u32[]{:S(2)}) async-start(bf16[16,32,1024]{2,1,0:T(8,128)(2,1)} %pad_maximum_fusion), calls=%async_computation | async-start | bytes 2097152 | tf_op jit(solution)/shard_map/all_to_all | solution.py:296
  149.1 28.9 %all-to-all-done = bf16[16,32,1024]{2,1,0:T(8,128)(2,1)} async-done(((bf16[16,32,1024]{2,1,0:T(8,128)(2,1)}), bf16[16,32,1024]{2,1,0:T(8,128)(2,1)}, u32[]{:S(2)}, u32[]{:S(2)}) %all-to-all-start) | async-done | bytes 1048608 | tf_op jit(solution)/shard_map/all_to_all | solution.py:296
  177.9 1.4 convert_reduce_fusion
  180.0 8.2 %shard_map.125 = (bf16[512,1792]{1,0:T(8,128)(2,1)}, bf16[512,1792]{1,0:T(8,128)(2,1)}, bf16[1792,512]{1,0:T(8,128)(2,1)}) custom-call(bf16[3,256,1792]{2,1,0:T(8,128)(2,1)} %get-tuple-element.41.acts, bf16[3,256,1792]{2,1,0:T(8,128)(2,1)} %collective-permute-done.31.acts_x, bf16[256,1024]{1,0:T(8,128)(2,1)} %get-tuple-element.25.own, ...), custom_call_target="tpu_custom_call" | custom-call | tf_op jit(solution)/shard_map/pallas_call | solution.py:22
  (114 shorter events, 17.1 us)
Async XLA Ops:
  2.2 11.5 %copy-start.8 = (bf16[32,1024]{1,0:T(8,128)(2,1)}, bf16[32,1024]{1,0:T(8,128)(2,1)S(1)}, u32[]{:S(2)}) copy-start(bf16[32,1024]{1,0:T(8,128)(2,1)S(1)} %constant_dynamic-update-slice_fusion.refs_0_) | copy-start | bytes 196612
  2.2 11.5 %collective-permute-start = (bf16[32,1024]{1,0:T(8,128)(2,1)S(1)}, bf16[32,1024]{1,0:T(8,128)(2,1)S(1)}, u32[]{:S(2)}, u32[]{:S(2)}) collective-permute-start(bf16[32,1024]{1,0:T(8,128)(2,1)S(1)} %constant_dynamic-update-slice_fusion.refs_0_), channel_id=1, source_target_pairs={{0,8},{8,0},{1,9},{9,1},{2,10},{10,2},{3,11},{11,3},{4,12},{12,4},... | collective-permute-start | bytes 196616 | tf_op jit(solution)/shard_map/ppermute | solution.py:205
  6.7 2.9 %copy-start.26 = (s32[4,14]{1,0:T(4,128)S(1)}, s32[4,14]{1,0:T(4,128)}, u32[]{:S(2)}) copy-start(s32[4,14]{1,0:T(4,128)} %param.14) | copy-start | bytes 676
  9.5 39.2 %collective-permute-start.12 = (bf16[1792,512]{1,0:T(8,128)(2,1)}, bf16[1792,512]{1,0:T(8,128)(2,1)S(1)}, u32[]{:S(2)}, u32[]{:S(2)}) collective-permute-start(bf16[1792,512]{1,0:T(8,128)(2,1)} %shard_map.121.down), channel_id=1, source_target_pairs={{0,16},{16,0},{1,17},{17,1},{2,18},{18,2},{3,19},{19,3},{4,20},{20... | collective-permute-start | bytes 5505032 | tf_op jit(solution)/shard_map/ppermute | solution.py:187
  10.3 3.4 %copy-start.27 = (s32[4,14]{1,0:T(4,128)S(1)}, s32[4,14]{1,0:T(4,128)}, u32[]{:S(2)}) copy-start(s32[4,14]{1,0:T(4,128)} %param.13) | copy-start | bytes 676
  13.1 35.7 %collective-permute-start.11 = (bf16[512,1792]{1,0:T(8,128)(2,1)}, bf16[512,1792]{1,0:T(8,128)(2,1)}, u32[]{:S(2)}, u32[]{:S(2)}) collective-permute-start(bf16[512,1792]{1,0:T(8,128)(2,1)} %shard_map.120.up), channel_id=1, source_target_pairs={{0,16},{16,0},{1,17},{17,1},{2,18},{18,2},{3,19},{19,3},{4,20},{20... | collective-permute-start | bytes 5505032 | tf_op jit(solution)/shard_map/ppermute | solution.py:187
  13.6 9.6 %copy-start.13 = (bf16[32,1024]{1,0:T(8,128)(2,1)}, bf16[32,1024]{1,0:T(8,128)(2,1)S(1)}, u32[]{:S(2)}) copy-start(bf16[32,1024]{1,0:T(8,128)(2,1)S(1)} %collective-permute-done.refs_1_) | copy-start | bytes 196612
  13.7 10.2 %collective-permute-start.2 = (bf16[2,32,1024]{2,1,0:T(8,128)(2,1)S(1)}, bf16[2,32,1024]{2,1,0:T(8,128)(2,1)S(1)}, u32[]{:S(2)}, u32[]{:S(2)}) collective-permute-start(bf16[2,32,1024]{2,1,0:T(8,128)(2,1)S(1)} %pad_maximum_fusion.1), channel_id=1, source_target_pairs={{0,1},{1,2},{2,3},{3,4},{4,5},{5,6},{6,7},{7,0},{8,9},{9,10},{10,1... | collective-permute-start | bytes 393224 | tf_op jit(solution)/shard_map/ppermute | solution.py:205
  15.7 8.2 %collective-permute-start.1 = (bf16[2,32,1024]{2,1,0:T(8,128)(2,1)S(1)}, bf16[2,32,1024]{2,1,0:T(8,128)(2,1)S(1)}, u32[]{:S(2)}, u32[]{:S(2)}) collective-permute-start(bf16[2,32,1024]{2,1,0:T(8,128)(2,1)S(1)} %pad_maximum_fusion.1), channel_id=1, source_target_pairs={{0,7},{1,0},{2,1},{3,2},{4,3},{5,4},{6,5},{7,6},{8,15},{9,8},{10,9... | collective-permute-start | bytes 393224 | tf_op jit(solution)/shard_map/ppermute | solution.py:205
  23.3 25.5 %collective-permute-start.10 = (bf16[512,1792]{1,0:T(8,128)(2,1)}, bf16[512,1792]{1,0:T(8,128)(2,1)}, u32[]{:S(2)}, u32[]{:S(2)}) collective-permute-start(bf16[512,1792]{1,0:T(8,128)(2,1)} %shard_map.119.gate), channel_id=1, source_target_pairs={{0,16},{16,0},{1,17},{17,1},{2,18},{18,2},{3,19},{19,3},{4,20},{20... | collective-permute-start | bytes 5505032 | tf_op jit(solution)/shard_map/ppermute | solution.py:187
  23.9 7.1 %collective-permute-start.4 = (bf16[2,32,1024]{2,1,0:T(8,128)(2,1)S(1)}, bf16[2,32,1024]{2,1,0:T(8,128)(2,1)S(1)}, u32[]{:S(2)}, u32[]{:S(2)}) collective-permute-start(bf16[2,32,1024]{2,1,0:T(8,128)(2,1)S(1)} %collective-permute-done.2), channel_id=1, source_target_pairs={{0,1},{1,2},{2,3},{3,4},{4,5},{5,6},{6,7},{7,0},{8,9},{9,10},{10,1... | collective-permute-start | bytes 393224 | tf_op jit(solution)/shard_map/ppermute | solution.py:205
  23.9 7.1 %collective-permute-start.3 = (bf16[2,32,1024]{2,1,0:T(8,128)(2,1)S(1)}, bf16[2,32,1024]{2,1,0:T(8,128)(2,1)S(1)}, u32[]{:S(2)}, u32[]{:S(2)}) collective-permute-start(bf16[2,32,1024]{2,1,0:T(8,128)(2,1)S(1)} %collective-permute-done.1), channel_id=1, source_target_pairs={{0,7},{1,0},{2,1},{3,2},{4,3},{5,4},{6,5},{7,6},{8,15},{9,8},{10,9... | collective-permute-start | bytes 393224 | tf_op jit(solution)/shard_map/ppermute | solution.py:205
  31.0 6.3 %collective-permute-start.6 = (bf16[2,32,1024]{2,1,0:T(8,128)(2,1)S(1)}, bf16[2,32,1024]{2,1,0:T(8,128)(2,1)S(1)}, u32[]{:S(2)}, u32[]{:S(2)}) collective-permute-start(bf16[2,32,1024]{2,1,0:T(8,128)(2,1)S(1)} %collective-permute-done.4), channel_id=1, source_target_pairs={{0,1},{1,2},{2,3},{3,4},{4,5},{5,6},{6,7},{7,0},{8,9},{9,10},{10,1... | collective-permute-start | bytes 393224 | tf_op jit(solution)/shard_map/ppermute | solution.py:205
  31.0 6.9 %collective-permute-start.5 = (bf16[2,32,1024]{2,1,0:T(8,128)(2,1)S(1)}, bf16[2,32,1024]{2,1,0:T(8,128)(2,1)S(1)}, u32[]{:S(2)}, u32[]{:S(2)}) collective-permute-start(bf16[2,32,1024]{2,1,0:T(8,128)(2,1)S(1)} %collective-permute-done.3), channel_id=1, source_target_pairs={{0,7},{1,0},{2,1},{3,2},{4,3},{5,4},{6,5},{7,6},{8,15},{9,8},{10,9... | collective-permute-start | bytes 393224 | tf_op jit(solution)/shard_map/ppermute | solution.py:205
  37.9 5.8 %copy-start.14 = (bf16[32,1024]{1,0:T(8,128)(2,1)}, bf16[32,1024]{1,0:T(8,128)(2,1)S(1)}, u32[]{:S(2)}) copy-start(bf16[32,1024]{1,0:T(8,128)(2,1)S(1)} %get-tuple-element.45.refs_13_) | copy-start | bytes 196612
  37.9 5.5 %collective-permute-start.8 = (bf16[32,1024]{1,0:T(8,128)(2,1)S(1)}, bf16[32,1024]{1,0:T(8,128)(2,1)S(1)}, u32[]{:S(2)}, u32[]{:S(2)}) collective-permute-start(bf16[32,1024]{1,0:T(8,128)(2,1)S(1)} %get-tuple-element.45.refs_13_), channel_id=1, source_target_pairs={{0,1},{1,2},{2,3},{3,4},{4,5},{5,6},{6,7},{7,0},{8,9},{9,10},{10,1... | collective-permute-start | bytes 196616 | tf_op jit(solution)/shard_map/ppermute | solution.py:205
  38.6 5.1 %copy-start.15 = (bf16[32,1024]{1,0:T(8,128)(2,1)}, bf16[32,1024]{1,0:T(8,128)(2,1)S(1)}, u32[]{:S(2)}) copy-start(bf16[32,1024]{1,0:T(8,128)(2,1)S(1)} %get-tuple-element.48.refs_10_) | copy-start | bytes 196612
  38.6 5.1 %collective-permute-start.7 = (bf16[32,1024]{1,0:T(8,128)(2,1)S(1)}, bf16[32,1024]{1,0:T(8,128)(2,1)S(1)}, u32[]{:S(2)}, u32[]{:S(2)}) collective-permute-start(bf16[32,1024]{1,0:T(8,128)(2,1)S(1)} %get-tuple-element.48.refs_10_), channel_id=1, source_target_pairs={{0,7},{1,0},{2,1},{3,2},{4,3},{5,4},{6,5},{7,6},{8,15},{9,8},{10,9... | collective-permute-start | bytes 196616 | tf_op jit(solution)/shard_map/ppermute | solution.py:205
  46.7 2.1 %collective-permute-start.9 = (bf16[256,1024]{1,0:T(8,128)(2,1)}, bf16[256,1024]{1,0:T(8,128)(2,1)S(1)}, u32[]{:S(2)}, u32[]{:S(2)}) collective-permute-start(bf16[256,1024]{1,0:T(8,128)(2,1)} %get-tuple-element.26.other), channel_id=1, source_target_pairs={{0,16},{16,0},{1,17},{17,1},{2,18},{18,2},{3,19},{19,3},{4,20},{20... | collective-permute-start | bytes 1572872 | tf_op jit(solution)/shard_map/ppermute | solution.py:187
  60.0 20.2 %collective-permute-start.13 = (bf16[3,64,1792]{2,1,0:T(8,128)(2,1)}, bf16[3,64,1792]{2,1,0:T(8,128)(2,1)S(1)}, u32[]{:S(2)}, u32[]{:S(2)}) collective-permute-start(bf16[3,64,1792]{2,1,0:T(8,128)(2,1)} %get-tuple-element.28), channel_id=1, source_target_pairs={{0,128},{128,0},{1,129},{129,1},{2,130},{130,2},{3,131},{131,3},{4... | collective-permute-start | bytes 2064392 | tf_op jit(solution)/shard_map/ppermute | solution.py:205
  60.7 11.1 %collective-permute-start.14 = (bf16[3,32,1792]{2,1,0:T(8,128)(2,1)}, bf16[3,32,1792]{2,1,0:T(8,128)(2,1)S(1)}, u32[]{:S(2)}, u32[]{:S(2)}) collective-permute-start(bf16[3,32,1792]{2,1,0:T(8,128)(2,1)} %get-tuple-element.30), channel_id=1, source_target_pairs={{0,32},{32,64},{64,96},{96,0},{1,33},{33,65},{65,97},{97,1},{2,34}... | collective-permute-start | bytes 1032200 | tf_op jit(solution)/shard_map/ppermute | solution.py:205
  62.3 12.6 %collective-permute-start.15 = (bf16[3,32,1792]{2,1,0:T(8,128)(2,1)}, bf16[3,32,1792]{2,1,0:T(8,128)(2,1)S(1)}, u32[]{:S(2)}, u32[]{:S(2)}) collective-permute-start(bf16[3,32,1792]{2,1,0:T(8,128)(2,1)} %get-tuple-element.31), channel_id=1, source_target_pairs={{0,64},{32,96},{64,0},{96,32},{1,65},{33,97},{65,1},{97,33},{2,66}... | collective-permute-start | bytes 1032200 | tf_op jit(solution)/shard_map/ppermute | solution.py:205
  63.2 17.0 %collective-permute-start.16 = (bf16[3,32,1792]{2,1,0:T(8,128)(2,1)}, bf16[3,32,1792]{2,1,0:T(8,128)(2,1)S(1)}, u32[]{:S(2)}, u32[]{:S(2)}) collective-permute-start(bf16[3,32,1792]{2,1,0:T(8,128)(2,1)} %get-tuple-element.32), channel_id=1, source_target_pairs={{0,96},{32,0},{64,32},{96,64},{1,97},{33,1},{65,33},{97,65},{2,98}... | collective-permute-start | bytes 1032200 | tf_op jit(solution)/shard_map/ppermute | solution.py:205
  71.8 8.3 %copy-start.10 = (bf16[3,32,1792]{2,1,0:T(8,128)(2,1)}, bf16[3,32,1792]{2,1,0:T(8,128)(2,1)S(1)}, u32[]{:S(2)}) copy-start(bf16[3,32,1792]{2,1,0:T(8,128)(2,1)S(1)} %collective-permute-done.14.refs_0_) | copy-start | bytes 1032196
  74.9 5.3 %copy-start.11 = (bf16[3,32,1792]{2,1,0:T(8,128)(2,1)}, bf16[3,32,1792]{2,1,0:T(8,128)(2,1)S(1)}, u32[]{:S(2)}) copy-start(bf16[3,32,1792]{2,1,0:T(8,128)(2,1)S(1)} %collective-permute-done.15.refs_1_) | copy-start | bytes 1032196
  84.3 6.6 %collective-permute-start.17 = (bf16[3,16,1792]{2,1,0:T(8,128)(2,1)}, bf16[3,16,1792]{2,1,0:T(8,128)(2,1)S(1)}, u32[]{:S(2)}, u32[]{:S(2)}) collective-permute-start(bf16[3,16,1792]{2,1,0:T(8,128)(2,1)} %get-tuple-element.34), channel_id=1, source_target_pairs={{0,32},{32,64},{64,96},{96,0},{1,33},{33,65},{65,97},{97,1},{2,34}... | collective-permute-start | bytes 516104 | tf_op jit(solution)/shard_map/ppermute | solution.py:205
  85.7 8.4 %collective-permute-start.18 = (bf16[3,16,1792]{2,1,0:T(8,128)(2,1)}, bf16[3,16,1792]{2,1,0:T(8,128)(2,1)S(1)}, u32[]{:S(2)}, u32[]{:S(2)}) collective-permute-start(bf16[3,16,1792]{2,1,0:T(8,128)(2,1)} %get-tuple-element.35), channel_id=1, source_target_pairs={{0,64},{32,96},{64,0},{96,32},{1,65},{33,97},{65,1},{97,33},{2,66}... | collective-permute-start | bytes 516104 | tf_op jit(solution)/shard_map/ppermute | solution.py:205
  87.3 8.5 %collective-permute-start.19 = (bf16[3,16,1792]{2,1,0:T(8,128)(2,1)}, bf16[3,16,1792]{2,1,0:T(8,128)(2,1)S(1)}, u32[]{:S(2)}, u32[]{:S(2)}) collective-permute-start(bf16[3,16,1792]{2,1,0:T(8,128)(2,1)} %get-tuple-element.36), channel_id=1, source_target_pairs={{0,96},{32,0},{64,32},{96,64},{1,97},{33,1},{65,33},{97,65},{2,98}... | collective-permute-start | bytes 516104 | tf_op jit(solution)/shard_map/ppermute | solution.py:205
  88.7 7.1 %collective-permute-start.20 = (bf16[3,16,1792]{2,1,0:T(8,128)(2,1)}, bf16[3,16,1792]{2,1,0:T(8,128)(2,1)S(1)}, u32[]{:S(2)}, u32[]{:S(2)}) collective-permute-start(bf16[3,16,1792]{2,1,0:T(8,128)(2,1)} %get-tuple-element.38), channel_id=1, source_target_pairs={{0,128},{128,0},{1,129},{129,1},{2,130},{130,2},{3,131},{131,3},{4... | collective-permute-start | bytes 516104 | tf_op jit(solution)/shard_map/ppermute | solution.py:205
  90.9 4.9 %copy-start.16 = (bf16[3,16,1792]{2,1,0:T(8,128)(2,1)}, bf16[3,16,1792]{2,1,0:T(8,128)(2,1)S(1)}, u32[]{:S(2)}) copy-start(bf16[3,16,1792]{2,1,0:T(8,128)(2,1)S(1)} %collective-permute-done.17.x_one) | copy-start | bytes 516100
  98.9 9.6 %collective-permute-start.23 = (bf16[3,32,1792]{2,1,0:T(8,128)(2,1)}, bf16[3,32,1792]{2,1,0:T(8,128)(2,1)S(1)}, u32[]{:S(2)}, u32[]{:S(2)}) collective-permute-start(bf16[3,32,1792]{2,1,0:T(8,128)(2,1)} %shard_map.123.refs_0_), channel_id=1, source_target_pairs={{0,128},{128,0},{1,129},{129,1},{2,130},{130,2},{3,131},{131,3},{4... | collective-permute-start | bytes 1032200 | tf_op jit(solution)/shard_map/ppermute | solution.py:276
  100.3 10.2 %collective-permute-start.22 = (bf16[3,32,1792]{2,1,0:T(8,128)(2,1)}, bf16[3,32,1792]{2,1,0:T(8,128)(2,1)S(1)}, u32[]{:S(2)}, u32[]{:S(2)}) collective-permute-start(bf16[3,32,1792]{2,1,0:T(8,128)(2,1)} %shard_map.123.refs_0_), channel_id=1, source_target_pairs={{0,32},{32,64},{64,96},{96,0},{1,33},{33,65},{65,97},{97,1},{2,34}... | collective-permute-start | bytes 1032200 | tf_op jit(solution)/shard_map/ppermute | solution.py:272
  100.9 9.9 %collective-permute-start.21 = (bf16[3,32,1792]{2,1,0:T(8,128)(2,1)}, bf16[3,32,1792]{2,1,0:T(8,128)(2,1)S(1)}, u32[]{:S(2)}, u32[]{:S(2)}) collective-permute-start(bf16[3,32,1792]{2,1,0:T(8,128)(2,1)} %shard_map.123.refs_0_), channel_id=1, source_target_pairs={{0,96},{32,0},{64,32},{96,64},{1,97},{33,1},{65,33},{97,65},{2,98}... | collective-permute-start | bytes 1032200 | tf_op jit(solution)/shard_map/ppermute | solution.py:269
  108.5 16.7 %copy-start.9 = (bf16[3,32,1792]{2,1,0:T(8,128)(2,1)}, bf16[3,32,1792]{2,1,0:T(8,128)(2,1)S(1)}, u32[]{:S(2)}) copy-start(bf16[3,32,1792]{2,1,0:T(8,128)(2,1)S(1)} %collective-permute-done.23.refs_3_) | copy-start | bytes 1032196
  108.5 10.9 %collective-permute-start.25 = (bf16[3,32,1792]{2,1,0:T(8,128)(2,1)S(1)}, bf16[3,32,1792]{2,1,0:T(8,128)(2,1)S(1)}, u32[]{:S(2)}, u32[]{:S(2)}) collective-permute-start(bf16[3,32,1792]{2,1,0:T(8,128)(2,1)S(1)} %collective-permute-done.23.refs_3_), channel_id=1, source_target_pairs={{0,32},{32,64},{64,96},{96,0},{1,33},{33,65},{65,97},{97,1},{2,34}... | collective-permute-start | bytes 1032200 | tf_op jit(solution)/shard_map/ppermute | solution.py:272
  108.5 11.1 %collective-permute-start.24 = (bf16[3,32,1792]{2,1,0:T(8,128)(2,1)S(1)}, bf16[3,32,1792]{2,1,0:T(8,128)(2,1)S(1)}, u32[]{:S(2)}, u32[]{:S(2)}) collective-permute-start(bf16[3,32,1792]{2,1,0:T(8,128)(2,1)S(1)} %collective-permute-done.23.refs_3_), channel_id=1, source_target_pairs={{0,96},{32,0},{64,32},{96,64},{1,97},{33,1},{65,33},{97,65},{2,98}... | collective-permute-start | bytes 1032200 | tf_op jit(solution)/shard_map/ppermute | solution.py:269
  110.5 14.7 %copy-start.2 = (bf16[3,32,1792]{2,1,0:T(8,128)(2,1)}, bf16[3,32,1792]{2,1,0:T(8,128)(2,1)S(1)}, u32[]{:S(2)}) copy-start(bf16[3,32,1792]{2,1,0:T(8,128)(2,1)S(1)} %collective-permute-done.22.refs_2_) | copy-start | bytes 1032196
  110.5 12.0 %collective-permute-start.27 = (bf16[3,32,896]{2,1,0:T(8,128)(2,1)S(1)}, bf16[3,32,896]{2,1,0:T(8,128)(2,1)S(1)}, u32[]{:S(2)}, u32[]{:S(2)}) collective-permute-start(bf16[3,32,896]{2,1,0:T(8,128)(2,1)S(1)} %slice.95), channel_id=1, source_target_pairs={{0,32},{32,64},{64,96},{96,0},{1,33},{33,65},{65,97},{97,1},{2,34}... | collective-permute-start | bytes 516104 | tf_op jit(solution)/shard_map/ppermute | solution.py:272
  110.8 14.4 %copy-start.3 = (bf16[3,32,1792]{2,1,0:T(8,128)(2,1)}, bf16[3,32,1792]{2,1,0:T(8,128)(2,1)S(1)}, u32[]{:S(2)}) copy-start(bf16[3,32,1792]{2,1,0:T(8,128)(2,1)S(1)} %collective-permute-done.21.refs_1_) | copy-start | bytes 1032196
  110.8 11.8 %collective-permute-start.26 = (bf16[3,32,896]{2,1,0:T(8,128)(2,1)S(1)}, bf16[3,32,896]{2,1,0:T(8,128)(2,1)S(1)}, u32[]{:S(2)}, u32[]{:S(2)}) collective-permute-start(bf16[3,32,896]{2,1,0:T(8,128)(2,1)S(1)} %slice.94), channel_id=1, source_target_pairs={{0,96},{32,0},{64,32},{96,64},{1,97},{33,1},{65,33},{97,65},{2,98}... | collective-permute-start | bytes 516104 | tf_op jit(solution)/shard_map/ppermute | solution.py:269
  119.4 5.8 %copy-start.4 = (bf16[3,32,1792]{2,1,0:T(8,128)(2,1)}, bf16[3,32,1792]{2,1,0:T(8,128)(2,1)S(1)}, u32[]{:S(2)}) copy-start(bf16[3,32,1792]{2,1,0:T(8,128)(2,1)S(1)} %collective-permute-done.25.refs_5_) | copy-start | bytes 1032196
  119.4 5.5 %collective-permute-start.29 = (bf16[3,32,896]{2,1,0:T(8,128)(2,1)S(1)}, bf16[3,32,896]{2,1,0:T(8,128)(2,1)S(1)}, u32[]{:S(2)}, u32[]{:S(2)}) collective-permute-start(bf16[3,32,896]{2,1,0:T(8,128)(2,1)S(1)} %slice.97), channel_id=1, source_target_pairs={{0,32},{32,64},{64,96},{96,0},{1,33},{33,65},{65,97},{97,1},{2,34}... | collective-permute-start | bytes 516104 | tf_op jit(solution)/shard_map/ppermute | solution.py:272
  119.6 5.6 %copy-start.5 = (bf16[3,32,1792]{2,1,0:T(8,128)(2,1)}, bf16[3,32,1792]{2,1,0:T(8,128)(2,1)S(1)}, u32[]{:S(2)}) copy-start(bf16[3,32,1792]{2,1,0:T(8,128)(2,1)S(1)} %collective-permute-done.24.refs_4_) | copy-start | bytes 1032196
  119.6 5.6 %collective-permute-start.28 = (bf16[3,32,896]{2,1,0:T(8,128)(2,1)S(1)}, bf16[3,32,896]{2,1,0:T(8,128)(2,1)S(1)}, u32[]{:S(2)}, u32[]{:S(2)}) collective-permute-start(bf16[3,32,896]{2,1,0:T(8,128)(2,1)S(1)} %slice.96), channel_id=1, source_target_pairs={{0,96},{32,0},{64,32},{96,64},{1,97},{33,1},{65,33},{97,65},{2,98}... | collective-permute-start | bytes 516104 | tf_op jit(solution)/shard_map/ppermute | solution.py:269
  132.3 6.0 %collective-permute-start.30 = (bf16[256,1024]{1,0:T(8,128)(2,1)}, bf16[256,1024]{1,0:T(8,128)(2,1)S(1)}, u32[]{:S(2)}, u32[]{:S(2)}) collective-permute-start(bf16[256,1024]{1,0:T(8,128)(2,1)} %get-tuple-element.40), channel_id=1, source_target_pairs={{0,16},{16,0},{1,17},{17,1},{2,18},{18,2},{3,19},{19,3},{4,20},{20... | collective-permute-start | bytes 1572872 | tf_op jit(solution)/shard_map/ppermute | solution.py:187
  132.3 8.1 %copy-start = (bf16[3,256,1792]{2,1,0:T(8,128)(2,1)S(1)}, bf16[3,256,1792]{2,1,0:T(8,128)(2,1)}, u32[]{:S(2)}) copy-start(bf16[3,256,1792]{2,1,0:T(8,128)(2,1)} %get-tuple-element.41.acts) | copy-start | bytes 8257540
  140.4 39.6 %collective-permute-start.31 = (bf16[3,256,1792]{2,1,0:T(8,128)(2,1)S(1)}, bf16[3,256,1792]{2,1,0:T(8,128)(2,1)}, u32[]{:S(2)}, u32[]{:S(2)}) collective-permute-start(bf16[3,256,1792]{2,1,0:T(8,128)(2,1)S(1)} %copy-done), channel_id=1, source_target_pairs={{0,16},{16,0},{1,17},{17,1},{2,18},{18,2},{3,19},{19,3},{4,20},{20... | collective-permute-start | bytes 8257544 | tf_op jit(solution)/shard_map/ppermute | solution.py:187
  140.8 37.1 %all-to-all-start = ((bf16[16,32,1024]{2,1,0:T(8,128)(2,1)}), bf16[16,32,1024]{2,1,0:T(8,128)(2,1)}, u32[]{:S(2)}, u32[]{:S(2)}) async-start(bf16[16,32,1024]{2,1,0:T(8,128)(2,1)} %pad_maximum_fusion), calls=%async_computation | async-start | bytes 2097152 | tf_op jit(solution)/shard_map/all_to_all | solution.py:296
  (13 other events, 15.1 us)

commit v6 on v4

--- a/solution.py
+++ b/solution.py
@@ -16,15 +16,19 @@
 STEP = 256
 
 
-def local_call(kernel, outs, *args):
+def local_call(kernel, mib, outs, *args, place=None, scratch=(), far=0):
     whole = pl.BlockSpec(memory_space=pltpu.VMEM)
     single = not isinstance(outs, list)
+    first = [] if place is None else [place]
+    specs = [whole] * (len(args) - far) + [pl.BlockSpec(memory_space=pl.ANY)] * far
     return pl.pallas_call(
         kernel,
         out_shape=outs,
-        in_specs=[whole] * len(args),
+        in_specs=[pl.BlockSpec(memory_space=pltpu.SMEM)] * len(first) + specs,
         out_specs=whole if single else [whole] * len(outs),
-    )(*args)
+        scratch_shapes=scratch,
+        compiler_params=pltpu.CompilerParams(vmem_limit_bytes=mib << 20),
+    )(*first, *args)
 
 
 def nn(left, right):
@@ -47,43 +51,48 @@
     gate = effs[0]
     tokens, both = own.shape
     width, hid = gate.shape
-    share = tokens // place.shape[0]
-
-    def kernel(place, own, cross, gate, up, down, gate_x, up_x, down_x, *refs):
-        outs, (left, left_x) = refs[:-2], refs[-2:]
-
-        @pl.when(pl.program_id(0) == 0)
-        def _():
-            for r in range(len(outs)):
-                source = pl.ds(pl.multiple_of(place[r] * share, share), share)
-                left[pl.ds(r * share, share), :] = own[source, :]
-                left_x[pl.ds(r * share, share), :] = cross[source, :]
-
-        values = (
-            nn(left[:, :width], gate[...]) + nn(left_x[:, :width], gate_x[...]),
-            nn(left[:, :width], up[...]) + nn(left_x[:, :width], up_x[...]),
-            nt(left[:, width:], down[...]) + nt(left_x[:, width:], down_x[...]),
+    chips = place.shape[0]
+    share = tokens // chips
+
+    def kernel(place, own, cross, *refs):
+        sources, outs, (left, left_x), held, sems = (
+            refs[:6],
+            refs[6 : 6 + chips],
+            refs[6 + chips : 8 + chips],
+            refs[8 + chips : 14 + chips],
+            refs[14 + chips],
         )
-        for part, value in enumerate(values):
-            for r, out in enumerate(outs):
-                out[part] = value[r * share : (r + 1) * share].astype(out.dtype)
-
-    wide = pl.BlockSpec((width, STEP), lambda j: (0, j))
-    tall = pl.BlockSpec((STEP, width), lambda j: (j, 0))
-    fixed = pl.BlockSpec((tokens, both), lambda j: (0, 0))
-    shape = (3, share, hid)
-    return pl.pallas_call(
-        kernel,
-        out_shape=[
-            jax.ShapeDtypeStruct(shape, F32 if r == 0 else BF) for r in range(place.shape[0])
-        ],
-        grid=(hid // STEP,),
-        in_specs=[pl.BlockSpec(memory_space=pltpu.SMEM), fixed, fixed]
-        + [wide, wide, tall, wide, wide, tall],
-        out_specs=[pl.BlockSpec((3, share, STEP), lambda j: (0, 0, j))] * place.shape[0],
-        scratch_shapes=[pltpu.VMEM((tokens, both), BF)] * 2,
-        name="partial_sums",
-    )(place, own, cross, *effs, *effs_x)
+        copies = [
+            pltpu.make_async_copy(source, hold, sems.at[i])
+            for i, (source, hold) in enumerate(zip(sources, held))
+        ]
+        for copy in copies:
+            copy.start()
+        for r in range(chips):
+            source = pl.ds(pl.multiple_of(place[r] * share, share), share)
+            left[pl.ds(r * share, share), :] = own[source, :]
+            left_x[pl.ds(r * share, share), :] = cross[source, :]
+        for part in range(3):
+            copies[2 * part].wait()
+            copies[2 * part + 1].wait()
+            weight, weight_x = held[2 * part], held[2 * part + 1]
+            for j in range(hid // STEP):
+                here = pl.ds(j * STEP, STEP)
+                if part < 2:
+                    value = nn(left[:, :width], weight[:, here])
+                    value += nn(left_x[:, :width], weight_x[:, here])
+                else:
+                    value = nt(left[:, width:], weight[here, :])
+                    value += nt(left_x[:, width:], weight_x[here, :])
+                for r, out in enumerate(outs):
+                    out[part, :, here] = value[r * share : (r + 1) * share].astype(out.dtype)
+
+    outs = [jax.ShapeDtypeStruct((3, share, hid), F32 if r == 0 else BF) for r in range(chips)]
+    weights = [weight for two in zip(effs, effs_x) for weight in two]
+    scratch = [pltpu.VMEM((tokens, both), BF)] * 2
+    scratch += [pltpu.VMEM(weight.shape, BF) for weight in weights]
+    scratch += [pltpu.SemaphoreType.DMA((6,))]
+    return local_call(kernel, 24, outs, own, cross, *weights, place=place, scratch=scratch, far=6)
 
 
 def activation_kernel(*refs):
@@ -107,29 +116,50 @@
         out[2, :, cols] = (d_hidden * activated).astype(BF)
 
 
-def results(acts, gate, up, down, out):
+def results(acts, weights, out, held, sems, ahead=lambda: None):
+    copies = [
+        pltpu.make_async_copy(weight, hold, sems.at[i])
+        for i, (weight, hold) in enumerate(zip(weights, held))
+    ]
+    for copy in copies:
+        copy.start()
+    ahead()
+    down, gate, up = held
     width = gate.shape[0]
+    copies[0].wait()
     out[:, :width] = nn(acts[0], down[...]).astype(BF)
-    out[:, width:] = (nt(acts[1], gate[...]) + nt(acts[2], up[...])).astype(BF)
-
-
-def result_kernel(acts, gate, up, down, out):
-    results(acts, gate, up, down, out)
+    copies[1].wait()
+    value = nt(acts[1], gate[...])
+    copies[2].wait()
+    out[:, width:] = (value + nt(acts[2], up[...])).astype(BF)
+
+
+def result_kernel(acts, down, gate, up, out, *refs):
+    results(acts, (down, gate, up), out, refs[:3], refs[3])
 
 
 def arrange_kernel(place, *refs):
-    shares, (gate, up, down), (acts, out) = refs[:10], refs[10:13], refs[13:]
+    shares, weights, (acts, out), held, sems = (
+        refs[:10],
+        refs[10:13],
+        refs[13:15],
+        refs[15:18],
+        refs[18],
+    )
     share = shares[0].shape[1]
     hid = acts.shape[2]
     full = (0, 1, 3, 4, 5, 7)
-    for r, ref in zip(full, shares[:6]):
-        rows = pl.ds(pl.multiple_of(place[r] * share, share), share)
-        acts[:, rows, :] = ref[...]
-    for r, first, second in ((2, shares[6], shares[7]), (6, shares[8], shares[9])):
-        rows = pl.ds(pl.multiple_of(place[r] * share, share), share)
-        acts[:, rows, : hid // 2] = first[...]
-        acts[:, rows, hid // 2 :] = second[...]
-    results(acts, gate, up, down, out)
+
+    def ahead():
+        for r, ref in zip(full, shares[:6]):
+            rows = pl.ds(pl.multiple_of(place[r] * share, share), share)
+            acts[:, rows, :] = ref[...]
+        for r, first, second in ((2, shares[6], shares[7]), (6, shares[8], shares[9])):
+            rows = pl.ds(pl.multiple_of(place[r] * share, share), share)
+            acts[:, rows, : hid // 2] = first[...]
+            acts[:, rows, hid // 2 :] = second[...]
+
+    results(acts, weights, out, held, sems, ahead)
 
 
 def gradient_kernel(acts, acts_x, own, other, *refs):
@@ -175,7 +205,7 @@
     wide = [
         jnp.repeat(mask.astype(F32), BLK, axis=1) for mask in (gate_mask, up_mask, down_mask)
     ]
-    effs = local_call(prepare_kernel, shapes, *weights, *wide)
+    effs = local_call(prepare_kernel, 20, shapes, *weights, *wide)
     effs_x = [swap(eff) for eff in effs]
 
     own = lax.dynamic_slice_in_dim(gathered, core * half, half, 1).reshape(-1, 2 * width)
@@ -197,6 +227,7 @@
         got[r] = lax.ppermute(parts[r], PAIR, moves)
     mine = local_call(
         activation_kernel,
+        12,
         jax.ShapeDtypeStruct((3, parts[0].shape[1], hid), BF),
         *[got[r] for r in range(pairs)],
     )
@@ -216,16 +247,28 @@
 
     tokens_n = own.shape[0]
     result_shape = jax.ShapeDtypeStruct((tokens_n, 2 * width), BF)
-    acts, away = pl.pallas_call(
+    fetch = [pltpu.VMEM(shapes[i].shape, BF) for i in (2, 0, 1)] + [pltpu.SemaphoreType.DMA((3,))]
+    acts, away = local_call(
         arrange_kernel,
-        out_shape=[jax.ShapeDtypeStruct((3, tokens_n, hid), BF), result_shape],
-        in_specs=[pl.BlockSpec(memory_space=pltpu.SMEM)]
-        + [pl.BlockSpec(memory_space=pltpu.VMEM)] * 13,
-        out_specs=[pl.BlockSpec(memory_space=pltpu.VMEM)] * 2,
-        name="arrange",
-    )(place, mine, up_one, down_one, facing, facing_up, facing_down, *far, *effs_x)
+        16,
+        [jax.ShapeDtypeStruct((3, tokens_n, hid), BF), result_shape],
+        mine,
+        up_one,
+        down_one,
+        facing,
+        facing_up,
+        facing_down,
+        *far,
+        effs_x[2],
+        *effs_x[:2],
+        place=place,
+        scratch=fetch,
+        far=3,
+    )
     away = swap(away)
-    here = local_call(result_kernel, result_shape, acts, *effs)
+    here = local_call(
+        result_kernel, 12, result_shape, acts, effs[2], *effs[:2], scratch=fetch, far=3
+    )
     send = jnp.concatenate(
         [here.reshape(cols, half, 2 * width), away.reshape(cols, half, 2 * width)], axis=1
     )
@@ -240,7 +283,7 @@
     send, acts_late = lax.optimization_barrier((send, acts))
     acts_x = swap(acts_late)
     grad_gate, grad_up, grad_down = local_call(
-        gradient_kernel, shapes, acts_late, acts_x, own, other, *wide
+        gradient_kernel, 20, shapes, acts_late, acts_x, own, other, *wide
     )
     return (output, d_tokens, grad_gate, grad_up, grad_down)
 

time: 189 us -> 178 us (0.942)
  Pallas kernels: 37.9 us -> 24 us
  starting transfers between devices: 52.4 us -> 56.8 us
  waiting for transfers between devices: 83.8 us -> 80.8 us
    pallas_call x6, Pallas kernels: 37.9 us -> 24 us  [local_call(): pl.pallas_call(kernel, out_shape=outs, in_specs=[pl.BlockSpec(memory_spac...]
    ppermute x4, starting transfers between devices: 5.74 us -> 9.11 us  [from_up(): return lax.ppermute(array, 'y', [(i, (i - 1) % y_n) for i in range(y_n)])]
    unnamed x50 -> x24, local copies, waits for them, and re-layouts: 3.02 us -> 5.72 us
    ppermute x4, waiting for transfers between devices: 4.03 us -> 2.05 us  [from_up(): return lax.ppermute(array, 'y', [(i, (i - 1) % y_n) for i in range(y_n)])]
  transfers between devices with their start and end apart: 24 -> 24, of which waited for: 14 -> 12; matrix products, arithmetic and copies ran while one was open for 3% -> 2% of each run, Pallas kernels for 6% -> 3%
where the time goes in v6:
time: 178 us; the launch traced here: 175 us
  waiting for transfers between devices  80.8 us (45%)
  starting transfers between devices  56.8 us (32%)
  Pallas kernels  24 us (13%)
  local copies, waits for them, and re-layouts  8.44 us (5%)
  other arithmetic  3.9 us (2%)
    all_to_all x1, waiting for transfers between devices, layer(): arrived = lax.all_to_all(send, COL, 0, 0, tiled=True)  28.9 us
    ppermute x7, starting transfers between devices, layer(): got[r] = lax.ppermute(parts[r], PAIR, moves)  27.5 us
    pallas_call x6, Pallas kernels, local_call(): pl.pallas_call(kernel, out_shape=outs, in_specs=[pl.BlockSpec(memory_spac...  24 us
    all_to_all x1, waiting for transfers between devices, layer(): lax.all_to_all(jnp.broadcast_to(both, (cols,) + both.shape), COL, 0, 0, t...  21 us
    ppermute x7, waiting for transfers between devices, layer(): got[r] = lax.ppermute(parts[r], PAIR, moves)  14 us
    all_to_all x1, starting transfers between devices, layer(): lax.all_to_all(jnp.broadcast_to(both, (cols,) + both.shape), COL, 0, 0, t...  11.1 us
    ppermute x4, waiting for transfers between devices, from_down(): return lax.ppermute(array, 'y', [(i, (i + 1) % y_n) for i in range(y_n)])  9.76 us
    ppermute x4, starting transfers between devices, from_up(): return lax.ppermute(array, 'y', [(i, (i - 1) % y_n) for i in range(y_n)])  9.11 us
  transfers between devices with their start and end apart: 24, of which 12 were waited for; matrix products, arithmetic and copies ran while one was open for 2% of the time, Pallas kernels for 3%

profile of v6, /device:TPU:8, one launch (start us, length us, event | category | flops | bytes accessed | tf_op | source)
XLA Modules:
  0.0 174.9 jit_solution(14292668451881354203)
XLA Ops:
  0.7 0.8 pad_maximum_fusion.1
  1.5 1.1 broadcast_in_dim.12
  2.6 11.1 %all-to-all-start = ((bf16[16,32,1024]{2,1,0:T(8,128)(2,1)}), bf16[16,32,1024]{2,1,0:T(8,128)(2,1)}, u32[]{:S(2)}, u32[]{:S(2)}) async-start(bf16[16,32,1024]{2,1,0:T(8,128)(2,1)} %broadcast_in_dim.12), calls=%async_computation | async-start | bytes 2097152 | tf_op jit(solution)/shard_map/all_to_all | solution.py:200
  13.7 0.1 copy.14
  14.1 1.5 copy-done.4
  15.6 1.5 copy-done.5
  17.1 1.5 copy-done.6
  18.6 2.2 %shard_map.119 = (bf16[512,1792]{1,0:T(8,128)(2,1)S(1)}, bf16[512,1792]{1,0:T(8,128)(2,1)}, bf16[1792,512]{1,0:T(8,128)(2,1)}) custom-call(bf16[512,1792]{1,0:T(8,128)(2,1)S(1)} %copy-done.4, bf16[512,1792]{1,0:T(8,128)(2,1)S(1)} %copy-done.5, bf16[1792,512]{1,0:T(8,128)(2,1)S(1)} %copy-done.6, f32[4,1792]{1,0:T(4,128)S(1)} %get-tuple-element.46.refs_3_.refs_0_, ...), custom_call_target="tpu_custom_call" | custom-call | tf_op jit(solution)/shard_map/pallas_call | solution.py:24
  20.8 0.5 collective-permute-start.2
  21.3 21.0 %all-to-all-done = bf16[16,32,1024]{2,1,0:T(8,128)(2,1)} async-done(((bf16[16,32,1024]{2,1,0:T(8,128)(2,1)}), bf16[16,32,1024]{2,1,0:T(8,128)(2,1)}, u32[]{:S(2)}, u32[]{:S(2)}) %all-to-all-start) | async-done | bytes 1048608 | tf_op jit(solution)/shard_map/all_to_all | solution.py:200
  42.3 1.3 constant_dynamic-slice_fusion
  43.6 0.1 collective-permute-start
  43.9 1.9 %collective-permute-done.cross = bf16[256,1024]{1,0:T(8,128)(2,1)} collective-permute-done((bf16[256,1024]{1,0:T(8,128)(2,1)S(1)}, bf16[256,1024]{1,0:T(8,128)(2,1)}, u32[]{:S(2)}, u32[]{:S(2)}) %collective-permute-start) | collective-permute-done | bytes 524320 | tf_op jit(solution)/shard_map/ppermute | solution.py:186
  45.8 6.4 %shard_map.120 = (f32[3,32,1792]{2,1,0:T(8,128)S(1)}, bf16[3,32,1792]{2,1,0:T(8,128)(2,1)S(1)}, bf16[3,32,1792]{2,1,0:T(8,128)(2,1)S(1)}, bf16[3,32,1792]{2,1,0:...) custom-call(s32[8]{0:T(128)S(1)} %stack.35.place, ...), custom_call_target="tpu_custom_call" | custom-call | tf_op jit(solution)/shard_map/pallas_call | solution.py:24
  52.2 1.7 collective-permute-start.4
  53.8 0.9 collective-permute-start.5
  54.8 2.4 %collective-permute-start.6 = (bf16[3,32,1792]{2,1,0:T(8,128)(2,1)S(1)}, bf16[3,32,1792]{2,1,0:T(8,128)(2,1)S(1)}, u32[]{:S(2)}, u32[]{:S(2)}) collective-permute-start(bf16[3,32,1792]{2,1,0:T(8,128)(2,1)S(1)} %get-tuple-element.28), channel_id=1, source_target_pairs={{0,96},{32,0},{64,32},{96,64},{128,224},{160,128},{192,160},{224,1... | collective-permute-start | bytes 1032200 | tf_op jit(solution)/shard_map/ppermute | solution.py:227
  57.2 0.6 collective-permute-start.7
  57.8 0.5 collective-permute-start.8
  58.3 4.9 %collective-permute-done.4.refs_1_ = bf16[3,32,1792]{2,1,0:T(8,128)(2,1)S(1)} collective-permute-done((bf16[3,32,1792]{2,1,0:T(8,128)(2,1)S(1)}, bf16[3,32,1792]{2,1,0:T(8,128)(2,1)S(1)}, u32[]{:S(2)}, u32[]{:S(2)}) %collective-permute-start.4) | collective-permute-done | bytes 344096 | tf_op jit(solution)/shard_map/ppermute | solution.py:227
  63.2 2.3 %collective-permute-start.9 = (bf16[3,32,1792]{2,1,0:T(8,128)(2,1)S(1)}, bf16[3,32,1792]{2,1,0:T(8,128)(2,1)S(1)}, u32[]{:S(2)}, u32[]{:S(2)}) collective-permute-start(bf16[3,32,1792]{2,1,0:T(8,128)(2,1)S(1)} %get-tuple-element.31), channel_id=1, source_target_pairs={{0,192},{32,224},{64,128},{96,160},{128,64},{160,96},{192,0},{224,... | collective-permute-start | bytes 1032200 | tf_op jit(solution)/shard_map/ppermute | solution.py:227
  65.5 0.8 collective-permute-done.5.refs_2_
  66.3 19.1 %collective-permute-start.10 = (bf16[3,32,1792]{2,1,0:T(8,128)(2,1)S(1)}, bf16[3,32,1792]{2,1,0:T(8,128)(2,1)S(1)}, u32[]{:S(2)}, u32[]{:S(2)}) collective-permute-start(bf16[3,32,1792]{2,1,0:T(8,128)(2,1)S(1)} %get-tuple-element.32), channel_id=1, source_target_pairs={{0,224},{32,128},{64,160},{96,192},{128,96},{160,0},{192,32},{224,... | collective-permute-start | bytes 1032200 | tf_op jit(solution)/shard_map/ppermute | solution.py:227
  85.3 8.3 %collective-permute-done.10.refs_7_ = bf16[3,32,1792]{2,1,0:T(8,128)(2,1)S(1)} collective-permute-done((bf16[3,32,1792]{2,1,0:T(8,128)(2,1)S(1)}, bf16[3,32,1792]{2,1,0:T(8,128)(2,1)S(1)}, u32[]{:S(2)}, u32[]{:S(2)}) %collective-permute-start.10) | collective-permute-done | bytes 344096 | tf_op jit(solution)/shard_map/ppermute | solution.py:227
  93.7 0.4 shard_map.121.refs_0_
  94.1 2.4 %collective-permute-start.13 = (bf16[3,32,1792]{2,1,0:T(8,128)(2,1)S(1)}, bf16[3,32,1792]{2,1,0:T(8,128)(2,1)S(1)}, u32[]{:S(2)}, u32[]{:S(2)}) collective-permute-start(bf16[3,32,1792]{2,1,0:T(8,128)(2,1)S(1)} %shard_map.121.refs_0_), channel_id=1, source_target_pairs={{0,128},{128,0},{1,129},{129,1},{2,130},{130,2},{3,131},{131,3},{4... | collective-permute-start | bytes 1032200 | tf_op jit(solution)/shard_map/ppermute | solution.py:243
  96.5 2.0 %collective-permute-start.11 = (bf16[3,32,1792]{2,1,0:T(8,128)(2,1)S(1)}, bf16[3,32,1792]{2,1,0:T(8,128)(2,1)S(1)}, u32[]{:S(2)}, u32[]{:S(2)}) collective-permute-start(bf16[3,32,1792]{2,1,0:T(8,128)(2,1)S(1)} %shard_map.121.refs_0_), channel_id=1, source_target_pairs={{0,96},{32,0},{64,32},{96,64},{1,97},{33,1},{65,33},{97,65},{2,98}... | collective-permute-start | bytes 1032200 | tf_op jit(solution)/shard_map/ppermute | solution.py:236
  98.5 3.2 %collective-permute-done.13.refs_3_ = bf16[3,32,1792]{2,1,0:T(8,128)(2,1)S(1)} collective-permute-done((bf16[3,32,1792]{2,1,0:T(8,128)(2,1)S(1)}, bf16[3,32,1792]{2,1,0:T(8,128)(2,1)S(1)}, u32[]{:S(2)}, u32[]{:S(2)}) %collective-permute-start.13) | collective-permute-done | bytes 344096 | tf_op jit(solution)/shard_map/ppermute | solution.py:243
  101.7 0.1 collective-permute-start.15
  101.8 2.4 %collective-permute-start.14 = (bf16[3,32,1792]{2,1,0:T(8,128)(2,1)S(1)}, bf16[3,32,1792]{2,1,0:T(8,128)(2,1)S(1)}, u32[]{:S(2)}, u32[]{:S(2)}) collective-permute-start(bf16[3,32,1792]{2,1,0:T(8,128)(2,1)S(1)} %collective-permute-done.13.refs_3_), channel_id=1, source_target_pairs={{0,96},{32,0},{64,32},{96,64},{1,97},{33,1},{65,33},{97,65},{2,98}... | collective-permute-start | bytes 1032200 | tf_op jit(solution)/shard_map/ppermute | solution.py:236
  104.2 3.2 %collective-permute-done.12.refs_2_ = bf16[3,32,1792]{2,1,0:T(8,128)(2,1)S(1)} collective-permute-done((bf16[3,32,1792]{2,1,0:T(8,128)(2,1)S(1)}, bf16[3,32,1792]{2,1,0:T(8,128)(2,1)S(1)}, u32[]{:S(2)}, u32[]{:S(2)}) %collective-permute-start.12) | collective-permute-done | bytes 344096 | tf_op jit(solution)/shard_map/ppermute | solution.py:239
  107.4 0.1 collective-permute-start.17
  107.5 1.8 %collective-permute-done.11.refs_1_ = bf16[3,32,1792]{2,1,0:T(8,128)(2,1)S(1)} collective-permute-done((bf16[3,32,1792]{2,1,0:T(8,128)(2,1)S(1)}, bf16[3,32,1792]{2,1,0:T(8,128)(2,1)S(1)}, u32[]{:S(2)}, u32[]{:S(2)}) %collective-permute-start.11) | collective-permute-done | bytes 344096 | tf_op jit(solution)/shard_map/ppermute | solution.py:236
  109.4 1.9 %collective-permute-start.16 = (bf16[3,32,896]{2,1,0:T(8,128)(2,1)S(1)}, bf16[3,32,896]{2,1,0:T(8,128)(2,1)S(1)}, u32[]{:S(2)}, u32[]{:S(2)}) collective-permute-start(bf16[3,32,896]{2,1,0:T(8,128)(2,1)S(1)} %slice.32), channel_id=1, source_target_pairs={{0,96},{32,0},{64,32},{96,64},{1,97},{33,1},{65,33},{97,65},{2,98}... | collective-permute-start | bytes 516104 | tf_op jit(solution)/shard_map/ppermute | solution.py:236
  111.2 3.3 %collective-permute-done.15.refs_5_ = bf16[3,32,1792]{2,1,0:T(8,128)(2,1)S(1)} collective-permute-done((bf16[3,32,1792]{2,1,0:T(8,128)(2,1)S(1)}, bf16[3,32,1792]{2,1,0:T(8,128)(2,1)S(1)}, u32[]{:S(2)}, u32[]{:S(2)}) %collective-permute-start.15) | collective-permute-done | bytes 344096 | tf_op jit(solution)/shard_map/ppermute | solution.py:239
  114.7 0.2 collective-permute-done.14.refs_4_
  114.9 2.8 %collective-permute-start.18 = (bf16[3,32,896]{2,1,0:T(8,128)(2,1)S(1)}, bf16[3,32,896]{2,1,0:T(8,128)(2,1)S(1)}, u32[]{:S(2)}, u32[]{:S(2)}) collective-permute-start(bf16[3,32,896]{2,1,0:T(8,128)(2,1)S(1)} %slice.34), channel_id=1, source_target_pairs={{0,96},{32,0},{64,32},{96,64},{1,97},{33,1},{65,33},{97,65},{2,98}... | collective-permute-start | bytes 516104 | tf_op jit(solution)/shard_map/ppermute | solution.py:236
  117.7 3.2 %collective-permute-done.19.refs_9_ = bf16[3,32,896]{2,1,0:T(8,128)(2,1)S(1)} collective-permute-done((bf16[3,32,896]{2,1,0:T(8,128)(2,1)S(1)}, bf16[3,32,896]{2,1,0:T(8,128)(2,1)S(1)}, u32[]{:S(2)}, u32[]{:S(2)}) %collective-permute-start.19) | collective-permute-done | bytes 172064 | tf_op jit(solution)/shard_map/ppermute | solution.py:239
  121.0 4.3 %shard_map.122 = (bf16[3,256,1792]{2,1,0:T(8,128)(2,1)S(1)}, bf16[256,1024]{1,0:T(8,128)(2,1)S(1)}) custom-call(s32[8]{0:T(128)S(1)} %stack.35.place, bf16[3,32,1792]{2,1,0:T(8,128)(2,1)S(1)} %shard_map.121.refs_0_, bf16[3,32,1792]{2,1,0:T(8,128)(2,1)S(1)} %collective-permute-done.11.refs_1_, bf16[3,32,1792]{2,1,0:T(8,128)(2,1)S(1)} %collective-permute-done.12.refs_2_, ...), custom_call_target="tpu_custom_call" | custom-call | tf_op jit(solution)/shard_map/pallas_call | solution.py:24
  125.4 3.5 %shard_map.123 = bf16[256,1024]{1,0:T(8,128)(2,1)S(1)} custom-call(bf16[3,256,1792]{2,1,0:T(8,128)(2,1)S(1)} %get-tuple-element.35.acts, bf16[1792,512]{1,0:T(8,128)(2,1)} %get-tuple-element.24.refs_4_.down, bf16[512,1792]{1,0:T(8,128)(2,1)S(1)} %copy-done.1, bf16[512,1792]{1,0:T(8,128)(2,1)} %get-tuple-element.23.refs_2_.up), custom_call_target="tpu_custom_call" | custom-call | tf_op jit(solution)/shard_map/pallas_call | solution.py:24
  128.9 1.1 pad_maximum_fusion
  130.0 0.5 collective-permute-start.21
  130.5 5.3 %all-to-all-start.1 = ((bf16[16,32,1024]{2,1,0:T(8,128)(2,1)}), bf16[16,32,1024]{2,1,0:T(8,128)(2,1)}, u32[]{:S(2)}, u32[]{:S(2)}) async-start(bf16[16,32,1024]{2,1,0:T(8,128)(2,1)} %pad_maximum_fusion), calls=%async_computation.1 | async-start | bytes 2097152 | tf_op jit(solution)/shard_map/all_to_all | solution.py:275
  135.8 28.9 %all-to-all-done.1 = bf16[16,32,1024]{2,1,0:T(8,128)(2,1)} async-done(((bf16[16,32,1024]{2,1,0:T(8,128)(2,1)}), bf16[16,32,1024]{2,1,0:T(8,128)(2,1)}, u32[]{:S(2)}, u32[]{:S(2)}) %all-to-all-start.1) | async-done | bytes 1048608 | tf_op jit(solution)/shard_map/all_to_all | solution.py:275
  164.7 1.4 convert_reduce_fusion
  166.1 0.6 pad_maximum_fusion.2
  166.7 1.0 copy-done.3
  167.7 7.2 %shard_map.124 = (bf16[512,1792]{1,0:T(8,128)(2,1)}, bf16[512,1792]{1,0:T(8,128)(2,1)}, bf16[1792,512]{1,0:T(8,128)(2,1)}) custom-call(bf16[3,256,1792]{2,1,0:T(8,128)(2,1)S(1)} %get-tuple-element.35.acts, bf16[3,256,1792]{2,1,0:T(8,128)(2,1)} %collective-permute-done.21.acts_x, bf16[256,1024]{1,0:T(8,128)(2,1)S(1)} %bitcast.24, ...), custom_call_target="tpu_custom_call" | custom-call | tf_op jit(solution)/shard_map/pallas_call | solution.py:24
  (48 shorter events, 0.7 us)
Async XLA Ops:
  0.6 13.0 %copy-start.7 = (s32[4,14]{1,0:T(4,128)S(1)}, s32[4,14]{1,0:T(4,128)}, u32[]{:S(2)}) copy-start(s32[4,14]{1,0:T(4,128)} %param.13) | copy-start | bytes 676
  0.6 13.0 %copy-start.8 = (s32[4,14]{1,0:T(4,128)S(1)}, s32[4,14]{1,0:T(4,128)}, u32[]{:S(2)}) copy-start(s32[4,14]{1,0:T(4,128)} %param.14) | copy-start | bytes 676
  0.7 13.0 %copy-start.9 = (s32[14,4]{0,1:T(4,128)S(1)}, s32[14,4]{0,1:T(4,128)}, u32[]{:S(2)}) copy-start(s32[14,4]{0,1:T(4,128)} %param.15) | copy-start | bytes 676
  2.6 39.8 %all-to-all-start = ((bf16[16,32,1024]{2,1,0:T(8,128)(2,1)}), bf16[16,32,1024]{2,1,0:T(8,128)(2,1)}, u32[]{:S(2)}, u32[]{:S(2)}) async-start(bf16[16,32,1024]{2,1,0:T(8,128)(2,1)} %broadcast_in_dim.12), calls=%async_computation | async-start | bytes 2097152 | tf_op jit(solution)/shard_map/all_to_all | solution.py:200
  14.1 1.5 copy-start.4
  15.6 1.5 copy-start.5
  17.1 1.5 copy-start.6
  20.8 31.3 %copy-start = (bf16[512,1792]{1,0:T(8,128)(2,1)}, bf16[512,1792]{1,0:T(8,128)(2,1)S(1)}, u32[]{:S(2)}) copy-start(bf16[512,1792]{1,0:T(8,128)(2,1)S(1)} %get-tuple-element.22.refs_0_.gate) | copy-start | bytes 5505028
  20.8 23.0 %collective-permute-start.1 = (bf16[512,1792]{1,0:T(8,128)(2,1)S(1)}, bf16[512,1792]{1,0:T(8,128)(2,1)}, u32[]{:S(2)}, u32[]{:S(2)}) collective-permute-start(bf16[512,1792]{1,0:T(8,128)(2,1)S(1)} %get-tuple-element.22.refs_0_.gate), channel_id=1, source_target_pairs={{0,16},{16,0},{1,17},{17,1},{2,18},{18,2},{3,19},{19,3},{4,20},{20... | collective-permute-start | bytes 5505032 | tf_op jit(solution)/shard_map/ppermute | solution.py:186
  20.8 23.0 %collective-permute-start.2 = (bf16[512,1792]{1,0:T(8,128)(2,1)}, bf16[512,1792]{1,0:T(8,128)(2,1)}, u32[]{:S(2)}, u32[]{:S(2)}) collective-permute-start(bf16[512,1792]{1,0:T(8,128)(2,1)} %get-tuple-element.23.refs_2_.up), channel_id=1, source_target_pairs={{0,16},{16,0},{1,17},{17,1},{2,18},{18,2},{3,19},{19,3},{4,20},{20... | collective-permute-start | bytes 5505032 | tf_op jit(solution)/shard_map/ppermute | solution.py:186
  21.3 22.5 %collective-permute-start.3 = (bf16[1792,512]{1,0:T(8,128)(2,1)}, bf16[1792,512]{1,0:T(8,128)(2,1)}, u32[]{:S(2)}, u32[]{:S(2)}) collective-permute-start(bf16[1792,512]{1,0:T(8,128)(2,1)} %get-tuple-element.24.refs_4_.down), channel_id=1, source_target_pairs={{0,16},{16,0},{1,17},{17,1},{2,18},{18,2},{3,19},{19,3},{4,20},{20... | collective-permute-start | bytes 5505032 | tf_op jit(solution)/shard_map/ppermute | solution.py:186
  43.6 8.5 %copy-start.2 = (bf16[16,16,1024]{2,1,0:T(8,128)(2,1)}, bf16[16,16,1024]{2,1,0:T(8,128)(2,1)S(1)}, u32[]{:S(2)}) copy-start(bf16[16,16,1024]{2,1,0:T(8,128)(2,1)S(1)} %get-tuple-element.39) | copy-start | bytes 1572868
  43.6 2.1 %collective-permute-start = (bf16[256,1024]{1,0:T(8,128)(2,1)S(1)}, bf16[256,1024]{1,0:T(8,128)(2,1)}, u32[]{:S(2)}, u32[]{:S(2)}) collective-permute-start(bf16[256,1024]{1,0:T(8,128)(2,1)S(1)} %bitcast.25), channel_id=1, source_target_pairs={{0,16},{16,0},{1,17},{17,1},{2,18},{18,2},{3,19},{19,3},{4,20},{20... | collective-permute-start | bytes 1572872 | tf_op jit(solution)/shard_map/ppermute | solution.py:186
  52.2 11.0 %collective-permute-start.4 = (bf16[3,32,1792]{2,1,0:T(8,128)(2,1)S(1)}, bf16[3,32,1792]{2,1,0:T(8,128)(2,1)S(1)}, u32[]{:S(2)}, u32[]{:S(2)}) collective-permute-start(bf16[3,32,1792]{2,1,0:T(8,128)(2,1)S(1)} %get-tuple-element.26), channel_id=1, source_target_pairs={{0,32},{32,64},{64,96},{96,0},{128,160},{160,192},{192,224},{224,1... | collective-permute-start | bytes 1032200 | tf_op jit(solution)/shard_map/ppermute | solution.py:227
  53.8 12.4 %collective-permute-start.5 = (bf16[3,32,1792]{2,1,0:T(8,128)(2,1)S(1)}, bf16[3,32,1792]{2,1,0:T(8,128)(2,1)S(1)}, u32[]{:S(2)}, u32[]{:S(2)}) collective-permute-start(bf16[3,32,1792]{2,1,0:T(8,128)(2,1)S(1)} %get-tuple-element.27), channel_id=1, source_target_pairs={{0,64},{32,96},{64,0},{96,32},{128,192},{160,224},{192,128},{224,1... | collective-permute-start | bytes 1032200 | tf_op jit(solution)/shard_map/ppermute | solution.py:227
  54.8 30.6 %collective-permute-start.6 = (bf16[3,32,1792]{2,1,0:T(8,128)(2,1)S(1)}, bf16[3,32,1792]{2,1,0:T(8,128)(2,1)S(1)}, u32[]{:S(2)}, u32[]{:S(2)}) collective-permute-start(bf16[3,32,1792]{2,1,0:T(8,128)(2,1)S(1)} %get-tuple-element.28), channel_id=1, source_target_pairs={{0,96},{32,0},{64,32},{96,64},{128,224},{160,128},{192,160},{224,1... | collective-permute-start | bytes 1032200 | tf_op jit(solution)/shard_map/ppermute | solution.py:227
  57.2 28.2 %collective-permute-start.7 = (bf16[3,32,1792]{2,1,0:T(8,128)(2,1)S(1)}, bf16[3,32,1792]{2,1,0:T(8,128)(2,1)S(1)}, u32[]{:S(2)}, u32[]{:S(2)}) collective-permute-start(bf16[3,32,1792]{2,1,0:T(8,128)(2,1)S(1)} %get-tuple-element.29), channel_id=1, source_target_pairs={{0,128},{32,160},{64,192},{96,224},{128,0},{160,32},{192,64},{224,... | collective-permute-start | bytes 1032200 | tf_op jit(solution)/shard_map/ppermute | solution.py:227
  57.8 27.6 %collective-permute-start.8 = (bf16[3,32,1792]{2,1,0:T(8,128)(2,1)S(1)}, bf16[3,32,1792]{2,1,0:T(8,128)(2,1)S(1)}, u32[]{:S(2)}, u32[]{:S(2)}) collective-permute-start(bf16[3,32,1792]{2,1,0:T(8,128)(2,1)S(1)} %get-tuple-element.30), channel_id=1, source_target_pairs={{0,160},{32,192},{64,224},{96,128},{128,32},{160,64},{192,96},{224... | collective-permute-start | bytes 1032200 | tf_op jit(solution)/shard_map/ppermute | solution.py:227
  63.2 22.2 %collective-permute-start.9 = (bf16[3,32,1792]{2,1,0:T(8,128)(2,1)S(1)}, bf16[3,32,1792]{2,1,0:T(8,128)(2,1)S(1)}, u32[]{:S(2)}, u32[]{:S(2)}) collective-permute-start(bf16[3,32,1792]{2,1,0:T(8,128)(2,1)S(1)} %get-tuple-element.31), channel_id=1, source_target_pairs={{0,192},{32,224},{64,128},{96,160},{128,64},{160,96},{192,0},{224,... | collective-permute-start | bytes 1032200 | tf_op jit(solution)/shard_map/ppermute | solution.py:227
  66.3 27.4 %collective-permute-start.10 = (bf16[3,32,1792]{2,1,0:T(8,128)(2,1)S(1)}, bf16[3,32,1792]{2,1,0:T(8,128)(2,1)S(1)}, u32[]{:S(2)}, u32[]{:S(2)}) collective-permute-start(bf16[3,32,1792]{2,1,0:T(8,128)(2,1)S(1)} %get-tuple-element.32), channel_id=1, source_target_pairs={{0,224},{32,128},{64,160},{96,192},{128,96},{160,0},{192,32},{224,... | collective-permute-start | bytes 1032200 | tf_op jit(solution)/shard_map/ppermute | solution.py:227
  94.1 7.6 %collective-permute-start.13 = (bf16[3,32,1792]{2,1,0:T(8,128)(2,1)S(1)}, bf16[3,32,1792]{2,1,0:T(8,128)(2,1)S(1)}, u32[]{:S(2)}, u32[]{:S(2)}) collective-permute-start(bf16[3,32,1792]{2,1,0:T(8,128)(2,1)S(1)} %shard_map.121.refs_0_), channel_id=1, source_target_pairs={{0,128},{128,0},{1,129},{129,1},{2,130},{130,2},{3,131},{131,3},{4... | collective-permute-start | bytes 1032200 | tf_op jit(solution)/shard_map/ppermute | solution.py:243
  96.5 10.9 %collective-permute-start.12 = (bf16[3,32,1792]{2,1,0:T(8,128)(2,1)S(1)}, bf16[3,32,1792]{2,1,0:T(8,128)(2,1)S(1)}, u32[]{:S(2)}, u32[]{:S(2)}) collective-permute-start(bf16[3,32,1792]{2,1,0:T(8,128)(2,1)S(1)} %shard_map.121.refs_0_), channel_id=1, source_target_pairs={{0,32},{32,64},{64,96},{96,0},{1,33},{33,65},{65,97},{97,1},{2,34}... | collective-permute-start | bytes 1032200 | tf_op jit(solution)/shard_map/ppermute | solution.py:239
  96.5 12.9 %collective-permute-start.11 = (bf16[3,32,1792]{2,1,0:T(8,128)(2,1)S(1)}, bf16[3,32,1792]{2,1,0:T(8,128)(2,1)S(1)}, u32[]{:S(2)}, u32[]{:S(2)}) collective-permute-start(bf16[3,32,1792]{2,1,0:T(8,128)(2,1)S(1)} %shard_map.121.refs_0_), channel_id=1, source_target_pairs={{0,96},{32,0},{64,32},{96,64},{1,97},{33,1},{65,33},{97,65},{2,98}... | collective-permute-start | bytes 1032200 | tf_op jit(solution)/shard_map/ppermute | solution.py:236
  101.7 12.8 %collective-permute-start.15 = (bf16[3,32,1792]{2,1,0:T(8,128)(2,1)S(1)}, bf16[3,32,1792]{2,1,0:T(8,128)(2,1)S(1)}, u32[]{:S(2)}, u32[]{:S(2)}) collective-permute-start(bf16[3,32,1792]{2,1,0:T(8,128)(2,1)S(1)} %collective-permute-done.13.refs_3_), channel_id=1, source_target_pairs={{0,32},{32,64},{64,96},{96,0},{1,33},{33,65},{65,97},{97,1},{2,34}... | collective-permute-start | bytes 1032200 | tf_op jit(solution)/shard_map/ppermute | solution.py:239
  101.8 13.1 %collective-permute-start.14 = (bf16[3,32,1792]{2,1,0:T(8,128)(2,1)S(1)}, bf16[3,32,1792]{2,1,0:T(8,128)(2,1)S(1)}, u32[]{:S(2)}, u32[]{:S(2)}) collective-permute-start(bf16[3,32,1792]{2,1,0:T(8,128)(2,1)S(1)} %collective-permute-done.13.refs_3_), channel_id=1, source_target_pairs={{0,96},{32,0},{64,32},{96,64},{1,97},{33,1},{65,33},{97,65},{2,98}... | collective-permute-start | bytes 1032200 | tf_op jit(solution)/shard_map/ppermute | solution.py:236
  107.4 10.3 %collective-permute-start.17 = (bf16[3,32,896]{2,1,0:T(8,128)(2,1)S(1)}, bf16[3,32,896]{2,1,0:T(8,128)(2,1)S(1)}, u32[]{:S(2)}, u32[]{:S(2)}) collective-permute-start(bf16[3,32,896]{2,1,0:T(8,128)(2,1)S(1)} %slice.33), channel_id=1, source_target_pairs={{0,32},{32,64},{64,96},{96,0},{1,33},{33,65},{65,97},{97,1},{2,34}... | collective-permute-start | bytes 516104 | tf_op jit(solution)/shard_map/ppermute | solution.py:239
  109.4 8.4 %collective-permute-start.16 = (bf16[3,32,896]{2,1,0:T(8,128)(2,1)S(1)}, bf16[3,32,896]{2,1,0:T(8,128)(2,1)S(1)}, u32[]{:S(2)}, u32[]{:S(2)}) collective-permute-start(bf16[3,32,896]{2,1,0:T(8,128)(2,1)S(1)} %slice.32), channel_id=1, source_target_pairs={{0,96},{32,0},{64,32},{96,64},{1,97},{33,1},{65,33},{97,65},{2,98}... | collective-permute-start | bytes 516104 | tf_op jit(solution)/shard_map/ppermute | solution.py:236
  114.6 6.4 %collective-permute-start.19 = (bf16[3,32,896]{2,1,0:T(8,128)(2,1)S(1)}, bf16[3,32,896]{2,1,0:T(8,128)(2,1)S(1)}, u32[]{:S(2)}, u32[]{:S(2)}) collective-permute-start(bf16[3,32,896]{2,1,0:T(8,128)(2,1)S(1)} %slice.35), channel_id=1, source_target_pairs={{0,32},{32,64},{64,96},{96,0},{1,33},{33,65},{65,97},{97,1},{2,34}... | collective-permute-start | bytes 516104 | tf_op jit(solution)/shard_map/ppermute | solution.py:239
  114.9 10.5 %copy-start.1 = (bf16[512,1792]{1,0:T(8,128)(2,1)S(1)}, bf16[512,1792]{1,0:T(8,128)(2,1)}, u32[]{:S(2)}) copy-start(bf16[512,1792]{1,0:T(8,128)(2,1)} %copy-done) | copy-start | bytes 5505028
  114.9 6.1 %collective-permute-start.18 = (bf16[3,32,896]{2,1,0:T(8,128)(2,1)S(1)}, bf16[3,32,896]{2,1,0:T(8,128)(2,1)S(1)}, u32[]{:S(2)}, u32[]{:S(2)}) collective-permute-start(bf16[3,32,896]{2,1,0:T(8,128)(2,1)S(1)} %slice.34), channel_id=1, source_target_pairs={{0,96},{32,0},{64,32},{96,64},{1,97},{33,1},{65,33},{97,65},{2,98}... | collective-permute-start | bytes 516104 | tf_op jit(solution)/shard_map/ppermute | solution.py:236
  125.3 3.6 %collective-permute-start.20 = (bf16[256,1024]{1,0:T(8,128)(2,1)S(1)}, bf16[256,1024]{1,0:T(8,128)(2,1)S(1)}, u32[]{:S(2)}, u32[]{:S(2)}) collective-permute-start(bf16[256,1024]{1,0:T(8,128)(2,1)S(1)} %get-tuple-element.34), channel_id=1, source_target_pairs={{0,16},{16,0},{1,17},{17,1},{2,18},{18,2},{3,19},{19,3},{4,20},{20... | collective-permute-start | bytes 1572872 | tf_op jit(solution)/shard_map/ppermute | solution.py:186
  130.0 36.7 %collective-permute-start.21 = (bf16[3,256,1792]{2,1,0:T(8,128)(2,1)S(1)}, bf16[3,256,1792]{2,1,0:T(8,128)(2,1)}, u32[]{:S(2)}, u32[]{:S(2)}) collective-permute-start(bf16[3,256,1792]{2,1,0:T(8,128)(2,1)S(1)} %get-tuple-element.35.acts), channel_id=1, source_target_pairs={{0,16},{16,0},{1,17},{17,1},{2,18},{18,2},{3,19},{19,3},{4,20},{20... | collective-permute-start | bytes 8257544 | tf_op jit(solution)/shard_map/ppermute | solution.py:186
  130.5 34.2 %all-to-all-start.1 = ((bf16[16,32,1024]{2,1,0:T(8,128)(2,1)}), bf16[16,32,1024]{2,1,0:T(8,128)(2,1)}, u32[]{:S(2)}, u32[]{:S(2)}) async-start(bf16[16,32,1024]{2,1,0:T(8,128)(2,1)} %pad_maximum_fusion), calls=%async_computation.1 | async-start | bytes 2097152 | tf_op jit(solution)/shard_map/all_to_all | solution.py:275
  166.7 1.0 copy-start.3

commit v7 on v6

v7 whole, which is shorter than its diff:
```python
import jax
import jax.numpy as jnp
from jax import lax
from jax.experimental import pallas as pl
from jax.experimental.pallas import tpu as pltpu
from jax.sharding import Mesh
from jax.sharding import PartitionSpec as P


ROW = ("x_lo", "y", "core")
COL = ("x_hi", "z")
PAIR = ("x_lo", "y")
BF = jnp.bfloat16
F32 = jnp.float32
BLK = 128
STEP = 256


def local_call(kernel, mib, outs, *args, place=None, scratch=(), far=0):
    whole = pl.BlockSpec(memory_space=pltpu.VMEM)
    single = not isinstance(outs, list)
    first = [] if place is None else [place]
    specs = [whole] * (len(args) - far) + [pl.BlockSpec(memory_space=pl.ANY)] * far
    return pl.pallas_call(
        kernel,
        out_shape=outs,
        in_specs=[pl.BlockSpec(memory_space=pltpu.SMEM)] * len(first) + specs,
        out_specs=whole if single else [whole] * len(outs),
        scratch_shapes=scratch,
        compiler_params=pltpu.CompilerParams(vmem_limit_bytes=mib << 20),
    )(*first, *args)


def nn(left, right):
    return jnp.dot(left, right, preferred_element_type=F32)


def nt(left, right):
    return lax.dot_general(left, right, (((1,), (1,)), ((), ())), preferred_element_type=F32)


def prepare_kernel(*refs):
    for weight, mask, eff in zip(refs[0:3], refs[3:6], refs[6:9]):
        for i in range(mask.shape[0]):
            rows = pl.ds(i * BLK, BLK)
            keep = jnp.broadcast_to(mask[pl.ds(i, 1), :], (BLK, mask.shape[1])).astype(BF)
            eff[rows, :] = weight[rows, :] * keep


def partial_sums(place, own, cross, effs, effs_x, product):
    tokens, width = own.shape
    hid = max(effs[0].shape)
    n = len(effs)
    chips = place.shape[0]
    share = tokens // chips

    def kernel(place, own, cross, *refs):
        sources, outs, (left, left_x), held, sems = (
            refs[: 2 * n],
            refs[2 * n : 2 * n + chips],
            refs[2 * n + chips : 2 * n + chips + 2],
            refs[2 * n + chips + 2 : -1],
            refs[-1],
        )
        copies = [
            pltpu.make_async_copy(source, hold, sems.at[i])
            for i, (source, hold) in enumerate(zip(sources, held))
        ]
        for copy in copies:
            copy.start()
        for r in range(chips):
            source = pl.ds(pl.multiple_of(place[r] * share, share), share)
            left[pl.ds(r * share, share), :] = own[source, :]
            left_x[pl.ds(r * share, share), :] = cross[source, :]
        for part in range(n):
            copies[2 * part].wait()
            copies[2 * part + 1].wait()
            weight, weight_x = held[2 * part], held[2 * part + 1]
            for j in range(hid // STEP):
                here = pl.ds(j * STEP, STEP)
                at = (slice(None), here) if product is nn else (here, slice(None))
                value = product(left[...], weight[at]) + product(left_x[...], weight_x[at])
                for r, out in enumerate(outs):
                    out[part, :, here] = value[r * share : (r + 1) * share].astype(out.dtype)

    outs = [jax.ShapeDtypeStruct((n, share, hid), F32 if r == 0 else BF) for r in range(chips)]
    weights = [weight for two in zip(effs, effs_x) for weight in two]
    scratch = [pltpu.VMEM((tokens, width), BF)] * 2
    scratch += [pltpu.VMEM(weight.shape, BF) for weight in weights]
    scratch += [pltpu.SemaphoreType.DMA((2 * n,))]
    return local_call(
        kernel, 20, outs, own, cross, *weights, place=place, scratch=scratch, far=2 * n
    )


def activation_kernel(*refs):
    got, got_back, out = refs[:8], refs[8:16], refs[16]
    hid = out.shape[2]

    def total(group, part, cols):
        acc = group[0][part, :, cols]
        for ref in group[1:]:
            acc = acc + ref[part, :, cols].astype(F32)
        return acc

    for j in range(hid // STEP):
        cols = pl.ds(j * STEP, STEP)
        gate, up, d_hidden = total(got, 0, cols), total(got, 1, cols), total(got_back, 0, cols)
        sigmoid = jax.nn.sigmoid(gate)
        activated = gate * sigmoid
        out[0, :, cols] = (activated * up).astype(BF)
        out[1, :, cols] = (
            d_hidden * up * sigmoid * (1.0 + gate * (1.0 - sigmoid))
        ).astype(BF)
        out[2, :, cols] = (d_hidden * activated).astype(BF)


def results(acts, weights, out, ready=lambda i: None):
    down, gate, up = weights
    width = gate.shape[0]
    ready(0)
    out[:, :width] = nn(acts[0], down[...]).astype(BF)
    ready(1)
    value = nt(acts[1], gate[...])
    ready(2)
    out[:, width:] = (value + nt(acts[2], up[...])).astype(BF)


def early_kernel(*refs):
    shares, sources, (acts, away, here), held, sems = (
        refs[:4],
        refs[4:10],
        refs[10:13],
        refs[13:19],
        refs[19],
    )
    share = shares[0].shape[1]
    copies = [
        pltpu.make_async_copy(source, hold, sems.at[i])
        for i, (source, hold) in enumerate(zip(sources, held))
    ]
    for copy in copies:
        copy.start()
    for i, ref in enumerate(shares):
        acts[:, pl.ds(i * share, share), :] = ref[...]
    results(acts, held[:3], away, lambda i: copies[i].wait())
    results(acts, held[3:], here, lambda i: copies[3 + i].wait())


def late_away_kernel(*refs):
    shares, weights, (acts, away) = refs[:6], refs[6:9], refs[9:]
    share, hid = shares[0].shape[1], acts.shape[2]
    for i in range(2):
        acts[:, pl.ds(i * share, share), :] = shares[i][...]
        rows = pl.ds((2 + i) * share, share)
        acts[:, rows, : hid // 2] = shares[2 + 2 * i][...]
        acts[:, rows, hid // 2 :] = shares[3 + 2 * i][...]
    results(acts, weights, away)


def late_here_kernel(acts, *refs):
    results(acts, refs[:3], refs[3])


EARLY = (0, 4, 1, 3)
LATE = (5, 7, 2, 6)


def assemble_kernel(place, here_early, here_late, away_early, away_late, send):
    half = send.shape[1] // 2
    for order, here, away in ((EARLY, here_early, away_early), (LATE, here_late, away_late)):
        for i, r in enumerate(order):
            for k in range(2):
                rows = pl.ds((2 * i + k) * half, half)
                send[2 * place[r] + k, :half, :] = here[rows, :]
                send[2 * place[r] + k, half:, :] = away[rows, :]


def gradient_kernel(place, *refs):
    early, late, early_x, late_x = refs[:4]
    sources, masks = refs[4:8], refs[8:11]
    grad_gate, grad_up, grad_down = refs[11:14]
    moved = refs[14:]
    width, hid = grad_gate.shape
    share = sources[0].shape[0] // place.shape[0]
    for source, target in zip(sources, moved):
        for i, r in enumerate(EARLY + LATE):
            rows = pl.ds(pl.multiple_of(place[r] * share, share), share)
            target[pl.ds(i * share, share), :] = source[rows, :]
    rows, rows_x = moved[0][...].T, moved[1][...].T
    cot, cot_x = moved[2][...], moved[3][...]
    for j in range(hid // STEP):
        here = pl.ds(j * STEP, STEP)

        def all_rows(first, second, part):
            return jnp.concatenate([first[part, :, here], second[part, :, here]], axis=0)

        for part, mask, grad in ((1, masks[0], grad_gate), (2, masks[1], grad_up)):
            value = nn(rows, all_rows(early, late, part))
            value += nn(rows_x, all_rows(early_x, late_x, part))
            for i in range(width // BLK):
                keep = mask[pl.ds(i, 1), here]
                grad[pl.ds(i * BLK, BLK), here] = (value[i * BLK : (i + 1) * BLK] * keep).astype(BF)
        value = nn(all_rows(early, late, 0).T, cot) + nn(all_rows(early_x, late_x, 0).T, cot_x)
        for i in range(STEP // BLK):
            keep = masks[2][pl.ds(j * (STEP // BLK) + i, 1), :]
            grad_down[pl.ds(j * STEP + i * BLK, BLK), :] = (
                value[i * BLK : (i + 1) * BLK] * keep
            ).astype(BF)


def swap(array):
    return lax.ppermute(array, "core", [(0, 1), (1, 0)])


def layer(
    tokens, cotangent, gate_weight, up_weight, down_weight, gate_mask, up_mask, down_mask
):
    share, width = tokens.shape
    hid = gate_weight.shape[1]
    core = lax.axis_index("core")
    pairs = lax.axis_size(PAIR)
    cols = lax.axis_size(COL)
    half = share // 2

    x_lo, y = lax.axis_index("x_lo"), lax.axis_index("y")
    y_n = lax.axis_size("y")
    place = jnp.stack(
        [(x_lo ^ (r // y_n)) * y_n + (y + r % y_n) % y_n for r in range(pairs)]
    ).astype(jnp.int32)

    def gather(array):
        return lax.all_to_all(
            jnp.broadcast_to(array, (cols,) + array.shape), COL, 0, 0, tiled=True
        )

    def by_core(gathered):
        own = lax.dynamic_slice_in_dim(gathered, core * half, half, 1)
        other = lax.dynamic_slice_in_dim(gathered, (1 - core) * half, half, 1)
        return own.reshape(-1, width), other.reshape(-1, width)

    def spread(parts):
        got = {0: parts[0]}
        for r in (6, 5, 7, 2, 4, 1, 3):
            moves = [
                (i, ((i // y_n) ^ (r // y_n)) * y_n + (i % y_n + r % y_n) % y_n)
                for i in range(pairs)
            ]
            got[r] = lax.ppermute(parts[r], PAIR, moves)
        return [got[r] for r in range(pairs)]

    gathered = gather(tokens)
    weights = (gate_weight, up_weight, down_weight)
    shapes = [jax.ShapeDtypeStruct(weight.shape, BF) for weight in weights]
    wide = [
        jnp.repeat(mask.astype(F32), BLK, axis=1) for mask in (gate_mask, up_mask, down_mask)
    ]
    effs = local_call(prepare_kernel, 20, shapes, *weights, *wide)
    effs_x = [swap(eff) for eff in effs]

    gathered, cot_in = lax.optimization_barrier((gathered, cotangent))
    gathered_cot = gather(cot_in)
    own, other = by_core(gathered)
    parts = partial_sums(place, own, swap(other), effs[:2], effs_x[:2], nn)
    got = spread(parts)
    own_cot, other_cot = by_core(gathered_cot)
    back = partial_sums(place, own_cot, swap(other_cot), effs[2:], effs_x[2:], nt)
    got_back = spread(back)
    mine = local_call(
        activation_kernel,
        12,
        jax.ShapeDtypeStruct((3, parts[0].shape[1], hid), BF),
        *got,
        *got_back,
    )

    def from_up(array):
        return lax.ppermute(array, "y", [(i, (i - 1) % y_n) for i in range(y_n)])

    def from_down(array):
        return lax.ppermute(array, "y", [(i, (i + 1) % y_n) for i in range(y_n)])

    mid = hid // 2
    up_one, down_one = from_up(mine), from_down(mine)
    facing = lax.ppermute(mine, "x_lo", [(0, 1), (1, 0)])
    distant = [from_up(up_one[:, :, :mid]), from_down(down_one[:, :, mid:])]
    facing_up, facing_down = from_up(facing), from_down(facing)
    distant += [from_up(facing_up[:, :, :mid]), from_down(facing_down[:, :, mid:])]

    rows_n = own.shape[0] // 2
    acts_shape = jax.ShapeDtypeStruct((3, rows_n, hid), BF)
    sums_shape = jax.ShapeDtypeStruct((rows_n, 2 * width), BF)
    ordered = [effs_x[2], *effs_x[:2], effs[2], *effs[:2]]
    early, away_early, here_early, *resident = local_call(
        early_kernel,
        24,
        [acts_shape, sums_shape, sums_shape]
        + [pltpu.VMEM(weight.shape, BF) for weight in ordered],
        mine,
        facing,
        up_one,
        down_one,
        *ordered,
        scratch=[pltpu.SemaphoreType.DMA((6,))],
        far=6,
    )
    late, away_late = local_call(
        late_away_kernel,
        16,
        [acts_shape, sums_shape],
        facing_up,
        facing_down,
        *distant,
        *resident[:3],
    )
    away_early, away_late = swap(away_early), swap(away_late)
    here_late = local_call(late_here_kernel, 12, sums_shape, late, *resident[3:])
    send = local_call(
        assemble_kernel,
        8,
        jax.ShapeDtypeStruct((cols, share, 2 * width), BF),
        here_early,
        here_late,
        away_early,
        away_late,
        place=place,
    )
    arrived = lax.all_to_all(send, COL, 0, 0, tiled=True)
    sums = jnp.sum(arrived.astype(F32), axis=0)
    first, second = sums[:half], sums[half:]
    sums = jnp.concatenate(
        [jnp.where(core == 0, first, second), jnp.where(core == 0, second, first)], axis=0
    ).astype(BF)
    output, d_tokens = sums[:, :width], sums[:, width:]

    send, early, late = lax.optimization_barrier((send, early, late))
    grad_gate, grad_up, grad_down = local_call(
        gradient_kernel,
        20,
        shapes,
        early,
        late,
        swap(early),
        swap(late),
        own,
        other,
        own_cot,
        other_cot,
        *wide,
        place=place,
        scratch=[pltpu.VMEM(own.shape, BF)] * 4,
    )
    return (output, d_tokens, grad_gate, grad_up, grad_down)


def solution(mesh):
    fine = Mesh(mesh.devices.reshape(2, 4, 2, 2, 8), ROW + COL)
    in_specs = (
        P(COL, ROW),
        P(COL, ROW),
        P(ROW, COL),
        P(ROW, COL),
        P(COL, ROW),
        P(ROW, COL),
        P(ROW, COL),
        P(COL, ROW),
    )
    out_specs = (P(COL, ROW), P(COL, ROW), P(ROW, COL), P(ROW, COL), P(COL, ROW))
    return jax.shard_map(layer, mesh=fine, in_specs=in_specs, out_specs=out_specs, check_vma=False)
```

time: 178 us -> 176 us (0.989)
  waiting for transfers between devices: 80.8 us -> 63.3 us
  starting transfers between devices: 56.8 us -> 65.6 us
  Pallas kernels: 24 us -> 28.8 us
    all_to_all x1, waiting for transfers between devices: 28.9 us -> 15.2 us  [layer(): arrived = lax.all_to_all(send, COL, 0, 0, tiled=True)]
    ppermute x4, waiting for transfers between devices: 9.76 us -> 0.01 us  [from_down(): return lax.ppermute(array, 'y', [(i, (i + 1) % y_n) for i in range(y_n)])]
    pallas_call x6 -> x9, Pallas kernels: 24 us -> 28.8 us  [local_call(): pl.pallas_call(kernel, out_shape=outs, in_specs=[pl.BlockSpec(memory_spac...]
    all_to_all x1 -> x2, starting transfers between devices: 11.1 us -> 15.7 us  [gather(): lax.all_to_all(jnp.broadcast_to(array, (cols,) + array.shape), COL, 0, 0,...]
    ppermute x7 -> x14, waiting for transfers between devices: 14 us -> 9.58 us  [spread(): got[r] = lax.ppermute(parts[r], PAIR, moves)]
    ppermute x4, waiting for transfers between devices: 2.05 us -> 6.42 us  [from_up(): return lax.ppermute(array, 'y', [(i, (i - 1) % y_n) for i in range(y_n)])]
    ppermute x6 -> x9, waiting for transfers between devices: 1.89 us -> 4.95 us  [swap(): return lax.ppermute(array, 'core', [(0, 1), (1, 0)])]
    all_to_all x1 -> x2, waiting for transfers between devices: 21 us -> 23.9 us  [gather(): lax.all_to_all(jnp.broadcast_to(array, (cols,) + array.shape), COL, 0, 0,...]
  transfers between devices with their start and end apart: 24 -> 35, of which waited for: 12 -> 13; matrix products, arithmetic and copies ran while one was open for 2% -> 3% of each run, Pallas kernels for 3% -> 15%
where the time goes in v7:
time: 176 us; the launch traced here: 173 us
  starting transfers between devices  65.6 us (37%)
  waiting for transfers between devices  63.3 us (36%)
  Pallas kernels  28.8 us (16%)
  local copies, waits for them, and re-layouts  9.9 us (6%)
  other arithmetic  4.09 us (2%)
    ppermute x14, starting transfers between devices, spread(): got[r] = lax.ppermute(parts[r], PAIR, moves)  30.1 us
    pallas_call x9, Pallas kernels, local_call(): pl.pallas_call(kernel, out_shape=outs, in_specs=[pl.BlockSpec(memory_spac...  28.8 us
    all_to_all x2, waiting for transfers between devices, gather(): lax.all_to_all(jnp.broadcast_to(array, (cols,) + array.shape), COL, 0, 0,...  23.9 us
    all_to_all x2, starting transfers between devices, gather(): lax.all_to_all(jnp.broadcast_to(array, (cols,) + array.shape), COL, 0, 0,...  15.7 us
    all_to_all x1, waiting for transfers between devices, layer(): arrived = lax.all_to_all(send, COL, 0, 0, tiled=True)  15.2 us
    ppermute x4, starting transfers between devices, from_up(): return lax.ppermute(array, 'y', [(i, (i - 1) % y_n) for i in range(y_n)])  11 us
    ppermute x14, waiting for transfers between devices, spread(): got[r] = lax.ppermute(parts[r], PAIR, moves)  9.58 us
    ppermute x4, waiting for transfers between devices, from_up(): return lax.ppermute(array, 'y', [(i, (i - 1) % y_n) for i in range(y_n)])  6.42 us
  transfers between devices with their start and end apart: 35, of which 13 were waited for; matrix products, arithmetic and copies ran while one was open for 3% of the time, Pallas kernels for 15%

profile of v7, /device:TPU:8, one launch (start us, length us, event | category | flops | bytes accessed | tf_op | source)
XLA Modules:
  0.0 172.6 jit_solution(2115468883347995736)
XLA Ops:
  0.6 1.6 broadcast_in_dim.15
  2.2 11.0 %all-to-all-start = ((bf16[16,32,512]{2,1,0:T(8,128)(2,1)}), bf16[16,32,512]{2,1,0:T(8,128)(2,1)S(1)}, u32[]{:S(2)}, u32[]{:S(2)}) async-start(bf16[16,32,512]{2,1,0:T(8,128)(2,1)} %broadcast_in_dim.15), calls=%async_computation | async-start | bytes 1048576 | tf_op jit(solution)/shard_map/all_to_all | solution.py:233
  14.0 0.7 convert_element_type.13
  14.8 0.7 convert_element_type.15
  15.7 1.5 copy-done
  17.2 1.5 copy-done.1
  18.7 1.5 copy-done.2
  20.2 2.2 %shard_map.119 = (bf16[512,1792]{1,0:T(8,128)(2,1)}, bf16[512,1792]{1,0:T(8,128)(2,1)}, bf16[1792,512]{1,0:T(8,128)(2,1)S(1)}) custom-call(bf16[512,1792]{1,0:T(8,128)(2,1)S(1)} %copy-done, bf16[512,1792]{1,0:T(8,128)(2,1)S(1)} %copy-done.1, bf16[1792,512]{1,0:T(8,128)(2,1)S(1)} %copy-done.2, f32[4,1792]{1,0:T(4,128)S(1)} %get-tuple-element.88.refs_3_.refs_8_, ...), custom_call_target="tpu_custom_call" | custom-call | tf_op jit(solution)/shard_map/pallas_call | solution.py:24
  23.0 7.5 %all-to-all-done = bf16[16,32,512]{2,1,0:T(8,128)(2,1)S(1)} async-done(((bf16[16,32,512]{2,1,0:T(8,128)(2,1)}), bf16[16,32,512]{2,1,0:T(8,128)(2,1)S(1)}, u32[]{:S(2)}, u32[]{:S(2)}) %all-to-all-start) | async-done | bytes 524320 | tf_op jit(solution)/shard_map/all_to_all | solution.py:233
  30.4 0.8 broadcast_in_dim.19
  31.3 4.6 %all-to-all-start.1 = ((bf16[16,32,512]{2,1,0:T(8,128)(2,1)}), bf16[16,32,512]{2,1,0:T(8,128)(2,1)}, u32[]{:S(2)}, u32[]{:S(2)}) async-start(bf16[16,32,512]{2,1,0:T(8,128)(2,1)} %broadcast_in_dim.19), calls=%async_computation.1 | async-start | bytes 1048576 | tf_op jit(solution)/shard_map/all_to_all | solution.py:233
  36.1 16.4 %all-to-all-done.1 = bf16[16,32,512]{2,1,0:T(8,128)(2,1)} async-done(((bf16[16,32,512]{2,1,0:T(8,128)(2,1)}), bf16[16,32,512]{2,1,0:T(8,128)(2,1)}, u32[]{:S(2)}, u32[]{:S(2)}) %all-to-all-start.1) | async-done | bytes 524320 | tf_op jit(solution)/shard_map/all_to_all | solution.py:233
  52.5 1.1 constant_dynamic-slice_fusion
  53.8 5.1 %shard_map.120 = (f32[2,32,1792]{2,1,0:T(8,128)S(1)}, bf16[2,32,1792]{2,1,0:T(8,128)(2,1)S(1)}, bf16[2,32,1792]{2,1,0:T(8,128)(2,1)S(1)}, bf16[2,32,1792]{2,1,0:...) custom-call(s32[8]{0:T(128)S(1)} %stack.35.place, ...), custom_call_target="tpu_custom_call" | custom-call | tf_op jit(solution)/shard_map/pallas_call | solution.py:24
  58.9 1.7 collective-permute-start.3
  60.6 0.9 collective-permute-start.4
  61.5 2.4 %collective-permute-start.5 = (bf16[2,32,1792]{2,1,0:T(8,128)(2,1)S(1)}, bf16[2,32,1792]{2,1,0:T(8,128)(2,1)S(1)}, u32[]{:S(2)}, u32[]{:S(2)}) collective-permute-start(bf16[2,32,1792]{2,1,0:T(8,128)(2,1)S(1)} %get-tuple-element.48), channel_id=1, source_target_pairs={{0,96},{32,0},{64,32},{96,64},{128,224},{160,128},{192,160},{224,1... | collective-permute-start | bytes 688136 | tf_op jit(solution)/shard_map/ppermute | solution.py:249
  64.5 3.0 %collective-permute-done.3.refs_1_ = bf16[2,32,1792]{2,1,0:T(8,128)(2,1)S(1)} collective-permute-done((bf16[2,32,1792]{2,1,0:T(8,128)(2,1)S(1)}, bf16[2,32,1792]{2,1,0:T(8,128)(2,1)S(1)}, u32[]{:S(2)}, u32[]{:S(2)}) %collective-permute-start.3) | collective-permute-done | bytes 229408 | tf_op jit(solution)/shard_map/ppermute | solution.py:249
  67.5 8.5 %collective-permute-start.7 = (bf16[2,32,1792]{2,1,0:T(8,128)(2,1)S(1)}, bf16[2,32,1792]{2,1,0:T(8,128)(2,1)S(1)}, u32[]{:S(2)}, u32[]{:S(2)}) collective-permute-start(bf16[2,32,1792]{2,1,0:T(8,128)(2,1)S(1)} %get-tuple-element.50), channel_id=1, source_target_pairs={{0,160},{32,192},{64,224},{96,128},{128,32},{160,64},{192,96},{224... | collective-permute-start | bytes 688136 | tf_op jit(solution)/shard_map/ppermute | solution.py:249
  76.0 3.1 %collective-permute-start.9 = (bf16[2,32,1792]{2,1,0:T(8,128)(2,1)S(1)}, bf16[2,32,1792]{2,1,0:T(8,128)(2,1)S(1)}, u32[]{:S(2)}, u32[]{:S(2)}) collective-permute-start(bf16[2,32,1792]{2,1,0:T(8,128)(2,1)S(1)} %get-tuple-element.52), channel_id=1, source_target_pairs={{0,224},{32,128},{64,160},{96,192},{128,96},{160,0},{192,32},{224,... | collective-permute-start | bytes 688136 | tf_op jit(solution)/shard_map/ppermute | solution.py:249
  79.0 3.3 %shard_map.121 = (f32[1,32,1792]{2,1,0:T(8,128)S(1)}, bf16[1,32,1792]{2,1,0:T(8,128)(2,1)S(1)}, bf16[1,32,1792]{2,1,0:T(8,128)(2,1)S(1)}, bf16[1,32,1792]{2,1,0:...) custom-call(s32[8]{0:T(128)S(1)} %stack.35.place, ...), custom_call_target="tpu_custom_call" | custom-call | tf_op jit(solution)/shard_map/pallas_call | solution.py:24
  82.4 1.7 collective-permute-start.12
  84.1 3.1 %collective-permute-start.13 = (bf16[1,32,1792]{2,1,0:T(8,128)(2,1)S(1)}, bf16[1,32,1792]{2,1,0:T(8,128)(2,1)S(1)}, u32[]{:S(2)}, u32[]{:S(2)}) collective-permute-start(bf16[1,32,1792]{2,1,0:T(8,128)(2,1)S(1)} %get-tuple-element.57), channel_id=1, source_target_pairs={{0,64},{32,96},{64,0},{96,32},{128,192},{160,224},{192,128},{224,1... | collective-permute-start | bytes 344072 | tf_op jit(solution)/shard_map/ppermute | solution.py:249
  87.2 1.8 %collective-permute-start.14 = (bf16[1,32,1792]{2,1,0:T(8,128)(2,1)S(1)}, bf16[1,32,1792]{2,1,0:T(8,128)(2,1)S(1)}, u32[]{:S(2)}, u32[]{:S(2)}) collective-permute-start(bf16[1,32,1792]{2,1,0:T(8,128)(2,1)S(1)} %get-tuple-element.58), channel_id=1, source_target_pairs={{0,96},{32,0},{64,32},{96,64},{128,224},{160,128},{192,160},{224,1... | collective-permute-start | bytes 344072 | tf_op jit(solution)/shard_map/ppermute | solution.py:249
  89.7 3.1 %collective-permute-done.9.refs_7_ = bf16[2,32,1792]{2,1,0:T(8,128)(2,1)S(1)} collective-permute-done((bf16[2,32,1792]{2,1,0:T(8,128)(2,1)S(1)}, bf16[2,32,1792]{2,1,0:T(8,128)(2,1)S(1)}, u32[]{:S(2)}, u32[]{:S(2)}) %collective-permute-start.9) | collective-permute-done | bytes 229408 | tf_op jit(solution)/shard_map/ppermute | solution.py:249
  92.7 2.2 %collective-permute-start.17 = (bf16[1,32,1792]{2,1,0:T(8,128)(2,1)S(1)}, bf16[1,32,1792]{2,1,0:T(8,128)(2,1)S(1)}, u32[]{:S(2)}, u32[]{:S(2)}) collective-permute-start(bf16[1,32,1792]{2,1,0:T(8,128)(2,1)S(1)} %get-tuple-element.61), channel_id=1, source_target_pairs={{0,192},{32,224},{64,128},{96,160},{128,64},{160,96},{192,0},{224,... | collective-permute-start | bytes 344072 | tf_op jit(solution)/shard_map/ppermute | solution.py:249
  94.9 3.5 %collective-permute-start.18 = (bf16[1,32,1792]{2,1,0:T(8,128)(2,1)S(1)}, bf16[1,32,1792]{2,1,0:T(8,128)(2,1)S(1)}, u32[]{:S(2)}, u32[]{:S(2)}) collective-permute-start(bf16[1,32,1792]{2,1,0:T(8,128)(2,1)S(1)} %get-tuple-element.62), channel_id=1, source_target_pairs={{0,224},{32,128},{64,160},{96,192},{128,96},{160,0},{192,32},{224,... | collective-permute-start | bytes 344072 | tf_op jit(solution)/shard_map/ppermute | solution.py:249
  99.1 1.1 collective-permute-done.17.refs_14_
  100.2 1.8 %collective-permute-done.18.refs_15_ = bf16[1,32,1792]{2,1,0:T(8,128)(2,1)S(1)} collective-permute-done((bf16[1,32,1792]{2,1,0:T(8,128)(2,1)S(1)}, bf16[1,32,1792]{2,1,0:T(8,128)(2,1)S(1)}, u32[]{:S(2)}, u32[]{:S(2)}) %collective-permute-start.18) | collective-permute-done | bytes 114720 | tf_op jit(solution)/shard_map/ppermute | solution.py:249
  102.4 0.7 collective-permute-start.19
  103.1 3.3 %collective-permute-start.20 = (bf16[3,32,1792]{2,1,0:T(8,128)(2,1)S(1)}, bf16[3,32,1792]{2,1,0:T(8,128)(2,1)S(1)}, u32[]{:S(2)}, u32[]{:S(2)}) collective-permute-start(bf16[3,32,1792]{2,1,0:T(8,128)(2,1)S(1)} %shard_map.122.refs_0_), channel_id=1, source_target_pairs={{0,96},{32,0},{64,32},{96,64},{1,97},{33,1},{65,33},{97,65},{2,98}... | collective-permute-start | bytes 1032200 | tf_op jit(solution)/shard_map/ppermute | solution.py:278
  106.5 3.3 %collective-permute-done.19.refs_1_ = bf16[3,32,1792]{2,1,0:T(8,128)(2,1)S(1)} collective-permute-done((bf16[3,32,1792]{2,1,0:T(8,128)(2,1)S(1)}, bf16[3,32,1792]{2,1,0:T(8,128)(2,1)S(1)}, u32[]{:S(2)}, u32[]{:S(2)}) %collective-permute-start.19) | collective-permute-done | bytes 344096 | tf_op jit(solution)/shard_map/ppermute | solution.py:285
  109.8 2.5 %collective-permute-start.22 = (bf16[3,32,1792]{2,1,0:T(8,128)(2,1)S(1)}, bf16[3,32,1792]{2,1,0:T(8,128)(2,1)S(1)}, u32[]{:S(2)}, u32[]{:S(2)}) collective-permute-start(bf16[3,32,1792]{2,1,0:T(8,128)(2,1)S(1)} %collective-permute-done.19.refs_1_), channel_id=1, source_target_pairs={{0,96},{32,0},{64,32},{96,64},{1,97},{33,1},{65,33},{97,65},{2,98}... | collective-permute-start | bytes 1032200 | tf_op jit(solution)/shard_map/ppermute | solution.py:278
  112.3 2.6 %collective-permute-done.20.refs_2_ = bf16[3,32,1792]{2,1,0:T(8,128)(2,1)S(1)} collective-permute-done((bf16[3,32,1792]{2,1,0:T(8,128)(2,1)S(1)}, bf16[3,32,1792]{2,1,0:T(8,128)(2,1)S(1)}, u32[]{:S(2)}, u32[]{:S(2)}) %collective-permute-start.20) | collective-permute-done | bytes 344096 | tf_op jit(solution)/shard_map/ppermute | solution.py:278
  114.9 2.6 %collective-permute-start.24 = (bf16[3,32,896]{2,1,0:T(8,128)(2,1)S(1)}, bf16[3,32,896]{2,1,0:T(8,128)(2,1)S(1)}, u32[]{:S(2)}, u32[]{:S(2)}) collective-permute-start(bf16[3,32,896]{2,1,0:T(8,128)(2,1)S(1)} %slice.32), channel_id=1, source_target_pairs={{0,96},{32,0},{64,32},{96,64},{1,97},{33,1},{65,33},{97,65},{2,98}... | collective-permute-start | bytes 516104 | tf_op jit(solution)/shard_map/ppermute | solution.py:278
  117.6 3.8 %collective-permute-done.22.refs_0_ = bf16[3,32,1792]{2,1,0:T(8,128)(2,1)S(1)} collective-permute-done((bf16[3,32,1792]{2,1,0:T(8,128)(2,1)S(1)}, bf16[3,32,1792]{2,1,0:T(8,128)(2,1)S(1)}, u32[]{:S(2)}, u32[]{:S(2)}) %collective-permute-start.22) | collective-permute-done | bytes 344096 | tf_op jit(solution)/shard_map/ppermute | solution.py:278
  121.4 2.6 %collective-permute-start.26 = (bf16[3,32,896]{2,1,0:T(8,128)(2,1)S(1)}, bf16[3,32,896]{2,1,0:T(8,128)(2,1)S(1)}, u32[]{:S(2)}, u32[]{:S(2)}) collective-permute-start(bf16[3,32,896]{2,1,0:T(8,128)(2,1)S(1)} %slice.34), channel_id=1, source_target_pairs={{0,96},{32,0},{64,32},{96,64},{1,97},{33,1},{65,33},{97,65},{2,98}... | collective-permute-start | bytes 516104 | tf_op jit(solution)/shard_map/ppermute | solution.py:278
  124.3 5.8 %shard_map.123 = (bf16[3,128,1792]{2,1,0:T(8,128)(2,1)S(1)}, bf16[128,1024]{1,0:T(8,128)(2,1)S(1)}, bf16[128,1024]{1,0:T(8,128)(2,1)S(1)}, bf16[1792,512]{1,0:T(...) custom-call(bf16[3,32,1792]{2,1,0:T(8,128)(2,1)S(1)} %shard_map.122., ...), custom_call_target="tpu_custom_call" | custom-call | tf_op jit(solution)/shard_map/pallas_call | solution.py:24
  130.3 1.6 shard_map.124
  132.4 1.5 shard_map.125.here_late
  134.0 1.6 shard_map.126
  135.6 5.8 %all-to-all-start.2 = ((bf16[16,32,1024]{2,1,0:T(8,128)(2,1)}), bf16[16,32,1024]{2,1,0:T(8,128)(2,1)}, u32[]{:S(2)}, u32[]{:S(2)}) async-start(bf16[16,32,1024]{2,1,0:T(8,128)(2,1)} %shard_map.126), calls=%async_computation.2 | async-start | bytes 2097152 | tf_op jit(solution)/shard_map/all_to_all | solution.py:328
  142.0 3.0 %collective-permute-done.30.refs_2_ = bf16[3,128,1792]{2,1,0:T(8,128)(2,1)} collective-permute-done((bf16[3,128,1792]{2,1,0:T(8,128)(2,1)}, bf16[3,128,1792]{2,1,0:T(8,128)(2,1)}, u32[]{:S(2)}, u32[]{:S(2)}) %collective-permute-start.30) | collective-permute-done | bytes 1376288 | tf_op jit(solution)/shard_map/ppermute | solution.py:213
  145.0 2.0 %collective-permute-done.31.refs_3_ = bf16[3,128,1792]{2,1,0:T(8,128)(2,1)} collective-permute-done((bf16[3,128,1792]{2,1,0:T(8,128)(2,1)S(1)}, bf16[3,128,1792]{2,1,0:T(8,128)(2,1)}, u32[]{:S(2)}, u32[]{:S(2)}) %collective-permute-start.31) | collective-permute-done | bytes 1376288 | tf_op jit(solution)/shard_map/ppermute | solution.py:213
  147.0 1.3 copy-done.4
  148.3 7.1 %shard_map.127 = (bf16[512,1792]{1,0:T(8,128)(2,1)}, bf16[512,1792]{1,0:T(8,128)(2,1)}, bf16[1792,512]{1,0:T(8,128)(2,1)}) custom-call(s32[8]{0:T(128)S(1)} %stack.35.place, bf16[3,128,1792]{2,1,0:T(8,128)(2,1)S(1)} %copy-done.4, bf16[3,128,1792]{2,1,0:T(8,128)(2,1)S(1)} %get-tuple-element.75.acts.refs_1_, ...), custom_call_target="tpu_custom_call" | custom-call | tf_op jit(solution)/shard_map/pallas_call | solution.py:24
  155.4 15.2 %all-to-all-done.2 = bf16[16,32,1024]{2,1,0:T(8,128)(2,1)} async-done(((bf16[16,32,1024]{2,1,0:T(8,128)(2,1)}), bf16[16,32,1024]{2,1,0:T(8,128)(2,1)}, u32[]{:S(2)}, u32[]{:S(2)}) %all-to-all-start.2) | async-done | bytes 1048608 | tf_op jit(solution)/shard_map/all_to_all | solution.py:328
  170.6 1.4 convert_reduce_fusion
  (65 shorter events, 6.6 us)
Async XLA Ops:
  2.2 28.2 %all-to-all-start = ((bf16[16,32,512]{2,1,0:T(8,128)(2,1)}), bf16[16,32,512]{2,1,0:T(8,128)(2,1)S(1)}, u32[]{:S(2)}, u32[]{:S(2)}) async-start(bf16[16,32,512]{2,1,0:T(8,128)(2,1)} %broadcast_in_dim.15), calls=%async_computation | async-start | bytes 1048576 | tf_op jit(solution)/shard_map/all_to_all | solution.py:233
  15.7 1.5 copy-start
  17.2 1.5 copy-start.1
  18.7 1.5 copy-start.2
  20.2 10.2 %copy-start.5 = (bf16[32,512]{1,0:T(8,128)(2,1)S(1)}, bf16[32,512]{1,0:T(8,128)(2,1)}, u32[]{:S(2)}) copy-start(bf16[32,512]{1,0:T(8,128)(2,1)} %param.9) | copy-start | bytes 98308
  22.4 31.4 %collective-permute-start.1 = (bf16[512,1792]{1,0:T(8,128)(2,1)}, bf16[512,1792]{1,0:T(8,128)(2,1)}, u32[]{:S(2)}, u32[]{:S(2)}) collective-permute-start(bf16[512,1792]{1,0:T(8,128)(2,1)} %get-tuple-element.43.refs_0_.refs_8_), channel_id=1, source_target_pairs={{0,16},{16,0},{1,17},{17,1},{2,18},{18,2},{3,19},{19,3},{4,20},{20... | collective-permute-start | bytes 5505032 | tf_op jit(solution)/shard_map/ppermute | solution.py:213
  22.4 31.4 %collective-permute-start.2 = (bf16[512,1792]{1,0:T(8,128)(2,1)}, bf16[512,1792]{1,0:T(8,128)(2,1)}, u32[]{:S(2)}, u32[]{:S(2)}) collective-permute-start(bf16[512,1792]{1,0:T(8,128)(2,1)} %get-tuple-element.44.refs_2_.refs_9_), channel_id=1, source_target_pairs={{0,16},{16,0},{1,17},{17,1},{2,18},{18,2},{3,19},{19,3},{4,20},{20... | collective-permute-start | bytes 5505032 | tf_op jit(solution)/shard_map/ppermute | solution.py:213
  23.0 41.0 %collective-permute-start.11 = (bf16[1792,512]{1,0:T(8,128)(2,1)S(1)}, bf16[1792,512]{1,0:T(8,128)(2,1)}, u32[]{:S(2)}, u32[]{:S(2)}) collective-permute-start(bf16[1792,512]{1,0:T(8,128)(2,1)S(1)} %get-tuple-element.54.refs_0_.refs_7_), channel_id=1, source_target_pairs={{0,16},{16,0},{1,17},{17,1},{2,18},{18,2},{3,19},{19,3},{4,20},{20... | collective-permute-start | bytes 5505032 | tf_op jit(solution)/shard_map/ppermute | solution.py:213
  31.3 21.2 %all-to-all-start.1 = ((bf16[16,32,512]{2,1,0:T(8,128)(2,1)}), bf16[16,32,512]{2,1,0:T(8,128)(2,1)}, u32[]{:S(2)}, u32[]{:S(2)}) async-start(bf16[16,32,512]{2,1,0:T(8,128)(2,1)} %broadcast_in_dim.19), calls=%async_computation.1 | async-start | bytes 1048576 | tf_op jit(solution)/shard_map/all_to_all | solution.py:233
  36.0 17.8 %collective-permute-start = (bf16[256,512]{1,0:T(8,128)(2,1)S(1)}, bf16[256,512]{1,0:T(8,128)(2,1)S(1)}, u32[]{:S(2)}, u32[]{:S(2)}) collective-permute-start(bf16[256,512]{1,0:T(8,128)(2,1)S(1)} %bitcast.27), channel_id=1, source_target_pairs={{0,16},{16,0},{1,17},{17,1},{2,18},{18,2},{3,19},{19,3},{4,20},{20... | collective-permute-start | bytes 786440 | tf_op jit(solution)/shard_map/ppermute | solution.py:213
  53.6 22.4 %collective-permute-start.10 = (bf16[256,512]{1,0:T(8,128)(2,1)S(1)}, bf16[256,512]{1,0:T(8,128)(2,1)S(1)}, u32[]{:S(2)}, u32[]{:S(2)}) collective-permute-start(bf16[256,512]{1,0:T(8,128)(2,1)S(1)} %bitcast.29), channel_id=1, source_target_pairs={{0,16},{16,0},{1,17},{17,1},{2,18},{18,2},{3,19},{19,3},{4,20},{20... | collective-permute-start | bytes 786440 | tf_op jit(solution)/shard_map/ppermute | solution.py:213
  58.9 8.6 %collective-permute-start.3 = (bf16[2,32,1792]{2,1,0:T(8,128)(2,1)S(1)}, bf16[2,32,1792]{2,1,0:T(8,128)(2,1)S(1)}, u32[]{:S(2)}, u32[]{:S(2)}) collective-permute-start(bf16[2,32,1792]{2,1,0:T(8,128)(2,1)S(1)} %get-tuple-element.46), channel_id=1, source_target_pairs={{0,32},{32,64},{64,96},{96,0},{128,160},{160,192},{192,224},{224,1... | collective-permute-start | bytes 688136 | tf_op jit(solution)/shard_map/ppermute | solution.py:249
  60.6 15.4 %collective-permute-start.4 = (bf16[2,32,1792]{2,1,0:T(8,128)(2,1)S(1)}, bf16[2,32,1792]{2,1,0:T(8,128)(2,1)S(1)}, u32[]{:S(2)}, u32[]{:S(2)}) collective-permute-start(bf16[2,32,1792]{2,1,0:T(8,128)(2,1)S(1)} %get-tuple-element.47), channel_id=1, source_target_pairs={{0,64},{32,96},{64,0},{96,32},{128,192},{160,224},{192,128},{224,1... | collective-permute-start | bytes 688136 | tf_op jit(solution)/shard_map/ppermute | solution.py:249
  61.5 20.8 %collective-permute-start.5 = (bf16[2,32,1792]{2,1,0:T(8,128)(2,1)S(1)}, bf16[2,32,1792]{2,1,0:T(8,128)(2,1)S(1)}, u32[]{:S(2)}, u32[]{:S(2)}) collective-permute-start(bf16[2,32,1792]{2,1,0:T(8,128)(2,1)S(1)} %get-tuple-element.48), channel_id=1, source_target_pairs={{0,96},{32,0},{64,32},{96,64},{128,224},{160,128},{192,160},{224,1... | collective-permute-start | bytes 688136 | tf_op jit(solution)/shard_map/ppermute | solution.py:249
  64.0 20.1 %collective-permute-start.6 = (bf16[2,32,1792]{2,1,0:T(8,128)(2,1)S(1)}, bf16[2,32,1792]{2,1,0:T(8,128)(2,1)S(1)}, u32[]{:S(2)}, u32[]{:S(2)}) collective-permute-start(bf16[2,32,1792]{2,1,0:T(8,128)(2,1)S(1)} %get-tuple-element.49), channel_id=1, source_target_pairs={{0,128},{32,160},{64,192},{96,224},{128,0},{160,32},{192,64},{224,... | collective-permute-start | bytes 688136 | tf_op jit(solution)/shard_map/ppermute | solution.py:249
  67.5 19.7 %collective-permute-start.7 = (bf16[2,32,1792]{2,1,0:T(8,128)(2,1)S(1)}, bf16[2,32,1792]{2,1,0:T(8,128)(2,1)S(1)}, u32[]{:S(2)}, u32[]{:S(2)}) collective-permute-start(bf16[2,32,1792]{2,1,0:T(8,128)(2,1)S(1)} %get-tuple-element.50), channel_id=1, source_target_pairs={{0,160},{32,192},{64,224},{96,128},{128,32},{160,64},{192,96},{224... | collective-permute-start | bytes 688136 | tf_op jit(solution)/shard_map/ppermute | solution.py:249
  76.0 13.1 %collective-permute-start.8 = (bf16[2,32,1792]{2,1,0:T(8,128)(2,1)S(1)}, bf16[2,32,1792]{2,1,0:T(8,128)(2,1)S(1)}, u32[]{:S(2)}, u32[]{:S(2)}) collective-permute-start(bf16[2,32,1792]{2,1,0:T(8,128)(2,1)S(1)} %get-tuple-element.51), channel_id=1, source_target_pairs={{0,192},{32,224},{64,128},{96,160},{128,64},{160,96},{192,0},{224,... | collective-permute-start | bytes 688136 | tf_op jit(solution)/shard_map/ppermute | solution.py:249
  76.0 16.8 %collective-permute-start.9 = (bf16[2,32,1792]{2,1,0:T(8,128)(2,1)S(1)}, bf16[2,32,1792]{2,1,0:T(8,128)(2,1)S(1)}, u32[]{:S(2)}, u32[]{:S(2)}) collective-permute-start(bf16[2,32,1792]{2,1,0:T(8,128)(2,1)S(1)} %get-tuple-element.52), channel_id=1, source_target_pairs={{0,224},{32,128},{64,160},{96,192},{128,96},{160,0},{192,32},{224,... | collective-permute-start | bytes 688136 | tf_op jit(solution)/shard_map/ppermute | solution.py:249
  82.4 10.4 %collective-permute-start.12 = (bf16[1,32,1792]{2,1,0:T(8,128)(2,1)S(1)}, bf16[1,32,1792]{2,1,0:T(8,128)(2,1)S(1)}, u32[]{:S(2)}, u32[]{:S(2)}) collective-permute-start(bf16[1,32,1792]{2,1,0:T(8,128)(2,1)S(1)} %get-tuple-element.56), channel_id=1, source_target_pairs={{0,32},{32,64},{64,96},{96,0},{128,160},{160,192},{192,224},{224,1... | collective-permute-start | bytes 344072 | tf_op jit(solution)/shard_map/ppermute | solution.py:249
  84.1 10.8 %collective-permute-start.13 = (bf16[1,32,1792]{2,1,0:T(8,128)(2,1)S(1)}, bf16[1,32,1792]{2,1,0:T(8,128)(2,1)S(1)}, u32[]{:S(2)}, u32[]{:S(2)}) collective-permute-start(bf16[1,32,1792]{2,1,0:T(8,128)(2,1)S(1)} %get-tuple-element.57), channel_id=1, source_target_pairs={{0,64},{32,96},{64,0},{96,32},{128,192},{160,224},{192,128},{224,1... | collective-permute-start | bytes 344072 | tf_op jit(solution)/shard_map/ppermute | solution.py:249
  87.2 11.2 %collective-permute-start.14 = (bf16[1,32,1792]{2,1,0:T(8,128)(2,1)S(1)}, bf16[1,32,1792]{2,1,0:T(8,128)(2,1)S(1)}, u32[]{:S(2)}, u32[]{:S(2)}) collective-permute-start(bf16[1,32,1792]{2,1,0:T(8,128)(2,1)S(1)} %get-tuple-element.58), channel_id=1, source_target_pairs={{0,96},{32,0},{64,32},{96,64},{128,224},{160,128},{192,160},{224,1... | collective-permute-start | bytes 344072 | tf_op jit(solution)/shard_map/ppermute | solution.py:249
  89.1 9.4 %collective-permute-start.15 = (bf16[1,32,1792]{2,1,0:T(8,128)(2,1)S(1)}, bf16[1,32,1792]{2,1,0:T(8,128)(2,1)S(1)}, u32[]{:S(2)}, u32[]{:S(2)}) collective-permute-start(bf16[1,32,1792]{2,1,0:T(8,128)(2,1)S(1)} %get-tuple-element.59), channel_id=1, source_target_pairs={{0,128},{32,160},{64,192},{96,224},{128,0},{160,32},{192,64},{224,... | collective-permute-start | bytes 344072 | tf_op jit(solution)/shard_map/ppermute | solution.py:249
  92.7 6.4 %collective-permute-start.16 = (bf16[1,32,1792]{2,1,0:T(8,128)(2,1)S(1)}, bf16[1,32,1792]{2,1,0:T(8,128)(2,1)S(1)}, u32[]{:S(2)}, u32[]{:S(2)}) collective-permute-start(bf16[1,32,1792]{2,1,0:T(8,128)(2,1)S(1)} %get-tuple-element.60), channel_id=1, source_target_pairs={{0,160},{32,192},{64,224},{96,128},{128,32},{160,64},{192,96},{224... | collective-permute-start | bytes 344072 | tf_op jit(solution)/shard_map/ppermute | solution.py:249
  92.7 7.4 %collective-permute-start.17 = (bf16[1,32,1792]{2,1,0:T(8,128)(2,1)S(1)}, bf16[1,32,1792]{2,1,0:T(8,128)(2,1)S(1)}, u32[]{:S(2)}, u32[]{:S(2)}) collective-permute-start(bf16[1,32,1792]{2,1,0:T(8,128)(2,1)S(1)} %get-tuple-element.61), channel_id=1, source_target_pairs={{0,192},{32,224},{64,128},{96,160},{128,64},{160,96},{192,0},{224,... | collective-permute-start | bytes 344072 | tf_op jit(solution)/shard_map/ppermute | solution.py:249
  94.9 7.1 %collective-permute-start.18 = (bf16[1,32,1792]{2,1,0:T(8,128)(2,1)S(1)}, bf16[1,32,1792]{2,1,0:T(8,128)(2,1)S(1)}, u32[]{:S(2)}, u32[]{:S(2)}) collective-permute-start(bf16[1,32,1792]{2,1,0:T(8,128)(2,1)S(1)} %get-tuple-element.62), channel_id=1, source_target_pairs={{0,224},{32,128},{64,160},{96,192},{128,96},{160,0},{192,32},{224,... | collective-permute-start | bytes 344072 | tf_op jit(solution)/shard_map/ppermute | solution.py:249
  102.4 7.3 %collective-permute-start.19 = (bf16[3,32,1792]{2,1,0:T(8,128)(2,1)S(1)}, bf16[3,32,1792]{2,1,0:T(8,128)(2,1)S(1)}, u32[]{:S(2)}, u32[]{:S(2)}) collective-permute-start(bf16[3,32,1792]{2,1,0:T(8,128)(2,1)S(1)} %shard_map.122.refs_0_), channel_id=1, source_target_pairs={{0,128},{128,0},{1,129},{129,1},{2,130},{130,2},{3,131},{131,3},{4... | collective-permute-start | bytes 1032200 | tf_op jit(solution)/shard_map/ppermute | solution.py:285
  103.1 11.8 %collective-permute-start.20 = (bf16[3,32,1792]{2,1,0:T(8,128)(2,1)S(1)}, bf16[3,32,1792]{2,1,0:T(8,128)(2,1)S(1)}, u32[]{:S(2)}, u32[]{:S(2)}) collective-permute-start(bf16[3,32,1792]{2,1,0:T(8,128)(2,1)S(1)} %shard_map.122.refs_0_), channel_id=1, source_target_pairs={{0,96},{32,0},{64,32},{96,64},{1,97},{33,1},{65,33},{97,65},{2,98}... | collective-permute-start | bytes 1032200 | tf_op jit(solution)/shard_map/ppermute | solution.py:278
  106.5 11.0 %collective-permute-start.21 = (bf16[3,32,1792]{2,1,0:T(8,128)(2,1)S(1)}, bf16[3,32,1792]{2,1,0:T(8,128)(2,1)S(1)}, u32[]{:S(2)}, u32[]{:S(2)}) collective-permute-start(bf16[3,32,1792]{2,1,0:T(8,128)(2,1)S(1)} %shard_map.122.refs_0_), channel_id=1, source_target_pairs={{0,32},{32,64},{64,96},{96,0},{1,33},{33,65},{65,97},{97,1},{2,34}... | collective-permute-start | bytes 1032200 | tf_op jit(solution)/shard_map/ppermute | solution.py:281
  109.8 11.6 %collective-permute-start.22 = (bf16[3,32,1792]{2,1,0:T(8,128)(2,1)S(1)}, bf16[3,32,1792]{2,1,0:T(8,128)(2,1)S(1)}, u32[]{:S(2)}, u32[]{:S(2)}) collective-permute-start(bf16[3,32,1792]{2,1,0:T(8,128)(2,1)S(1)} %collective-permute-done.19.refs_1_), channel_id=1, source_target_pairs={{0,96},{32,0},{64,32},{96,64},{1,97},{33,1},{65,33},{97,65},{2,98}... | collective-permute-start | bytes 1032200 | tf_op jit(solution)/shard_map/ppermute | solution.py:278
  112.3 11.7 %collective-permute-start.23 = (bf16[3,32,1792]{2,1,0:T(8,128)(2,1)S(1)}, bf16[3,32,1792]{2,1,0:T(8,128)(2,1)S(1)}, u32[]{:S(2)}, u32[]{:S(2)}) collective-permute-start(bf16[3,32,1792]{2,1,0:T(8,128)(2,1)S(1)} %collective-permute-done.19.refs_1_), channel_id=1, source_target_pairs={{0,32},{32,64},{64,96},{96,0},{1,33},{33,65},{65,97},{97,1},{2,34}... | collective-permute-start | bytes 1032200 | tf_op jit(solution)/shard_map/ppermute | solution.py:281
  114.9 15.3 %collective-permute-start.24 = (bf16[3,32,896]{2,1,0:T(8,128)(2,1)S(1)}, bf16[3,32,896]{2,1,0:T(8,128)(2,1)S(1)}, u32[]{:S(2)}, u32[]{:S(2)}) collective-permute-start(bf16[3,32,896]{2,1,0:T(8,128)(2,1)S(1)} %slice.32), channel_id=1, source_target_pairs={{0,96},{32,0},{64,32},{96,64},{1,97},{33,1},{65,33},{97,65},{2,98}... | collective-permute-start | bytes 516104 | tf_op jit(solution)/shard_map/ppermute | solution.py:278
  117.5 12.8 %collective-permute-start.25 = (bf16[3,32,896]{2,1,0:T(8,128)(2,1)S(1)}, bf16[3,32,896]{2,1,0:T(8,128)(2,1)S(1)}, u32[]{:S(2)}, u32[]{:S(2)}) collective-permute-start(bf16[3,32,896]{2,1,0:T(8,128)(2,1)S(1)} %slice.33), channel_id=1, source_target_pairs={{0,32},{32,64},{64,96},{96,0},{1,33},{33,65},{65,97},{97,1},{2,34}... | collective-permute-start | bytes 516104 | tf_op jit(solution)/shard_map/ppermute | solution.py:281
  121.4 8.9 %collective-permute-start.26 = (bf16[3,32,896]{2,1,0:T(8,128)(2,1)S(1)}, bf16[3,32,896]{2,1,0:T(8,128)(2,1)S(1)}, u32[]{:S(2)}, u32[]{:S(2)}) collective-permute-start(bf16[3,32,896]{2,1,0:T(8,128)(2,1)S(1)} %slice.34), channel_id=1, source_target_pairs={{0,96},{32,0},{64,32},{96,64},{1,97},{33,1},{65,33},{97,65},{2,98}... | collective-permute-start | bytes 516104 | tf_op jit(solution)/shard_map/ppermute | solution.py:278
  124.0 6.3 %collective-permute-start.27 = (bf16[3,32,896]{2,1,0:T(8,128)(2,1)S(1)}, bf16[3,32,896]{2,1,0:T(8,128)(2,1)S(1)}, u32[]{:S(2)}, u32[]{:S(2)}) collective-permute-start(bf16[3,32,896]{2,1,0:T(8,128)(2,1)S(1)} %slice.35), channel_id=1, source_target_pairs={{0,32},{32,64},{64,96},{96,0},{1,33},{33,65},{65,97},{97,1},{2,34}... | collective-permute-start | bytes 516104 | tf_op jit(solution)/shard_map/ppermute | solution.py:281
  130.2 1.7 copy-start.3
  130.2 3.8 %collective-permute-start.28 = (bf16[128,1024]{1,0:T(8,128)(2,1)S(1)}, bf16[128,1024]{1,0:T(8,128)(2,1)S(1)}, u32[]{:S(2)}, u32[]{:S(2)}) collective-permute-start(bf16[128,1024]{1,0:T(8,128)(2,1)S(1)} %get-tuple-element.71), channel_id=1, source_target_pairs={{0,16},{16,0},{1,17},{17,1},{2,18},{18,2},{3,19},{19,3},{4,20},{20... | collective-permute-start | bytes 786440 | tf_op jit(solution)/shard_map/ppermute | solution.py:213
  131.9 2.1 %collective-permute-start.29 = (bf16[128,1024]{1,0:T(8,128)(2,1)S(1)}, bf16[128,1024]{1,0:T(8,128)(2,1)S(1)}, u32[]{:S(2)}, u32[]{:S(2)}) collective-permute-start(bf16[128,1024]{1,0:T(8,128)(2,1)S(1)} %get-tuple-element.72), channel_id=1, source_target_pairs={{0,16},{16,0},{1,17},{17,1},{2,18},{18,2},{3,19},{19,3},{4,20},{20... | collective-permute-start | bytes 786440 | tf_op jit(solution)/shard_map/ppermute | solution.py:213
  135.6 35.0 %all-to-all-start.2 = ((bf16[16,32,1024]{2,1,0:T(8,128)(2,1)}), bf16[16,32,1024]{2,1,0:T(8,128)(2,1)}, u32[]{:S(2)}, u32[]{:S(2)}) async-start(bf16[16,32,1024]{2,1,0:T(8,128)(2,1)} %shard_map.126), calls=%async_computation.2 | async-start | bytes 2097152 | tf_op jit(solution)/shard_map/all_to_all | solution.py:328
  141.4 3.6 %collective-permute-start.30 = (bf16[3,128,1792]{2,1,0:T(8,128)(2,1)}, bf16[3,128,1792]{2,1,0:T(8,128)(2,1)}, u32[]{:S(2)}, u32[]{:S(2)}) collective-permute-start(bf16[3,128,1792]{2,1,0:T(8,128)(2,1)} %copy-done.3), channel_id=1, source_target_pairs={{0,16},{16,0},{1,17},{17,1},{2,18},{18,2},{3,19},{19,3},{4,20},{20... | collective-permute-start | bytes 4128776 | tf_op jit(solution)/shard_map/ppermute | solution.py:213
  141.6 5.4 %collective-permute-start.31 = (bf16[3,128,1792]{2,1,0:T(8,128)(2,1)S(1)}, bf16[3,128,1792]{2,1,0:T(8,128)(2,1)}, u32[]{:S(2)}, u32[]{:S(2)}) collective-permute-start(bf16[3,128,1792]{2,1,0:T(8,128)(2,1)S(1)} %get-tuple-element.75.acts.refs_1_), channel_id=1, source_target_pairs={{0,16},{16,0},{1,17},{17,1},{2,18},{18,2},{3,19},{19,3},{4,20},{20... | collective-permute-start | bytes 4128776 | tf_op jit(solution)/shard_map/ppermute | solution.py:213
  146.9 1.3 copy-start.4

commit v8 on v7

--- a/solution.py
+++ b/solution.py
@@ -93,19 +93,27 @@
     )
 
 
-def activation_kernel(*refs):
-    got, got_back, out = refs[:8], refs[8:16], refs[16]
+def total(group, part, cols):
+    acc = group[0][part, :, cols]
+    for ref in group[1:]:
+        acc = acc + ref[part, :, cols].astype(F32)
+    return acc
+
+
+def sum_kernel(*refs):
+    got, out = refs[:-1], refs[-1]
+    for part in range(out.shape[0]):
+        for j in range(out.shape[2] // STEP):
+            cols = pl.ds(j * STEP, STEP)
+            out[part, :, cols] = total(got, part, cols)
+
+
+def activation_kernel(forward, *refs):
+    got_back, out = refs[:-1], refs[-1]
     hid = out.shape[2]
-
-    def total(group, part, cols):
-        acc = group[0][part, :, cols]
-        for ref in group[1:]:
-            acc = acc + ref[part, :, cols].astype(F32)
-        return acc
-
     for j in range(hid // STEP):
         cols = pl.ds(j * STEP, STEP)
-        gate, up, d_hidden = total(got, 0, cols), total(got, 1, cols), total(got_back, 0, cols)
+        gate, up, d_hidden = forward[0, :, cols], forward[1, :, cols], total(got_back, 0, cols)
         sigmoid = jax.nn.sigmoid(gate)
         activated = gate * sigmoid
         out[0, :, cols] = (activated * up).astype(BF)
@@ -174,6 +182,21 @@
                 rows = pl.ds((2 * i + k) * half, half)
                 send[2 * place[r] + k, :half, :] = here[rows, :]
                 send[2 * place[r] + k, half:, :] = away[rows, :]
+
+
+def finish_kernel(place, arrived, *outs):
+    half = arrived.shape[1] // 2
+    width = outs[0].shape[1]
+    starts = (place[0] * half, (1 - place[0]) * half)
+    for which, out in enumerate(outs):
+        for j in range(width // STEP):
+            cols = pl.ds(which * width + j * STEP, STEP)
+            acc = arrived[0, :, cols].astype(F32)
+            for i in range(1, arrived.shape[0]):
+                acc = acc + arrived[i, :, cols].astype(F32)
+            for k, start in enumerate(starts):
+                rows = pl.ds(pl.multiple_of(start, half), half)
+                out[rows, pl.ds(j * STEP, STEP)] = acc[k * half : (k + 1) * half].astype(BF)
 
 
 def gradient_kernel(place, *refs):
@@ -229,10 +252,11 @@
         [(x_lo ^ (r // y_n)) * y_n + (y + r % y_n) % y_n for r in range(pairs)]
     ).astype(jnp.int32)
 
+    def copies(array):
+        return jnp.broadcast_to(array, (cols,) + array.shape)
+
     def gather(array):
-        return lax.all_to_all(
-            jnp.broadcast_to(array, (cols,) + array.shape), COL, 0, 0, tiled=True
-        )
+        return lax.all_to_all(array, COL, 0, 0, tiled=True)
 
     def by_core(gathered):
         own = lax.dynamic_slice_in_dim(gathered, core * half, half, 1)
@@ -249,7 +273,7 @@
             got[r] = lax.ppermute(parts[r], PAIR, moves)
         return [got[r] for r in range(pairs)]
 
-    gathered = gather(tokens)
+    gathered = gather(copies(tokens))
     weights = (gate_weight, up_weight, down_weight)
     shapes = [jax.ShapeDtypeStruct(weight.shape, BF) for weight in weights]
     wide = [
@@ -258,7 +282,7 @@
     effs = local_call(prepare_kernel, 20, shapes, *weights, *wide)
     effs_x = [swap(eff) for eff in effs]
 
-    gathered, cot_in = lax.optimization_barrier((gathered, cotangent))
+    gathered, cot_in = lax.optimization_barrier((gathered, copies(cotangent)))
     gathered_cot = gather(cot_in)
     own, other = by_core(gathered)
     parts = partial_sums(place, own, swap(other), effs[:2], effs_x[:2], nn)
@@ -266,11 +290,12 @@
     own_cot, other_cot = by_core(gathered_cot)
     back = partial_sums(place, own_cot, swap(other_cot), effs[2:], effs_x[2:], nt)
     got_back = spread(back)
+    forward = local_call(sum_kernel, 12, jax.ShapeDtypeStruct(parts[0].shape, F32), *got)
     mine = local_call(
         activation_kernel,
         12,
         jax.ShapeDtypeStruct((3, parts[0].shape[1], hid), BF),
-        *got,
+        forward,
         *got_back,
     )
 
@@ -326,12 +351,13 @@
         place=place,
     )
     arrived = lax.all_to_all(send, COL, 0, 0, tiled=True)
-    sums = jnp.sum(arrived.astype(F32), axis=0)
-    first, second = sums[:half], sums[half:]
-    sums = jnp.concatenate(
-        [jnp.where(core == 0, first, second), jnp.where(core == 0, second, first)], axis=0
-    ).astype(BF)
-    output, d_tokens = sums[:, :width], sums[:, width:]
+    output, d_tokens = local_call(
+        finish_kernel,
+        8,
+        [jax.ShapeDtypeStruct(tokens.shape, BF)] * 2,
+        arrived,
+        place=core.reshape(1),
+    )
 
     send, early, late = lax.optimization_barrier((send, early, late))
     grad_gate, grad_up, grad_down = local_call(

time: 176 us -> 175 us (level)
  other arithmetic: 4.09 us -> 2.06 us
    unnamed x16 -> x24, local copies, waits for them, and re-layouts: 6 us -> 6.97 us
    pallas_call x9 -> x11, Pallas kernels: 28.8 us -> 28.3 us  [local_call(): pl.pallas_call(kernel, out_shape=outs, in_specs=[pl.BlockSpec(memory_spac...]
  transfers between devices with their start and end apart: 35 -> 35, of which waited for: 13 -> 14; matrix products, arithmetic and copies ran while one was open for 3% -> 3% of each run, Pallas kernels for 15% -> 15%
where the time goes in v8:
time: 175 us; the launch traced here: 172 us
  starting transfers between devices  65.4 us (37%)
  waiting for transfers between devices  63.8 us (36%)
  Pallas kernels  28.3 us (16%)
  local copies, waits for them, and re-layouts  10.9 us (6%)
  other arithmetic  2.06 us (1%)
    ppermute x14, starting transfers between devices, spread(): got[r] = lax.ppermute(parts[r], PAIR, moves)  30.1 us
    pallas_call x11, Pallas kernels, local_call(): pl.pallas_call(kernel, out_shape=outs, in_specs=[pl.BlockSpec(memory_spac...  28.3 us
    all_to_all x2, waiting for transfers between devices, gather(): return lax.all_to_all(array, COL, 0, 0, tiled=True)  23.9 us
    all_to_all x1, waiting for transfers between devices, layer(): arrived = lax.all_to_all(send, COL, 0, 0, tiled=True)  15.8 us
    all_to_all x2, starting transfers between devices, gather(): return lax.all_to_all(array, COL, 0, 0, tiled=True)  15.7 us
    ppermute x4, starting transfers between devices, from_up(): return lax.ppermute(array, 'y', [(i, (i - 1) % y_n) for i in range(y_n)])  11 us
    ppermute x14, waiting for transfers between devices, spread(): got[r] = lax.ppermute(parts[r], PAIR, moves)  9.36 us
    unnamed x24, local copies, waits for them, and re-layouts  6.97 us
  transfers between devices with their start and end apart: 35, of which 14 were waited for; matrix products, arithmetic and copies ran while one was open for 3% of the time, Pallas kernels for 15%

profile of v8, /device:TPU:8, one launch (start us, length us, event | category | flops | bytes accessed | tf_op | source)
XLA Modules:
  0.0 171.5 jit_solution(4242804489783519868)
XLA Ops:
  0.6 1.6 broadcast_in_dim.15
  2.2 11.0 %all-to-all-start = ((bf16[16,32,512]{2,1,0:T(8,128)(2,1)}), bf16[16,32,512]{2,1,0:T(8,128)(2,1)S(1)}, u32[]{:S(2)}, u32[]{:S(2)}) async-start(bf16[16,32,512]{2,1,0:T(8,128)(2,1)} %broadcast_in_dim.15), calls=%async_computation | async-start | bytes 1048576 | tf_op jit(solution)/shard_map/all_to_all | solution.py:259
  14.8 0.7 convert_element_type.11
  15.7 1.5 copy-done
  17.2 1.5 copy-done.1
  18.7 1.5 copy-done.2
  20.2 2.2 %shard_map.119 = (bf16[512,1792]{1,0:T(8,128)(2,1)}, bf16[512,1792]{1,0:T(8,128)(2,1)}, bf16[1792,512]{1,0:T(8,128)(2,1)S(1)}) custom-call(bf16[512,1792]{1,0:T(8,128)(2,1)S(1)} %copy-done, bf16[512,1792]{1,0:T(8,128)(2,1)S(1)} %copy-done.1, bf16[1792,512]{1,0:T(8,128)(2,1)S(1)} %copy-done.2, f32[4,1792]{1,0:T(4,128)S(1)} %get-tuple-element.88.refs_3_.refs_8_, ...), custom_call_target="tpu_custom_call" | custom-call | tf_op jit(solution)/shard_map/pallas_call | solution.py:24
  23.0 7.5 %all-to-all-done = bf16[16,32,512]{2,1,0:T(8,128)(2,1)S(1)} async-done(((bf16[16,32,512]{2,1,0:T(8,128)(2,1)}), bf16[16,32,512]{2,1,0:T(8,128)(2,1)S(1)}, u32[]{:S(2)}, u32[]{:S(2)}) %all-to-all-start) | async-done | bytes 524320 | tf_op jit(solution)/shard_map/all_to_all | solution.py:259
  30.4 0.8 broadcast_in_dim.16
  31.3 4.6 %all-to-all-start.1 = ((bf16[16,32,512]{2,1,0:T(8,128)(2,1)}), bf16[16,32,512]{2,1,0:T(8,128)(2,1)}, u32[]{:S(2)}, u32[]{:S(2)}) async-start(bf16[16,32,512]{2,1,0:T(8,128)(2,1)} %broadcast_in_dim.16), calls=%async_computation.1 | async-start | bytes 1048576 | tf_op jit(solution)/shard_map/all_to_all | solution.py:259
  36.1 16.4 %all-to-all-done.1 = bf16[16,32,512]{2,1,0:T(8,128)(2,1)} async-done(((bf16[16,32,512]{2,1,0:T(8,128)(2,1)}), bf16[16,32,512]{2,1,0:T(8,128)(2,1)}, u32[]{:S(2)}, u32[]{:S(2)}) %all-to-all-start.1) | async-done | bytes 524320 | tf_op jit(solution)/shard_map/all_to_all | solution.py:259
  52.5 1.1 constant_dynamic-slice_fusion
  53.8 5.1 %shard_map.120 = (f32[2,32,1792]{2,1,0:T(8,128)S(1)}, bf16[2,32,1792]{2,1,0:T(8,128)(2,1)S(1)}, bf16[2,32,1792]{2,1,0:T(8,128)(2,1)S(1)}, bf16[2,32,1792]{2,1,0:...) custom-call(s32[8]{0:T(128)S(1)} %stack.35.place, ...), custom_call_target="tpu_custom_call" | custom-call | tf_op jit(solution)/shard_map/pallas_call | solution.py:24
  59.0 1.7 collective-permute-start.3
  60.6 0.9 collective-permute-start.4
  61.6 2.4 %collective-permute-start.5 = (bf16[2,32,1792]{2,1,0:T(8,128)(2,1)S(1)}, bf16[2,32,1792]{2,1,0:T(8,128)(2,1)S(1)}, u32[]{:S(2)}, u32[]{:S(2)}) collective-permute-start(bf16[2,32,1792]{2,1,0:T(8,128)(2,1)S(1)} %get-tuple-element.50), channel_id=1, source_target_pairs={{0,96},{32,0},{64,32},{96,64},{128,224},{160,128},{192,160},{224,1... | collective-permute-start | bytes 688136 | tf_op jit(solution)/shard_map/ppermute | solution.py:273
  64.6 3.0 %collective-permute-done.3.refs_1_ = bf16[2,32,1792]{2,1,0:T(8,128)(2,1)S(1)} collective-permute-done((bf16[2,32,1792]{2,1,0:T(8,128)(2,1)S(1)}, bf16[2,32,1792]{2,1,0:T(8,128)(2,1)S(1)}, u32[]{:S(2)}, u32[]{:S(2)}) %collective-permute-start.3) | collective-permute-done | bytes 229408 | tf_op jit(solution)/shard_map/ppermute | solution.py:273
  67.5 8.5 %collective-permute-start.7 = (bf16[2,32,1792]{2,1,0:T(8,128)(2,1)S(1)}, bf16[2,32,1792]{2,1,0:T(8,128)(2,1)S(1)}, u32[]{:S(2)}, u32[]{:S(2)}) collective-permute-start(bf16[2,32,1792]{2,1,0:T(8,128)(2,1)S(1)} %get-tuple-element.52), channel_id=1, source_target_pairs={{0,160},{32,192},{64,224},{96,128},{128,32},{160,64},{192,96},{224... | collective-permute-start | bytes 688136 | tf_op jit(solution)/shard_map/ppermute | solution.py:273
  76.0 3.1 %collective-permute-start.9 = (bf16[2,32,1792]{2,1,0:T(8,128)(2,1)S(1)}, bf16[2,32,1792]{2,1,0:T(8,128)(2,1)S(1)}, u32[]{:S(2)}, u32[]{:S(2)}) collective-permute-start(bf16[2,32,1792]{2,1,0:T(8,128)(2,1)S(1)} %get-tuple-element.54), channel_id=1, source_target_pairs={{0,224},{32,128},{64,160},{96,192},{128,96},{160,0},{192,32},{224,... | collective-permute-start | bytes 688136 | tf_op jit(solution)/shard_map/ppermute | solution.py:273
  79.1 3.3 %shard_map.122 = (f32[1,32,1792]{2,1,0:T(8,128)S(1)}, bf16[1,32,1792]{2,1,0:T(8,128)(2,1)S(1)}, bf16[1,32,1792]{2,1,0:T(8,128)(2,1)S(1)}, bf16[1,32,1792]{2,1,0:...) custom-call(s32[8]{0:T(128)S(1)} %stack.35.place, ...), custom_call_target="tpu_custom_call" | custom-call | tf_op jit(solution)/shard_map/pallas_call | solution.py:24
  82.4 1.7 collective-permute-start.12
  84.1 3.1 %collective-permute-start.13 = (bf16[1,32,1792]{2,1,0:T(8,128)(2,1)S(1)}, bf16[1,32,1792]{2,1,0:T(8,128)(2,1)S(1)}, u32[]{:S(2)}, u32[]{:S(2)}) collective-permute-start(bf16[1,32,1792]{2,1,0:T(8,128)(2,1)S(1)} %get-tuple-element.59), channel_id=1, source_target_pairs={{0,64},{32,96},{64,0},{96,32},{128,192},{160,224},{192,128},{224,1... | collective-permute-start | bytes 344072 | tf_op jit(solution)/shard_map/ppermute | solution.py:273
  87.3 1.8 %collective-permute-start.14 = (bf16[1,32,1792]{2,1,0:T(8,128)(2,1)S(1)}, bf16[1,32,1792]{2,1,0:T(8,128)(2,1)S(1)}, u32[]{:S(2)}, u32[]{:S(2)}) collective-permute-start(bf16[1,32,1792]{2,1,0:T(8,128)(2,1)S(1)} %get-tuple-element.60), channel_id=1, source_target_pairs={{0,96},{32,0},{64,32},{96,64},{128,224},{160,128},{192,160},{224,1... | collective-permute-start | bytes 344072 | tf_op jit(solution)/shard_map/ppermute | solution.py:273
  89.7 3.1 %collective-permute-done.9.refs_7_ = bf16[2,32,1792]{2,1,0:T(8,128)(2,1)S(1)} collective-permute-done((bf16[2,32,1792]{2,1,0:T(8,128)(2,1)S(1)}, bf16[2,32,1792]{2,1,0:T(8,128)(2,1)S(1)}, u32[]{:S(2)}, u32[]{:S(2)}) %collective-permute-start.9) | collective-permute-done | bytes 229408 | tf_op jit(solution)/shard_map/ppermute | solution.py:273
  92.8 2.2 %collective-permute-start.17 = (bf16[1,32,1792]{2,1,0:T(8,128)(2,1)S(1)}, bf16[1,32,1792]{2,1,0:T(8,128)(2,1)S(1)}, u32[]{:S(2)}, u32[]{:S(2)}) collective-permute-start(bf16[1,32,1792]{2,1,0:T(8,128)(2,1)S(1)} %get-tuple-element.63), channel_id=1, source_target_pairs={{0,192},{32,224},{64,128},{96,160},{128,64},{160,96},{192,0},{224,... | collective-permute-start | bytes 344072 | tf_op jit(solution)/shard_map/ppermute | solution.py:273
  95.0 3.5 %collective-permute-start.18 = (bf16[1,32,1792]{2,1,0:T(8,128)(2,1)S(1)}, bf16[1,32,1792]{2,1,0:T(8,128)(2,1)S(1)}, u32[]{:S(2)}, u32[]{:S(2)}) collective-permute-start(bf16[1,32,1792]{2,1,0:T(8,128)(2,1)S(1)} %get-tuple-element.64), channel_id=1, source_target_pairs={{0,224},{32,128},{64,160},{96,192},{128,96},{160,0},{192,32},{224,... | collective-permute-start | bytes 344072 | tf_op jit(solution)/shard_map/ppermute | solution.py:273
  99.2 1.1 collective-permute-done.17.refs_6_
  100.3 1.8 %collective-permute-done.18.refs_7_ = bf16[1,32,1792]{2,1,0:T(8,128)(2,1)S(1)} collective-permute-done((bf16[1,32,1792]{2,1,0:T(8,128)(2,1)S(1)}, bf16[1,32,1792]{2,1,0:T(8,128)(2,1)S(1)}, u32[]{:S(2)}, u32[]{:S(2)}) %collective-permute-start.18) | collective-permute-done | bytes 114720 | tf_op jit(solution)/shard_map/ppermute | solution.py:273
  102.2 0.7 collective-permute-start.19
  103.0 3.3 %collective-permute-start.20 = (bf16[3,32,1792]{2,1,0:T(8,128)(2,1)S(1)}, bf16[3,32,1792]{2,1,0:T(8,128)(2,1)S(1)}, u32[]{:S(2)}, u32[]{:S(2)}) collective-permute-start(bf16[3,32,1792]{2,1,0:T(8,128)(2,1)S(1)} %shard_map.123.refs_0_), channel_id=1, source_target_pairs={{0,96},{32,0},{64,32},{96,64},{1,97},{33,1},{65,33},{97,65},{2,98}... | collective-permute-start | bytes 1032200 | tf_op jit(solution)/shard_map/ppermute | solution.py:303
  106.3 3.3 %collective-permute-done.19.refs_1_ = bf16[3,32,1792]{2,1,0:T(8,128)(2,1)S(1)} collective-permute-done((bf16[3,32,1792]{2,1,0:T(8,128)(2,1)S(1)}, bf16[3,32,1792]{2,1,0:T(8,128)(2,1)S(1)}, u32[]{:S(2)}, u32[]{:S(2)}) %collective-permute-start.19) | collective-permute-done | bytes 344096 | tf_op jit(solution)/shard_map/ppermute | solution.py:310
  109.6 2.5 %collective-permute-start.22 = (bf16[3,32,1792]{2,1,0:T(8,128)(2,1)S(1)}, bf16[3,32,1792]{2,1,0:T(8,128)(2,1)S(1)}, u32[]{:S(2)}, u32[]{:S(2)}) collective-permute-start(bf16[3,32,1792]{2,1,0:T(8,128)(2,1)S(1)} %collective-permute-done.19.refs_1_), channel_id=1, source_target_pairs={{0,96},{32,0},{64,32},{96,64},{1,97},{33,1},{65,33},{97,65},{2,98}... | collective-permute-start | bytes 1032200 | tf_op jit(solution)/shard_map/ppermute | solution.py:303
  112.1 2.6 %collective-permute-done.20.refs_2_ = bf16[3,32,1792]{2,1,0:T(8,128)(2,1)S(1)} collective-permute-done((bf16[3,32,1792]{2,1,0:T(8,128)(2,1)S(1)}, bf16[3,32,1792]{2,1,0:T(8,128)(2,1)S(1)}, u32[]{:S(2)}, u32[]{:S(2)}) %collective-permute-start.20) | collective-permute-done | bytes 344096 | tf_op jit(solution)/shard_map/ppermute | solution.py:303
  114.8 2.6 %collective-permute-start.24 = (bf16[3,32,896]{2,1,0:T(8,128)(2,1)S(1)}, bf16[3,32,896]{2,1,0:T(8,128)(2,1)S(1)}, u32[]{:S(2)}, u32[]{:S(2)}) collective-permute-start(bf16[3,32,896]{2,1,0:T(8,128)(2,1)S(1)} %slice.16), channel_id=1, source_target_pairs={{0,96},{32,0},{64,32},{96,64},{1,97},{33,1},{65,33},{97,65},{2,98}... | collective-permute-start | bytes 516104 | tf_op jit(solution)/shard_map/ppermute | solution.py:303
  117.4 4.0 %collective-permute-done.22.refs_0_ = bf16[3,32,1792]{2,1,0:T(8,128)(2,1)S(1)} collective-permute-done((bf16[3,32,1792]{2,1,0:T(8,128)(2,1)S(1)}, bf16[3,32,1792]{2,1,0:T(8,128)(2,1)S(1)}, u32[]{:S(2)}, u32[]{:S(2)}) %collective-permute-start.22) | collective-permute-done | bytes 344096 | tf_op jit(solution)/shard_map/ppermute | solution.py:303
  121.4 2.6 %collective-permute-start.26 = (bf16[3,32,896]{2,1,0:T(8,128)(2,1)S(1)}, bf16[3,32,896]{2,1,0:T(8,128)(2,1)S(1)}, u32[]{:S(2)}, u32[]{:S(2)}) collective-permute-start(bf16[3,32,896]{2,1,0:T(8,128)(2,1)S(1)} %slice.18), channel_id=1, source_target_pairs={{0,96},{32,0},{64,32},{96,64},{1,97},{33,1},{65,33},{97,65},{2,98}... | collective-permute-start | bytes 516104 | tf_op jit(solution)/shard_map/ppermute | solution.py:303
  124.4 5.8 %shard_map.124 = (bf16[3,128,1792]{2,1,0:T(8,128)(2,1)S(1)}, bf16[128,1024]{1,0:T(8,128)(2,1)S(1)}, bf16[128,1024]{1,0:T(8,128)(2,1)S(1)}, bf16[1792,512]{1,0:T(...) custom-call(bf16[3,32,1792]{2,1,0:T(8,128)(2,1)S(1)} %shard_map.123., ...), custom_call_target="tpu_custom_call" | custom-call | tf_op jit(solution)/shard_map/pallas_call | solution.py:24
  130.4 1.6 shard_map.125
  132.5 1.5 shard_map.126.here_late
  134.1 1.6 shard_map.127
  135.7 5.6 %all-to-all-start.2 = ((bf16[16,32,1024]{2,1,0:T(8,128)(2,1)}), bf16[16,32,1024]{2,1,0:T(8,128)(2,1)S(1)}, u32[]{:S(2)}, u32[]{:S(2)}) async-start(bf16[16,32,1024]{2,1,0:T(8,128)(2,1)} %shard_map.127), calls=%async_computation.2 | async-start | bytes 2097152 | tf_op jit(solution)/shard_map/all_to_all | solution.py:353
  142.0 2.8 %collective-permute-done.30.refs_2_ = bf16[3,128,1792]{2,1,0:T(8,128)(2,1)S(1)} collective-permute-done((bf16[3,128,1792]{2,1,0:T(8,128)(2,1)}, bf16[3,128,1792]{2,1,0:T(8,128)(2,1)S(1)}, u32[]{:S(2)}, u32[]{:S(2)}) %collective-permute-start.30) | collective-permute-done | bytes 1376288 | tf_op jit(solution)/shard_map/ppermute | solution.py:236
  144.8 2.0 %collective-permute-done.31.refs_3_ = bf16[3,128,1792]{2,1,0:T(8,128)(2,1)S(1)} collective-permute-done((bf16[3,128,1792]{2,1,0:T(8,128)(2,1)S(1)}, bf16[3,128,1792]{2,1,0:T(8,128)(2,1)S(1)}, u32[]{:S(2)}, u32[]{:S(2)}) %collective-permute-start.31) | collective-permute-done | bytes 1376288 | tf_op jit(solution)/shard_map/ppermute | solution.py:236
  146.8 1.3 copy-done.4
  148.1 0.9 copy-done.8
  149.1 5.9 %shard_map.129 = (bf16[512,1792]{1,0:T(8,128)(2,1)}, bf16[512,1792]{1,0:T(8,128)(2,1)}, bf16[1792,512]{1,0:T(8,128)(2,1)}) custom-call(s32[8]{0:T(128)S(1)} %stack.35.place, bf16[3,128,1792]{2,1,0:T(8,128)(2,1)S(1)} %copy-done.4, bf16[3,128,1792]{2,1,0:T(8,128)(2,1)S(1)} %get-tuple-element.79.acts.refs_1_, ...), custom_call_target="tpu_custom_call" | custom-call | tf_op jit(solution)/shard_map/pallas_call | solution.py:24
  155.0 15.8 %all-to-all-done.2.arrived = bf16[16,32,1024]{2,1,0:T(8,128)(2,1)S(1)} async-done(((bf16[16,32,1024]{2,1,0:T(8,128)(2,1)}), bf16[16,32,1024]{2,1,0:T(8,128)(2,1)S(1)}, u32[]{:S(2)}, u32[]{:S(2)}) %all-to-all-start.2) | async-done | bytes 1048608 | tf_op jit(solution)/shard_map/all_to_all | solution.py:353
  170.7 0.8 shard_map.128
  (72 shorter events, 6.5 us)
Async XLA Ops:
  2.2 28.2 %all-to-all-start = ((bf16[16,32,512]{2,1,0:T(8,128)(2,1)}), bf16[16,32,512]{2,1,0:T(8,128)(2,1)S(1)}, u32[]{:S(2)}, u32[]{:S(2)}) async-start(bf16[16,32,512]{2,1,0:T(8,128)(2,1)} %broadcast_in_dim.15), calls=%async_computation | async-start | bytes 1048576 | tf_op jit(solution)/shard_map/all_to_all | solution.py:259
  15.7 1.5 copy-start
  17.2 1.5 copy-start.1
  18.7 1.5 copy-start.2
  20.2 10.2 %copy-start.9 = (bf16[32,512]{1,0:T(8,128)(2,1)S(1)}, bf16[32,512]{1,0:T(8,128)(2,1)}, u32[]{:S(2)}) copy-start(bf16[32,512]{1,0:T(8,128)(2,1)} %param.9) | copy-start | bytes 98308
  22.4 31.4 %collective-permute-start.1 = (bf16[512,1792]{1,0:T(8,128)(2,1)}, bf16[512,1792]{1,0:T(8,128)(2,1)}, u32[]{:S(2)}, u32[]{:S(2)}) collective-permute-start(bf16[512,1792]{1,0:T(8,128)(2,1)} %get-tuple-element.45.refs_0_.refs_8_), channel_id=1, source_target_pairs={{0,16},{16,0},{1,17},{17,1},{2,18},{18,2},{3,19},{19,3},{4,20},{20... | collective-permute-start | bytes 5505032 | tf_op jit(solution)/shard_map/ppermute | solution.py:236
  22.4 31.4 %collective-permute-start.2 = (bf16[512,1792]{1,0:T(8,128)(2,1)}, bf16[512,1792]{1,0:T(8,128)(2,1)}, u32[]{:S(2)}, u32[]{:S(2)}) collective-permute-start(bf16[512,1792]{1,0:T(8,128)(2,1)} %get-tuple-element.46.refs_2_.refs_9_), channel_id=1, source_target_pairs={{0,16},{16,0},{1,17},{17,1},{2,18},{18,2},{3,19},{19,3},{4,20},{20... | collective-permute-start | bytes 5505032 | tf_op jit(solution)/shard_map/ppermute | solution.py:236
  23.0 41.0 %collective-permute-start.11 = (bf16[1792,512]{1,0:T(8,128)(2,1)S(1)}, bf16[1792,512]{1,0:T(8,128)(2,1)}, u32[]{:S(2)}, u32[]{:S(2)}) collective-permute-start(bf16[1792,512]{1,0:T(8,128)(2,1)S(1)} %get-tuple-element.56.refs_0_.refs_7_), channel_id=1, source_target_pairs={{0,16},{16,0},{1,17},{17,1},{2,18},{18,2},{3,19},{19,3},{4,20},{20... | collective-permute-start | bytes 5505032 | tf_op jit(solution)/shard_map/ppermute | solution.py:236
  31.3 21.2 %all-to-all-start.1 = ((bf16[16,32,512]{2,1,0:T(8,128)(2,1)}), bf16[16,32,512]{2,1,0:T(8,128)(2,1)}, u32[]{:S(2)}, u32[]{:S(2)}) async-start(bf16[16,32,512]{2,1,0:T(8,128)(2,1)} %broadcast_in_dim.16), calls=%async_computation.1 | async-start | bytes 1048576 | tf_op jit(solution)/shard_map/all_to_all | solution.py:259
  36.0 23.0 %copy-start.5 = (bf16[16,16,512]{2,1,0:T(8,128)(2,1)}, bf16[16,16,512]{2,1,0:T(8,128)(2,1)S(1)}, u32[]{:S(2)}) copy-start(bf16[16,16,512]{2,1,0:T(8,128)(2,1)S(1)} %get-tuple-element.85) | copy-start | bytes 786436
  36.0 17.8 %collective-permute-start = (bf16[256,512]{1,0:T(8,128)(2,1)S(1)}, bf16[256,512]{1,0:T(8,128)(2,1)S(1)}, u32[]{:S(2)}, u32[]{:S(2)}) collective-permute-start(bf16[256,512]{1,0:T(8,128)(2,1)S(1)} %bitcast.28), channel_id=1, source_target_pairs={{0,16},{16,0},{1,17},{17,1},{2,18},{18,2},{3,19},{19,3},{4,20},{20... | collective-permute-start | bytes 786440 | tf_op jit(solution)/shard_map/ppermute | solution.py:236
  53.6 5.4 %copy-start.7 = (bf16[16,16,512]{2,1,0:T(8,128)(2,1)}, bf16[16,16,512]{2,1,0:T(8,128)(2,1)S(1)}, u32[]{:S(2)}) copy-start(bf16[16,16,512]{2,1,0:T(8,128)(2,1)S(1)} %get-tuple-element.83) | copy-start | bytes 786436
  53.6 22.4 %collective-permute-start.10 = (bf16[256,512]{1,0:T(8,128)(2,1)S(1)}, bf16[256,512]{1,0:T(8,128)(2,1)S(1)}, u32[]{:S(2)}, u32[]{:S(2)}) collective-permute-start(bf16[256,512]{1,0:T(8,128)(2,1)S(1)} %bitcast.30), channel_id=1, source_target_pairs={{0,16},{16,0},{1,17},{17,1},{2,18},{18,2},{3,19},{19,3},{4,20},{20... | collective-permute-start | bytes 786440 | tf_op jit(solution)/shard_map/ppermute | solution.py:236
  59.0 8.6 %collective-permute-start.3 = (bf16[2,32,1792]{2,1,0:T(8,128)(2,1)S(1)}, bf16[2,32,1792]{2,1,0:T(8,128)(2,1)S(1)}, u32[]{:S(2)}, u32[]{:S(2)}) collective-permute-start(bf16[2,32,1792]{2,1,0:T(8,128)(2,1)S(1)} %get-tuple-element.48), channel_id=1, source_target_pairs={{0,32},{32,64},{64,96},{96,0},{128,160},{160,192},{192,224},{224,1... | collective-permute-start | bytes 688136 | tf_op jit(solution)/shard_map/ppermute | solution.py:273
  60.6 15.4 %collective-permute-start.4 = (bf16[2,32,1792]{2,1,0:T(8,128)(2,1)S(1)}, bf16[2,32,1792]{2,1,0:T(8,128)(2,1)S(1)}, u32[]{:S(2)}, u32[]{:S(2)}) collective-permute-start(bf16[2,32,1792]{2,1,0:T(8,128)(2,1)S(1)} %get-tuple-element.49), channel_id=1, source_target_pairs={{0,64},{32,96},{64,0},{96,32},{128,192},{160,224},{192,128},{224,1... | collective-permute-start | bytes 688136 | tf_op jit(solution)/shard_map/ppermute | solution.py:273
  61.6 20.8 %collective-permute-start.5 = (bf16[2,32,1792]{2,1,0:T(8,128)(2,1)S(1)}, bf16[2,32,1792]{2,1,0:T(8,128)(2,1)S(1)}, u32[]{:S(2)}, u32[]{:S(2)}) collective-permute-start(bf16[2,32,1792]{2,1,0:T(8,128)(2,1)S(1)} %get-tuple-element.50), channel_id=1, source_target_pairs={{0,96},{32,0},{64,32},{96,64},{128,224},{160,128},{192,160},{224,1... | collective-permute-start | bytes 688136 | tf_op jit(solution)/shard_map/ppermute | solution.py:273
  64.0 20.1 %collective-permute-start.6 = (bf16[2,32,1792]{2,1,0:T(8,128)(2,1)S(1)}, bf16[2,32,1792]{2,1,0:T(8,128)(2,1)S(1)}, u32[]{:S(2)}, u32[]{:S(2)}) collective-permute-start(bf16[2,32,1792]{2,1,0:T(8,128)(2,1)S(1)} %get-tuple-element.51), channel_id=1, source_target_pairs={{0,128},{32,160},{64,192},{96,224},{128,0},{160,32},{192,64},{224,... | collective-permute-start | bytes 688136 | tf_op jit(solution)/shard_map/ppermute | solution.py:273
  67.5 19.7 %collective-permute-start.7 = (bf16[2,32,1792]{2,1,0:T(8,128)(2,1)S(1)}, bf16[2,32,1792]{2,1,0:T(8,128)(2,1)S(1)}, u32[]{:S(2)}, u32[]{:S(2)}) collective-permute-start(bf16[2,32,1792]{2,1,0:T(8,128)(2,1)S(1)} %get-tuple-element.52), channel_id=1, source_target_pairs={{0,160},{32,192},{64,224},{96,128},{128,32},{160,64},{192,96},{224... | collective-permute-start | bytes 688136 | tf_op jit(solution)/shard_map/ppermute | solution.py:273
  76.0 13.1 %collective-permute-start.8 = (bf16[2,32,1792]{2,1,0:T(8,128)(2,1)S(1)}, bf16[2,32,1792]{2,1,0:T(8,128)(2,1)S(1)}, u32[]{:S(2)}, u32[]{:S(2)}) collective-permute-start(bf16[2,32,1792]{2,1,0:T(8,128)(2,1)S(1)} %get-tuple-element.53), channel_id=1, source_target_pairs={{0,192},{32,224},{64,128},{96,160},{128,64},{160,96},{192,0},{224,... | collective-permute-start | bytes 688136 | tf_op jit(solution)/shard_map/ppermute | solution.py:273
  76.0 16.8 %collective-permute-start.9 = (bf16[2,32,1792]{2,1,0:T(8,128)(2,1)S(1)}, bf16[2,32,1792]{2,1,0:T(8,128)(2,1)S(1)}, u32[]{:S(2)}, u32[]{:S(2)}) collective-permute-start(bf16[2,32,1792]{2,1,0:T(8,128)(2,1)S(1)} %get-tuple-element.54), channel_id=1, source_target_pairs={{0,224},{32,128},{64,160},{96,192},{128,96},{160,0},{192,32},{224,... | collective-permute-start | bytes 688136 | tf_op jit(solution)/shard_map/ppermute | solution.py:273
  82.4 10.4 %collective-permute-start.12 = (bf16[1,32,1792]{2,1,0:T(8,128)(2,1)S(1)}, bf16[1,32,1792]{2,1,0:T(8,128)(2,1)S(1)}, u32[]{:S(2)}, u32[]{:S(2)}) collective-permute-start(bf16[1,32,1792]{2,1,0:T(8,128)(2,1)S(1)} %get-tuple-element.58), channel_id=1, source_target_pairs={{0,32},{32,64},{64,96},{96,0},{128,160},{160,192},{192,224},{224,1... | collective-permute-start | bytes 344072 | tf_op jit(solution)/shard_map/ppermute | solution.py:273
  84.1 10.8 %collective-permute-start.13 = (bf16[1,32,1792]{2,1,0:T(8,128)(2,1)S(1)}, bf16[1,32,1792]{2,1,0:T(8,128)(2,1)S(1)}, u32[]{:S(2)}, u32[]{:S(2)}) collective-permute-start(bf16[1,32,1792]{2,1,0:T(8,128)(2,1)S(1)} %get-tuple-element.59), channel_id=1, source_target_pairs={{0,64},{32,96},{64,0},{96,32},{128,192},{160,224},{192,128},{224,1... | collective-permute-start | bytes 344072 | tf_op jit(solution)/shard_map/ppermute | solution.py:273
  87.3 11.4 %collective-permute-start.14 = (bf16[1,32,1792]{2,1,0:T(8,128)(2,1)S(1)}, bf16[1,32,1792]{2,1,0:T(8,128)(2,1)S(1)}, u32[]{:S(2)}, u32[]{:S(2)}) collective-permute-start(bf16[1,32,1792]{2,1,0:T(8,128)(2,1)S(1)} %get-tuple-element.60), channel_id=1, source_target_pairs={{0,96},{32,0},{64,32},{96,64},{128,224},{160,128},{192,160},{224,1... | collective-permute-start | bytes 344072 | tf_op jit(solution)/shard_map/ppermute | solution.py:273
  89.1 9.6 %collective-permute-start.15 = (bf16[1,32,1792]{2,1,0:T(8,128)(2,1)S(1)}, bf16[1,32,1792]{2,1,0:T(8,128)(2,1)S(1)}, u32[]{:S(2)}, u32[]{:S(2)}) collective-permute-start(bf16[1,32,1792]{2,1,0:T(8,128)(2,1)S(1)} %get-tuple-element.61), channel_id=1, source_target_pairs={{0,128},{32,160},{64,192},{96,224},{128,0},{160,32},{192,64},{224,... | collective-permute-start | bytes 344072 | tf_op jit(solution)/shard_map/ppermute | solution.py:273
  92.8 6.4 %collective-permute-start.16 = (bf16[1,32,1792]{2,1,0:T(8,128)(2,1)S(1)}, bf16[1,32,1792]{2,1,0:T(8,128)(2,1)S(1)}, u32[]{:S(2)}, u32[]{:S(2)}) collective-permute-start(bf16[1,32,1792]{2,1,0:T(8,128)(2,1)S(1)} %get-tuple-element.62), channel_id=1, source_target_pairs={{0,160},{32,192},{64,224},{96,128},{128,32},{160,64},{192,96},{224... | collective-permute-start | bytes 344072 | tf_op jit(solution)/shard_map/ppermute | solution.py:273
  92.8 7.5 %collective-permute-start.17 = (bf16[1,32,1792]{2,1,0:T(8,128)(2,1)S(1)}, bf16[1,32,1792]{2,1,0:T(8,128)(2,1)S(1)}, u32[]{:S(2)}, u32[]{:S(2)}) collective-permute-start(bf16[1,32,1792]{2,1,0:T(8,128)(2,1)S(1)} %get-tuple-element.63), channel_id=1, source_target_pairs={{0,192},{32,224},{64,128},{96,160},{128,64},{160,96},{192,0},{224,... | collective-permute-start | bytes 344072 | tf_op jit(solution)/shard_map/ppermute | solution.py:273
  95.0 7.1 %collective-permute-start.18 = (bf16[1,32,1792]{2,1,0:T(8,128)(2,1)S(1)}, bf16[1,32,1792]{2,1,0:T(8,128)(2,1)S(1)}, u32[]{:S(2)}, u32[]{:S(2)}) collective-permute-start(bf16[1,32,1792]{2,1,0:T(8,128)(2,1)S(1)} %get-tuple-element.64), channel_id=1, source_target_pairs={{0,224},{32,128},{64,160},{96,192},{128,96},{160,0},{192,32},{224,... | collective-permute-start | bytes 344072 | tf_op jit(solution)/shard_map/ppermute | solution.py:273
  102.2 7.3 %collective-permute-start.19 = (bf16[3,32,1792]{2,1,0:T(8,128)(2,1)S(1)}, bf16[3,32,1792]{2,1,0:T(8,128)(2,1)S(1)}, u32[]{:S(2)}, u32[]{:S(2)}) collective-permute-start(bf16[3,32,1792]{2,1,0:T(8,128)(2,1)S(1)} %shard_map.123.refs_0_), channel_id=1, source_target_pairs={{0,128},{128,0},{1,129},{129,1},{2,130},{130,2},{3,131},{131,3},{4... | collective-permute-start | bytes 1032200 | tf_op jit(solution)/shard_map/ppermute | solution.py:310
  103.0 11.8 %collective-permute-start.20 = (bf16[3,32,1792]{2,1,0:T(8,128)(2,1)S(1)}, bf16[3,32,1792]{2,1,0:T(8,128)(2,1)S(1)}, u32[]{:S(2)}, u32[]{:S(2)}) collective-permute-start(bf16[3,32,1792]{2,1,0:T(8,128)(2,1)S(1)} %shard_map.123.refs_0_), channel_id=1, source_target_pairs={{0,96},{32,0},{64,32},{96,64},{1,97},{33,1},{65,33},{97,65},{2,98}... | collective-permute-start | bytes 1032200 | tf_op jit(solution)/shard_map/ppermute | solution.py:303
  106.3 11.0 %collective-permute-start.21 = (bf16[3,32,1792]{2,1,0:T(8,128)(2,1)S(1)}, bf16[3,32,1792]{2,1,0:T(8,128)(2,1)S(1)}, u32[]{:S(2)}, u32[]{:S(2)}) collective-permute-start(bf16[3,32,1792]{2,1,0:T(8,128)(2,1)S(1)} %shard_map.123.refs_0_), channel_id=1, source_target_pairs={{0,32},{32,64},{64,96},{96,0},{1,33},{33,65},{65,97},{97,1},{2,34}... | collective-permute-start | bytes 1032200 | tf_op jit(solution)/shard_map/ppermute | solution.py:306
  109.6 11.8 %collective-permute-start.22 = (bf16[3,32,1792]{2,1,0:T(8,128)(2,1)S(1)}, bf16[3,32,1792]{2,1,0:T(8,128)(2,1)S(1)}, u32[]{:S(2)}, u32[]{:S(2)}) collective-permute-start(bf16[3,32,1792]{2,1,0:T(8,128)(2,1)S(1)} %collective-permute-done.19.refs_1_), channel_id=1, source_target_pairs={{0,96},{32,0},{64,32},{96,64},{1,97},{33,1},{65,33},{97,65},{2,98}... | collective-permute-start | bytes 1032200 | tf_op jit(solution)/shard_map/ppermute | solution.py:303
  112.1 12.0 %collective-permute-start.23 = (bf16[3,32,1792]{2,1,0:T(8,128)(2,1)S(1)}, bf16[3,32,1792]{2,1,0:T(8,128)(2,1)S(1)}, u32[]{:S(2)}, u32[]{:S(2)}) collective-permute-start(bf16[3,32,1792]{2,1,0:T(8,128)(2,1)S(1)} %collective-permute-done.19.refs_1_), channel_id=1, source_target_pairs={{0,32},{32,64},{64,96},{96,0},{1,33},{33,65},{65,97},{97,1},{2,34}... | collective-permute-start | bytes 1032200 | tf_op jit(solution)/shard_map/ppermute | solution.py:306
  114.8 15.6 %collective-permute-start.24 = (bf16[3,32,896]{2,1,0:T(8,128)(2,1)S(1)}, bf16[3,32,896]{2,1,0:T(8,128)(2,1)S(1)}, u32[]{:S(2)}, u32[]{:S(2)}) collective-permute-start(bf16[3,32,896]{2,1,0:T(8,128)(2,1)S(1)} %slice.16), channel_id=1, source_target_pairs={{0,96},{32,0},{64,32},{96,64},{1,97},{33,1},{65,33},{97,65},{2,98}... | collective-permute-start | bytes 516104 | tf_op jit(solution)/shard_map/ppermute | solution.py:303
  117.3 13.0 %collective-permute-start.25 = (bf16[3,32,896]{2,1,0:T(8,128)(2,1)S(1)}, bf16[3,32,896]{2,1,0:T(8,128)(2,1)S(1)}, u32[]{:S(2)}, u32[]{:S(2)}) collective-permute-start(bf16[3,32,896]{2,1,0:T(8,128)(2,1)S(1)} %slice.17), channel_id=1, source_target_pairs={{0,32},{32,64},{64,96},{96,0},{1,33},{33,65},{65,97},{97,1},{2,34}... | collective-permute-start | bytes 516104 | tf_op jit(solution)/shard_map/ppermute | solution.py:306
  121.4 8.9 %collective-permute-start.26 = (bf16[3,32,896]{2,1,0:T(8,128)(2,1)S(1)}, bf16[3,32,896]{2,1,0:T(8,128)(2,1)S(1)}, u32[]{:S(2)}, u32[]{:S(2)}) collective-permute-start(bf16[3,32,896]{2,1,0:T(8,128)(2,1)S(1)} %slice.18), channel_id=1, source_target_pairs={{0,96},{32,0},{64,32},{96,64},{1,97},{33,1},{65,33},{97,65},{2,98}... | collective-permute-start | bytes 516104 | tf_op jit(solution)/shard_map/ppermute | solution.py:303
  124.1 6.3 %collective-permute-start.27 = (bf16[3,32,896]{2,1,0:T(8,128)(2,1)S(1)}, bf16[3,32,896]{2,1,0:T(8,128)(2,1)S(1)}, u32[]{:S(2)}, u32[]{:S(2)}) collective-permute-start(bf16[3,32,896]{2,1,0:T(8,128)(2,1)S(1)} %slice.19), channel_id=1, source_target_pairs={{0,32},{32,64},{64,96},{96,0},{1,33},{33,65},{65,97},{97,1},{2,34}... | collective-permute-start | bytes 516104 | tf_op jit(solution)/shard_map/ppermute | solution.py:306
  130.2 1.7 %copy-start.3 = (bf16[3,128,1792]{2,1,0:T(8,128)(2,1)}, bf16[3,128,1792]{2,1,0:T(8,128)(2,1)S(1)}, u32[]{:S(2)}) copy-start(bf16[3,128,1792]{2,1,0:T(8,128)(2,1)S(1)} %get-tuple-element.78.refs_0_) | copy-start | bytes 4128772
  130.3 3.8 %collective-permute-start.28 = (bf16[128,1024]{1,0:T(8,128)(2,1)S(1)}, bf16[128,1024]{1,0:T(8,128)(2,1)S(1)}, u32[]{:S(2)}, u32[]{:S(2)}) collective-permute-start(bf16[128,1024]{1,0:T(8,128)(2,1)S(1)} %get-tuple-element.73), channel_id=1, source_target_pairs={{0,16},{16,0},{1,17},{17,1},{2,18},{18,2},{3,19},{19,3},{4,20},{20... | collective-permute-start | bytes 786440 | tf_op jit(solution)/shard_map/ppermute | solution.py:236
  132.0 2.1 %collective-permute-start.29 = (bf16[128,1024]{1,0:T(8,128)(2,1)S(1)}, bf16[128,1024]{1,0:T(8,128)(2,1)S(1)}, u32[]{:S(2)}, u32[]{:S(2)}) collective-permute-start(bf16[128,1024]{1,0:T(8,128)(2,1)S(1)} %get-tuple-element.74), channel_id=1, source_target_pairs={{0,16},{16,0},{1,17},{17,1},{2,18},{18,2},{3,19},{19,3},{4,20},{20... | collective-permute-start | bytes 786440 | tf_op jit(solution)/shard_map/ppermute | solution.py:236
  135.7 11.0 %copy-start.6 = (bf16[16,16,512]{2,1,0:T(8,128)(2,1)S(1)}, bf16[16,16,512]{2,1,0:T(8,128)(2,1)}, u32[]{:S(2)}) copy-start(bf16[16,16,512]{2,1,0:T(8,128)(2,1)} %copy-done.5) | copy-start | bytes 786436
  135.7 35.0 %all-to-all-start.2 = ((bf16[16,32,1024]{2,1,0:T(8,128)(2,1)}), bf16[16,32,1024]{2,1,0:T(8,128)(2,1)S(1)}, u32[]{:S(2)}, u32[]{:S(2)}) async-start(bf16[16,32,1024]{2,1,0:T(8,128)(2,1)} %shard_map.127), calls=%async_computation.2 | async-start | bytes 2097152 | tf_op jit(solution)/shard_map/all_to_all | solution.py:353
  141.4 3.4 %collective-permute-start.30 = (bf16[3,128,1792]{2,1,0:T(8,128)(2,1)}, bf16[3,128,1792]{2,1,0:T(8,128)(2,1)S(1)}, u32[]{:S(2)}, u32[]{:S(2)}) collective-permute-start(bf16[3,128,1792]{2,1,0:T(8,128)(2,1)} %copy-done.3), channel_id=1, source_target_pairs={{0,16},{16,0},{1,17},{17,1},{2,18},{18,2},{3,19},{19,3},{4,20},{20... | collective-permute-start | bytes 4128776 | tf_op jit(solution)/shard_map/ppermute | solution.py:236
  141.7 5.1 %collective-permute-start.31 = (bf16[3,128,1792]{2,1,0:T(8,128)(2,1)S(1)}, bf16[3,128,1792]{2,1,0:T(8,128)(2,1)S(1)}, u32[]{:S(2)}, u32[]{:S(2)}) collective-permute-start(bf16[3,128,1792]{2,1,0:T(8,128)(2,1)S(1)} %get-tuple-element.79.acts.refs_1_), channel_id=1, source_target_pairs={{0,16},{16,0},{1,17},{17,1},{2,18},{18,2},{3,19},{19,3},{4,20},{20... | collective-permute-start | bytes 4128776 | tf_op jit(solution)/shard_map/ppermute | solution.py:236
  146.8 1.3 copy-start.4
  148.1 0.9 copy-start.8

commit v9 on v8

--- a/solution.py
+++ b/solution.py
@@ -100,6 +100,12 @@
     return acc
 
 
+def copy_kernel(source, out):
+    value = source[...]
+    for i in range(out.shape[0]):
+        out[i] = value
+
+
 def sum_kernel(*refs):
     got, out = refs[:-1], refs[-1]
     for part in range(out.shape[0]):
@@ -156,13 +162,13 @@
 
 
 def late_away_kernel(*refs):
-    shares, weights, (acts, away) = refs[:6], refs[6:9], refs[9:]
+    shares, weights, (acts, away) = refs[:5], refs[5:8], refs[8:]
     share, hid = shares[0].shape[1], acts.shape[2]
-    for i in range(2):
-        acts[:, pl.ds(i * share, share), :] = shares[i][...]
-        rows = pl.ds((2 + i) * share, share)
-        acts[:, rows, : hid // 2] = shares[2 + 2 * i][...]
-        acts[:, rows, hid // 2 :] = shares[3 + 2 * i][...]
+    for i, ref in ((0, shares[0]), (1, shares[1]), (3, shares[4])):
+        acts[:, pl.ds(i * share, share), :] = ref[...]
+    rows = pl.ds(2 * share, share)
+    acts[:, rows, : hid // 2] = shares[2][...]
+    acts[:, rows, hid // 2 :] = shares[3][...]
     results(acts, weights, away)
 
 
@@ -253,7 +259,7 @@
     ).astype(jnp.int32)
 
     def copies(array):
-        return jnp.broadcast_to(array, (cols,) + array.shape)
+        return local_call(copy_kernel, 8, jax.ShapeDtypeStruct((cols,) + array.shape, BF), array)
 
     def gather(array):
         return lax.all_to_all(array, COL, 0, 0, tiled=True)
@@ -310,7 +316,7 @@
     facing = lax.ppermute(mine, "x_lo", [(0, 1), (1, 0)])
     distant = [from_up(up_one[:, :, :mid]), from_down(down_one[:, :, mid:])]
     facing_up, facing_down = from_up(facing), from_down(facing)
-    distant += [from_up(facing_up[:, :, :mid]), from_down(facing_down[:, :, mid:])]
+    distant += [lax.ppermute(facing, "y", [(i, (i + 2) % y_n) for i in range(y_n)])]
 
     rows_n = own.shape[0] // 2
     acts_shape = jax.ShapeDtypeStruct((3, rows_n, hid), BF)

time: 175 us -> 174 us (level)
  local copies, waits for them, and re-layouts: 10.9 us -> 9.14 us
    ppermute x0 -> x1, starting transfers between devices: none -> 3.79 us  [layer(): lax.ppermute(facing, 'y', [(i, (i + 2) % y_n) for i in range(y_n)])]
    ppermute x4 -> x3, starting transfers between devices: 11 us -> 7.22 us  [from_up(): return lax.ppermute(array, 'y', [(i, (i - 1) % y_n) for i in range(y_n)])]
    ppermute x4 -> x3, waiting for transfers between devices: 0.07 us -> 3.16 us  [from_down(): return lax.ppermute(array, 'y', [(i, (i + 1) % y_n) for i in range(y_n)])]
    broadcast_in_dim x2 -> x0, local copies, waits for them, and re-layouts: 2.45 us -> none  [copies(): return jnp.broadcast_to(array, (cols,) + array.shape)]
    ppermute x4 -> x3, waiting for transfers between devices: 6.62 us -> 4.83 us  [from_up(): return lax.ppermute(array, 'y', [(i, (i - 1) % y_n) for i in range(y_n)])]
    pallas_call x11 -> x13, Pallas kernels: 28.3 us -> 30 us  [local_call(): pl.pallas_call(kernel, out_shape=outs, in_specs=[pl.BlockSpec(memory_spac...]
    unnamed x24 -> x26, local copies, waits for them, and re-layouts: 6.97 us -> 7.72 us
  transfers between devices with their start and end apart: 35 -> 34, of which waited for: 14 -> 13; matrix products, arithmetic and copies ran while one was open for 3% -> 2% of each run, Pallas kernels for 15% -> 16%
where the time goes in v9:
time: 174 us; the launch traced here: 171 us
  starting transfers between devices  64.6 us (37%)
  waiting for transfers between devices  64.2 us (37%)
  Pallas kernels  30 us (17%)
  local copies, waits for them, and re-layouts  9.14 us (5%)
  other arithmetic  2.06 us (1%)
    ppermute x14, starting transfers between devices, spread(): got[r] = lax.ppermute(parts[r], PAIR, moves)  30.1 us
    pallas_call x13, Pallas kernels, local_call(): pl.pallas_call(kernel, out_shape=outs, in_specs=[pl.BlockSpec(memory_spac...  30 us
    all_to_all x2, waiting for transfers between devices, gather(): return lax.all_to_all(array, COL, 0, 0, tiled=True)  23 us
    all_to_all x1, waiting for transfers between devices, layer(): arrived = lax.all_to_all(send, COL, 0, 0, tiled=True)  15.8 us
    all_to_all x2, starting transfers between devices, gather(): return lax.all_to_all(array, COL, 0, 0, tiled=True)  15.7 us
    ppermute x14, waiting for transfers between devices, spread(): got[r] = lax.ppermute(parts[r], PAIR, moves)  9.34 us
    unnamed x26, local copies, waits for them, and re-layouts  7.72 us
    ppermute x3, starting transfers between devices, from_up(): return lax.ppermute(array, 'y', [(i, (i - 1) % y_n) for i in range(y_n)])  7.22 us
  transfers between devices with their start and end apart: 34, of which 13 were waited for; matrix products, arithmetic and copies ran while one was open for 2% of the time, Pallas kernels for 16%

profile of v9, /device:TPU:8, one launch (start us, length us, event | category | flops | bytes accessed | tf_op | source)
XLA Modules:
  0.0 171.1 jit_solution(6357573212010076114)
XLA Ops:
  0.6 0.7 copy-done.9
  1.4 0.8 shard_map.119
  2.2 11.0 %all-to-all-start = ((bf16[16,32,512]{2,1,0:T(8,128)(2,1)}), bf16[16,32,512]{2,1,0:T(8,128)(2,1)S(1)}, u32[]{:S(2)}, u32[]{:S(2)}) async-start(bf16[16,32,512]{2,1,0:T(8,128)(2,1)} %shard_map.119), calls=%async_computation | async-start | bytes 1048576 | tf_op jit(solution)/shard_map/all_to_all | solution.py:265
  15.7 1.5 copy-done
  17.2 1.5 copy-done.1
  18.7 1.5 copy-done.2
  20.2 2.2 %shard_map.121 = (bf16[512,1792]{1,0:T(8,128)(2,1)}, bf16[512,1792]{1,0:T(8,128)(2,1)}, bf16[1792,512]{1,0:T(8,128)(2,1)S(1)}) custom-call(bf16[512,1792]{1,0:T(8,128)(2,1)S(1)} %copy-done, bf16[512,1792]{1,0:T(8,128)(2,1)S(1)} %copy-done.1, bf16[1792,512]{1,0:T(8,128)(2,1)S(1)} %copy-done.2, f32[4,1792]{1,0:T(4,128)S(1)} %get-tuple-element.88.refs_3_.refs_8_, ...), custom_call_target="tpu_custom_call" | custom-call | tf_op jit(solution)/shard_map/pallas_call | solution.py:24
  23.0 0.9 shard_map.120
  23.8 6.6 %all-to-all-done = bf16[16,32,512]{2,1,0:T(8,128)(2,1)S(1)} async-done(((bf16[16,32,512]{2,1,0:T(8,128)(2,1)}), bf16[16,32,512]{2,1,0:T(8,128)(2,1)S(1)}, u32[]{:S(2)}, u32[]{:S(2)}) %all-to-all-start) | async-done | bytes 524320 | tf_op jit(solution)/shard_map/all_to_all | solution.py:265
  30.4 4.6 %all-to-all-start.1 = ((bf16[16,32,512]{2,1,0:T(8,128)(2,1)}), bf16[16,32,512]{2,1,0:T(8,128)(2,1)}, u32[]{:S(2)}, u32[]{:S(2)}) async-start(bf16[16,32,512]{2,1,0:T(8,128)(2,1)} %shard_map.120), calls=%async_computation.1 | async-start | bytes 1048576 | tf_op jit(solution)/shard_map/all_to_all | solution.py:265
  35.2 16.4 %all-to-all-done.1 = bf16[16,32,512]{2,1,0:T(8,128)(2,1)} async-done(((bf16[16,32,512]{2,1,0:T(8,128)(2,1)}), bf16[16,32,512]{2,1,0:T(8,128)(2,1)}, u32[]{:S(2)}, u32[]{:S(2)}) %all-to-all-start.1) | async-done | bytes 524320 | tf_op jit(solution)/shard_map/all_to_all | solution.py:265
  51.6 1.1 constant_dynamic-slice_fusion
  53.0 5.1 %shard_map.122 = (f32[2,32,1792]{2,1,0:T(8,128)S(1)}, bf16[2,32,1792]{2,1,0:T(8,128)(2,1)S(1)}, bf16[2,32,1792]{2,1,0:T(8,128)(2,1)S(1)}, bf16[2,32,1792]{2,1,0:...) custom-call(s32[8]{0:T(128)S(1)} %stack.35.place, ...), custom_call_target="tpu_custom_call" | custom-call | tf_op jit(solution)/shard_map/pallas_call | solution.py:24
  58.1 1.7 collective-permute-start.3
  59.8 0.9 collective-permute-start.4
  60.7 2.4 %collective-permute-start.5 = (bf16[2,32,1792]{2,1,0:T(8,128)(2,1)S(1)}, bf16[2,32,1792]{2,1,0:T(8,128)(2,1)S(1)}, u32[]{:S(2)}, u32[]{:S(2)}) collective-permute-start(bf16[2,32,1792]{2,1,0:T(8,128)(2,1)S(1)} %get-tuple-element.50), channel_id=1, source_target_pairs={{0,96},{32,0},{64,32},{96,64},{128,224},{160,128},{192,160},{224,1... | collective-permute-start | bytes 688136 | tf_op jit(solution)/shard_map/ppermute | solution.py:279
  63.7 3.0 %collective-permute-done.3.refs_1_ = bf16[2,32,1792]{2,1,0:T(8,128)(2,1)S(1)} collective-permute-done((bf16[2,32,1792]{2,1,0:T(8,128)(2,1)S(1)}, bf16[2,32,1792]{2,1,0:T(8,128)(2,1)S(1)}, u32[]{:S(2)}, u32[]{:S(2)}) %collective-permute-start.3) | collective-permute-done | bytes 229408 | tf_op jit(solution)/shard_map/ppermute | solution.py:279
  66.7 8.5 %collective-permute-start.7 = (bf16[2,32,1792]{2,1,0:T(8,128)(2,1)S(1)}, bf16[2,32,1792]{2,1,0:T(8,128)(2,1)S(1)}, u32[]{:S(2)}, u32[]{:S(2)}) collective-permute-start(bf16[2,32,1792]{2,1,0:T(8,128)(2,1)S(1)} %get-tuple-element.52), channel_id=1, source_target_pairs={{0,160},{32,192},{64,224},{96,128},{128,32},{160,64},{192,96},{224... | collective-permute-start | bytes 688136 | tf_op jit(solution)/shard_map/ppermute | solution.py:279
  75.2 3.1 %collective-permute-start.9 = (bf16[2,32,1792]{2,1,0:T(8,128)(2,1)S(1)}, bf16[2,32,1792]{2,1,0:T(8,128)(2,1)S(1)}, u32[]{:S(2)}, u32[]{:S(2)}) collective-permute-start(bf16[2,32,1792]{2,1,0:T(8,128)(2,1)S(1)} %get-tuple-element.54), channel_id=1, source_target_pairs={{0,224},{32,128},{64,160},{96,192},{128,96},{160,0},{192,32},{224,... | collective-permute-start | bytes 688136 | tf_op jit(solution)/shard_map/ppermute | solution.py:279
  78.2 3.3 %shard_map.124 = (f32[1,32,1792]{2,1,0:T(8,128)S(1)}, bf16[1,32,1792]{2,1,0:T(8,128)(2,1)S(1)}, bf16[1,32,1792]{2,1,0:T(8,128)(2,1)S(1)}, bf16[1,32,1792]{2,1,0:...) custom-call(s32[8]{0:T(128)S(1)} %stack.35.place, ...), custom_call_target="tpu_custom_call" | custom-call | tf_op jit(solution)/shard_map/pallas_call | solution.py:24
  81.6 1.7 %collective-permute-start.12 = (bf16[1,32,1792]{2,1,0:T(8,128)(2,1)S(1)}, bf16[1,32,1792]{2,1,0:T(8,128)(2,1)S(1)}, u32[]{:S(2)}, u32[]{:S(2)}) collective-permute-start(bf16[1,32,1792]{2,1,0:T(8,128)(2,1)S(1)} %get-tuple-element.58), channel_id=1, source_target_pairs={{0,32},{32,64},{64,96},{96,0},{128,160},{160,192},{192,224},{224,1... | collective-permute-start | bytes 344072 | tf_op jit(solution)/shard_map/ppermute | solution.py:279
  83.3 3.1 %collective-permute-start.13 = (bf16[1,32,1792]{2,1,0:T(8,128)(2,1)S(1)}, bf16[1,32,1792]{2,1,0:T(8,128)(2,1)S(1)}, u32[]{:S(2)}, u32[]{:S(2)}) collective-permute-start(bf16[1,32,1792]{2,1,0:T(8,128)(2,1)S(1)} %get-tuple-element.59), channel_id=1, source_target_pairs={{0,64},{32,96},{64,0},{96,32},{128,192},{160,224},{192,128},{224,1... | collective-permute-start | bytes 344072 | tf_op jit(solution)/shard_map/ppermute | solution.py:279
  86.4 1.8 %collective-permute-start.14 = (bf16[1,32,1792]{2,1,0:T(8,128)(2,1)S(1)}, bf16[1,32,1792]{2,1,0:T(8,128)(2,1)S(1)}, u32[]{:S(2)}, u32[]{:S(2)}) collective-permute-start(bf16[1,32,1792]{2,1,0:T(8,128)(2,1)S(1)} %get-tuple-element.60), channel_id=1, source_target_pairs={{0,96},{32,0},{64,32},{96,64},{128,224},{160,128},{192,160},{224,1... | collective-permute-start | bytes 344072 | tf_op jit(solution)/shard_map/ppermute | solution.py:279
  88.9 3.1 %collective-permute-done.9.refs_7_ = bf16[2,32,1792]{2,1,0:T(8,128)(2,1)S(1)} collective-permute-done((bf16[2,32,1792]{2,1,0:T(8,128)(2,1)S(1)}, bf16[2,32,1792]{2,1,0:T(8,128)(2,1)S(1)}, u32[]{:S(2)}, u32[]{:S(2)}) %collective-permute-start.9) | collective-permute-done | bytes 229408 | tf_op jit(solution)/shard_map/ppermute | solution.py:279
  91.9 2.2 %collective-permute-start.17 = (bf16[1,32,1792]{2,1,0:T(8,128)(2,1)S(1)}, bf16[1,32,1792]{2,1,0:T(8,128)(2,1)S(1)}, u32[]{:S(2)}, u32[]{:S(2)}) collective-permute-start(bf16[1,32,1792]{2,1,0:T(8,128)(2,1)S(1)} %get-tuple-element.63), channel_id=1, source_target_pairs={{0,192},{32,224},{64,128},{96,160},{128,64},{160,96},{192,0},{224,... | collective-permute-start | bytes 344072 | tf_op jit(solution)/shard_map/ppermute | solution.py:279
  94.1 3.5 %collective-permute-start.18 = (bf16[1,32,1792]{2,1,0:T(8,128)(2,1)S(1)}, bf16[1,32,1792]{2,1,0:T(8,128)(2,1)S(1)}, u32[]{:S(2)}, u32[]{:S(2)}) collective-permute-start(bf16[1,32,1792]{2,1,0:T(8,128)(2,1)S(1)} %get-tuple-element.64), channel_id=1, source_target_pairs={{0,224},{32,128},{64,160},{96,192},{128,96},{160,0},{192,32},{224,... | collective-permute-start | bytes 344072 | tf_op jit(solution)/shard_map/ppermute | solution.py:279
  98.3 1.1 collective-permute-done.17.refs_6_
  99.4 1.8 %collective-permute-done.18.refs_7_ = bf16[1,32,1792]{2,1,0:T(8,128)(2,1)S(1)} collective-permute-done((bf16[1,32,1792]{2,1,0:T(8,128)(2,1)S(1)}, bf16[1,32,1792]{2,1,0:T(8,128)(2,1)S(1)}, u32[]{:S(2)}, u32[]{:S(2)}) %collective-permute-start.18) | collective-permute-done | bytes 114720 | tf_op jit(solution)/shard_map/ppermute | solution.py:279
  102.1 3.3 %collective-permute-start.20 = (bf16[3,32,1792]{2,1,0:T(8,128)(2,1)S(1)}, bf16[3,32,1792]{2,1,0:T(8,128)(2,1)S(1)}, u32[]{:S(2)}, u32[]{:S(2)}) collective-permute-start(bf16[3,32,1792]{2,1,0:T(8,128)(2,1)S(1)} %shard_map.125.refs_0_), channel_id=1, source_target_pairs={{0,96},{32,0},{64,32},{96,64},{1,97},{33,1},{65,33},{97,65},{2,98}... | collective-permute-start | bytes 1032200 | tf_op jit(solution)/shard_map/ppermute | solution.py:309
  105.4 3.3 %collective-permute-done.19.refs_1_ = bf16[3,32,1792]{2,1,0:T(8,128)(2,1)S(1)} collective-permute-done((bf16[3,32,1792]{2,1,0:T(8,128)(2,1)S(1)}, bf16[3,32,1792]{2,1,0:T(8,128)(2,1)S(1)}, u32[]{:S(2)}, u32[]{:S(2)}) %collective-permute-start.19) | collective-permute-done | bytes 344096 | tf_op jit(solution)/shard_map/ppermute | solution.py:316
  108.7 2.6 %collective-permute-start.22 = (bf16[3,32,1792]{2,1,0:T(8,128)(2,1)S(1)}, bf16[3,32,1792]{2,1,0:T(8,128)(2,1)S(1)}, u32[]{:S(2)}, u32[]{:S(2)}) collective-permute-start(bf16[3,32,1792]{2,1,0:T(8,128)(2,1)S(1)} %collective-permute-done.19.refs_1_), channel_id=1, source_target_pairs={{0,96},{32,0},{64,32},{96,64},{1,97},{33,1},{65,33},{97,65},{2,98}... | collective-permute-start | bytes 1032200 | tf_op jit(solution)/shard_map/ppermute | solution.py:309
  111.3 3.8 %collective-permute-start.26 = (bf16[3,32,1792]{2,1,0:T(8,128)(2,1)S(1)}, bf16[3,32,1792]{2,1,0:T(8,128)(2,1)S(1)}, u32[]{:S(2)}, u32[]{:S(2)}) collective-permute-start(bf16[3,32,1792]{2,1,0:T(8,128)(2,1)S(1)} %collective-permute-done.19.refs_1_), channel_id=1, source_target_pairs={{0,64},{32,96},{64,0},{96,32},{1,65},{33,97},{65,1},{97,33},{2,66}... | collective-permute-start | bytes 1032200 | tf_op jit(solution)/shard_map/ppermute | solution.py:319
  115.1 1.4 collective-permute-start.24
  116.5 0.8 collective-permute-start.25
  117.3 5.8 %shard_map.126 = (bf16[3,128,1792]{2,1,0:T(8,128)(2,1)S(1)}, bf16[128,1024]{1,0:T(8,128)(2,1)S(1)}, bf16[128,1024]{1,0:T(8,128)(2,1)S(1)}, bf16[1792,512]{1,0:T(...) custom-call(bf16[3,32,1792]{2,1,0:T(8,128)(2,1)S(1)} %shard_map.125., ...), custom_call_target="tpu_custom_call" | custom-call | tf_op jit(solution)/shard_map/pallas_call | solution.py:24
  123.2 4.8 %collective-permute-done.24.refs_2_ = bf16[3,32,896]{2,1,0:T(8,128)(2,1)S(1)} collective-permute-done((bf16[3,32,896]{2,1,0:T(8,128)(2,1)S(1)}, bf16[3,32,896]{2,1,0:T(8,128)(2,1)S(1)}, u32[]{:S(2)}, u32[]{:S(2)}) %collective-permute-start.24) | collective-permute-done | bytes 172064 | tf_op jit(solution)/shard_map/ppermute | solution.py:309
  128.0 3.2 %collective-permute-done.25.refs_3_ = bf16[3,32,896]{2,1,0:T(8,128)(2,1)S(1)} collective-permute-done((bf16[3,32,896]{2,1,0:T(8,128)(2,1)S(1)}, bf16[3,32,896]{2,1,0:T(8,128)(2,1)S(1)}, u32[]{:S(2)}, u32[]{:S(2)}) %collective-permute-start.25) | collective-permute-done | bytes 172064 | tf_op jit(solution)/shard_map/ppermute | solution.py:312
  131.2 1.6 shard_map.127
  132.8 1.5 shard_map.128.here_late
  134.4 1.6 shard_map.129
  136.0 4.9 %all-to-all-start.2 = ((bf16[16,32,1024]{2,1,0:T(8,128)(2,1)}), bf16[16,32,1024]{2,1,0:T(8,128)(2,1)S(1)}, u32[]{:S(2)}, u32[]{:S(2)}) async-start(bf16[16,32,1024]{2,1,0:T(8,128)(2,1)} %shard_map.129), calls=%async_computation.2 | async-start | bytes 2097152 | tf_op jit(solution)/shard_map/all_to_all | solution.py:359
  141.6 2.8 %collective-permute-done.29.refs_2_ = bf16[3,128,1792]{2,1,0:T(8,128)(2,1)S(1)} collective-permute-done((bf16[3,128,1792]{2,1,0:T(8,128)(2,1)}, bf16[3,128,1792]{2,1,0:T(8,128)(2,1)S(1)}, u32[]{:S(2)}, u32[]{:S(2)}) %collective-permute-start.29) | collective-permute-done | bytes 1376288 | tf_op jit(solution)/shard_map/ppermute | solution.py:242
  144.4 2.0 %collective-permute-done.30.refs_3_ = bf16[3,128,1792]{2,1,0:T(8,128)(2,1)S(1)} collective-permute-done((bf16[3,128,1792]{2,1,0:T(8,128)(2,1)S(1)}, bf16[3,128,1792]{2,1,0:T(8,128)(2,1)S(1)}, u32[]{:S(2)}, u32[]{:S(2)}) %collective-permute-start.30) | collective-permute-done | bytes 1376288 | tf_op jit(solution)/shard_map/ppermute | solution.py:242
  146.4 1.3 copy-done.4
  147.7 0.9 copy-done.8
  148.6 5.9 %shard_map.131 = (bf16[512,1792]{1,0:T(8,128)(2,1)}, bf16[512,1792]{1,0:T(8,128)(2,1)}, bf16[1792,512]{1,0:T(8,128)(2,1)}) custom-call(s32[8]{0:T(128)S(1)} %stack.35.place, bf16[3,128,1792]{2,1,0:T(8,128)(2,1)S(1)} %copy-done.4, bf16[3,128,1792]{2,1,0:T(8,128)(2,1)S(1)} %get-tuple-element.79.acts.refs_1_, ...), custom_call_target="tpu_custom_call" | custom-call | tf_op jit(solution)/shard_map/pallas_call | solution.py:24
  154.5 15.8 %all-to-all-done.2.arrived = bf16[16,32,1024]{2,1,0:T(8,128)(2,1)S(1)} async-done(((bf16[16,32,1024]{2,1,0:T(8,128)(2,1)}), bf16[16,32,1024]{2,1,0:T(8,128)(2,1)S(1)}, u32[]{:S(2)}, u32[]{:S(2)}) %all-to-all-start.2) | async-done | bytes 1048608 | tf_op jit(solution)/shard_map/all_to_all | solution.py:359
  170.3 0.8 shard_map.130
  (70 shorter events, 6.9 us)
Async XLA Ops:
  0.6 0.8 copy-start.9
  2.2 28.2 %all-to-all-start = ((bf16[16,32,512]{2,1,0:T(8,128)(2,1)}), bf16[16,32,512]{2,1,0:T(8,128)(2,1)S(1)}, u32[]{:S(2)}, u32[]{:S(2)}) async-start(bf16[16,32,512]{2,1,0:T(8,128)(2,1)} %shard_map.119), calls=%async_computation | async-start | bytes 1048576 | tf_op jit(solution)/shard_map/all_to_all | solution.py:265
  15.7 1.5 copy-start
  17.2 1.5 copy-start.1
  18.7 1.5 copy-start.2
  20.2 2.7 %copy-start.10 = (bf16[32,512]{1,0:T(8,128)(2,1)S(1)}, bf16[32,512]{1,0:T(8,128)(2,1)}, u32[]{:S(2)}) copy-start(bf16[32,512]{1,0:T(8,128)(2,1)} %source.3) | copy-start | bytes 98308
  22.4 30.5 %collective-permute-start.1 = (bf16[512,1792]{1,0:T(8,128)(2,1)}, bf16[512,1792]{1,0:T(8,128)(2,1)}, u32[]{:S(2)}, u32[]{:S(2)}) collective-permute-start(bf16[512,1792]{1,0:T(8,128)(2,1)} %get-tuple-element.45.refs_0_.refs_8_), channel_id=1, source_target_pairs={{0,16},{16,0},{1,17},{17,1},{2,18},{18,2},{3,19},{19,3},{4,20},{20... | collective-permute-start | bytes 5505032 | tf_op jit(solution)/shard_map/ppermute | solution.py:242
  22.5 30.5 %collective-permute-start.2 = (bf16[512,1792]{1,0:T(8,128)(2,1)}, bf16[512,1792]{1,0:T(8,128)(2,1)}, u32[]{:S(2)}, u32[]{:S(2)}) collective-permute-start(bf16[512,1792]{1,0:T(8,128)(2,1)} %get-tuple-element.46.refs_2_.refs_9_), channel_id=1, source_target_pairs={{0,16},{16,0},{1,17},{17,1},{2,18},{18,2},{3,19},{19,3},{4,20},{20... | collective-permute-start | bytes 5505032 | tf_op jit(solution)/shard_map/ppermute | solution.py:242
  23.0 40.2 %collective-permute-start.11 = (bf16[1792,512]{1,0:T(8,128)(2,1)S(1)}, bf16[1792,512]{1,0:T(8,128)(2,1)}, u32[]{:S(2)}, u32[]{:S(2)}) collective-permute-start(bf16[1792,512]{1,0:T(8,128)(2,1)S(1)} %get-tuple-element.56.refs_0_.refs_7_), channel_id=1, source_target_pairs={{0,16},{16,0},{1,17},{17,1},{2,18},{18,2},{3,19},{19,3},{4,20},{20... | collective-permute-start | bytes 5505032 | tf_op jit(solution)/shard_map/ppermute | solution.py:242
  30.4 21.2 %all-to-all-start.1 = ((bf16[16,32,512]{2,1,0:T(8,128)(2,1)}), bf16[16,32,512]{2,1,0:T(8,128)(2,1)}, u32[]{:S(2)}, u32[]{:S(2)}) async-start(bf16[16,32,512]{2,1,0:T(8,128)(2,1)} %shard_map.120), calls=%async_computation.1 | async-start | bytes 1048576 | tf_op jit(solution)/shard_map/all_to_all | solution.py:265
  35.1 23.0 %copy-start.5 = (bf16[16,16,512]{2,1,0:T(8,128)(2,1)}, bf16[16,16,512]{2,1,0:T(8,128)(2,1)S(1)}, u32[]{:S(2)}) copy-start(bf16[16,16,512]{2,1,0:T(8,128)(2,1)S(1)} %get-tuple-element.85) | copy-start | bytes 786436
  35.1 17.8 %collective-permute-start = (bf16[256,512]{1,0:T(8,128)(2,1)S(1)}, bf16[256,512]{1,0:T(8,128)(2,1)S(1)}, u32[]{:S(2)}, u32[]{:S(2)}) collective-permute-start(bf16[256,512]{1,0:T(8,128)(2,1)S(1)} %bitcast.28), channel_id=1, source_target_pairs={{0,16},{16,0},{1,17},{17,1},{2,18},{18,2},{3,19},{19,3},{4,20},{20... | collective-permute-start | bytes 786440 | tf_op jit(solution)/shard_map/ppermute | solution.py:242
  52.7 5.4 %copy-start.7 = (bf16[16,16,512]{2,1,0:T(8,128)(2,1)}, bf16[16,16,512]{2,1,0:T(8,128)(2,1)S(1)}, u32[]{:S(2)}) copy-start(bf16[16,16,512]{2,1,0:T(8,128)(2,1)S(1)} %get-tuple-element.83) | copy-start | bytes 786436
  52.7 22.4 %collective-permute-start.10 = (bf16[256,512]{1,0:T(8,128)(2,1)S(1)}, bf16[256,512]{1,0:T(8,128)(2,1)S(1)}, u32[]{:S(2)}, u32[]{:S(2)}) collective-permute-start(bf16[256,512]{1,0:T(8,128)(2,1)S(1)} %bitcast.30), channel_id=1, source_target_pairs={{0,16},{16,0},{1,17},{17,1},{2,18},{18,2},{3,19},{19,3},{4,20},{20... | collective-permute-start | bytes 786440 | tf_op jit(solution)/shard_map/ppermute | solution.py:242
  58.1 8.6 %collective-permute-start.3 = (bf16[2,32,1792]{2,1,0:T(8,128)(2,1)S(1)}, bf16[2,32,1792]{2,1,0:T(8,128)(2,1)S(1)}, u32[]{:S(2)}, u32[]{:S(2)}) collective-permute-start(bf16[2,32,1792]{2,1,0:T(8,128)(2,1)S(1)} %get-tuple-element.48), channel_id=1, source_target_pairs={{0,32},{32,64},{64,96},{96,0},{128,160},{160,192},{192,224},{224,1... | collective-permute-start | bytes 688136 | tf_op jit(solution)/shard_map/ppermute | solution.py:279
  59.8 15.4 %collective-permute-start.4 = (bf16[2,32,1792]{2,1,0:T(8,128)(2,1)S(1)}, bf16[2,32,1792]{2,1,0:T(8,128)(2,1)S(1)}, u32[]{:S(2)}, u32[]{:S(2)}) collective-permute-start(bf16[2,32,1792]{2,1,0:T(8,128)(2,1)S(1)} %get-tuple-element.49), channel_id=1, source_target_pairs={{0,64},{32,96},{64,0},{96,32},{128,192},{160,224},{192,128},{224,1... | collective-permute-start | bytes 688136 | tf_op jit(solution)/shard_map/ppermute | solution.py:279
  60.7 20.8 %collective-permute-start.5 = (bf16[2,32,1792]{2,1,0:T(8,128)(2,1)S(1)}, bf16[2,32,1792]{2,1,0:T(8,128)(2,1)S(1)}, u32[]{:S(2)}, u32[]{:S(2)}) collective-permute-start(bf16[2,32,1792]{2,1,0:T(8,128)(2,1)S(1)} %get-tuple-element.50), channel_id=1, source_target_pairs={{0,96},{32,0},{64,32},{96,64},{128,224},{160,128},{192,160},{224,1... | collective-permute-start | bytes 688136 | tf_op jit(solution)/shard_map/ppermute | solution.py:279
  63.1 20.2 %collective-permute-start.6 = (bf16[2,32,1792]{2,1,0:T(8,128)(2,1)S(1)}, bf16[2,32,1792]{2,1,0:T(8,128)(2,1)S(1)}, u32[]{:S(2)}, u32[]{:S(2)}) collective-permute-start(bf16[2,32,1792]{2,1,0:T(8,128)(2,1)S(1)} %get-tuple-element.51), channel_id=1, source_target_pairs={{0,128},{32,160},{64,192},{96,224},{128,0},{160,32},{192,64},{224,... | collective-permute-start | bytes 688136 | tf_op jit(solution)/shard_map/ppermute | solution.py:279
  66.7 19.7 %collective-permute-start.7 = (bf16[2,32,1792]{2,1,0:T(8,128)(2,1)S(1)}, bf16[2,32,1792]{2,1,0:T(8,128)(2,1)S(1)}, u32[]{:S(2)}, u32[]{:S(2)}) collective-permute-start(bf16[2,32,1792]{2,1,0:T(8,128)(2,1)S(1)} %get-tuple-element.52), channel_id=1, source_target_pairs={{0,160},{32,192},{64,224},{96,128},{128,32},{160,64},{192,96},{224... | collective-permute-start | bytes 688136 | tf_op jit(solution)/shard_map/ppermute | solution.py:279
  75.2 13.1 %collective-permute-start.8 = (bf16[2,32,1792]{2,1,0:T(8,128)(2,1)S(1)}, bf16[2,32,1792]{2,1,0:T(8,128)(2,1)S(1)}, u32[]{:S(2)}, u32[]{:S(2)}) collective-permute-start(bf16[2,32,1792]{2,1,0:T(8,128)(2,1)S(1)} %get-tuple-element.53), channel_id=1, source_target_pairs={{0,192},{32,224},{64,128},{96,160},{128,64},{160,96},{192,0},{224,... | collective-permute-start | bytes 688136 | tf_op jit(solution)/shard_map/ppermute | solution.py:279
  75.2 16.8 %collective-permute-start.9 = (bf16[2,32,1792]{2,1,0:T(8,128)(2,1)S(1)}, bf16[2,32,1792]{2,1,0:T(8,128)(2,1)S(1)}, u32[]{:S(2)}, u32[]{:S(2)}) collective-permute-start(bf16[2,32,1792]{2,1,0:T(8,128)(2,1)S(1)} %get-tuple-element.54), channel_id=1, source_target_pairs={{0,224},{32,128},{64,160},{96,192},{128,96},{160,0},{192,32},{224,... | collective-permute-start | bytes 688136 | tf_op jit(solution)/shard_map/ppermute | solution.py:279
  81.6 10.4 %collective-permute-start.12 = (bf16[1,32,1792]{2,1,0:T(8,128)(2,1)S(1)}, bf16[1,32,1792]{2,1,0:T(8,128)(2,1)S(1)}, u32[]{:S(2)}, u32[]{:S(2)}) collective-permute-start(bf16[1,32,1792]{2,1,0:T(8,128)(2,1)S(1)} %get-tuple-element.58), channel_id=1, source_target_pairs={{0,32},{32,64},{64,96},{96,0},{128,160},{160,192},{192,224},{224,1... | collective-permute-start | bytes 344072 | tf_op jit(solution)/shard_map/ppermute | solution.py:279
  83.3 10.8 %collective-permute-start.13 = (bf16[1,32,1792]{2,1,0:T(8,128)(2,1)S(1)}, bf16[1,32,1792]{2,1,0:T(8,128)(2,1)S(1)}, u32[]{:S(2)}, u32[]{:S(2)}) collective-permute-start(bf16[1,32,1792]{2,1,0:T(8,128)(2,1)S(1)} %get-tuple-element.59), channel_id=1, source_target_pairs={{0,64},{32,96},{64,0},{96,32},{128,192},{160,224},{192,128},{224,1... | collective-permute-start | bytes 344072 | tf_op jit(solution)/shard_map/ppermute | solution.py:279
  86.4 11.4 %collective-permute-start.14 = (bf16[1,32,1792]{2,1,0:T(8,128)(2,1)S(1)}, bf16[1,32,1792]{2,1,0:T(8,128)(2,1)S(1)}, u32[]{:S(2)}, u32[]{:S(2)}) collective-permute-start(bf16[1,32,1792]{2,1,0:T(8,128)(2,1)S(1)} %get-tuple-element.60), channel_id=1, source_target_pairs={{0,96},{32,0},{64,32},{96,64},{128,224},{160,128},{192,160},{224,1... | collective-permute-start | bytes 344072 | tf_op jit(solution)/shard_map/ppermute | solution.py:279
  88.3 9.6 %collective-permute-start.15 = (bf16[1,32,1792]{2,1,0:T(8,128)(2,1)S(1)}, bf16[1,32,1792]{2,1,0:T(8,128)(2,1)S(1)}, u32[]{:S(2)}, u32[]{:S(2)}) collective-permute-start(bf16[1,32,1792]{2,1,0:T(8,128)(2,1)S(1)} %get-tuple-element.61), channel_id=1, source_target_pairs={{0,128},{32,160},{64,192},{96,224},{128,0},{160,32},{192,64},{224,... | collective-permute-start | bytes 344072 | tf_op jit(solution)/shard_map/ppermute | solution.py:279
  91.9 6.4 %collective-permute-start.16 = (bf16[1,32,1792]{2,1,0:T(8,128)(2,1)S(1)}, bf16[1,32,1792]{2,1,0:T(8,128)(2,1)S(1)}, u32[]{:S(2)}, u32[]{:S(2)}) collective-permute-start(bf16[1,32,1792]{2,1,0:T(8,128)(2,1)S(1)} %get-tuple-element.62), channel_id=1, source_target_pairs={{0,160},{32,192},{64,224},{96,128},{128,32},{160,64},{192,96},{224... | collective-permute-start | bytes 344072 | tf_op jit(solution)/shard_map/ppermute | solution.py:279
  91.9 7.4 %collective-permute-start.17 = (bf16[1,32,1792]{2,1,0:T(8,128)(2,1)S(1)}, bf16[1,32,1792]{2,1,0:T(8,128)(2,1)S(1)}, u32[]{:S(2)}, u32[]{:S(2)}) collective-permute-start(bf16[1,32,1792]{2,1,0:T(8,128)(2,1)S(1)} %get-tuple-element.63), channel_id=1, source_target_pairs={{0,192},{32,224},{64,128},{96,160},{128,64},{160,96},{192,0},{224,... | collective-permute-start | bytes 344072 | tf_op jit(solution)/shard_map/ppermute | solution.py:279
  94.1 7.1 %collective-permute-start.18 = (bf16[1,32,1792]{2,1,0:T(8,128)(2,1)S(1)}, bf16[1,32,1792]{2,1,0:T(8,128)(2,1)S(1)}, u32[]{:S(2)}, u32[]{:S(2)}) collective-permute-start(bf16[1,32,1792]{2,1,0:T(8,128)(2,1)S(1)} %get-tuple-element.64), channel_id=1, source_target_pairs={{0,224},{32,128},{64,160},{96,192},{128,96},{160,0},{192,32},{224,... | collective-permute-start | bytes 344072 | tf_op jit(solution)/shard_map/ppermute | solution.py:279
  101.4 7.3 %collective-permute-start.19 = (bf16[3,32,1792]{2,1,0:T(8,128)(2,1)S(1)}, bf16[3,32,1792]{2,1,0:T(8,128)(2,1)S(1)}, u32[]{:S(2)}, u32[]{:S(2)}) collective-permute-start(bf16[3,32,1792]{2,1,0:T(8,128)(2,1)S(1)} %shard_map.125.refs_0_), channel_id=1, source_target_pairs={{0,128},{128,0},{1,129},{129,1},{2,130},{130,2},{3,131},{131,3},{4... | collective-permute-start | bytes 1032200 | tf_op jit(solution)/shard_map/ppermute | solution.py:316
  102.1 13.0 %collective-permute-start.20 = (bf16[3,32,1792]{2,1,0:T(8,128)(2,1)S(1)}, bf16[3,32,1792]{2,1,0:T(8,128)(2,1)S(1)}, u32[]{:S(2)}, u32[]{:S(2)}) collective-permute-start(bf16[3,32,1792]{2,1,0:T(8,128)(2,1)S(1)} %shard_map.125.refs_0_), channel_id=1, source_target_pairs={{0,96},{32,0},{64,32},{96,64},{1,97},{33,1},{65,33},{97,65},{2,98}... | collective-permute-start | bytes 1032200 | tf_op jit(solution)/shard_map/ppermute | solution.py:309
  105.4 11.0 %collective-permute-start.21 = (bf16[3,32,1792]{2,1,0:T(8,128)(2,1)S(1)}, bf16[3,32,1792]{2,1,0:T(8,128)(2,1)S(1)}, u32[]{:S(2)}, u32[]{:S(2)}) collective-permute-start(bf16[3,32,1792]{2,1,0:T(8,128)(2,1)S(1)} %shard_map.125.refs_0_), channel_id=1, source_target_pairs={{0,32},{32,64},{64,96},{96,0},{1,33},{33,65},{65,97},{97,1},{2,34}... | collective-permute-start | bytes 1032200 | tf_op jit(solution)/shard_map/ppermute | solution.py:312
  108.7 22.4 %collective-permute-start.22 = (bf16[3,32,1792]{2,1,0:T(8,128)(2,1)S(1)}, bf16[3,32,1792]{2,1,0:T(8,128)(2,1)S(1)}, u32[]{:S(2)}, u32[]{:S(2)}) collective-permute-start(bf16[3,32,1792]{2,1,0:T(8,128)(2,1)S(1)} %collective-permute-done.19.refs_1_), channel_id=1, source_target_pairs={{0,96},{32,0},{64,32},{96,64},{1,97},{33,1},{65,33},{97,65},{2,98}... | collective-permute-start | bytes 1032200 | tf_op jit(solution)/shard_map/ppermute | solution.py:309
  111.3 19.9 %collective-permute-start.23 = (bf16[3,32,1792]{2,1,0:T(8,128)(2,1)S(1)}, bf16[3,32,1792]{2,1,0:T(8,128)(2,1)S(1)}, u32[]{:S(2)}, u32[]{:S(2)}) collective-permute-start(bf16[3,32,1792]{2,1,0:T(8,128)(2,1)S(1)} %collective-permute-done.19.refs_1_), channel_id=1, source_target_pairs={{0,32},{32,64},{64,96},{96,0},{1,33},{33,65},{65,97},{97,1},{2,34}... | collective-permute-start | bytes 1032200 | tf_op jit(solution)/shard_map/ppermute | solution.py:312
  111.3 19.9 %collective-permute-start.26 = (bf16[3,32,1792]{2,1,0:T(8,128)(2,1)S(1)}, bf16[3,32,1792]{2,1,0:T(8,128)(2,1)S(1)}, u32[]{:S(2)}, u32[]{:S(2)}) collective-permute-start(bf16[3,32,1792]{2,1,0:T(8,128)(2,1)S(1)} %collective-permute-done.19.refs_1_), channel_id=1, source_target_pairs={{0,64},{32,96},{64,0},{96,32},{1,65},{33,97},{65,1},{97,33},{2,66}... | collective-permute-start | bytes 1032200 | tf_op jit(solution)/shard_map/ppermute | solution.py:319
  115.1 12.9 %collective-permute-start.24 = (bf16[3,32,896]{2,1,0:T(8,128)(2,1)S(1)}, bf16[3,32,896]{2,1,0:T(8,128)(2,1)S(1)}, u32[]{:S(2)}, u32[]{:S(2)}) collective-permute-start(bf16[3,32,896]{2,1,0:T(8,128)(2,1)S(1)} %slice.8), channel_id=1, source_target_pairs={{0,96},{32,0},{64,32},{96,64},{1,97},{33,1},{65,33},{97,65},{2,98}... | collective-permute-start | bytes 516104 | tf_op jit(solution)/shard_map/ppermute | solution.py:309
  116.5 14.7 %collective-permute-start.25 = (bf16[3,32,896]{2,1,0:T(8,128)(2,1)S(1)}, bf16[3,32,896]{2,1,0:T(8,128)(2,1)S(1)}, u32[]{:S(2)}, u32[]{:S(2)}) collective-permute-start(bf16[3,32,896]{2,1,0:T(8,128)(2,1)S(1)} %slice.9), channel_id=1, source_target_pairs={{0,32},{32,64},{64,96},{96,0},{1,33},{33,65},{65,97},{97,1},{2,34}... | collective-permute-start | bytes 516104 | tf_op jit(solution)/shard_map/ppermute | solution.py:312
  123.2 9.6 %copy-start.3 = (bf16[3,128,1792]{2,1,0:T(8,128)(2,1)}, bf16[3,128,1792]{2,1,0:T(8,128)(2,1)S(1)}, u32[]{:S(2)}) copy-start(bf16[3,128,1792]{2,1,0:T(8,128)(2,1)S(1)} %get-tuple-element.78.refs_0_) | copy-start | bytes 4128772
  128.0 6.4 %collective-permute-start.27 = (bf16[128,1024]{1,0:T(8,128)(2,1)S(1)}, bf16[128,1024]{1,0:T(8,128)(2,1)S(1)}, u32[]{:S(2)}, u32[]{:S(2)}) collective-permute-start(bf16[128,1024]{1,0:T(8,128)(2,1)S(1)} %get-tuple-element.73), channel_id=1, source_target_pairs={{0,16},{16,0},{1,17},{17,1},{2,18},{18,2},{3,19},{19,3},{4,20},{20... | collective-permute-start | bytes 786440 | tf_op jit(solution)/shard_map/ppermute | solution.py:242
  132.7 1.7 collective-permute-start.28
  136.0 10.3 %copy-start.6 = (bf16[16,16,512]{2,1,0:T(8,128)(2,1)S(1)}, bf16[16,16,512]{2,1,0:T(8,128)(2,1)}, u32[]{:S(2)}) copy-start(bf16[16,16,512]{2,1,0:T(8,128)(2,1)} %copy-done.5) | copy-start | bytes 786436
  136.0 34.3 %all-to-all-start.2 = ((bf16[16,32,1024]{2,1,0:T(8,128)(2,1)}), bf16[16,32,1024]{2,1,0:T(8,128)(2,1)S(1)}, u32[]{:S(2)}, u32[]{:S(2)}) async-start(bf16[16,32,1024]{2,1,0:T(8,128)(2,1)} %shard_map.129), calls=%async_computation.2 | async-start | bytes 2097152 | tf_op jit(solution)/shard_map/all_to_all | solution.py:359
  141.0 3.4 %collective-permute-start.29 = (bf16[3,128,1792]{2,1,0:T(8,128)(2,1)}, bf16[3,128,1792]{2,1,0:T(8,128)(2,1)S(1)}, u32[]{:S(2)}, u32[]{:S(2)}) collective-permute-start(bf16[3,128,1792]{2,1,0:T(8,128)(2,1)} %copy-done.3), channel_id=1, source_target_pairs={{0,16},{16,0},{1,17},{17,1},{2,18},{18,2},{3,19},{19,3},{4,20},{20... | collective-permute-start | bytes 4128776 | tf_op jit(solution)/shard_map/ppermute | solution.py:242
  141.3 5.1 %collective-permute-start.30 = (bf16[3,128,1792]{2,1,0:T(8,128)(2,1)S(1)}, bf16[3,128,1792]{2,1,0:T(8,128)(2,1)S(1)}, u32[]{:S(2)}, u32[]{:S(2)}) collective-permute-start(bf16[3,128,1792]{2,1,0:T(8,128)(2,1)S(1)} %get-tuple-element.79.acts.refs_1_), channel_id=1, source_target_pairs={{0,16},{16,0},{1,17},{17,1},{2,18},{18,2},{3,19},{19,3},{4,20},{20... | collective-permute-start | bytes 4128776 | tf_op jit(solution)/shard_map/ppermute | solution.py:242
  146.4 1.3 copy-start.4
  147.7 0.9 copy-start.8

commit v10 on v9

--- a/solution.py
+++ b/solution.py
@@ -258,11 +258,12 @@
         [(x_lo ^ (r // y_n)) * y_n + (y + r % y_n) % y_n for r in range(pairs)]
     ).astype(jnp.int32)
 
-    def copies(array):
-        return local_call(copy_kernel, 8, jax.ShapeDtypeStruct((cols,) + array.shape, BF), array)
-
-    def gather(array):
-        return lax.all_to_all(array, COL, 0, 0, tiled=True)
+    def copies(array, axis):
+        shape = (lax.axis_size(axis),) + array.shape
+        return local_call(copy_kernel, 8, jax.ShapeDtypeStruct(shape, BF), array)
+
+    def gather(array, axis):
+        return lax.all_to_all(array, axis, 0, 0, tiled=True)
 
     def by_core(gathered):
         own = lax.dynamic_slice_in_dim(gathered, core * half, half, 1)
@@ -279,7 +280,7 @@
             got[r] = lax.ppermute(parts[r], PAIR, moves)
         return [got[r] for r in range(pairs)]
 
-    gathered = gather(copies(tokens))
+    gathered = gather(copies(tokens, COL), COL)
     weights = (gate_weight, up_weight, down_weight)
     shapes = [jax.ShapeDtypeStruct(weight.shape, BF) for weight in weights]
     wide = [
@@ -288,12 +289,22 @@
     effs = local_call(prepare_kernel, 20, shapes, *weights, *wide)
     effs_x = [swap(eff) for eff in effs]
 
-    gathered, cot_in = lax.optimization_barrier((gathered, copies(cotangent)))
-    gathered_cot = gather(cot_in)
+    high = lax.axis_index("x_hi")
+    cot_facing = lax.ppermute(cotangent, "x_hi", [(0, 1), (1, 0)])
+    cot_pair = jnp.stack(
+        [
+            jnp.where(high == 0, cotangent, cot_facing),
+            jnp.where(high == 0, cot_facing, cotangent),
+        ]
+    )
+    gathered, cot_in = lax.optimization_barrier((gathered, copies(cot_pair, "z")))
+    gathered_cot = gather(cot_in, "z")
     own, other = by_core(gathered)
     parts = partial_sums(place, own, swap(other), effs[:2], effs_x[:2], nn)
     got = spread(parts)
-    own_cot, other_cot = by_core(gathered_cot)
+    own_cot, other_cot = by_core(
+        jnp.swapaxes(gathered_cot, 0, 1).reshape(cols, share, width)
+    )
     back = partial_sums(place, own_cot, swap(other_cot), effs[2:], effs_x[2:], nt)
     got_back = spread(back)
     forward = local_call(sum_kernel, 12, jax.ShapeDtypeStruct(parts[0].shape, F32), *got)

time: 174 us -> 177 us (1.017)
  waiting for transfers between devices: 64.2 us -> 67.1 us
    ppermute x3, starting transfers between devices: 7.22 us -> 0.68 us  [from_up(): return lax.ppermute(array, 'y', [(i, (i - 1) % y_n) for i in range(y_n)])]
    all_to_all x2, waiting for transfers between devices: 23 us -> 17.6 us  [gather(): return lax.all_to_all(array, axis, 0, 0, tiled=True)]
    ppermute x14, waiting for transfers between devices: 9.34 us -> 14.3 us  [spread(): got[r] = lax.ppermute(parts[r], PAIR, moves)]
    ppermute x3, starting transfers between devices: 0.83 us -> 5.76 us  [from_down(): return lax.ppermute(array, 'y', [(i, (i + 1) % y_n) for i in range(y_n)])]
    ppermute x0 -> x1, starting transfers between devices: none -> 3.43 us  [layer(): cot_facing = lax.ppermute(cotangent, 'x_hi', [(0, 1), (1, 0)])]
    ppermute x3, waiting for transfers between devices: 3.16 us -> 0.26 us  [from_down(): return lax.ppermute(array, 'y', [(i, (i + 1) % y_n) for i in range(y_n)])]
    ppermute x14, starting transfers between devices: 30.1 us -> 27.3 us  [spread(): got[r] = lax.ppermute(parts[r], PAIR, moves)]
    ppermute x0 -> x1, waiting for transfers between devices: none -> 2.54 us  [layer(): cot_facing = lax.ppermute(cotangent, 'x_hi', [(0, 1), (1, 0)])]
  transfers between devices with their start and end apart: 34 -> 35, of which waited for: 13 -> 14; matrix products, arithmetic and copies ran while one was open for 2% -> 2% of each run, Pallas kernels for 16% -> 15%
where the time goes in v10:
time: 177 us; the launch traced here: 175 us
  waiting for transfers between devices  67.1 us (38%)
  starting transfers between devices  65.9 us (37%)
  Pallas kernels  30 us (17%)
  local copies, waits for them, and re-layouts  9.19 us (5%)
  other arithmetic  2.08 us (1%)
    pallas_call x13, Pallas kernels, local_call(): pl.pallas_call(kernel, out_shape=outs, in_specs=[pl.BlockSpec(memory_spac...  30 us
    ppermute x14, starting transfers between devices, spread(): got[r] = lax.ppermute(parts[r], PAIR, moves)  27.3 us
    all_to_all x2, waiting for transfers between devices, gather(): return lax.all_to_all(array, axis, 0, 0, tiled=True)  17.6 us
    all_to_all x2, starting transfers between devices, gather(): return lax.all_to_all(array, axis, 0, 0, tiled=True)  16.9 us
    all_to_all x1, waiting for transfers between devices, layer(): arrived = lax.all_to_all(send, COL, 0, 0, tiled=True)  15.5 us
    ppermute x14, waiting for transfers between devices, spread(): got[r] = lax.ppermute(parts[r], PAIR, moves)  14.3 us
    unnamed x26, local copies, waits for them, and re-layouts  7.72 us
    ppermute x3, waiting for transfers between devices, from_up(): return lax.ppermute(array, 'y', [(i, (i - 1) % y_n) for i in range(y_n)])  6.91 us
  transfers between devices with their start and end apart: 35, of which 14 were waited for; matrix products, arithmetic and copies ran while one was open for 2% of the time, Pallas kernels for 15%

profile of v10, /device:TPU:8, one launch (start us, length us, event | category | flops | bytes accessed | tf_op | source)
XLA Modules:
  0.0 175.4 jit_solution(17971594836051799054)
XLA Ops:
  0.6 0.7 copy-done.9
  1.4 0.8 shard_map.119
  2.2 11.0 %all-to-all-start = ((bf16[16,32,512]{2,1,0:T(8,128)(2,1)}), bf16[16,32,512]{2,1,0:T(8,128)(2,1)S(1)}, u32[]{:S(2)}, u32[]{:S(2)}) async-start(bf16[16,32,512]{2,1,0:T(8,128)(2,1)} %shard_map.119), calls=%async_computation | async-start | bytes 1048576 | tf_op jit(solution)/shard_map/all_to_all | solution.py:266
  14.0 0.7 convert_element_type.9
  15.7 1.5 copy-done
  17.2 1.5 copy-done.1
  18.7 1.5 copy-done.2
  20.2 2.2 %shard_map.121 = (bf16[512,1792]{1,0:T(8,128)(2,1)}, bf16[512,1792]{1,0:T(8,128)(2,1)}, bf16[1792,512]{1,0:T(8,128)(2,1)S(1)}) custom-call(bf16[512,1792]{1,0:T(8,128)(2,1)S(1)} %copy-done, bf16[512,1792]{1,0:T(8,128)(2,1)S(1)} %copy-done.1, bf16[1792,512]{1,0:T(8,128)(2,1)S(1)} %copy-done.2, f32[4,1792]{1,0:T(4,128)S(1)} %get-tuple-element.90.refs_3_.refs_8_, ...), custom_call_target="tpu_custom_call" | custom-call | tf_op jit(solution)/shard_map/pallas_call | solution.py:24
  23.0 3.4 %collective-permute-start = (bf16[32,512]{1,0:T(8,128)(2,1)S(1)}, bf16[32,512]{1,0:T(8,128)(2,1)S(1)}, u32[]{:S(2)}, u32[]{:S(2)}) collective-permute-start(bf16[32,512]{1,0:T(8,128)(2,1)S(1)} %copy-done.10), channel_id=1, source_target_pairs={{0,8},{8,0},{1,9},{9,1},{2,10},{10,2},{3,11},{11,3},{4,12},{12,4},... | collective-permute-start | bytes 98312 | tf_op jit(solution)/shard_map/ppermute | solution.py:293
  26.4 2.5 %collective-permute-done = bf16[32,512]{1,0:T(8,128)(2,1)S(1)} collective-permute-done((bf16[32,512]{1,0:T(8,128)(2,1)S(1)}, bf16[32,512]{1,0:T(8,128)(2,1)S(1)}, u32[]{:S(2)}, u32[]{:S(2)}) %collective-permute-start) | collective-permute-done | bytes 32800 | tf_op jit(solution)/shard_map/ppermute | solution.py:293
  29.0 0.8 shard_map.120
  30.4 5.9 %all-to-all-start.1 = ((bf16[8,2,32,512]{3,2,1,0:T(8,128)(2,1)}), bf16[8,2,32,512]{3,2,1,0:T(8,128)(2,1)}, u32[]{:S(2)}, u32[]{:S(2)}) async-start(bf16[8,2,32,512]{3,2,1,0:T(8,128)(2,1)} %shard_map.120), calls=%async_computation.1 | async-start | bytes 1048576 | tf_op jit(solution)/shard_map/all_to_all | solution.py:266
  36.5 17.0 %all-to-all-done.1 = bf16[8,2,32,512]{3,2,1,0:T(8,128)(2,1)} async-done(((bf16[8,2,32,512]{3,2,1,0:T(8,128)(2,1)}), bf16[8,2,32,512]{3,2,1,0:T(8,128)(2,1)}, u32[]{:S(2)}, u32[]{:S(2)}) %all-to-all-start.1) | async-done | bytes 524320 | tf_op jit(solution)/shard_map/all_to_all | solution.py:266
  53.5 1.1 copy.15
  54.9 5.1 %shard_map.122 = (f32[2,32,1792]{2,1,0:T(8,128)S(1)}, bf16[2,32,1792]{2,1,0:T(8,128)(2,1)S(1)}, bf16[2,32,1792]{2,1,0:T(8,128)(2,1)S(1)}, bf16[2,32,1792]{2,1,0:...) custom-call(s32[8]{0:T(128)S(1)} %stack.44.place, ...), custom_call_target="tpu_custom_call" | custom-call | tf_op jit(solution)/shard_map/pallas_call | solution.py:24
  60.6 1.6 collective-permute-start.4
  62.2 3.5 %collective-permute-start.5 = (bf16[2,32,1792]{2,1,0:T(8,128)(2,1)S(1)}, bf16[2,32,1792]{2,1,0:T(8,128)(2,1)S(1)}, u32[]{:S(2)}, u32[]{:S(2)}) collective-permute-start(bf16[2,32,1792]{2,1,0:T(8,128)(2,1)S(1)} %get-tuple-element.49), channel_id=1, source_target_pairs={{0,64},{32,96},{64,0},{96,32},{128,192},{160,224},{192,128},{224,1... | collective-permute-start | bytes 688136 | tf_op jit(solution)/shard_map/ppermute | solution.py:280
  65.8 3.4 %collective-permute-done.10.refs_7_ = bf16[2,32,1792]{2,1,0:T(8,128)(2,1)S(1)} collective-permute-done((bf16[2,32,1792]{2,1,0:T(8,128)(2,1)S(1)}, bf16[2,32,1792]{2,1,0:T(8,128)(2,1)S(1)}, u32[]{:S(2)}, u32[]{:S(2)}) %collective-permute-start.10) | collective-permute-done | bytes 229408 | tf_op jit(solution)/shard_map/ppermute | solution.py:280
  70.1 2.1 %collective-permute-start.8 = (bf16[2,32,1792]{2,1,0:T(8,128)(2,1)S(1)}, bf16[2,32,1792]{2,1,0:T(8,128)(2,1)S(1)}, u32[]{:S(2)}, u32[]{:S(2)}) collective-permute-start(bf16[2,32,1792]{2,1,0:T(8,128)(2,1)S(1)} %get-tuple-element.52), channel_id=1, source_target_pairs={{0,160},{32,192},{64,224},{96,128},{128,32},{160,64},{192,96},{224... | collective-permute-start | bytes 688136 | tf_op jit(solution)/shard_map/ppermute | solution.py:280
  72.1 8.3 %collective-permute-start.9 = (bf16[2,32,1792]{2,1,0:T(8,128)(2,1)S(1)}, bf16[2,32,1792]{2,1,0:T(8,128)(2,1)S(1)}, u32[]{:S(2)}, u32[]{:S(2)}) collective-permute-start(bf16[2,32,1792]{2,1,0:T(8,128)(2,1)S(1)} %get-tuple-element.53), channel_id=1, source_target_pairs={{0,192},{32,224},{64,128},{96,160},{128,64},{160,96},{192,0},{224,... | collective-permute-start | bytes 688136 | tf_op jit(solution)/shard_map/ppermute | solution.py:280
  80.4 3.3 %shard_map.124 = (f32[1,32,1792]{2,1,0:T(8,128)S(1)}, bf16[1,32,1792]{2,1,0:T(8,128)(2,1)S(1)}, bf16[1,32,1792]{2,1,0:T(8,128)(2,1)S(1)}, bf16[1,32,1792]{2,1,0:...) custom-call(s32[8]{0:T(128)S(1)} %stack.44.place, ...), custom_call_target="tpu_custom_call" | custom-call | tf_op jit(solution)/shard_map/pallas_call | solution.py:24
  83.8 1.0 collective-permute-start.14
  84.9 1.6 collective-permute-start.15
  86.4 0.9 collective-permute-start.16
  87.4 4.9 %collective-permute-done.9.refs_6_ = bf16[2,32,1792]{2,1,0:T(8,128)(2,1)S(1)} collective-permute-done((bf16[2,32,1792]{2,1,0:T(8,128)(2,1)S(1)}, bf16[2,32,1792]{2,1,0:T(8,128)(2,1)S(1)}, u32[]{:S(2)}, u32[]{:S(2)}) %collective-permute-start.9) | collective-permute-done | bytes 229408 | tf_op jit(solution)/shard_map/ppermute | solution.py:280
  92.2 5.3 %collective-permute-start.18 = (bf16[1,32,1792]{2,1,0:T(8,128)(2,1)S(1)}, bf16[1,32,1792]{2,1,0:T(8,128)(2,1)S(1)}, u32[]{:S(2)}, u32[]{:S(2)}) collective-permute-start(bf16[1,32,1792]{2,1,0:T(8,128)(2,1)S(1)} %get-tuple-element.63), channel_id=1, source_target_pairs={{0,192},{32,224},{64,128},{96,160},{128,64},{160,96},{192,0},{224,... | collective-permute-start | bytes 344072 | tf_op jit(solution)/shard_map/ppermute | solution.py:280
  97.5 1.8 %collective-permute-start.19 = (bf16[1,32,1792]{2,1,0:T(8,128)(2,1)S(1)}, bf16[1,32,1792]{2,1,0:T(8,128)(2,1)S(1)}, u32[]{:S(2)}, u32[]{:S(2)}) collective-permute-start(bf16[1,32,1792]{2,1,0:T(8,128)(2,1)S(1)} %get-tuple-element.64), channel_id=1, source_target_pairs={{0,224},{32,128},{64,160},{96,192},{128,96},{160,0},{192,32},{224,... | collective-permute-start | bytes 344072 | tf_op jit(solution)/shard_map/ppermute | solution.py:280
  99.6 0.9 collective-permute-done.18.refs_6_
  100.5 4.8 %collective-permute-done.19.refs_7_ = bf16[1,32,1792]{2,1,0:T(8,128)(2,1)S(1)} collective-permute-done((bf16[1,32,1792]{2,1,0:T(8,128)(2,1)S(1)}, bf16[1,32,1792]{2,1,0:T(8,128)(2,1)S(1)}, u32[]{:S(2)}, u32[]{:S(2)}) %collective-permute-start.19) | collective-permute-done | bytes 114720 | tf_op jit(solution)/shard_map/ppermute | solution.py:280
  105.5 2.5 %collective-permute-start.20 = (bf16[3,32,1792]{2,1,0:T(8,128)(2,1)S(1)}, bf16[3,32,1792]{2,1,0:T(8,128)(2,1)S(1)}, u32[]{:S(2)}, u32[]{:S(2)}) collective-permute-start(bf16[3,32,1792]{2,1,0:T(8,128)(2,1)S(1)} %shard_map.125.refs_0_), channel_id=1, source_target_pairs={{0,128},{128,0},{1,129},{129,1},{2,130},{130,2},{3,131},{131,3},{4... | collective-permute-start | bytes 1032200 | tf_op jit(solution)/shard_map/ppermute | solution.py:327
  108.6 1.4 collective-permute-start.22
  110.0 5.2 %collective-permute-done.20.refs_1_ = bf16[3,32,1792]{2,1,0:T(8,128)(2,1)S(1)} collective-permute-done((bf16[3,32,1792]{2,1,0:T(8,128)(2,1)S(1)}, bf16[3,32,1792]{2,1,0:T(8,128)(2,1)S(1)}, u32[]{:S(2)}, u32[]{:S(2)}) %collective-permute-start.20) | collective-permute-done | bytes 344096 | tf_op jit(solution)/shard_map/ppermute | solution.py:327
  115.2 2.0 %collective-permute-start.24 = (bf16[3,32,1792]{2,1,0:T(8,128)(2,1)S(1)}, bf16[3,32,1792]{2,1,0:T(8,128)(2,1)S(1)}, u32[]{:S(2)}, u32[]{:S(2)}) collective-permute-start(bf16[3,32,1792]{2,1,0:T(8,128)(2,1)S(1)} %collective-permute-done.20.refs_1_), channel_id=1, source_target_pairs={{0,32},{32,64},{64,96},{96,0},{1,33},{33,65},{65,97},{97,1},{2,34}... | collective-permute-start | bytes 1032200 | tf_op jit(solution)/shard_map/ppermute | solution.py:323
  117.2 2.7 %collective-permute-start.27 = (bf16[3,32,1792]{2,1,0:T(8,128)(2,1)S(1)}, bf16[3,32,1792]{2,1,0:T(8,128)(2,1)S(1)}, u32[]{:S(2)}, u32[]{:S(2)}) collective-permute-start(bf16[3,32,1792]{2,1,0:T(8,128)(2,1)S(1)} %collective-permute-done.20.refs_1_), channel_id=1, source_target_pairs={{0,64},{32,96},{64,0},{96,32},{1,65},{33,97},{65,1},{97,33},{2,66}... | collective-permute-start | bytes 1032200 | tf_op jit(solution)/shard_map/ppermute | solution.py:330
  120.0 2.3 %collective-permute-start.26 = (bf16[3,32,896]{2,1,0:T(8,128)(2,1)S(1)}, bf16[3,32,896]{2,1,0:T(8,128)(2,1)S(1)}, u32[]{:S(2)}, u32[]{:S(2)}) collective-permute-start(bf16[3,32,896]{2,1,0:T(8,128)(2,1)S(1)} %slice.9), channel_id=1, source_target_pairs={{0,32},{32,64},{64,96},{96,0},{1,33},{33,65},{65,97},{97,1},{2,34}... | collective-permute-start | bytes 516104 | tf_op jit(solution)/shard_map/ppermute | solution.py:323
  122.3 5.8 %shard_map.126 = (bf16[3,128,1792]{2,1,0:T(8,128)(2,1)S(1)}, bf16[128,1024]{1,0:T(8,128)(2,1)S(1)}, bf16[128,1024]{1,0:T(8,128)(2,1)S(1)}, bf16[1792,512]{1,0:T(...) custom-call(bf16[3,32,1792]{2,1,0:T(8,128)(2,1)S(1)} %shard_map.125., ...), custom_call_target="tpu_custom_call" | custom-call | tf_op jit(solution)/shard_map/pallas_call | solution.py:24
  128.2 6.9 %collective-permute-done.25.refs_2_ = bf16[3,32,896]{2,1,0:T(8,128)(2,1)S(1)} collective-permute-done((bf16[3,32,896]{2,1,0:T(8,128)(2,1)S(1)}, bf16[3,32,896]{2,1,0:T(8,128)(2,1)S(1)}, u32[]{:S(2)}, u32[]{:S(2)}) %collective-permute-start.25) | collective-permute-done | bytes 172064 | tf_op jit(solution)/shard_map/ppermute | solution.py:320
  135.4 1.6 shard_map.127
  137.3 1.5 shard_map.128.here_late
  138.9 1.6 shard_map.129
  140.5 5.0 %all-to-all-start.2 = ((bf16[16,32,1024]{2,1,0:T(8,128)(2,1)}), bf16[16,32,1024]{2,1,0:T(8,128)(2,1)S(1)}, u32[]{:S(2)}, u32[]{:S(2)}) async-start(bf16[16,32,1024]{2,1,0:T(8,128)(2,1)} %shard_map.129), calls=%async_computation.2 | async-start | bytes 2097152 | tf_op jit(solution)/shard_map/all_to_all | solution.py:370
  146.1 2.8 %collective-permute-done.30.refs_2_ = bf16[3,128,1792]{2,1,0:T(8,128)(2,1)S(1)} collective-permute-done((bf16[3,128,1792]{2,1,0:T(8,128)(2,1)}, bf16[3,128,1792]{2,1,0:T(8,128)(2,1)S(1)}, u32[]{:S(2)}, u32[]{:S(2)}) %collective-permute-start.30) | collective-permute-done | bytes 1376288 | tf_op jit(solution)/shard_map/ppermute | solution.py:242
  148.9 2.0 %collective-permute-done.31.refs_3_ = bf16[3,128,1792]{2,1,0:T(8,128)(2,1)S(1)} collective-permute-done((bf16[3,128,1792]{2,1,0:T(8,128)(2,1)S(1)}, bf16[3,128,1792]{2,1,0:T(8,128)(2,1)S(1)}, u32[]{:S(2)}, u32[]{:S(2)}) %collective-permute-start.31) | collective-permute-done | bytes 1376288 | tf_op jit(solution)/shard_map/ppermute | solution.py:242
  150.9 1.3 copy-done.4
  152.3 0.9 copy-done.8
  153.2 5.9 %shard_map.131 = (bf16[512,1792]{1,0:T(8,128)(2,1)}, bf16[512,1792]{1,0:T(8,128)(2,1)}, bf16[1792,512]{1,0:T(8,128)(2,1)}) custom-call(s32[8]{0:T(128)S(1)} %stack.44.place, bf16[3,128,1792]{2,1,0:T(8,128)(2,1)S(1)} %copy-done.4, bf16[3,128,1792]{2,1,0:T(8,128)(2,1)S(1)} %get-tuple-element.79.acts.refs_1_, ...), custom_call_target="tpu_custom_call" | custom-call | tf_op jit(solution)/shard_map/pallas_call | solution.py:24
  159.1 15.5 %all-to-all-done.2.arrived = bf16[16,32,1024]{2,1,0:T(8,128)(2,1)S(1)} async-done(((bf16[16,32,1024]{2,1,0:T(8,128)(2,1)}), bf16[16,32,1024]{2,1,0:T(8,128)(2,1)S(1)}, u32[]{:S(2)}, u32[]{:S(2)}) %all-to-all-start.2) | async-done | bytes 1048608 | tf_op jit(solution)/shard_map/all_to_all | solution.py:370
  174.6 0.8 shard_map.130
  (75 shorter events, 7.4 us)
Async XLA Ops:
  0.6 0.8 copy-start.9
  2.2 28.2 %all-to-all-start = ((bf16[16,32,512]{2,1,0:T(8,128)(2,1)}), bf16[16,32,512]{2,1,0:T(8,128)(2,1)S(1)}, u32[]{:S(2)}, u32[]{:S(2)}) async-start(bf16[16,32,512]{2,1,0:T(8,128)(2,1)} %shard_map.119), calls=%async_computation | async-start | bytes 1048576 | tf_op jit(solution)/shard_map/all_to_all | solution.py:266
  15.7 1.5 copy-start
  17.2 1.5 copy-start.1
  18.7 1.5 copy-start.2
  20.2 2.7 %copy-start.10 = (bf16[32,512]{1,0:T(8,128)(2,1)S(1)}, bf16[32,512]{1,0:T(8,128)(2,1)}, u32[]{:S(2)}) copy-start(bf16[32,512]{1,0:T(8,128)(2,1)} %param.9) | copy-start | bytes 98308
  22.4 32.4 %collective-permute-start.2 = (bf16[512,1792]{1,0:T(8,128)(2,1)}, bf16[512,1792]{1,0:T(8,128)(2,1)}, u32[]{:S(2)}, u32[]{:S(2)}) collective-permute-start(bf16[512,1792]{1,0:T(8,128)(2,1)} %get-tuple-element.45.refs_0_.refs_8_), channel_id=1, source_target_pairs={{0,16},{16,0},{1,17},{17,1},{2,18},{18,2},{3,19},{19,3},{4,20},{20... | collective-permute-start | bytes 5505032 | tf_op jit(solution)/shard_map/ppermute | solution.py:242
  22.4 32.4 %collective-permute-start.3 = (bf16[512,1792]{1,0:T(8,128)(2,1)}, bf16[512,1792]{1,0:T(8,128)(2,1)}, u32[]{:S(2)}, u32[]{:S(2)}) collective-permute-start(bf16[512,1792]{1,0:T(8,128)(2,1)} %get-tuple-element.46.refs_2_.refs_9_), channel_id=1, source_target_pairs={{0,16},{16,0},{1,17},{17,1},{2,18},{18,2},{3,19},{19,3},{4,20},{20... | collective-permute-start | bytes 5505032 | tf_op jit(solution)/shard_map/ppermute | solution.py:242
  23.0 42.7 %collective-permute-start.12 = (bf16[1792,512]{1,0:T(8,128)(2,1)S(1)}, bf16[1792,512]{1,0:T(8,128)(2,1)}, u32[]{:S(2)}, u32[]{:S(2)}) collective-permute-start(bf16[1792,512]{1,0:T(8,128)(2,1)S(1)} %get-tuple-element.56.refs_0_.refs_7_), channel_id=1, source_target_pairs={{0,16},{16,0},{1,17},{17,1},{2,18},{18,2},{3,19},{19,3},{4,20},{20... | collective-permute-start | bytes 5505032 | tf_op jit(solution)/shard_map/ppermute | solution.py:242
  23.0 6.0 %collective-permute-start = (bf16[32,512]{1,0:T(8,128)(2,1)S(1)}, bf16[32,512]{1,0:T(8,128)(2,1)S(1)}, u32[]{:S(2)}, u32[]{:S(2)}) collective-permute-start(bf16[32,512]{1,0:T(8,128)(2,1)S(1)} %copy-done.10), channel_id=1, source_target_pairs={{0,8},{8,0},{1,9},{9,1},{2,10},{10,2},{3,11},{11,3},{4,12},{12,4},... | collective-permute-start | bytes 98312 | tf_op jit(solution)/shard_map/ppermute | solution.py:293
  30.4 23.0 %all-to-all-start.1 = ((bf16[8,2,32,512]{3,2,1,0:T(8,128)(2,1)}), bf16[8,2,32,512]{3,2,1,0:T(8,128)(2,1)}, u32[]{:S(2)}, u32[]{:S(2)}) async-start(bf16[8,2,32,512]{3,2,1,0:T(8,128)(2,1)} %shard_map.120), calls=%async_computation.1 | async-start | bytes 1048576 | tf_op jit(solution)/shard_map/all_to_all | solution.py:266
  36.4 23.6 %copy-start.5 = (bf16[16,16,512]{2,1,0:T(8,128)(2,1)}, bf16[16,16,512]{2,1,0:T(8,128)(2,1)S(1)}, u32[]{:S(2)}) copy-start(bf16[16,16,512]{2,1,0:T(8,128)(2,1)S(1)} %get-tuple-element.85) | copy-start | bytes 786436
  36.4 18.4 %collective-permute-start.1 = (bf16[256,512]{1,0:T(8,128)(2,1)S(1)}, bf16[256,512]{1,0:T(8,128)(2,1)S(1)}, u32[]{:S(2)}, u32[]{:S(2)}) collective-permute-start(bf16[256,512]{1,0:T(8,128)(2,1)S(1)} %bitcast.34), channel_id=1, source_target_pairs={{0,16},{16,0},{1,17},{17,1},{2,18},{18,2},{3,19},{19,3},{4,20},{20... | collective-permute-start | bytes 786440 | tf_op jit(solution)/shard_map/ppermute | solution.py:242
  54.6 5.4 %copy-start.7 = (bf16[16,16,512]{2,1,0:T(8,128)(2,1)}, bf16[16,16,512]{2,1,0:T(8,128)(2,1)S(1)}, u32[]{:S(2)}) copy-start(bf16[16,16,512]{2,1,0:T(8,128)(2,1)S(1)} %get-tuple-element.83) | copy-start | bytes 786436
  54.6 17.5 %collective-permute-start.11 = (bf16[256,512]{1,0:T(8,128)(2,1)S(1)}, bf16[256,512]{1,0:T(8,128)(2,1)S(1)}, u32[]{:S(2)}, u32[]{:S(2)}) collective-permute-start(bf16[256,512]{1,0:T(8,128)(2,1)S(1)} %bitcast.36), channel_id=1, source_target_pairs={{0,16},{16,0},{1,17},{17,1},{2,18},{18,2},{3,19},{19,3},{4,20},{20... | collective-permute-start | bytes 786440 | tf_op jit(solution)/shard_map/ppermute | solution.py:242
  60.0 9.1 %collective-permute-start.10 = (bf16[2,32,1792]{2,1,0:T(8,128)(2,1)S(1)}, bf16[2,32,1792]{2,1,0:T(8,128)(2,1)S(1)}, u32[]{:S(2)}, u32[]{:S(2)}) collective-permute-start(bf16[2,32,1792]{2,1,0:T(8,128)(2,1)S(1)} %get-tuple-element.54), channel_id=1, source_target_pairs={{0,224},{32,128},{64,160},{96,192},{128,96},{160,0},{192,32},{224,... | collective-permute-start | bytes 688136 | tf_op jit(solution)/shard_map/ppermute | solution.py:280
  60.6 9.5 %collective-permute-start.4 = (bf16[2,32,1792]{2,1,0:T(8,128)(2,1)S(1)}, bf16[2,32,1792]{2,1,0:T(8,128)(2,1)S(1)}, u32[]{:S(2)}, u32[]{:S(2)}) collective-permute-start(bf16[2,32,1792]{2,1,0:T(8,128)(2,1)S(1)} %get-tuple-element.48), channel_id=1, source_target_pairs={{0,32},{32,64},{64,96},{96,0},{128,160},{160,192},{192,224},{224,1... | collective-permute-start | bytes 688136 | tf_op jit(solution)/shard_map/ppermute | solution.py:280
  62.2 21.6 %collective-permute-start.5 = (bf16[2,32,1792]{2,1,0:T(8,128)(2,1)S(1)}, bf16[2,32,1792]{2,1,0:T(8,128)(2,1)S(1)}, u32[]{:S(2)}, u32[]{:S(2)}) collective-permute-start(bf16[2,32,1792]{2,1,0:T(8,128)(2,1)S(1)} %get-tuple-element.49), channel_id=1, source_target_pairs={{0,64},{32,96},{64,0},{96,32},{128,192},{160,224},{192,128},{224,1... | collective-permute-start | bytes 688136 | tf_op jit(solution)/shard_map/ppermute | solution.py:280
  65.7 18.1 %collective-permute-start.6 = (bf16[2,32,1792]{2,1,0:T(8,128)(2,1)S(1)}, bf16[2,32,1792]{2,1,0:T(8,128)(2,1)S(1)}, u32[]{:S(2)}, u32[]{:S(2)}) collective-permute-start(bf16[2,32,1792]{2,1,0:T(8,128)(2,1)S(1)} %get-tuple-element.50), channel_id=1, source_target_pairs={{0,96},{32,0},{64,32},{96,64},{128,224},{160,128},{192,160},{224,1... | collective-permute-start | bytes 688136 | tf_op jit(solution)/shard_map/ppermute | solution.py:280
  69.2 15.7 %collective-permute-start.7 = (bf16[2,32,1792]{2,1,0:T(8,128)(2,1)S(1)}, bf16[2,32,1792]{2,1,0:T(8,128)(2,1)S(1)}, u32[]{:S(2)}, u32[]{:S(2)}) collective-permute-start(bf16[2,32,1792]{2,1,0:T(8,128)(2,1)S(1)} %get-tuple-element.51), channel_id=1, source_target_pairs={{0,128},{32,160},{64,192},{96,224},{128,0},{160,32},{192,64},{224,... | collective-permute-start | bytes 688136 | tf_op jit(solution)/shard_map/ppermute | solution.py:280
  70.1 16.4 %collective-permute-start.8 = (bf16[2,32,1792]{2,1,0:T(8,128)(2,1)S(1)}, bf16[2,32,1792]{2,1,0:T(8,128)(2,1)S(1)}, u32[]{:S(2)}, u32[]{:S(2)}) collective-permute-start(bf16[2,32,1792]{2,1,0:T(8,128)(2,1)S(1)} %get-tuple-element.52), channel_id=1, source_target_pairs={{0,160},{32,192},{64,224},{96,128},{128,32},{160,64},{192,96},{224... | collective-permute-start | bytes 688136 | tf_op jit(solution)/shard_map/ppermute | solution.py:280
  72.1 20.1 %collective-permute-start.9 = (bf16[2,32,1792]{2,1,0:T(8,128)(2,1)S(1)}, bf16[2,32,1792]{2,1,0:T(8,128)(2,1)S(1)}, u32[]{:S(2)}, u32[]{:S(2)}) collective-permute-start(bf16[2,32,1792]{2,1,0:T(8,128)(2,1)S(1)} %get-tuple-element.53), channel_id=1, source_target_pairs={{0,192},{32,224},{64,128},{96,160},{128,64},{160,96},{192,0},{224,... | collective-permute-start | bytes 688136 | tf_op jit(solution)/shard_map/ppermute | solution.py:280
  83.7 8.5 %collective-permute-start.13 = (bf16[1,32,1792]{2,1,0:T(8,128)(2,1)S(1)}, bf16[1,32,1792]{2,1,0:T(8,128)(2,1)S(1)}, u32[]{:S(2)}, u32[]{:S(2)}) collective-permute-start(bf16[1,32,1792]{2,1,0:T(8,128)(2,1)S(1)} %get-tuple-element.58), channel_id=1, source_target_pairs={{0,32},{32,64},{64,96},{96,0},{128,160},{160,192},{192,224},{224,1... | collective-permute-start | bytes 344072 | tf_op jit(solution)/shard_map/ppermute | solution.py:280
  83.8 13.7 %collective-permute-start.14 = (bf16[1,32,1792]{2,1,0:T(8,128)(2,1)S(1)}, bf16[1,32,1792]{2,1,0:T(8,128)(2,1)S(1)}, u32[]{:S(2)}, u32[]{:S(2)}) collective-permute-start(bf16[1,32,1792]{2,1,0:T(8,128)(2,1)S(1)} %get-tuple-element.59), channel_id=1, source_target_pairs={{0,64},{32,96},{64,0},{96,32},{128,192},{160,224},{192,128},{224,1... | collective-permute-start | bytes 344072 | tf_op jit(solution)/shard_map/ppermute | solution.py:280
  84.9 14.7 %collective-permute-start.15 = (bf16[1,32,1792]{2,1,0:T(8,128)(2,1)S(1)}, bf16[1,32,1792]{2,1,0:T(8,128)(2,1)S(1)}, u32[]{:S(2)}, u32[]{:S(2)}) collective-permute-start(bf16[1,32,1792]{2,1,0:T(8,128)(2,1)S(1)} %get-tuple-element.60), channel_id=1, source_target_pairs={{0,96},{32,0},{64,32},{96,64},{128,224},{160,128},{192,160},{224,1... | collective-permute-start | bytes 344072 | tf_op jit(solution)/shard_map/ppermute | solution.py:280
  86.4 13.1 %collective-permute-start.16 = (bf16[1,32,1792]{2,1,0:T(8,128)(2,1)S(1)}, bf16[1,32,1792]{2,1,0:T(8,128)(2,1)S(1)}, u32[]{:S(2)}, u32[]{:S(2)}) collective-permute-start(bf16[1,32,1792]{2,1,0:T(8,128)(2,1)S(1)} %get-tuple-element.61), channel_id=1, source_target_pairs={{0,128},{32,160},{64,192},{96,224},{128,0},{160,32},{192,64},{224,... | collective-permute-start | bytes 344072 | tf_op jit(solution)/shard_map/ppermute | solution.py:280
  92.2 7.4 %collective-permute-start.17 = (bf16[1,32,1792]{2,1,0:T(8,128)(2,1)S(1)}, bf16[1,32,1792]{2,1,0:T(8,128)(2,1)S(1)}, u32[]{:S(2)}, u32[]{:S(2)}) collective-permute-start(bf16[1,32,1792]{2,1,0:T(8,128)(2,1)S(1)} %get-tuple-element.62), channel_id=1, source_target_pairs={{0,160},{32,192},{64,224},{96,128},{128,32},{160,64},{192,96},{224... | collective-permute-start | bytes 344072 | tf_op jit(solution)/shard_map/ppermute | solution.py:280
  92.2 8.2 %collective-permute-start.18 = (bf16[1,32,1792]{2,1,0:T(8,128)(2,1)S(1)}, bf16[1,32,1792]{2,1,0:T(8,128)(2,1)S(1)}, u32[]{:S(2)}, u32[]{:S(2)}) collective-permute-start(bf16[1,32,1792]{2,1,0:T(8,128)(2,1)S(1)} %get-tuple-element.63), channel_id=1, source_target_pairs={{0,192},{32,224},{64,128},{96,160},{128,64},{160,96},{192,0},{224,... | collective-permute-start | bytes 344072 | tf_op jit(solution)/shard_map/ppermute | solution.py:280
  97.5 7.7 %collective-permute-start.19 = (bf16[1,32,1792]{2,1,0:T(8,128)(2,1)S(1)}, bf16[1,32,1792]{2,1,0:T(8,128)(2,1)S(1)}, u32[]{:S(2)}, u32[]{:S(2)}) collective-permute-start(bf16[1,32,1792]{2,1,0:T(8,128)(2,1)S(1)} %get-tuple-element.64), channel_id=1, source_target_pairs={{0,224},{32,128},{64,160},{96,192},{128,96},{160,0},{192,32},{224,... | collective-permute-start | bytes 344072 | tf_op jit(solution)/shard_map/ppermute | solution.py:280
  105.5 9.7 %collective-permute-start.20 = (bf16[3,32,1792]{2,1,0:T(8,128)(2,1)S(1)}, bf16[3,32,1792]{2,1,0:T(8,128)(2,1)S(1)}, u32[]{:S(2)}, u32[]{:S(2)}) collective-permute-start(bf16[3,32,1792]{2,1,0:T(8,128)(2,1)S(1)} %shard_map.125.refs_0_), channel_id=1, source_target_pairs={{0,128},{128,0},{1,129},{129,1},{2,130},{130,2},{3,131},{131,3},{4... | collective-permute-start | bytes 1032200 | tf_op jit(solution)/shard_map/ppermute | solution.py:327
  108.0 11.9 %collective-permute-start.21 = (bf16[3,32,1792]{2,1,0:T(8,128)(2,1)S(1)}, bf16[3,32,1792]{2,1,0:T(8,128)(2,1)S(1)}, u32[]{:S(2)}, u32[]{:S(2)}) collective-permute-start(bf16[3,32,1792]{2,1,0:T(8,128)(2,1)S(1)} %shard_map.125.refs_0_), channel_id=1, source_target_pairs={{0,96},{32,0},{64,32},{96,64},{1,97},{33,1},{65,33},{97,65},{2,98}... | collective-permute-start | bytes 1032200 | tf_op jit(solution)/shard_map/ppermute | solution.py:320
  108.6 11.4 %collective-permute-start.22 = (bf16[3,32,1792]{2,1,0:T(8,128)(2,1)S(1)}, bf16[3,32,1792]{2,1,0:T(8,128)(2,1)S(1)}, u32[]{:S(2)}, u32[]{:S(2)}) collective-permute-start(bf16[3,32,1792]{2,1,0:T(8,128)(2,1)S(1)} %shard_map.125.refs_0_), channel_id=1, source_target_pairs={{0,32},{32,64},{64,96},{96,0},{1,33},{33,65},{65,97},{97,1},{2,34}... | collective-permute-start | bytes 1032200 | tf_op jit(solution)/shard_map/ppermute | solution.py:323
  115.2 20.2 %collective-permute-start.23 = (bf16[3,32,1792]{2,1,0:T(8,128)(2,1)S(1)}, bf16[3,32,1792]{2,1,0:T(8,128)(2,1)S(1)}, u32[]{:S(2)}, u32[]{:S(2)}) collective-permute-start(bf16[3,32,1792]{2,1,0:T(8,128)(2,1)S(1)} %collective-permute-done.20.refs_1_), channel_id=1, source_target_pairs={{0,96},{32,0},{64,32},{96,64},{1,97},{33,1},{65,33},{97,65},{2,98}... | collective-permute-start | bytes 1032200 | tf_op jit(solution)/shard_map/ppermute | solution.py:320
  115.2 20.2 %collective-permute-start.24 = (bf16[3,32,1792]{2,1,0:T(8,128)(2,1)S(1)}, bf16[3,32,1792]{2,1,0:T(8,128)(2,1)S(1)}, u32[]{:S(2)}, u32[]{:S(2)}) collective-permute-start(bf16[3,32,1792]{2,1,0:T(8,128)(2,1)S(1)} %collective-permute-done.20.refs_1_), channel_id=1, source_target_pairs={{0,32},{32,64},{64,96},{96,0},{1,33},{33,65},{65,97},{97,1},{2,34}... | collective-permute-start | bytes 1032200 | tf_op jit(solution)/shard_map/ppermute | solution.py:323
  117.2 18.1 %collective-permute-start.27 = (bf16[3,32,1792]{2,1,0:T(8,128)(2,1)S(1)}, bf16[3,32,1792]{2,1,0:T(8,128)(2,1)S(1)}, u32[]{:S(2)}, u32[]{:S(2)}) collective-permute-start(bf16[3,32,1792]{2,1,0:T(8,128)(2,1)S(1)} %collective-permute-done.20.refs_1_), channel_id=1, source_target_pairs={{0,64},{32,96},{64,0},{96,32},{1,65},{33,97},{65,1},{97,33},{2,66}... | collective-permute-start | bytes 1032200 | tf_op jit(solution)/shard_map/ppermute | solution.py:330
  119.9 15.2 %collective-permute-start.25 = (bf16[3,32,896]{2,1,0:T(8,128)(2,1)S(1)}, bf16[3,32,896]{2,1,0:T(8,128)(2,1)S(1)}, u32[]{:S(2)}, u32[]{:S(2)}) collective-permute-start(bf16[3,32,896]{2,1,0:T(8,128)(2,1)S(1)} %slice.8), channel_id=1, source_target_pairs={{0,96},{32,0},{64,32},{96,64},{1,97},{33,1},{65,33},{97,65},{2,98}... | collective-permute-start | bytes 516104 | tf_op jit(solution)/shard_map/ppermute | solution.py:320
  120.0 15.3 %collective-permute-start.26 = (bf16[3,32,896]{2,1,0:T(8,128)(2,1)S(1)}, bf16[3,32,896]{2,1,0:T(8,128)(2,1)S(1)}, u32[]{:S(2)}, u32[]{:S(2)}) collective-permute-start(bf16[3,32,896]{2,1,0:T(8,128)(2,1)S(1)} %slice.9), channel_id=1, source_target_pairs={{0,32},{32,64},{64,96},{96,0},{1,33},{33,65},{65,97},{97,1},{2,34}... | collective-permute-start | bytes 516104 | tf_op jit(solution)/shard_map/ppermute | solution.py:323
  128.2 8.8 %copy-start.3 = (bf16[3,128,1792]{2,1,0:T(8,128)(2,1)}, bf16[3,128,1792]{2,1,0:T(8,128)(2,1)S(1)}, u32[]{:S(2)}) copy-start(bf16[3,128,1792]{2,1,0:T(8,128)(2,1)S(1)} %get-tuple-element.78.refs_0_) | copy-start | bytes 4128772
  135.1 3.8 %collective-permute-start.28 = (bf16[128,1024]{1,0:T(8,128)(2,1)S(1)}, bf16[128,1024]{1,0:T(8,128)(2,1)S(1)}, u32[]{:S(2)}, u32[]{:S(2)}) collective-permute-start(bf16[128,1024]{1,0:T(8,128)(2,1)S(1)} %get-tuple-element.73), channel_id=1, source_target_pairs={{0,16},{16,0},{1,17},{17,1},{2,18},{18,2},{3,19},{19,3},{4,20},{20... | collective-permute-start | bytes 786440 | tf_op jit(solution)/shard_map/ppermute | solution.py:242
  137.0 1.9 %collective-permute-start.29 = (bf16[128,1024]{1,0:T(8,128)(2,1)S(1)}, bf16[128,1024]{1,0:T(8,128)(2,1)S(1)}, u32[]{:S(2)}, u32[]{:S(2)}) collective-permute-start(bf16[128,1024]{1,0:T(8,128)(2,1)S(1)} %get-tuple-element.74), channel_id=1, source_target_pairs={{0,16},{16,0},{1,17},{17,1},{2,18},{18,2},{3,19},{19,3},{4,20},{20... | collective-permute-start | bytes 786440 | tf_op jit(solution)/shard_map/ppermute | solution.py:242
  140.5 10.4 %copy-start.6 = (bf16[16,16,512]{2,1,0:T(8,128)(2,1)S(1)}, bf16[16,16,512]{2,1,0:T(8,128)(2,1)}, u32[]{:S(2)}) copy-start(bf16[16,16,512]{2,1,0:T(8,128)(2,1)} %copy-done.5) | copy-start | bytes 786436
  140.5 34.1 %all-to-all-start.2 = ((bf16[16,32,1024]{2,1,0:T(8,128)(2,1)}), bf16[16,32,1024]{2,1,0:T(8,128)(2,1)S(1)}, u32[]{:S(2)}, u32[]{:S(2)}) async-start(bf16[16,32,1024]{2,1,0:T(8,128)(2,1)} %shard_map.129), calls=%async_computation.2 | async-start | bytes 2097152 | tf_op jit(solution)/shard_map/all_to_all | solution.py:370
  145.5 3.4 %collective-permute-start.30 = (bf16[3,128,1792]{2,1,0:T(8,128)(2,1)}, bf16[3,128,1792]{2,1,0:T(8,128)(2,1)S(1)}, u32[]{:S(2)}, u32[]{:S(2)}) collective-permute-start(bf16[3,128,1792]{2,1,0:T(8,128)(2,1)} %copy-done.3), channel_id=1, source_target_pairs={{0,16},{16,0},{1,17},{17,1},{2,18},{18,2},{3,19},{19,3},{4,20},{20... | collective-permute-start | bytes 4128776 | tf_op jit(solution)/shard_map/ppermute | solution.py:242
  145.6 5.3 %collective-permute-start.31 = (bf16[3,128,1792]{2,1,0:T(8,128)(2,1)S(1)}, bf16[3,128,1792]{2,1,0:T(8,128)(2,1)S(1)}, u32[]{:S(2)}, u32[]{:S(2)}) collective-permute-start(bf16[3,128,1792]{2,1,0:T(8,128)(2,1)S(1)} %get-tuple-element.79.acts.refs_1_), channel_id=1, source_target_pairs={{0,16},{16,0},{1,17},{17,1},{2,18},{18,2},{3,19},{19,3},{4,20},{20... | collective-permute-start | bytes 4128776 | tf_op jit(solution)/shard_map/ppermute | solution.py:242
  150.9 1.3 copy-start.4
  152.2 0.9 copy-start.8
